TPU v7x, 32 devices: a whole 2x2x4 slice. The times are simulated.
32 devices in a mesh: expert: 8 (over z, y), wshard: 4 (over x, core).
Axes of the slice: x: 2, y: 2, z: 4, core: 2. Of those that a mesh axis runs over, the one named last changes fastest.
Arguments:
- tokens: bfloat16 [4096, 2048], P(('expert', 'wshard')), may hold values from -6 to 6
- doc_lengths: int32 [32, 4], P(('expert', 'wshard')), may hold values from 1 to 64, 128 in all within a row
- expert_ids: int32 [4096, 8], P(('expert', 'wshard')), may hold values from 0 to 15, all different within a row; in each aligned block of 128 rows (0 to 127, 128 to 255, ...) at most 128 rows name the same one
- attn_gain: bfloat16 [2048], P('wshard'), may hold values from 0.5 to 1.5
- query_weight: bfloat16 [2048, 2048], P('wshard'), may hold values from -0.125 to 0.125
- key_weight: bfloat16 [2048, 2048], P('wshard'), may hold values from -0.125 to 0.125
- value_weight: bfloat16 [2048, 2048], P('wshard'), may hold values from -0.125 to 0.125
- query_gain: bfloat16 [2048], P('wshard'), may hold values from 0.5 to 1.5
- key_gain: bfloat16 [2048], P('wshard'), may hold values from 0.5 to 1.5
- output_weight: bfloat16 [2048, 2048], P('wshard'), may hold values from -0.5 to 0.5
- ffn_gain: bfloat16 [2048], P('wshard'), may hold values from 0.5 to 1.5
- router_weight: bfloat16 [2048, 16], P('wshard'), may hold values from -0.03125 to 0.03125
- gate_weight: bfloat16 [16, 2048, 1024], P('expert', 'wshard'), may hold values from -0.125 to 0.125
- up_weight: bfloat16 [16, 2048, 1024], P('expert', 'wshard'), may hold values from -0.125 to 0.125
- down_weight: bfloat16 [16, 1024, 2048], P('expert', None, 'wshard'), may hold values from -3 to 3
- cotangent: float32 [4096, 2048], P(('expert', 'wshard')), may hold values from -6 to 6
Outputs:
- block_output: float32 [4096, 2048], P(('expert', 'wshard'))
- tokens_grad: float32 [4096, 2048], P(('expert', 'wshard'))
- attn_gain_grad: float32 [2048], P(('expert', 'wshard'))
- query_weight_grad: float32 [2048, 2048], P(('expert', 'wshard'))
- key_weight_grad: float32 [2048, 2048], P(('expert', 'wshard'))
- value_weight_grad: float32 [2048, 2048], P(('expert', 'wshard'))
- query_gain_grad: float32 [2048], P(('expert', 'wshard'))
- key_gain_grad: float32 [2048], P(('expert', 'wshard'))
- output_weight_grad: float32 [2048, 2048], P(('expert', 'wshard'))
- ffn_gain_grad: float32 [2048], P(('expert', 'wshard'))
- router_weight_grad: float32 [2048, 16], P(('expert', 'wshard'))
- gate_weight_grad: float32 [16, 2048, 1024], P('expert', 'wshard')
- up_weight_grad: float32 [16, 2048, 1024], P('expert', 'wshard')
- down_weight_grad: float32 [16, 1024, 2048], P('expert', None, 'wshard')
Inputs may be any that keep to these rules, and one draw needn't show every extreme that they name: `doc_lengths`: each device's row of lengths sums to 128, and its largest length is half of 128. `expert_ids`: each token names 8 different experts; within the rows of one device no expert is named more than 128 times, and in every draw some device names some expert exactly 128 times.
All inputs are finite; a program needn't handle non-finite values.
Results may differ from a plain program's by a relative error of at most 0.017.
Values may be sent and summed in bfloat16 or wider, within the bound.
No kernel may reach another device: no remote copies, remote signals or barrier semaphores. Data moves between devices by JAX's collectives and lax.ppermute only.
A program may use at most 384 MiB of HBM per device.

v0:
```python
import jax
import jax.numpy as jnp
from jax import lax
from jax.sharding import PartitionSpec as P

HEADS = 16
HEAD_DIM = 128
TOP = 8
EXP_DEV = 2


epsilon = 1e-05
theta_base = 10000.0


def rms_forward(activation, gain):
    inverse = lax.rsqrt(jnp.mean(activation * activation, axis=-1, keepdims=True) + epsilon)
    normed = activation * inverse
    return (normed * gain.astype(jnp.float32), normed, inverse)


def rms_backward(grad_out, normed, inverse, gain):
    gain_grad = jnp.sum(grad_out * normed, axis=0)
    grad_normed = grad_out * gain.astype(jnp.float32)
    centred = grad_normed - normed * jnp.mean(grad_normed * normed, axis=-1, keepdims=True)
    return (inverse * centred, gain_grad)


def segment_info(doc_lengths, row_count):
    doc_ends = jnp.cumsum(doc_lengths)
    row_index = jnp.arange(row_count, dtype=jnp.int32)
    passed = (row_index[:, None] >= doc_ends[None, :]).astype(jnp.int32)
    doc_start = jnp.sum(passed * doc_lengths[None, :], axis=1)
    allowed = (row_index[None, :] <= row_index[:, None]) & (
        row_index[None, :] >= doc_start[:, None]
    )
    return (row_index - doc_start, allowed)


def rope_tables(offsets):
    half_dim = HEAD_DIM // 2
    frequency = theta_base ** (-2.0 * jnp.arange(half_dim, dtype=jnp.float32) / HEAD_DIM)
    angles = offsets.astype(jnp.float32)[:, None] * frequency[None, :]
    return (jnp.cos(angles)[:, None, :], jnp.sin(angles)[:, None, :])


def rotate(head_rows, cosine, sine_table):
    half_dim = HEAD_DIM // 2
    first_half = head_rows[..., :half_dim]
    second_half = head_rows[..., half_dim:]
    return jnp.concatenate(
        [
            first_half * cosine - second_half * sine_table,
            second_half * cosine + first_half * sine_table,
        ],
        axis=-1,
    )


def unrotate(head_grads, cosine, sine_table):
    half_dim = HEAD_DIM // 2
    first_half = head_grads[..., :half_dim]
    second_half = head_grads[..., half_dim:]
    return jnp.concatenate(
        [
            first_half * cosine + second_half * sine_table,
            second_half * cosine - first_half * sine_table,
        ],
        axis=-1,
    )


def masked_scores(queries, key_rows, allowed):
    scale_factor = HEAD_DIM ** (-0.5)
    scores = (
        jnp.einsum("qhd,khd->hqk", queries, key_rows, preferred_element_type=jnp.float32)
        * scale_factor
    )
    return jnp.where(allowed[None, :, :], scores, -1e30)


def attend_forward(queries, key_rows, value_rows, allowed):
    scores = masked_scores(queries, key_rows, allowed)
    row_max = jnp.max(scores, axis=-1, keepdims=True)
    log_total = row_max + jnp.log(jnp.sum(jnp.exp(scores - row_max), axis=-1, keepdims=True))
    probs_b = jnp.exp(scores - log_total).astype(jnp.bfloat16)
    mixed_heads = jnp.einsum(
        "hqk,khd->qhd", probs_b, value_rows, preferred_element_type=jnp.float32
    )
    return (mixed_heads.astype(jnp.bfloat16), log_total)


def attend_backward(queries, key_rows, value_rows, allowed, log_total, mixed_b, grad_b):
    scale_factor = HEAD_DIM ** (-0.5)
    probs = jnp.exp(masked_scores(queries, key_rows, allowed) - log_total)
    probs_b = probs.astype(jnp.bfloat16)
    delta_rows = jnp.sum(grad_b.astype(jnp.float32) * mixed_b.astype(jnp.float32), axis=-1)
    grad_probs = jnp.einsum("qhd,khd->hqk", grad_b, value_rows, preferred_element_type=jnp.float32)
    score_grad = (probs * (grad_probs - delta_rows.T[:, :, None])).astype(jnp.bfloat16)
    grad_queries = (
        jnp.einsum("hqk,khd->qhd", score_grad, key_rows, preferred_element_type=jnp.float32)
        * scale_factor
    )
    grad_keys = (
        jnp.einsum("hqk,qhd->khd", score_grad, queries, preferred_element_type=jnp.float32)
        * scale_factor
    )
    grad_values = jnp.einsum("hqk,qhd->khd", probs_b, grad_b, preferred_element_type=jnp.float32)
    return (grad_queries, grad_keys, grad_values)


def softmax_rows(logits):
    row_max = jnp.max(logits, axis=-1, keepdims=True)
    shifted = jnp.exp(logits - row_max)
    return shifted / jnp.sum(shifted, axis=-1, keepdims=True)


def expert_forward(arrived, gate_all, up_all):
    gate_lin = jnp.einsum("erd,edf->erf", arrived, gate_all, preferred_element_type=jnp.float32)
    up_lin = jnp.einsum("erd,edf->erf", arrived, up_all, preferred_element_type=jnp.float32)
    sigmoid_gate = jax.nn.sigmoid(gate_lin)
    swish = gate_lin * sigmoid_gate
    hidden_b = (swish * up_lin).astype(jnp.bfloat16)
    return (gate_lin, up_lin, sigmoid_gate, swish, hidden_b)


def local(
    tokens,
    doc_lengths,
    expert_ids,
    attn_gain,
    query_weight,
    key_weight,
    value_weight,
    query_gain,
    key_gain,
    output_weight,
    ffn_gain,
    router_weight,
    gate_weight,
    up_weight,
    down_weight,
    cotangent,
):
    row_count = tokens.shape[0]
    width = tokens.shape[1]
    owners = lax.axis_size("expert")
    expert_count = EXP_DEV * owners
    capacity = 2 * row_count * TOP // expert_count
    assign_total = row_count * TOP
    head_shape = (row_count, HEADS, HEAD_DIM)
    gathered = (
        lax.all_gather(attn_gain, "wshard", axis=0, tiled=True),
        lax.all_gather(query_weight, "wshard", axis=0, tiled=True),
        lax.all_gather(key_weight, "wshard", axis=0, tiled=True),
        lax.all_gather(value_weight, "wshard", axis=0, tiled=True),
        lax.all_gather(query_gain, "wshard", axis=0, tiled=True),
        lax.all_gather(key_gain, "wshard", axis=0, tiled=True),
        lax.all_gather(output_weight, "wshard", axis=0, tiled=True),
        lax.all_gather(ffn_gain, "wshard", axis=0, tiled=True),
        lax.all_gather(router_weight, "wshard", axis=0, tiled=True),
    )
    (
        attn_gain_all,
        query_all,
        key_all,
        value_all,
        query_gain_all,
        key_gain_all,
        output_all,
        ffn_gain_all,
        router_all,
    ) = gathered
    gate_all, up_all, down_all = (
        lax.all_gather(gate_weight, "wshard", axis=1, tiled=True),
        lax.all_gather(up_weight, "wshard", axis=1, tiled=True),
        lax.all_gather(down_weight, "wshard", axis=2, tiled=True),
    )
    residual = tokens.astype(jnp.float32)
    normed_in, unit_one, inverse_one = rms_forward(residual, attn_gain_all)
    attn_in = normed_in.astype(jnp.bfloat16)
    query_lin = jnp.dot(attn_in, query_all, preferred_element_type=jnp.float32)
    key_lin = jnp.dot(attn_in, key_all, preferred_element_type=jnp.float32)
    value_lin = jnp.dot(attn_in, value_all, preferred_element_type=jnp.float32)
    query_normed, query_unit, query_inverse = rms_forward(query_lin, query_gain_all)
    key_normed, key_unit, key_inverse = rms_forward(key_lin, key_gain_all)
    value_rows = value_lin.astype(jnp.bfloat16).reshape(head_shape)
    offsets, allowed = segment_info(doc_lengths[0], row_count)
    cosine, sine_table = rope_tables(offsets)
    queries = rotate(query_normed.reshape(head_shape), cosine, sine_table).astype(jnp.bfloat16)
    key_rows = rotate(key_normed.reshape(head_shape), cosine, sine_table).astype(jnp.bfloat16)
    mixed_b, log_total = attend_forward(queries, key_rows, value_rows, allowed)
    attn_mix = mixed_b.reshape(row_count, width)
    middle = residual + jnp.dot(attn_mix, output_all, preferred_element_type=jnp.float32)
    ffn_normed, unit_two, inverse_two = rms_forward(middle, ffn_gain_all)
    ffn_in = ffn_normed.astype(jnp.bfloat16)
    router_probs = softmax_rows(jnp.dot(ffn_in, router_all, preferred_element_type=jnp.float32))
    expert_range = jnp.arange(expert_count, dtype=jnp.int32)
    hot_table = (expert_ids[:, :, None] == expert_range[None, None, :]).astype(jnp.float32)
    route_weights = jnp.sum(hot_table * router_probs[:, None, :], axis=2)
    flat_ids = expert_ids.reshape(-1)
    one_hot = (flat_ids[:, None] == expert_range[None, :]).astype(jnp.int32)
    earlier = jnp.cumsum(one_hot, axis=0) - one_hot
    slot_index = jnp.sum(earlier * one_hot, axis=1)
    slot_place = (flat_ids % EXP_DEV * owners + flat_ids // EXP_DEV) * capacity + slot_index
    slot_table = jnp.full((expert_count * capacity,), assign_total, dtype=jnp.int32)
    slot_table = slot_table.at[slot_place].set(jnp.arange(assign_total, dtype=jnp.int32))
    occupied = slot_table < assign_total
    safe_assign = jnp.where(occupied, slot_table, 0)
    send_shape = (EXP_DEV, owners * capacity, width)
    send_rows = jnp.where(
        occupied[:, None], ffn_in[safe_assign // TOP], jnp.zeros((), jnp.bfloat16)
    ).reshape(send_shape)
    arrived = lax.all_to_all(send_rows, "expert", split_axis=1, concat_axis=1, tiled=True)
    gate_lin, up_lin, sigmoid_gate, swish, hidden_b = expert_forward(arrived, gate_all, up_all)
    expert_out = jnp.einsum(
        "erf,efd->erd", hidden_b, down_all, preferred_element_type=jnp.float32
    ).astype(jnp.bfloat16)
    returned = lax.all_to_all(
        expert_out, "expert", split_axis=1, concat_axis=1, tiled=True
    ).reshape(expert_count * capacity, width)
    assign_out = returned[slot_place].astype(jnp.float32).reshape(row_count, TOP, width)
    block_output = middle + jnp.sum(assign_out * route_weights[:, :, None], axis=1)
    out_grad = (
        (route_weights[:, :, None] * cotangent[:, None, :])
        .astype(jnp.bfloat16)
        .reshape(assign_total, width)
    )
    route_grad = jnp.sum(assign_out * cotangent[:, None, :], axis=2)
    send_grads = jnp.where(
        occupied[:, None], out_grad[safe_assign], jnp.zeros((), jnp.bfloat16)
    ).reshape(send_shape)
    arrived_grad = lax.all_to_all(send_grads, "expert", split_axis=1, concat_axis=1, tiled=True)
    hidden_grad = jnp.einsum(
        "erd,efd->erf", arrived_grad, down_all, preferred_element_type=jnp.float32
    )
    down_grad_local = jnp.einsum(
        "erf,erd->efd", hidden_b, arrived_grad, preferred_element_type=jnp.float32
    )
    gate_grad_b = (
        hidden_grad * up_lin * sigmoid_gate * (1.0 + gate_lin * (1.0 - sigmoid_gate))
    ).astype(jnp.bfloat16)
    up_grad_b = (hidden_grad * swish).astype(jnp.bfloat16)
    gate_grad_local = jnp.einsum(
        "erd,erf->edf", arrived, gate_grad_b, preferred_element_type=jnp.float32
    )
    up_grad_local = jnp.einsum(
        "erd,erf->edf", arrived, up_grad_b, preferred_element_type=jnp.float32
    )
    arrived_back = jnp.einsum(
        "erf,edf->erd", gate_grad_b, gate_all, preferred_element_type=jnp.float32
    )
    arrived_back = (
        arrived_back
        + jnp.einsum("erf,edf->erd", up_grad_b, up_all, preferred_element_type=jnp.float32)
    ).astype(jnp.bfloat16)
    back_rows = lax.all_to_all(
        arrived_back, "expert", split_axis=1, concat_axis=1, tiled=True
    ).reshape(expert_count * capacity, width)
    row_grads = jnp.sum(
        back_rows[slot_place].astype(jnp.float32).reshape(row_count, TOP, width), axis=1
    )
    gate_weight_grad, up_weight_grad, down_weight_grad = (
        lax.psum_scatter(
            gate_grad_local.astype(jnp.bfloat16), "wshard", scatter_dimension=1, tiled=True
        ).astype(jnp.float32),
        lax.psum_scatter(
            up_grad_local.astype(jnp.bfloat16), "wshard", scatter_dimension=1, tiled=True
        ).astype(jnp.float32),
        lax.psum_scatter(
            down_grad_local.astype(jnp.bfloat16), "wshard", scatter_dimension=2, tiled=True
        ).astype(jnp.float32),
    )
    prob_grad = jnp.sum(hot_table * route_grad[:, :, None], axis=1)
    logit_grad = router_probs * (
        prob_grad - jnp.sum(router_probs * prob_grad, axis=1, keepdims=True)
    )
    logit_grad_b = logit_grad.astype(jnp.bfloat16)
    ffn_in_grad = row_grads + jnp.dot(
        logit_grad_b, router_all.T, preferred_element_type=jnp.float32
    )
    middle_part, ffn_gain_grad = rms_backward(ffn_in_grad, unit_two, inverse_two, ffn_gain_all)
    middle_grad = cotangent + middle_part
    middle_grad_b = middle_grad.astype(jnp.bfloat16)
    attn_mix_grad = jnp.dot(middle_grad_b, output_all.T, preferred_element_type=jnp.float32).astype(
        jnp.bfloat16
    )
    grad_queries, grad_keys, grad_values = attend_backward(
        queries,
        key_rows,
        value_rows,
        allowed,
        log_total,
        mixed_b,
        attn_mix_grad.reshape(head_shape),
    )
    query_rot_grad = unrotate(grad_queries, cosine, sine_table).reshape(row_count, width)
    key_rot_grad = unrotate(grad_keys, cosine, sine_table).reshape(row_count, width)
    query_lin_grad, query_gain_grad = rms_backward(
        query_rot_grad, query_unit, query_inverse, query_gain_all
    )
    key_lin_grad, key_gain_grad = rms_backward(key_rot_grad, key_unit, key_inverse, key_gain_all)
    query_grad_b = query_lin_grad.astype(jnp.bfloat16)
    key_grad_b = key_lin_grad.astype(jnp.bfloat16)
    value_grad_b = grad_values.reshape(row_count, width).astype(jnp.bfloat16)
    attn_in_grad = jnp.dot(query_grad_b, query_all.T, preferred_element_type=jnp.float32)
    attn_in_grad = attn_in_grad + jnp.dot(key_grad_b, key_all.T, preferred_element_type=jnp.float32)
    attn_in_grad = attn_in_grad + jnp.dot(
        value_grad_b, value_all.T, preferred_element_type=jnp.float32
    )
    input_part, attn_gain_grad = rms_backward(attn_in_grad, unit_one, inverse_one, attn_gain_all)
    tokens_grad = middle_grad + input_part
    mixer_terms = (
        attn_gain_grad,
        jnp.dot(attn_in.T, query_grad_b, preferred_element_type=jnp.float32),
        jnp.dot(attn_in.T, key_grad_b, preferred_element_type=jnp.float32),
        jnp.dot(attn_in.T, value_grad_b, preferred_element_type=jnp.float32),
        query_gain_grad,
        key_gain_grad,
        jnp.dot(attn_mix.T, middle_grad_b, preferred_element_type=jnp.float32),
        ffn_gain_grad,
        jnp.dot(ffn_in.T, logit_grad_b, preferred_element_type=jnp.float32),
    )
    reduced = (
        lax.psum_scatter(mixer_terms[0], ("expert", "wshard"), scatter_dimension=0, tiled=True),
        lax.psum_scatter(mixer_terms[1], ("expert", "wshard"), scatter_dimension=0, tiled=True),
        lax.psum_scatter(mixer_terms[2], ("expert", "wshard"), scatter_dimension=0, tiled=True),
        lax.psum_scatter(mixer_terms[3], ("expert", "wshard"), scatter_dimension=0, tiled=True),
        lax.psum_scatter(mixer_terms[4], ("expert", "wshard"), scatter_dimension=0, tiled=True),
        lax.psum_scatter(mixer_terms[5], ("expert", "wshard"), scatter_dimension=0, tiled=True),
        lax.psum_scatter(mixer_terms[6], ("expert", "wshard"), scatter_dimension=0, tiled=True),
        lax.psum_scatter(mixer_terms[7], ("expert", "wshard"), scatter_dimension=0, tiled=True),
        lax.psum_scatter(mixer_terms[8], ("expert", "wshard"), scatter_dimension=0, tiled=True),
    )
    (
        attn_gain_out,
        query_weight_out,
        key_weight_out,
        value_weight_out,
        query_gain_out,
        key_gain_out,
        output_weight_out,
        ffn_gain_out,
        router_weight_out,
    ) = reduced
    return (
        block_output,
        tokens_grad,
        attn_gain_out,
        query_weight_out,
        key_weight_out,
        value_weight_out,
        query_gain_out,
        key_gain_out,
        output_weight_out,
        ffn_gain_out,
        router_weight_out,
        gate_weight_grad,
        up_weight_grad,
        down_weight_grad,
    )


def solution(mesh):
    in_specs = (
        P(("expert", "wshard"), None),
        P(("expert", "wshard"), None),
        P(("expert", "wshard"), None),
        P("wshard"),
        P("wshard", None),
        P("wshard", None),
        P("wshard", None),
        P("wshard"),
        P("wshard"),
        P("wshard", None),
        P("wshard"),
        P("wshard", None),
        P("expert", "wshard", None),
        P("expert", "wshard", None),
        P("expert", None, "wshard"),
        P(("expert", "wshard"), None),
    )
    out_specs = (
        P(("expert", "wshard"), None),
        P(("expert", "wshard"), None),
        P(("expert", "wshard")),
        P(("expert", "wshard"), None),
        P(("expert", "wshard"), None),
        P(("expert", "wshard"), None),
        P(("expert", "wshard")),
        P(("expert", "wshard")),
        P(("expert", "wshard"), None),
        P(("expert", "wshard")),
        P(("expert", "wshard"), None),
        P("expert", "wshard", None),
        P("expert", "wshard", None),
        P("expert", None, "wshard"),
    )
    return jax.shard_map(local, mesh=mesh, in_specs=in_specs, out_specs=out_specs, check_vma=False)
```

profile of v0, /device:TPU:13, one launch (start us, length us, event | category | flops | bytes accessed | tf_op | source)
XLA Modules:
  0.0 2095.4 jit_solution(12383428971815660097)
XLA Ops:
  49.9 20.1 all-gather.16.cloned.1.call-done
  76.1 53.7 %all-gather.14.cloned.1.call-done = bf16[2048,2048]{1,0:T(8,128)(2,1)} async-done(((bf16[512,2048]{1,0:T(8,128)(2,1)}), bf16[2048,2048]{1,0:T(8,128)(2,1)}) %all-gather.14.cloned.1.call-update) | async-done | bytes 8388624 | tf_op jit(solution)/shard_map/all_gather | solution.py:154
  139.8 49.9 %all-gather.12.cloned.1.call-done = bf16[2048,2048]{1,0:T(8,128)(2,1)} async-done(((bf16[512,2048]{1,0:T(8,128)(2,1)}), bf16[2048,2048]{1,0:T(8,128)(2,1)}) %all-gather.12.cloned.1.call-update) | async-done | bytes 8388624 | tf_op jit(solution)/shard_map/all_gather | solution.py:156
  195.6 53.8 %all-gather.18.cloned.1.call-done = bf16[2048,2048]{1,0:T(8,128)(2,1)} async-done(((bf16[512,2048]{1,0:T(8,128)(2,1)}), bf16[2048,2048]{1,0:T(8,128)(2,1)}) %all-gather.18.cloned.1.call-update) | async-done | bytes 8388624 | tf_op jit(solution)/shard_map/all_gather | solution.py:159
  270.5 19.1 gather_fusion.2
  289.6 31.5 %broadcast_select_fusion = (bf16[2,1024,2048]{2,0,1:T(2,128)(2,1)}, bf16[2,1024,2048]{2,0,1:T(2,128)(2,1)}) fusion(pred[2,1024]{0,1:T(8,128)(4,1)S(1)} %copy.215, bf16[2,1024,2048]{2,1,0:T(8,128)(2,1)} %bitcast.143, bf16[2,1024,2048]{2,1,0:T(8,128)(2,1)} %bitcast.142), kind=kLoop, calls=%fused_computation.6 | loop fusion | flops 8388608 | bytes 33556480 | tf_op jit(solution)/shard_map/jit(_where)/select_n | solution.py:230
  327.1 180.0 %all-to-all-done = bf16[2,1024,2048]{2,0,1:T(2,128)(2,1)} async-done(((bf16[2,1024,2048]{2,0,1:T(2,128)(2,1)}), bf16[2,1024,2048]{2,0,1:T(2,128)(2,1)}, u32[]{:S(2)}, u32[]{:S(2)}) %all-to-all-start) | async-done | bytes 8388640 | tf_op jit(solution)/shard_map/all_to_all | solution.py:214
  514.9 21.5 %copy.241 = bf16[2,1024,2048]{1,2,0:T(8,128)(2,1)} copy(bf16[2,1024,2048]{2,0,1:T(2,128)(2,1)} %all-to-all-done) | data formatting | bytes 16777216 | tf_op jit(solution)/shard_map/all_to_all | solution.py:214
  536.4 15.7 fusion.73
  552.0 15.7 fusion.74
  576.2 118.5 %all-to-all-done.2 = bf16[2,1024,2048]{2,0,1:T(2,128)(2,1)} async-done(((bf16[2,1024,2048]{2,0,1:T(2,128)(2,1)}), bf16[2,1024,2048]{2,0,1:T(2,128)(2,1)}, u32[]{:S(2)}, u32[]{:S(2)}) %all-to-all-start.2) | async-done | bytes 8388640 | tf_op jit(solution)/shard_map/all_to_all | solution.py:233
  694.7 24.5 %multiply_convert_fusion = (bf16[2,1024,1024]{2,1,0:T(8,128)(2,1)}, bf16[2,1024,1024]{2,1,0:T(8,128)(2,1)}, bf16[2,1024,1024]{2,1,0:T(8,128)(2,1)}) fusion(f32[2,1024,1024]{2,1,0:T(8,128)} %fusion.73, f32[2,1024,1024]{2,1,0:T(8,128)} %fusion.74, bf16[2,1024,2048]{2,1,0:T(8,128)(2,1)} %all-gather.24.cloned.1.call-done, bf16[2,1024,2048]{2,0,1:T(2,128)(2,1)} %all-to-all-done.2), kind=kOutput, calls=%fused_computation.15 | convolution fusion | flops 8621391872 | bytes 46137344 | tf_op jit(solution)/shard_map/erd,efd->erf/dot_general | solution.py:234
  732.3 24.9 %copy.219 = bf16[2,1024,2048]{2,0,1:T(2,128)(2,1)} copy(bf16[2,1024,2048]{2,1,0:T(8,128)(2,1)S(1)} %convolution_convert_fusion.2) | data formatting | bytes 16777216 | tf_op jit(solution)/shard_map/convert_element_type | solution.py:218
  764.2 179.8 %all-to-all-done.1 = bf16[2,1024,2048]{2,0,1:T(2,128)(2,1)} async-done(((bf16[2,1024,2048]{2,0,1:T(2,128)(2,1)}), bf16[2,1024,2048]{2,0,1:T(2,128)(2,1)}, u32[]{:S(2)}, u32[]{:S(2)}) %all-to-all-start.1) | async-done | bytes 8388640 | tf_op jit(solution)/shard_map/all_to_all | solution.py:219
  1004.6 15.9 fusion.75
  1020.6 17.0 add_convert_fusion
  1037.6 16.4 copy.225
  1061.2 19.7 fusion.8
  1081.0 160.3 %all-to-all-done.3 = bf16[2,1024,2048]{2,0,1:T(2,128)(2,1)} async-done(((bf16[2,1024,2048]{2,0,1:T(2,128)(2,1)}), bf16[2,1024,2048]{2,0,1:T(2,128)(2,1)}, u32[]{:S(2)}, u32[]{:S(2)}) %all-to-all-start.3) | async-done | bytes 8388640 | tf_op jit(solution)/shard_map/all_to_all | solution.py:257
  1351.8 45.1 %all-reduce.4 = (f32[2048]{0:T(1024)S(1)}, f32[2048]{0:T(1024)S(1)}, f32[2048]{0:T(1024)S(1)}, f32[2048]{0:T(1024)S(1)}) all-reduce(f32[2048]{0:T(1024)S(1)} %get-tuple-element.22, f32[2048]{0:T(1024)S(1)} %get-tuple-element.20, f32[2048]{0:T(1024)S(1)} %get-tuple-element.18, ...), channel_id=2, replica_groups=mesh['expert'=8,'wshard'=4] {'expert','wshard'}, use_global_device_ids=true, to_apply=%region_26.27.clone | all-reduce | flops 8192 | bytes 65536
  1415.7 110.2 %reduce-scatter.17.cloned.1.call-done = f32[64,2048]{1,0:T(8,128)} async-done(((f32[2048,2048]{1,0:T(8,128)}), f32[64,2048]{1,0:T(8,128)}) %reduce-scatter.17.cloned.1.call-update) | async-done | bytes 524304 | tf_op jit(solution)/shard_map/reduce_scatter | solution.py:331
  1526.0 187.9 %reduce-scatter.15.cloned.1.call-done = f32[64,2048]{1,0:T(8,128)} async-done(((f32[2048,2048]{1,0:T(8,128)}), f32[64,2048]{1,0:T(8,128)}) %reduce-scatter.15.cloned.1.call-update) | async-done | bytes 524304 | tf_op jit(solution)/shard_map/reduce_scatter | solution.py:328
  1713.9 187.4 %reduce-scatter.13.cloned.1.call-done = f32[64,2048]{1,0:T(8,128)} async-done(((f32[2048,2048]{1,0:T(8,128)}), f32[64,2048]{1,0:T(8,128)}) %reduce-scatter.13.cloned.1.call-update) | async-done | bytes 524304 | tf_op jit(solution)/shard_map/reduce_scatter | solution.py:327
  1901.3 187.4 %reduce-scatter.11.cloned.1.call-done = f32[64,2048]{1,0:T(8,128)} async-done(((f32[2048,2048]{1,0:T(8,128)}), f32[64,2048]{1,0:T(8,128)}) %reduce-scatter.11.cloned.1.call-update) | async-done | bytes 524304 | tf_op jit(solution)/shard_map/reduce_scatter | solution.py:326
  (300 shorter events, 324.2 us)
Async XLA Ops:
  7.3 62.7 %all-gather.16.cloned.1.call-start = ((), (), s32[]{:S(2)}) async-start(), calls=%async_computation.14 | async-start | bytes 10485760 | tf_op jit(solution)/shard_map/all_gather | solution.py:155
  8.0 121.8 %all-gather.14.cloned.1.call-start = ((), (), s32[]{:S(2)}) async-start(), calls=%async_computation.13 | async-start | bytes 10485760 | tf_op jit(solution)/shard_map/all_gather | solution.py:154
  8.7 180.9 %all-gather.12.cloned.1.call-start = ((), (), s32[]{:S(2)}) async-start(), calls=%async_computation.12 | async-start | bytes 10485760 | tf_op jit(solution)/shard_map/all_gather | solution.py:156
  9.5 239.9 %all-gather.18.cloned.1.call-start = ((), (), s32[]{:S(2)}) async-start(), calls=%async_computation.15 | async-start | bytes 10485760 | tf_op jit(solution)/shard_map/all_gather | solution.py:159
  10.1 526.3 %all-gather.20.cloned.1.call-start = ((), (), s32[]{:S(2)}) async-start(), calls=%async_computation.16 | async-start | bytes 10485760 | tf_op jit(solution)/shard_map/all_gather | solution.py:175
  26.7 163.0 %copy-start.27 = (f32[4,1,512]{2,1,0:T(1,128)}, f32[4,1,512]{2,1,0:T(1,128)S(1)}, u32[]{:S(2)}) copy-start(f32[4,1,512]{2,1,0:T(1,128)S(1)} %convert_element_type.187) | copy-start | bytes 24580
  26.9 162.8 %copy-start.47 = (f32[128]{0:T(128)}, f32[128]{0:T(128)S(1)}, u32[]{:S(2)}) copy-start(f32[128]{0:T(128)S(1)} %add_rsqrt_fusion.3) | copy-start | bytes 1540
  37.7 96.9 %copy-start.41 = (f32[4,1,512]{2,1,0:T(1,128)}, f32[4,1,512]{2,1,0:T(1,128)S(1)}, u32[]{:S(2)}) copy-start(f32[4,1,512]{2,1,0:T(1,128)S(1)} %convert_element_type.188) | copy-start | bytes 24580
  43.1 211.1 %copy-start.45 = (f32[4,1,512]{2,1,0:T(1,128)}, f32[4,1,512]{2,1,0:T(1,128)S(1)}, u32[]{:S(2)}) copy-start(f32[4,1,512]{2,1,0:T(1,128)S(1)} %convert_element_type.190) | copy-start | bytes 24580
  49.3 206.0 %copy-start.35 = (bf16[2048,16]{0,1:T(8,128)(2,1)}, bf16[2048,16]{0,1:T(8,128)(2,1)S(1)}, u32[]{:S(2)}) copy-start(bf16[2048,16]{0,1:T(8,128)(2,1)S(1)} %all_gather.47) | copy-start | bytes 196612
  321.1 186.0 %all-to-all-start = ((bf16[2,1024,2048]{2,0,1:T(2,128)(2,1)}), bf16[2,1024,2048]{2,0,1:T(2,128)(2,1)}, u32[]{:S(2)}, u32[]{:S(2)}) async-start(bf16[2,1024,2048]{2,0,1:T(2,128)(2,1)} %get-tuple-element.48), calls=%async_computation | async-start | bytes 16777216 | tf_op jit(solution)/shard_map/all_to_all | solution.py:214
  326.6 225.5 %all-gather.22.cloned.1.call-start = ((), (), s32[]{:S(2)}) async-start(), calls=%async_computation.17 | async-start | bytes 10485760 | tf_op jit(solution)/shard_map/all_gather | solution.py:176
  507.1 187.6 %all-to-all-start.2 = ((bf16[2,1024,2048]{2,0,1:T(2,128)(2,1)}), bf16[2,1024,2048]{2,0,1:T(2,128)(2,1)}, u32[]{:S(2)}, u32[]{:S(2)}) async-start(bf16[2,1024,2048]{2,0,1:T(2,128)(2,1)} %get-tuple-element.47), calls=%async_computation.2 | async-start | bytes 16777216 | tf_op jit(solution)/shard_map/all_to_all | solution.py:233
  514.2 62.0 %all-gather.24.cloned.1.call-start = ((), (), s32[]{:S(2)}) async-start(), calls=%async_computation.18 | async-start | bytes 10485760 | tf_op jit(solution)/shard_map/all_gather | solution.py:177
  757.2 186.8 %all-to-all-start.1 = ((bf16[2,1024,2048]{2,0,1:T(2,128)(2,1)}), bf16[2,1024,2048]{2,0,1:T(2,128)(2,1)}, u32[]{:S(2)}, u32[]{:S(2)}) async-start(bf16[2,1024,2048]{2,0,1:T(2,128)(2,1)} %copy.219), calls=%async_computation.1 | async-start | bytes 16777216 | tf_op jit(solution)/shard_map/all_to_all | solution.py:219
  763.8 638.1 %reduce-scatter.25.cloned.1.call-start = ((), (), s32[]{:S(2)}) async-start(), calls=%async_computation.26 | async-start | bytes 1081344
  975.3 428.0 %reduce-scatter.19.cloned.1.call-start = ((), (), s32[]{:S(2)}) async-start(), calls=%async_computation.23 | async-start | bytes 10485760 | tf_op jit(solution)/shard_map/reduce_scatter | solution.py:264
  989.9 417.5 %reduce-scatter.21.cloned.1.call-start = ((), (), s32[]{:S(2)}) async-start(), calls=%async_computation.24 | async-start | bytes 10485760 | tf_op jit(solution)/shard_map/reduce_scatter | solution.py:267
  1054.0 187.3 %all-to-all-start.3 = ((bf16[2,1024,2048]{2,0,1:T(2,128)(2,1)}), bf16[2,1024,2048]{2,0,1:T(2,128)(2,1)}, u32[]{:S(2)}, u32[]{:S(2)}) async-start(bf16[2,1024,2048]{2,0,1:T(2,128)(2,1)} %copy.225), calls=%async_computation.3 | async-start | bytes 16777216 | tf_op jit(solution)/shard_map/all_to_all | solution.py:257
  1061.0 350.5 %reduce-scatter.23.cloned.1.call-start = ((), (), s32[]{:S(2)}) async-start(), calls=%async_computation.25 | async-start | bytes 10485760 | tf_op jit(solution)/shard_map/reduce_scatter | solution.py:270
  1081.0 445.0 %reduce-scatter.17.cloned.1.call-start = ((), (), s32[]{:S(2)}) async-start(), calls=%async_computation.22 | async-start | bytes 17301504 | tf_op jit(solution)/shard_map/reduce_scatter | solution.py:331
  1283.4 430.5 %reduce-scatter.15.cloned.1.call-start = ((), (), s32[]{:S(2)}) async-start(), calls=%async_computation.21 | async-start | bytes 17301504 | tf_op jit(solution)/shard_map/reduce_scatter | solution.py:328
  1303.6 597.7 %reduce-scatter.13.cloned.1.call-start = ((), (), s32[]{:S(2)}) async-start(), calls=%async_computation.20 | async-start | bytes 17301504 | tf_op jit(solution)/shard_map/reduce_scatter | solution.py:327
  1321.3 767.4 %reduce-scatter.11.cloned.1.call-start = ((), (), s32[]{:S(2)}) async-start(), calls=%async_computation.19 | async-start | bytes 17301504 | tf_op jit(solution)/shard_map/reduce_scatter | solution.py:326
  (66 other events, 1047.5 us)
Sparse Core Ops, SparseCore 0:
  9.6 60.3 all-gather.15
  71.5 58.2 all-gather.13
  131.4 58.2 all-gather.11
  191.1 58.2 all-gather.17
  250.8 58.2 all-gather.19
  328.6 58.7 all-gather.21
  516.5 59.6 all-gather.23
  975.5 128.3 reduce-scatter.24
  1106.5 82.7 reduce-scatter.18
  1191.7 71.4 reduce-scatter.20
  1265.7 71.2 reduce-scatter.22
  1339.7 186.2 reduce-scatter.16
  1528.9 185.0 reduce-scatter.14
  1716.6 184.6 reduce-scatter.12
  1904.0 184.6 reduce-scatter.10
where the time goes:
time: 2100 us
  waiting for transfers between devices  1500 us (71%)
  matrix products  239 us (11%)
  local copies, waits for them, and re-layouts  161 us (8%)
  other arithmetic  77.4 us (4%)
  blocking collectives  73.2 us (3%)
  starting transfers between devices  27.7 us (1%)
    reduce_scatter x1, waiting for transfers between devices, local(): lax.psum_scatter(mixer_terms[3], ('expert', 'wshard'), scatter_dimension=...  188 us
    reduce_scatter x1, waiting for transfers between devices, local(): lax.psum_scatter(mixer_terms[2], ('expert', 'wshard'), scatter_dimension=...  187 us
    reduce_scatter x1, waiting for transfers between devices, local(): lax.psum_scatter(mixer_terms[1], ('expert', 'wshard'), scatter_dimension=...  187 us
    all_to_all x1, waiting for transfers between devices, local(): lax.all_to_all(send_rows, 'expert', split_axis=1, concat_axis=1, tiled=True)  180 us
    all_to_all x1, waiting for transfers between devices, local(): lax.all_to_all(expert_out, 'expert', split_axis=1, concat_axis=1, tiled=T...  180 us
    all_to_all x1, waiting for transfers between devices, local(): lax.all_to_all(arrived_back, 'expert', split_axis=1, concat_axis=1, tiled...  160 us
    all_to_all x1, waiting for transfers between devices, local(): lax.all_to_all(send_grads, 'expert', split_axis=1, concat_axis=1, tiled=T...  118 us
    reduce_scatter x1, waiting for transfers between devices, local(): lax.psum_scatter(mixer_terms[6], ('expert', 'wshard'), scatter_dimension=...  110 us
  transfers between devices with their start and end apart: 19, of which 13 were waited for; matrix products, arithmetic and copies ran while one was open for 18% of the time, Pallas kernels for 0%

commit v1 on v0

v1 whole, which is shorter than its diff:
```python
import jax
import jax.numpy as jnp
from jax import lax
from jax.sharding import PartitionSpec as P

HEADS = 16
HEAD_DIM = 128
TOP = 8
EXP_DEV = 2


epsilon = 1e-05
theta_base = 10000.0


def rms_unit(activation):
    inverse = lax.rsqrt(jnp.mean(activation * activation, axis=-1, keepdims=True) + epsilon)
    return (activation * inverse, inverse)


def rms_backward(grad_out, normed, inverse, gain):
    gain_grad = jnp.sum(grad_out * normed, axis=0)
    grad_normed = grad_out * gain
    centred = grad_normed - normed * jnp.mean(grad_normed * normed, axis=-1, keepdims=True)
    return (inverse * centred, gain_grad)


def block_tables(lengths, rows):
    ends = jnp.cumsum(lengths, axis=1)
    row_index = jnp.arange(rows, dtype=jnp.int32)
    passed = (row_index[None, :, None] >= ends[:, None, :]).astype(jnp.int32)
    start = jnp.sum(passed * lengths[:, None, :], axis=2)
    allowed = (row_index[None, None, :] <= row_index[None, :, None]) & (
        row_index[None, None, :] >= start[:, :, None]
    )
    offsets = (row_index[None, :] - start).reshape(-1)
    half_dim = HEAD_DIM // 2
    frequency = theta_base ** (-2.0 * jnp.arange(half_dim, dtype=jnp.float32) / HEAD_DIM)
    angles = offsets.astype(jnp.float32)[:, None] * frequency[None, :]
    return (allowed, jnp.cos(angles), jnp.sin(angles))


def rotate(rows, cosine, sine):
    half_dim = HEAD_DIM // 2
    first = rows[..., :half_dim]
    second = rows[..., half_dim:]
    cosine = cosine[:, None, :]
    sine = sine[:, None, :]
    return jnp.concatenate([first * cosine - second * sine, second * cosine + first * sine], axis=-1)


def softmax_rows(logits):
    row_max = jnp.max(logits, axis=-1, keepdims=True)
    shifted = jnp.exp(logits - row_max)
    return shifted / jnp.sum(shifted, axis=-1, keepdims=True)


def dot(a, b):
    return jnp.dot(a, b, preferred_element_type=jnp.float32)


def dot_t(a, b):
    return lax.dot_general(a, b, (((1,), (1,)), ((), ())), preferred_element_type=jnp.float32)


def t_dot(a, b):
    return lax.dot_general(a, b, (((0,), (0,)), ((), ())), preferred_element_type=jnp.float32)


def group_sum(values, axis_name):
    return jnp.sum(lax.all_gather(values, axis_name, axis=0), axis=0)


def local(
    tokens,
    doc_lengths,
    expert_ids,
    attn_gain,
    query_weight,
    key_weight,
    value_weight,
    query_gain,
    key_gain,
    output_weight,
    ffn_gain,
    router_weight,
    gate_weight,
    up_weight,
    down_weight,
    cotangent,
):
    bf16 = jnp.bfloat16
    f32 = jnp.float32
    rows, width = tokens.shape
    owners = lax.axis_size("expert")
    parts = lax.axis_size("wshard")
    w_index = lax.axis_index("wshard")
    experts = EXP_DEV * owners
    group = parts * rows
    cols = width // parts
    heads = HEADS // parts
    ff = gate_weight.shape[2]

    tokens_all = lax.all_gather(tokens, "wshard", axis=0, tiled=True)
    docs = doc_lengths.shape[1]
    lengths_row = jnp.zeros((1, cols), bf16).at[:, :docs].set(doc_lengths.astype(bf16))
    small = jnp.concatenate(
        [attn_gain[None, :], ffn_gain[None, :], lengths_row, router_weight.T], axis=0
    )
    small_all = lax.all_gather(small, "wshard", axis=0)
    attn_gain_all = small_all[:, 0, :].reshape(width).astype(f32)
    ffn_gain_all = small_all[:, 1, :].reshape(width).astype(f32)
    lengths_all = small_all[:, 2, :docs].astype(jnp.int32)
    router_t = small_all[:, 3:, :].transpose(1, 0, 2).reshape(experts, width)
    qkv_send = jnp.stack(
        [
            weight.reshape(cols, parts, cols)
            for weight in (query_weight, key_weight, value_weight)
        ],
        axis=2,
    )
    qkv_send = qkv_send.transpose(1, 0, 2, 3).reshape(parts * cols, 3 * cols)
    qkv_w = lax.all_to_all(qkv_send, "wshard", split_axis=0, concat_axis=0, tiled=True)

    gate_all = lax.all_gather(gate_weight, "wshard", axis=1, tiled=True)
    up_all = lax.all_gather(up_weight, "wshard", axis=1, tiled=True)
    down_all = lax.all_gather(down_weight, "wshard", axis=2, tiled=True)
    cot_all = lax.all_gather(cotangent.astype(bf16), "expert", axis=0, tiled=True)

    unit_all, _ = rms_unit(tokens_all.astype(f32))
    attn_in = (unit_all * attn_gain_all).astype(bf16)
    qkv = dot(attn_in, qkv_w)
    query_lin, key_lin, value_lin = (qkv[:, i * cols : (i + 1) * cols] for i in range(3))
    squares = jnp.stack(
        [jnp.sum(query_lin * query_lin, axis=1), jnp.sum(key_lin * key_lin, axis=1)], axis=0
    )
    squares = group_sum(squares, "wshard")
    inverses = lax.rsqrt(squares / width + epsilon)
    query_inverse = inverses[0][:, None]
    key_inverse = inverses[1][:, None]
    query_unit = query_lin * query_inverse
    key_unit = key_lin * key_inverse
    query_gain_f = query_gain.astype(f32)
    key_gain_f = key_gain.astype(f32)
    allowed, cosine, sine = block_tables(lengths_all, rows)
    wide = (group, heads, HEAD_DIM)
    blocked = (parts, rows, heads, HEAD_DIM)
    queries = rotate((query_unit * query_gain_f).reshape(wide), cosine, sine).astype(bf16)
    queries = queries.reshape(blocked)
    keys = rotate((key_unit * key_gain_f).reshape(wide), cosine, sine).astype(bf16)
    keys = keys.reshape(blocked)
    values = value_lin.astype(bf16).reshape(blocked)
    scale = HEAD_DIM ** (-0.5)
    scores = jnp.einsum("bqhd,bkhd->bhqk", queries, keys, preferred_element_type=f32) * scale
    scores = jnp.where(allowed[:, None, :, :], scores, -1e30)
    row_max = jnp.max(scores, axis=-1, keepdims=True)
    log_total = row_max + jnp.log(jnp.sum(jnp.exp(scores - row_max), axis=-1, keepdims=True))
    probs = jnp.exp(scores - log_total)
    probs_b = probs.astype(bf16)
    mixed = jnp.einsum("bhqk,bkhd->bqhd", probs_b, values, preferred_element_type=f32).astype(bf16)
    attn_mix = mixed.reshape(group, cols)
    attn_out = dot(attn_mix, output_weight).astype(bf16)
    attn_out = lax.psum_scatter(attn_out, "wshard", scatter_dimension=0, tiled=True)

    residual = tokens.astype(f32)
    middle = residual + attn_out.astype(f32)
    unit_two, inverse_two = rms_unit(middle)
    ffn_in = (unit_two * ffn_gain_all).astype(bf16)
    router_probs = softmax_rows(dot_t(ffn_in, router_t))
    expert_range = jnp.arange(experts, dtype=jnp.int32)
    named = jnp.any(expert_ids[:, :, None] == expert_range[None, None, :], axis=1)
    route_table = jnp.where(named, router_probs, 0.0)

    arrived = lax.all_gather(ffn_in, "expert", axis=0, tiled=True)
    weights = lax.all_to_all(
        route_table.reshape(rows, owners, EXP_DEV).transpose(1, 2, 0),
        "expert",
        split_axis=0,
        concat_axis=0,
        tiled=True,
    )
    weights = weights.transpose(1, 0, 2).reshape(EXP_DEV, owners * rows)
    gate_lin = jnp.einsum("rd,edf->erf", arrived, gate_all, preferred_element_type=f32)
    up_lin = jnp.einsum("rd,edf->erf", arrived, up_all, preferred_element_type=f32)
    hidden_back = jnp.einsum("rd,efd->erf", cot_all, down_all, preferred_element_type=f32)
    weight_col = weights[:, :, None]
    sigmoid_gate = jax.nn.sigmoid(gate_lin)
    swish = gate_lin * sigmoid_gate
    hidden = swish * up_lin
    route_back = jnp.sum(hidden * hidden_back, axis=2)
    hidden_w = (hidden * weight_col).astype(bf16)
    hidden_grad = hidden_back * weight_col
    gate_grad_b = (
        hidden_grad * up_lin * sigmoid_gate * (1.0 + gate_lin * (1.0 - sigmoid_gate))
    ).astype(bf16)
    up_grad_b = (hidden_grad * swish).astype(bf16)
    row_partial = jnp.einsum("erf,edf->rd", gate_grad_b, gate_all, preferred_element_type=f32)
    row_partial = row_partial + jnp.einsum(
        "erf,edf->rd", up_grad_b, up_all, preferred_element_type=f32
    )
    row_grads = lax.psum_scatter(
        row_partial.astype(bf16), "expert", scatter_dimension=0, tiled=True
    )
    route_back = lax.all_to_all(
        route_back.reshape(EXP_DEV, owners, rows).transpose(1, 0, 2),
        "expert",
        split_axis=0,
        concat_axis=0,
        tiled=True,
    )
    out_partial = jnp.einsum("erf,efd->rd", hidden_w, down_all, preferred_element_type=f32)
    moe_out = lax.psum_scatter(out_partial.astype(bf16), "expert", scatter_dimension=0, tiled=True)
    block_output = middle + moe_out.astype(f32)
    gate_part = jnp.einsum("rd,erf->edf", arrived, gate_grad_b, preferred_element_type=f32)
    up_part = jnp.einsum("rd,erf->edf", arrived, up_grad_b, preferred_element_type=f32)
    down_part = jnp.einsum("erf,rd->efd", hidden_w, cot_all, preferred_element_type=f32)
    gate_weight_grad = lax.psum_scatter(
        gate_part.astype(bf16), "wshard", scatter_dimension=1, tiled=True
    ).astype(f32)
    up_weight_grad = lax.psum_scatter(
        up_part.astype(bf16), "wshard", scatter_dimension=1, tiled=True
    ).astype(f32)
    down_weight_grad = lax.psum_scatter(
        down_part.astype(bf16), "wshard", scatter_dimension=2, tiled=True
    ).astype(f32)

    route_grad = route_back.reshape(experts, rows).T
    prob_grad = jnp.where(named, route_grad, 0.0)
    logit_grad = router_probs * (
        prob_grad - jnp.sum(router_probs * prob_grad, axis=1, keepdims=True)
    )
    logit_grad_b = logit_grad.astype(bf16)
    ffn_in_grad = row_grads.astype(f32) + dot(logit_grad_b, router_t)
    middle_part, ffn_gain_grad = rms_backward(ffn_in_grad, unit_two, inverse_two, ffn_gain_all)
    middle_grad = cotangent + middle_part
    router_grad = t_dot(logit_grad_b, ffn_in)

    mid_all = lax.all_gather(middle_grad.astype(bf16), "wshard", axis=0, tiled=True)
    output_part = t_dot(attn_mix, mid_all).astype(bf16)
    mix_grad = dot_t(mid_all, output_weight).astype(bf16).reshape(blocked)
    delta = jnp.sum(mix_grad.astype(f32) * mixed.astype(f32), axis=-1)
    prob_back = jnp.einsum("bqhd,bkhd->bhqk", mix_grad, values, preferred_element_type=f32)
    score_grad = (probs * (prob_back - delta.transpose(0, 2, 1)[:, :, :, None])).astype(bf16)
    grad_queries = jnp.einsum("bhqk,bkhd->bqhd", score_grad, keys, preferred_element_type=f32)
    grad_keys = jnp.einsum("bhqk,bqhd->bkhd", score_grad, queries, preferred_element_type=f32)
    grad_values = jnp.einsum("bhqk,bqhd->bkhd", probs_b, mix_grad, preferred_element_type=f32)
    grad_queries = rotate((grad_queries * scale).reshape(wide), cosine, -sine).reshape(group, cols)
    grad_keys = rotate((grad_keys * scale).reshape(wide), cosine, -sine).reshape(group, cols)
    query_gain_grad = jnp.sum(grad_queries * query_unit, axis=0)
    key_gain_grad = jnp.sum(grad_keys * key_unit, axis=0)
    grad_queries = grad_queries * query_gain_f
    grad_keys = grad_keys * key_gain_f
    means = jnp.stack(
        [jnp.sum(grad_queries * query_unit, axis=1), jnp.sum(grad_keys * key_unit, axis=1)], axis=0
    )
    means = group_sum(means, "wshard") / width
    query_grad_b = (query_inverse * (grad_queries - query_unit * means[0][:, None])).astype(bf16)
    key_grad_b = (key_inverse * (grad_keys - key_unit * means[1][:, None])).astype(bf16)
    value_grad_b = grad_values.reshape(group, cols).astype(bf16)
    qkv_grad = jnp.concatenate([query_grad_b, key_grad_b, value_grad_b], axis=1)
    attn_in_part = dot_t(qkv_grad, qkv_w).astype(bf16)
    attn_in_grad = lax.psum_scatter(attn_in_part, "wshard", scatter_dimension=0, tiled=True)
    qkv_part = t_dot(attn_in, qkv_grad).astype(bf16)

    unit_one, inverse_one = rms_unit(residual)
    input_part, attn_gain_grad = rms_backward(
        attn_in_grad.astype(f32), unit_one, inverse_one, attn_gain_all
    )
    tokens_grad = middle_grad + input_part

    qkv_sum = lax.psum_scatter(qkv_part, "expert", scatter_dimension=0, tiled=True)
    qkv_sum = lax.all_to_all(qkv_sum, "wshard", split_axis=0, concat_axis=0, tiled=True)
    final_rows = width // (owners * parts)
    qkv_sum = qkv_sum.reshape(parts, final_rows, 3, cols).transpose(2, 1, 0, 3)
    qkv_sum = qkv_sum.reshape(3, final_rows, width).astype(f32)
    output_sum = lax.psum_scatter(output_part, "expert", scatter_dimension=0, tiled=True)
    moves = []
    for e in range(owners):
        for w in range(parts):
            moves.append((e * parts + w, w * owners + e))
    output_sum = lax.ppermute(output_sum, ("expert", "wshard"), moves).astype(f32)

    own = jnp.zeros((2, parts, cols), f32)
    own = lax.dynamic_update_slice(
        own, jnp.stack([query_gain_grad, key_gain_grad])[:, None, :], (0, w_index, 0)
    ).reshape(2, width)
    table = jnp.concatenate([attn_gain_grad[None], ffn_gain_grad[None], own, router_grad], axis=0)
    count = table.shape[0]
    table = table.reshape(count, owners, parts * final_rows).transpose(1, 0, 2)
    table = jnp.sum(
        lax.all_to_all(table, "expert", split_axis=0, concat_axis=0, tiled=True), axis=0
    )
    table = table.reshape(count, parts, final_rows).transpose(1, 0, 2)
    table = jnp.sum(
        lax.all_to_all(table, "wshard", split_axis=0, concat_axis=0, tiled=True), axis=0
    )
    return (
        block_output,
        tokens_grad,
        table[0],
        qkv_sum[0],
        qkv_sum[1],
        qkv_sum[2],
        table[2],
        table[3],
        output_sum,
        table[1],
        table[4:].T,
        gate_weight_grad,
        up_weight_grad,
        down_weight_grad,
    )


def solution(mesh):
    in_specs = (
        P(("expert", "wshard"), None),
        P(("expert", "wshard"), None),
        P(("expert", "wshard"), None),
        P("wshard"),
        P("wshard", None),
        P("wshard", None),
        P("wshard", None),
        P("wshard"),
        P("wshard"),
        P("wshard", None),
        P("wshard"),
        P("wshard", None),
        P("expert", "wshard", None),
        P("expert", "wshard", None),
        P("expert", None, "wshard"),
        P(("expert", "wshard"), None),
    )
    out_specs = (
        P(("expert", "wshard"), None),
        P(("expert", "wshard"), None),
        P(("expert", "wshard")),
        P(("expert", "wshard"), None),
        P(("expert", "wshard"), None),
        P(("expert", "wshard"), None),
        P(("expert", "wshard")),
        P(("expert", "wshard")),
        P(("expert", "wshard"), None),
        P(("expert", "wshard")),
        P(("expert", "wshard"), None),
        P("expert", "wshard", None),
        P("expert", "wshard", None),
        P("expert", None, "wshard"),
    )
    return jax.shard_map(local, mesh=mesh, in_specs=in_specs, out_specs=out_specs, check_vma=False)
```

time: 2100 us -> 1260 us (0.60)
  waiting for transfers between devices: 1500 us -> 812 us
  local copies, waits for them, and re-layouts: 161 us -> 68.9 us
  matrix products: 239 us -> 174 us
  blocking collectives: 73.2 us -> 111 us
  other arithmetic: 77.4 us -> 43.2 us
    all_to_all x4, waiting for transfers between devices: 639 us -> 0.01 us  [the longest x1 0.01 us: local(): lax.all_to_all(route_table.reshape(rows, owners, EXP_DEV).transpose(1, 2,...]
    reduce_scatter x7 -> x9, waiting for transfers between devices: 673 us -> 533 us  [the longest x1 125 us: local(): lax.psum_scatter(qkv_part, 'expert', scatter_dimension=0, tiled=True)]
    all_gather x7, waiting for transfers between devices: 186 us -> 277 us  [the longest x1 71.9 us: local(): arrived = lax.all_gather(ffn_in, 'expert', axis=0, tiled=True)]
    all_gather x5 -> x3, blocking collectives: 28.1 us -> 91.5 us  [the longest x1 80.8 us: local(): small_all = lax.all_gather(small, 'wshard', axis=0)]
    dot_general x29 -> x24, matrix products: 237 us -> 174 us  [the longest x1 22.9 us: local(): jnp.einsum('rd,edf->erf', arrived, up_all, preferred_element_type=f32)]
    gather x4 -> x0, local copies, waits for them, and re-layouts: 57.4 us -> none  [the longest x1 19.1 us: local(): out_grad[safe_assign]]
    unnamed x1 -> x0, blocking collectives: 45.1 us -> none
    convert_element_type x3, local copies, waits for them, and re-layouts: 43.4 us -> 4.38 us  [the longest x1 3.76 us: local(): qkv_sum = qkv_sum.reshape(3, final_rows, width).astype(f32)]
  transfers between devices with their start and end apart: 19 -> 21, of which waited for: 13 -> 14; matrix products, arithmetic and copies ran while one was open for 18% -> 11% of each run, Pallas kernels for 0% -> 0%
where the time goes in v1:
time: 1260 us; the launch traced here: 1250 us
  waiting for transfers between devices  812 us (64%)
  matrix products  174 us (14%)
  blocking collectives  111 us (9%)
  local copies, waits for them, and re-layouts  68.9 us (5%)
  other arithmetic  43.2 us (3%)
  starting transfers between devices  25.7 us (2%)
  between operations  17.1 us (1%)
    reduce_scatter x1, waiting for transfers between devices, local(): lax.psum_scatter(qkv_part, 'expert', scatter_dimension=0, tiled=True)  125 us
    reduce_scatter x1, waiting for transfers between devices, local(): lax.psum_scatter(out_partial.astype(bf16), 'expert', scatter_dimension=0,...  86.7 us
    all_gather x1, blocking collectives, local(): small_all = lax.all_gather(small, 'wshard', axis=0)  80.8 us
    reduce_scatter x1, waiting for transfers between devices, local(): lax.psum_scatter(row_partial.astype(bf16), 'expert', scatter_dimension=0,...  78.5 us
    all_gather x1, waiting for transfers between devices, local(): arrived = lax.all_gather(ffn_in, 'expert', axis=0, tiled=True)  71.9 us
    reduce_scatter x1, waiting for transfers between devices, local(): lax.psum_scatter(up_part.astype(bf16), 'wshard', scatter_dimension=1, til...  69.7 us
    reduce_scatter x1, waiting for transfers between devices, local(): lax.psum_scatter(down_part.astype(bf16), 'wshard', scatter_dimension=2, t...  69.6 us
    reduce_scatter x1, waiting for transfers between devices, local(): lax.psum_scatter(gate_part.astype(bf16), 'wshard', scatter_dimension=1, t...  67 us
  transfers between devices with their start and end apart: 21, of which 14 were waited for; matrix products, arithmetic and copies ran while one was open for 11% of the time, Pallas kernels for 0%

profile of v1, /device:TPU:13, one launch (start us, length us, event | category | flops | bytes accessed | tf_op | source)
XLA Modules:
  0.0 1251.9 jit_solution(697781144343572902)
XLA Ops:
  34.5 80.8 %all-gather.3 = bf16[4,19,512]{2,1,0:T(8,128)(2,1)S(1)} all-gather(bf16[1,19,512]{2,1,0:T(8,128)(2,1)S(1)} %fusion.65), channel_id=2, replica_groups=mesh['expert'=8,'wshard'=4] {'wshard'}, dimensions={0}, use_global_device_ids=true | all-gather | bytes 97280 | tf_op jit(solution)/shard_map/all_gather | solution.py:110
  167.1 23.8 %reduce-scatter.10.cloned.1.call-done = bf16[128,2048]{1,0:T(8,128)(2,1)} async-done(((bf16[512,2048]{1,0:T(8,128)(2,1)}), bf16[128,2048]{1,0:T(8,128)(2,1)}) %reduce-scatter.10.cloned.1.call-update) | async-done | bytes 524304 | tf_op jit(solution)/shard_map/reduce_scatter | solution.py:163
  205.4 27.2 %all-gather.24.cloned.1.call-done = bf16[1024,2048]{1,0:T(8,128)(2,1)} async-done(((bf16[128,2048]{1,0:T(8,128)(2,1)}), bf16[1024,2048]{1,0:T(8,128)(2,1)}) %all-gather.24.cloned.1.call-update) | async-done | bytes 4194320 | tf_op jit(solution)/shard_map/all_gather | solution.py:128
  232.6 61.5 %all-gather.22.cloned.1.call-done = bf16[2,1024,2048]{2,1,0:T(8,128)(2,1)} async-done(((bf16[2,1024,512]{2,1,0:T(8,128)(2,1)}), bf16[2,1024,2048]{2,1,0:T(8,128)(2,1)}) %all-gather.22.cloned.1.call-update) | async-done | bytes 8388624 | tf_op jit(solution)/shard_map/all_gather | solution.py:127
  294.2 14.8 %fusion.13 = f32[2,1024,1024]{2,1,0:T(8,128)} fusion(bf16[2,1024,2048]{2,1,0:T(8,128)(2,1)} %all-gather.22.cloned.1.call-done, bf16[1024,2048]{1,0:T(8,128)(2,1)} %all-gather.24.cloned.1.call-done), kind=kOutput, calls=%fused_computation.31 | convolution fusion | flops 8589934592 | bytes 20971520 | tf_op jit(solution)/shard_map/rd,efd->erf/dot_general | solution.py:185
  309.0 45.4 %all-gather.18.cloned.1.call-done = bf16[2,2048,1024]{1,2,0:T(8,128)(2,1)} async-done(((bf16[2,512,1024]{1,2,0:T(8,128)(2,1)}), bf16[2,2048,1024]{1,2,0:T(8,128)(2,1)}) %all-gather.18.cloned.1.call-update) | async-done | bytes 8388624 | tf_op jit(solution)/shard_map/all_gather | solution.py:125
  354.4 71.9 %all-gather.16.cloned.1.call-done = bf16[1024,2048]{1,0:T(8,128)(2,1)} async-done(((bf16[128,2048]{1,0:T(8,128)(2,1)}), bf16[1024,2048]{1,0:T(8,128)(2,1)}) %all-gather.16.cloned.1.call-update) | async-done | bytes 4194320 | tf_op jit(solution)/shard_map/all_gather | solution.py:174
  426.3 14.6 %fusion.19 = f32[1024,2,1024]{0,2,1:T(8,128)} fusion(bf16[2,2048,1024]{1,2,0:T(8,128)(2,1)} %all-gather.18.cloned.1.call-done, bf16[1024,2048]{1,0:T(8,128)(2,1)} %all-gather.16.cloned.1.call-done), kind=kOutput, calls=%fused_computation.37 | convolution fusion | flops 8589934592 | bytes 20971520 | tf_op jit(solution)/shard_map/rd,edf->erf/dot_general | solution.py:183
  440.9 47.7 %all-gather.20.cloned.1.call-done = bf16[2,2048,1024]{1,2,0:T(8,128)(2,1)} async-done(((bf16[2,512,1024]{1,2,0:T(8,128)(2,1)}), bf16[2,2048,1024]{1,2,0:T(8,128)(2,1)}) %all-gather.20.cloned.1.call-update) | async-done | bytes 8388624 | tf_op jit(solution)/shard_map/all_gather | solution.py:126
  488.6 22.9 %fusion.4 = (bf16[2,1024,1024]{1,2,0:T(8,128)(2,1)}, f32[2,1024]{1,0:T(2,128)S(1)}, bf16[2,1024,1024]{1,2,0:T(8,128)(2,1)}, bf16[2,1024,1024]{1,2,0:T(8,128)(2,1)}) fusion(f32[1024,2,1024]{0,2,1:T(8,128)} %fusion.19, f32[2,1024,1024]{2,1,0:T(8,128)} %fusion.13, f32[2,1024]{1,0:T(2,128)S(1)} %bitcast.298, ...), kind=kOutput, calls=%fused_computation.10 | convolution fusion | flops 8629778432 | bytes 41959424 | tf_op jit(solution)/shard_map/rd,edf->erf/dot_general | solution.py:184
  511.5 12.8 %fusion.78 = f32[1024,2048,1]{1,0,2:T(8,128)S(1)} fusion(bf16[2,1024,1024]{1,2,0:T(8,128)(2,1)} %get-tuple-element.123, bf16[2,2048,1024]{1,2,0:T(8,128)(2,1)} %all-gather.18.cloned.1.call-done), kind=kOutput, calls=%fused_computation.183 | convolution fusion | flops 8589934592 | bytes 20971520 | tf_op jit(solution)/shard_map/erf,edf->rd/dot_general | solution.py:197
  524.4 11.0 fusion
  544.2 78.5 %reduce-scatter.14.cloned.1.call-done = bf16[128,2048]{1,0:T(8,128)(2,1)} async-done(((bf16[1024,2048]{1,0:T(8,128)(2,1)}), bf16[128,2048]{1,0:T(8,128)(2,1)}) %reduce-scatter.14.cloned.1.call-update) | async-done | bytes 524304 | tf_op jit(solution)/shard_map/reduce_scatter | solution.py:201
  627.9 23.2 %all-gather.26.cloned.1.call-done = bf16[512,2048]{1,0:T(8,128)(2,1)} async-done(((bf16[128,2048]{1,0:T(8,128)(2,1)}), bf16[512,2048]{1,0:T(8,128)(2,1)}) %all-gather.26.cloned.1.call-update) | async-done | bytes 2097168 | tf_op jit(solution)/shard_map/all_gather | solution.py:238
  697.2 14.1 %bitcast_convert_fusion = bf16[1024,2048]{1,0:T(8,128)(2,1)} fusion(bf16[2,1024,1024]{1,2,0:T(8,128)(2,1)} %get-tuple-element.126, bf16[2,1024,2048]{2,1,0:T(8,128)(2,1)} %all-gather.22.cloned.1.call-done), kind=kOutput, calls=%fused_computation.5 | convolution fusion | flops 8592031744 | bytes 16777216 | tf_op jit(solution)/shard_map/erf,efd->rd/dot_general | solution.py:211
  711.5 14.1 %convert_bitcast_fusion.1 = bf16[2,2048,1024]{1,2,0:T(8,128)(2,1)} fusion(bf16[2,1024,1024]{1,2,0:T(8,128)(2,1)} %get-tuple-element.123, bf16[1024,2048]{1,0:T(8,128)(2,1)} %all-gather.16.cloned.1.call-done), kind=kOutput, calls=%fused_computation.19 | convolution fusion | flops 8594128896 | bytes 16777216 | tf_op jit(solution)/shard_map/rd,erf->edf/dot_general | solution.py:214
  725.7 14.1 %convert_bitcast_fusion = bf16[2,2048,1024]{1,2,0:T(8,128)(2,1)} fusion(bf16[2,1024,1024]{1,2,0:T(8,128)(2,1)} %get-tuple-element.125, bf16[1024,2048]{1,0:T(8,128)(2,1)} %all-gather.16.cloned.1.call-done), kind=kOutput, calls=%fused_computation.18 | convolution fusion | flops 8594128896 | bytes 16777216 | tf_op jit(solution)/shard_map/rd,erf->edf/dot_general | solution.py:215
  740.1 14.1 %convolution_convert_fusion.1 = bf16[2,1024,2048]{2,1,0:T(8,128)(2,1)} fusion(bf16[2,1024,1024]{1,2,0:T(8,128)(2,1)} %get-tuple-element.126, bf16[1024,2048]{1,0:T(8,128)(2,1)} %all-gather.24.cloned.1.call-done), kind=kOutput, calls=%fused_computation.24 | convolution fusion | flops 8594128896 | bytes 16777216 | tf_op jit(solution)/shard_map/erf,rd->efd/dot_general | solution.py:216
  773.7 12.2 reduce-scatter.20.cloned.1.call-done
  788.9 125.5 %reduce-scatter.18.cloned.1.call-done = bf16[256,1536]{1,0:T(8,128)(2,1)} async-done(((bf16[2048,1536]{1,0:T(8,128)(2,1)}), bf16[256,1536]{1,0:T(8,128)(2,1)}) %reduce-scatter.18.cloned.1.call-update) | async-done | bytes 786448 | tf_op jit(solution)/shard_map/reduce_scatter | solution.py:271
  919.6 86.7 %reduce-scatter.12.cloned.1.call-done = bf16[128,2048]{1,0:T(8,128)(2,1)} async-done(((bf16[1024,2048]{1,0:T(8,128)(2,1)}), bf16[128,2048]{1,0:T(8,128)(2,1)}) %reduce-scatter.12.cloned.1.call-update) | async-done | bytes 524304 | tf_op jit(solution)/shard_map/reduce_scatter | solution.py:212
  1012.9 67.0 %reduce-scatter.22.cloned.1.call-done = bf16[2,512,1024]{1,2,0:T(8,128)(2,1)} async-done(((bf16[2,2048,1024]{1,2,0:T(8,128)(2,1)}), bf16[2,512,1024]{1,2,0:T(8,128)(2,1)}) %reduce-scatter.22.cloned.1.call-update) | async-done | bytes 2097168 | tf_op jit(solution)/shard_map/reduce_scatter | solution.py:217
  1084.0 69.7 %reduce-scatter.24.cloned.1.call-done = bf16[2,512,1024]{1,2,0:T(8,128)(2,1)} async-done(((bf16[2,2048,1024]{1,2,0:T(8,128)(2,1)}), bf16[2,512,1024]{1,2,0:T(8,128)(2,1)}) %reduce-scatter.24.cloned.1.call-update) | async-done | bytes 2097168 | tf_op jit(solution)/shard_map/reduce_scatter | solution.py:220
  1157.8 69.6 %reduce-scatter.26.cloned.1.call-done = bf16[2,1024,512]{2,1,0:T(8,128)(2,1)} async-done(((bf16[2,1024,2048]{2,1,0:T(8,128)(2,1)}), bf16[2,1024,512]{2,1,0:T(8,128)(2,1)}) %reduce-scatter.26.cloned.1.call-update) | async-done | bytes 2097168 | tf_op jit(solution)/shard_map/reduce_scatter | solution.py:223
  (254 shorter events, 211.6 us)
Async XLA Ops:
  26.3 94.0 %all-to-all-start = ((bf16[4,512,1536]{1,2,0:T(8,128)(2,1)}), bf16[4,512,1536]{1,2,0:T(8,128)(2,1)}, u32[]{:S(2)}, u32[]{:S(2)}) async-start(bf16[4,512,1536]{1,2,0:T(8,128)(2,1)} %bitcast.233), calls=%async_computation | async-start | bytes 12582912 | tf_op jit(solution)/shard_map/all_to_all | solution.py:123
  32.3 85.9 %all-gather.14.cloned.1.call-start = ((), (), s32[]{:S(2)}) async-start(), calls=%async_computation.15 | async-start | bytes 2621440 | tf_op jit(solution)/shard_map/all_gather | solution.py:104
  33.1 157.8 %reduce-scatter.10.cloned.1.call-start = ((), (), s32[]{:S(2)}) async-start(), calls=%async_computation.16 | async-start | bytes 2621440 | tf_op jit(solution)/shard_map/reduce_scatter | solution.py:163
  160.1 72.6 %all-gather.24.cloned.1.call-start = ((), (), s32[]{:S(2)}) async-start(), calls=%async_computation.22 | async-start | bytes 4718592 | tf_op jit(solution)/shard_map/all_gather | solution.py:128
  162.2 131.9 %all-gather.22.cloned.1.call-start = ((), (), s32[]{:S(2)}) async-start(), calls=%async_computation.20 | async-start | bytes 10485760 | tf_op jit(solution)/shard_map/all_gather | solution.py:127
  162.8 191.5 %all-gather.18.cloned.1.call-start = ((), (), s32[]{:S(2)}) async-start(), calls=%async_computation.18 | async-start | bytes 10485760 | tf_op jit(solution)/shard_map/all_gather | solution.py:125
  166.9 259.4 %all-gather.16.cloned.1.call-start = ((), (), s32[]{:S(2)}) async-start(), calls=%async_computation.17 | async-start | bytes 4718592 | tf_op jit(solution)/shard_map/all_gather | solution.py:174
  194.8 293.8 %all-gather.20.cloned.1.call-start = ((), (), s32[]{:S(2)}) async-start(), calls=%async_computation.19 | async-start | bytes 10485760 | tf_op jit(solution)/shard_map/all_gather | solution.py:126
  199.9 240.9 %all-to-all-start.1 = ((f32[8,2,128]{2,1,0:T(2,128)}), f32[8,2,128]{2,1,0:T(2,128)S(1)}, u32[]{:S(2)}, u32[]{:S(2)}) async-start(f32[8,2,128]{2,1,0:T(2,128)} %bitcast.27), calls=%async_computation.2 | async-start | bytes 16384 | tf_op jit(solution)/shard_map/all_to_all | solution.py:175
  205.4 417.3 %reduce-scatter.14.cloned.1.call-start = ((), (), s32[]{:S(2)}) async-start(), calls=%async_computation.23 | async-start | bytes 4718592 | tf_op jit(solution)/shard_map/reduce_scatter | solution.py:201
  535.4 115.8 %all-gather.26.cloned.1.call-start = ((), (), s32[]{:S(2)}) async-start(), calls=%async_computation.24 | async-start | bytes 2621440 | tf_op jit(solution)/shard_map/all_gather | solution.py:238
  627.9 127.7 %reduce-scatter.16.cloned.1.call-start = ((), (), s32[]{:S(2)}) async-start(), calls=%async_computation.25 | async-start | bytes 2621440 | tf_op jit(solution)/shard_map/reduce_scatter | solution.py:262
  685.1 100.7 %reduce-scatter.20.cloned.1.call-start = ((), (), s32[]{:S(2)}) async-start(), calls=%async_computation.27 | async-start | bytes 2359296 | tf_op jit(solution)/shard_map/reduce_scatter | solution.py:276
  689.8 224.6 %reduce-scatter.18.cloned.1.call-start = ((), (), s32[]{:S(2)}) async-start(), calls=%async_computation.26 | async-start | bytes 7077888 | tf_op jit(solution)/shard_map/reduce_scatter | solution.py:271
  697.2 309.2 %reduce-scatter.12.cloned.1.call-start = ((), (), s32[]{:S(2)}) async-start(), calls=%async_computation.21 | async-start | bytes 4718592 | tf_op jit(solution)/shard_map/reduce_scatter | solution.py:212
  711.3 368.6 %reduce-scatter.22.cloned.1.call-start = ((), (), s32[]{:S(2)}) async-start(), calls=%async_computation.28 | async-start | bytes 10485760 | tf_op jit(solution)/shard_map/reduce_scatter | solution.py:217
  725.6 428.1 %reduce-scatter.24.cloned.1.call-start = ((), (), s32[]{:S(2)}) async-start(), calls=%async_computation.29 | async-start | bytes 10485760 | tf_op jit(solution)/shard_map/reduce_scatter | solution.py:220
  739.8 487.6 %reduce-scatter.26.cloned.1.call-start = ((), (), s32[]{:S(2)}) async-start(), calls=%async_computation.30 | async-start | bytes 10485760 | tf_op jit(solution)/shard_map/reduce_scatter | solution.py:223
  754.2 252.1 %copy-start.11 = (f32[128,2048]{1,0:T(8,128)S(1)}, f32[128,2048]{1,0:T(8,128)}, u32[]{:S(2)}) copy-start(f32[128,2048]{1,0:T(8,128)} %param.33) | copy-start | bytes 3145732
  754.2 252.1 %copy-start.34 = (f32[128]{0:T(128)S(1)}, f32[128]{0:T(128)}, u32[]{:S(2)}) copy-start(f32[128]{0:T(128)} %copy-done.33) | copy-start | bytes 1540
  755.4 250.9 %copy-start.18 = (f32[128,2048]{1,0:T(8,128)S(1)}, f32[128,2048]{1,0:T(8,128)}, u32[]{:S(2)}) copy-start(f32[128,2048]{1,0:T(8,128)} %copy-done.17) | copy-start | bytes 3145732
  768.9 20.0 %all-to-all-start.4 = ((f32[4,1,1280]{2,1,0:T(1,128)}), f32[4,1,1280]{2,1,0:T(1,128)S(1)}, u32[]{:S(2)}, u32[]{:S(2)}) async-start(f32[4,1,1280]{2,1,0:T(1,128)} %reshape.353), calls=%async_computation.8 | async-start | bytes 40960 | tf_op jit(solution)/shard_map/all_to_all | solution.py:295
  785.9 223.7 %collective-permute-start = (bf16[64,2048]{1,0:T(8,128)(2,1)}, bf16[64,2048]{1,0:T(8,128)(2,1)S(1)}, u32[]{:S(2)}, u32[]{:S(2)}) collective-permute-start(bf16[64,2048]{1,0:T(8,128)(2,1)} %reduce-scatter.20.cloned.1.call-done), channel_id=1, source_target_pairs={{0,0},{1,8},{2,16},{3,24},{4,1},{5,9},{6,17},{7,25},{8,2},{9,10},{... | collective-permute-start | bytes 786440 | tf_op jit(solution)/shard_map/ppermute | solution.py:281
  914.4 317.2 %all-to-all-start.5 = ((bf16[4,64,1536]{2,1,0:T(8,128)(2,1)}), bf16[4,64,1536]{2,1,0:T(8,128)(2,1)}, u32[]{:S(2)}, u32[]{:S(2)}) async-start(bf16[4,64,1536]{2,1,0:T(8,128)(2,1)} %bitcast.254), calls=%async_computation.10 | async-start | bytes 1572864 | tf_op jit(solution)/shard_map/all_to_all | solution.py:272
  (42 other events, 450.2 us)
Sparse Core Ops, SparseCore 0:
  34.7 35.2 all-gather.13
  160.2 30.6 reduce-scatter.9
  628.0 23.1 all-gather.25
  685.2 30.4 reduce-scatter.15
  719.1 66.6 reduce-scatter.19
  789.3 125.0 reduce-scatter.17
  918.0 88.2 reduce-scatter.11
  1008.9 70.9 reduce-scatter.21
  1082.5 71.1 reduce-scatter.23
  1156.1 71.2 reduce-scatter.25
Sparse Core Ops, SparseCore 1:
  163.3 69.3 all-gather.23
  234.1 60.1 all-gather.21
  296.2 58.1 all-gather.17
  357.1 69.2 all-gather.15
  428.5 60.1 all-gather.19
  535.5 87.2 reduce-scatter.13

commit v2 on v1

v2 whole, which is shorter than its diff:
```python
import jax
import jax.numpy as jnp
from jax import lax
from jax.sharding import PartitionSpec as P


HEADS = 16
HEAD_DIM = 128
EXP_DEV = 2


epsilon = 1e-05
theta_base = 10000.0


def rms_unit(activation):
    inverse = lax.rsqrt(jnp.mean(activation * activation, axis=-1, keepdims=True) + epsilon)
    return (activation * inverse, inverse)


def rms_backward(grad_out, normed, inverse, gain):
    gain_grad = jnp.sum(grad_out * normed, axis=0)
    grad_normed = grad_out * gain
    centred = grad_normed - normed * jnp.mean(grad_normed * normed, axis=-1, keepdims=True)
    return (inverse * centred, gain_grad)


def block_tables(lengths, rows):
    ends = jnp.cumsum(lengths, axis=1)
    row_index = jnp.arange(rows, dtype=jnp.int32)
    passed = (row_index[None, :, None] >= ends[:, None, :]).astype(jnp.int32)
    start = jnp.sum(passed * lengths[:, None, :], axis=2)
    allowed = (row_index[None, None, :] <= row_index[None, :, None]) & (
        row_index[None, None, :] >= start[:, :, None]
    )
    offsets = (row_index[None, :] - start).reshape(-1)
    half_dim = HEAD_DIM // 2
    frequency = theta_base ** (-2.0 * jnp.arange(half_dim, dtype=jnp.float32) / HEAD_DIM)
    angles = offsets.astype(jnp.float32)[:, None] * frequency[None, :]
    return (allowed, jnp.cos(angles), jnp.sin(angles))


def rotate(rows, cosine, sine):
    half_dim = HEAD_DIM // 2
    first = rows[..., :half_dim]
    second = rows[..., half_dim:]
    cosine = cosine[None, :, :]
    sine = sine[None, :, :]
    return jnp.concatenate([first * cosine - second * sine, second * cosine + first * sine], axis=-1)


def softmax_rows(logits):
    row_max = jnp.max(logits, axis=-1, keepdims=True)
    shifted = jnp.exp(logits - row_max)
    return shifted / jnp.sum(shifted, axis=-1, keepdims=True)


def dot(a, b):
    return jnp.dot(a, b, preferred_element_type=jnp.float32)


def dot_t(a, b):
    return lax.dot_general(a, b, (((1,), (1,)), ((), ())), preferred_element_type=jnp.float32)


def t_dot(a, b):
    return lax.dot_general(a, b, (((0,), (0,)), ((), ())), preferred_element_type=jnp.float32)


def swap(values, mask, axis_name="wshard"):
    count = lax.axis_size(axis_name)
    return lax.ppermute(values, axis_name, [(i, i ^ mask) for i in range(count)])


def after(values, *others):
    return lax.optimization_barrier((values, *others))[0]


def bits_of(count):
    return [1 << k for k in range(count.bit_length() - 1)]


def gather_pieces(shard):
    pieces = {0: shard}
    for bit in reversed(bits_of(lax.axis_size("wshard"))):
        for mask in list(pieces):
            pieces[mask ^ bit] = swap(pieces[mask], bit)
    return [pieces[mask] for mask in sorted(pieces)]


def scatter_stage(blocks, bit):
    masks = sorted(blocks, reverse=True)
    arrived = {m ^ bit: swap(blocks[m].astype(jnp.bfloat16), bit) for m in masks if m & bit}
    return {m: blocks[m] + arrived[m].astype(jnp.float32) for m in arrived}


def scatter_near(blocks):
    return scatter_stage(dict(enumerate(blocks)), 1)


def scatter_far(blocks):
    for bit in bits_of(lax.axis_size("wshard"))[1:]:
        blocks = scatter_stage(blocks, bit)
    return blocks[0]


def scatter_pieces(blocks):
    return scatter_far(scatter_near(blocks))


def block_of(array, index, count, axis):
    size = array.shape[axis] // count
    return lax.dynamic_slice_in_dim(array, index * size, size, axis)


def mixed_order(array, w_index, count):
    return jnp.concatenate(
        [block_of(array, w_index ^ mask, count, array.ndim - 1) for mask in range(count)], axis=-1
    )


def group_sum(values, axis_name):
    return jnp.sum(lax.all_gather(values, axis_name, axis=0), axis=0)


def local(
    tokens,
    doc_lengths,
    expert_ids,
    attn_gain,
    query_weight,
    key_weight,
    value_weight,
    query_gain,
    key_gain,
    output_weight,
    ffn_gain,
    router_weight,
    gate_weight,
    up_weight,
    down_weight,
    cotangent,
):
    bf16 = jnp.bfloat16
    f32 = jnp.float32
    rows, width = tokens.shape
    owners = lax.axis_size("expert")
    parts = lax.axis_size("wshard")
    w_index = lax.axis_index("wshard")
    experts = EXP_DEV * owners
    group = parts * rows
    cols = width // parts
    heads = HEADS // parts
    final_rows = width // (owners * parts)
    ff = gate_weight.shape[2]

    e_index = lax.axis_index("expert")
    half = cols // 2
    unit = 2 * w_index + e_index % 2
    units = 2 * parts

    tokens_all = lax.all_gather(tokens, "wshard", axis=0, tiled=True)
    docs = doc_lengths.shape[1]
    lengths_row = jnp.zeros((1, cols), bf16).at[:, :docs].set(doc_lengths.astype(bf16))
    small = jnp.concatenate(
        [attn_gain[None, :], ffn_gain[None, :], lengths_row, router_weight.T], axis=0
    )
    small_all = lax.all_gather(small, "wshard", axis=0)
    attn_gain_all = small_all[:, 0, :].reshape(width).astype(f32)
    ffn_gain_all = small_all[:, 1, :].reshape(width).astype(f32)
    lengths_all = small_all[:, 2, :docs].astype(jnp.int32)
    router_t = small_all[:, 3:, :].transpose(1, 0, 2).reshape(experts, width)

    weights_in = after((query_weight, key_weight, value_weight), small_all)
    pieces = [None] * units
    for mask in reversed(range(parts)):
        piece = jnp.concatenate(
            [block_of(weight, w_index ^ mask, parts, 1) for weight in weights_in], axis=1
        )
        for side in range(2):
            pieces[2 * mask + side] = block_of(piece, side ^ (e_index % 2), 2, 0)
    for mask in reversed(range(1, parts)):
        pieces[2 * mask] = swap(pieces[2 * mask], mask)
        if mask == 1:
            pieces[3] = swap(pieces[3], 1)
    for mask in reversed(range(2, parts)):
        pieces[2 * mask + 1] = swap(pieces[2 * mask], 1, "expert")
    cot_b = mixed_order(cotangent, w_index, parts).astype(bf16)
    cot_all = lax.all_gather(cot_b, "expert", axis=0, tiled=True)
    down_in = after(down_weight, pieces[4])
    down_pieces = gather_pieces(down_in)

    unit_all, _ = rms_unit(tokens_all.astype(f32))
    attn_in = (unit_all * attn_gain_all).astype(bf16)
    attn_in_mixed = mixed_order(attn_in, unit, units)
    qkv = 0.0
    for at in [0, 1, 2, 3] + [2 * m for m in range(2, parts)] + [2 * m + 1 for m in range(2, parts)]:
        qkv = qkv + dot(attn_in_mixed[:, at * half : (at + 1) * half], pieces[at])
    query_lin, key_lin, value_lin = (qkv[:, i * cols : (i + 1) * cols] for i in range(3))
    squares = jnp.stack(
        [jnp.sum(query_lin * query_lin, axis=1), jnp.sum(key_lin * key_lin, axis=1)], axis=0
    )
    squares = group_sum(squares, "wshard")
    inverses = lax.rsqrt(squares / width + epsilon)
    query_inverse = inverses[0][:, None]
    key_inverse = inverses[1][:, None]
    query_unit = query_lin * query_inverse
    key_unit = key_lin * key_inverse
    query_gain_f = query_gain.astype(f32)
    key_gain_f = key_gain.astype(f32)
    allowed, cosine, sine = block_tables(lengths_all, rows)
    scale = HEAD_DIM ** (-0.5)

    def by_head(array):
        return jnp.stack(
            [array[:, h * HEAD_DIM : (h + 1) * HEAD_DIM] for h in range(heads)], axis=0
        )

    def by_row(array):
        return jnp.concatenate([array[h] for h in range(heads)], axis=1)

    blocked = (heads, parts, rows, HEAD_DIM)
    whole = (heads, group, HEAD_DIM)
    queries = rotate(by_head(query_unit * query_gain_f), cosine, sine).astype(bf16)
    queries = queries.reshape(blocked)
    keys = rotate(by_head(key_unit * key_gain_f), cosine, sine).astype(bf16).reshape(blocked)
    values = by_head(value_lin).astype(bf16).reshape(blocked)
    scores = jnp.einsum("hbqd,hbkd->hbqk", queries, keys, preferred_element_type=f32) * scale
    scores = jnp.where(allowed[None, :, :, :], scores, -1e30)
    row_max = jnp.max(scores, axis=-1, keepdims=True)
    log_total = row_max + jnp.log(jnp.sum(jnp.exp(scores - row_max), axis=-1, keepdims=True))
    probs = jnp.exp(scores - log_total)
    probs_b = probs.astype(bf16)
    mixed = jnp.einsum("hbqk,hbkd->hbqd", probs_b, values, preferred_element_type=f32).astype(bf16)
    attn_mix = by_row(mixed.reshape(whole))
    attn_out = dot(attn_mix, output_weight)
    attn_out = scatter_pieces(
        [block_of(attn_out, w_index ^ mask, parts, 0) for mask in range(parts)]
    )
    attn_out, cot_all, down_pieces, *pieces = lax.optimization_barrier(
        (attn_out, cot_all, down_pieces, *pieces)
    )
    qkv_w = jnp.concatenate([block_of(jnp.concatenate(pieces, axis=0), unit ^ k, units, 0) for k in range(units)], axis=0)
    down_all = jnp.concatenate(
        [piece.reshape(EXP_DEV * ff, cols) for piece in down_pieces], axis=1
    )
    residual = tokens.astype(f32)
    middle = residual + attn_out
    unit_two, inverse_two = rms_unit(middle)
    ffn_in = (unit_two * ffn_gain_all).astype(bf16)
    ffn_in_mixed = mixed_order(ffn_in, w_index, parts)
    gate_in, up_in, ffn_in_mixed, ffn_in = lax.optimization_barrier(
        (gate_weight, up_weight, ffn_in_mixed, ffn_in)
    )
    gate_pieces = gather_pieces(gate_in)
    up_pieces = gather_pieces(up_in)
    gate_up = jnp.concatenate(
        [
            jnp.concatenate([g[0], g[1], u[0], u[1]], axis=1)
            for g, u in zip(gate_pieces, up_pieces)
        ],
        axis=0,
    )

    router_probs = softmax_rows(dot_t(ffn_in, router_t))
    expert_range = jnp.arange(experts, dtype=jnp.int32)
    named = jnp.any(expert_ids[:, :, None] == expert_range[None, None, :], axis=1)
    route_table = jnp.where(named, router_probs, 0.0)

    arrived = lax.all_gather(ffn_in_mixed, "expert", axis=0, tiled=True)
    weights = lax.all_to_all(
        route_table.reshape(rows, owners, EXP_DEV).transpose(1, 2, 0),
        "expert",
        split_axis=0,
        concat_axis=0,
        tiled=True,
    )
    weights = weights.transpose(1, 0, 2).reshape(EXP_DEV, owners * rows)
    weight_cols = jnp.concatenate(
        [jnp.broadcast_to(w[:, None], (owners * rows, ff)) for w in weights], axis=1
    )
    wide = EXP_DEV * ff
    lin = dot(arrived, gate_up)
    gate_lin = lin[:, :wide]
    up_lin = lin[:, wide:]
    hidden_back = dot_t(cot_all, down_all)
    sigmoid_gate = jax.nn.sigmoid(gate_lin)
    swish = gate_lin * sigmoid_gate
    hidden = swish * up_lin
    route_back = jnp.sum((hidden * hidden_back).reshape(owners * rows, EXP_DEV, ff), axis=2).T
    hidden_w = (hidden * weight_cols).astype(bf16)
    hidden_grad = hidden_back * weight_cols
    gate_grad_b = (
        hidden_grad * up_lin * sigmoid_gate * (1.0 + gate_lin * (1.0 - sigmoid_gate))
    ).astype(bf16)
    up_grad_b = (hidden_grad * swish).astype(bf16)
    grads_b = jnp.concatenate([gate_grad_b, up_grad_b], axis=1)
    row_partial = dot_t(grads_b, gate_up).astype(bf16)
    row_grads = lax.psum_scatter(row_partial, "expert", scatter_dimension=0, tiled=True)
    route_back = lax.all_to_all(
        route_back.reshape(EXP_DEV, owners, rows).transpose(1, 0, 2),
        "expert",
        split_axis=0,
        concat_axis=0,
        tiled=True,
    )
    grads_b = after(grads_b, row_partial)
    part_of = lambda array, mask: array[:, mask * cols : (mask + 1) * cols]
    blocks = [None] * parts
    order = sorted(range(parts), key=lambda m: (m < parts // 2, -m))
    for mask in order[: parts // 2]:
        blocks[mask] = t_dot(part_of(arrived, mask), grads_b)
    grads_b = after(grads_b, *(blocks[mask] for mask in order[: parts // 2]))
    for mask in order[parts // 2 :]:
        blocks[mask] = t_dot(part_of(arrived, mask), grads_b)
    gate_up_sum = scatter_pieces(blocks)
    gate_up_sum = [gate_up_sum[:, k * ff : (k + 1) * ff] for k in range(2 * EXP_DEV)]
    gate_weight_grad = jnp.stack(gate_up_sum[:EXP_DEV])
    up_weight_grad = jnp.stack(gate_up_sum[EXP_DEV:])
    hidden_w, qkv_w, *_ = lax.optimization_barrier((hidden_w, qkv_w, *blocks))
    down_blocks = [t_dot(hidden_w, part_of(cot_all, mask)) for mask in range(parts)]
    down_blocks = scatter_near(down_blocks)
    out_partial = dot(hidden_w, down_all).astype(bf16)
    row_grads, out_partial = lax.optimization_barrier((row_grads, out_partial))
    moe_out = lax.psum_scatter(out_partial, "expert", scatter_dimension=0, tiled=True)

    route_grad = route_back.reshape(experts, rows).T
    prob_grad = jnp.where(named, route_grad, 0.0)
    logit_grad = router_probs * (
        prob_grad - jnp.sum(router_probs * prob_grad, axis=1, keepdims=True)
    )
    logit_grad_b = logit_grad.astype(bf16)
    ffn_in_grad = mixed_order(row_grads, w_index, parts).astype(f32) + dot(logit_grad_b, router_t)
    middle_part, ffn_gain_grad = rms_backward(ffn_in_grad, unit_two, inverse_two, ffn_gain_all)
    middle_grad = cotangent + middle_part
    router_grad = t_dot(logit_grad_b, ffn_in)

    mid_all = jnp.zeros((group, width), bf16)
    mid_pieces = gather_pieces(middle_grad.astype(bf16))
    down_blocks = after(down_blocks, *mid_pieces)
    down_weight_grad = scatter_far(down_blocks).reshape(EXP_DEV, ff, cols)
    for mask, piece in enumerate(mid_pieces):
        mid_all = lax.dynamic_update_slice(mid_all, piece, ((w_index ^ mask) * rows, 0))
    output_part = t_dot(attn_mix, mid_all).astype(bf16)
    output_sum = lax.all_to_all(
        output_part.reshape(owners, final_rows, width),
        "expert",
        split_axis=0,
        concat_axis=0,
        tiled=True,
    )
    output_sum = jnp.sum(output_sum.astype(f32), axis=0).astype(bf16)
    mix_grad = by_head(dot_t(mid_all, output_weight).astype(bf16)).reshape(blocked)
    delta = jnp.sum(mix_grad.astype(f32) * mixed.astype(f32), axis=-1, keepdims=True)
    prob_back = jnp.einsum("hbqd,hbkd->hbqk", mix_grad, values, preferred_element_type=f32)
    score_grad = (probs * (prob_back - delta)).astype(bf16)
    grad_queries = jnp.einsum("hbqk,hbkd->hbqd", score_grad, keys, preferred_element_type=f32)
    grad_keys = jnp.einsum("hbqk,hbqd->hbkd", score_grad, queries, preferred_element_type=f32)
    grad_values = jnp.einsum("hbqk,hbqd->hbkd", probs_b, mix_grad, preferred_element_type=f32)
    grad_queries = by_row(rotate((grad_queries * scale).reshape(whole), cosine, -sine))
    grad_keys = by_row(rotate((grad_keys * scale).reshape(whole), cosine, -sine))
    query_gain_grad = jnp.sum(grad_queries * query_unit, axis=0)
    key_gain_grad = jnp.sum(grad_keys * key_unit, axis=0)
    grad_queries = grad_queries * query_gain_f
    grad_keys = grad_keys * key_gain_f
    means = jnp.stack(
        [jnp.sum(grad_queries * query_unit, axis=1), jnp.sum(grad_keys * key_unit, axis=1)], axis=0
    )
    means = group_sum(means, "wshard") / width
    query_grad_b = (query_inverse * (grad_queries - query_unit * means[0][:, None])).astype(bf16)
    key_grad_b = (key_inverse * (grad_keys - key_unit * means[1][:, None])).astype(bf16)
    value_grad_b = by_row(grad_values.reshape(whole)).astype(bf16)
    qkv_grad = jnp.concatenate([query_grad_b, key_grad_b, value_grad_b], axis=1)
    attn_in_part = dot_t(qkv_grad, qkv_w)
    attn_in_grad = scatter_pieces(
        [block_of(attn_in_part, w_index ^ mask, parts, 0) for mask in range(parts)]
    )
    value_part = t_dot(attn_in, value_grad_b).astype(bf16).reshape(owners, parts * final_rows, cols)
    value_sum = lax.all_to_all(value_part, "expert", split_axis=0, concat_axis=0, tiled=True)
    value_sum = jnp.sum(value_sum.astype(f32), axis=0).astype(bf16)
    qk_part = t_dot(attn_in, qkv_grad[:, : 2 * cols]).astype(bf16)

    unit_one, inverse_one = rms_unit(residual)
    input_part, attn_gain_grad = rms_backward(
        attn_in_grad, unit_one, inverse_one, attn_gain_all
    )
    tokens_grad = middle_grad + input_part
    moe_out = after(moe_out, attn_in_part)
    block_output = middle + mixed_order(moe_out, w_index, parts).astype(f32)

    qk_sum = lax.psum_scatter(qk_part, "expert", scatter_dimension=0, tiled=True)
    qkv_sum = jnp.concatenate([qk_sum, value_sum], axis=1)
    qkv_sum = lax.all_to_all(qkv_sum, "wshard", split_axis=0, concat_axis=0, tiled=True)
    qkv_sum = qkv_sum.reshape(parts, final_rows, 3, cols).transpose(2, 1, 0, 3)
    qkv_sum = qkv_sum.reshape(3, final_rows, width).astype(f32)
    moves = []
    for e in range(owners):
        for w in range(parts):
            moves.append((e * parts + w, w * owners + e))
    output_sum = lax.ppermute(output_sum, ("expert", "wshard"), moves).astype(f32)

    own = jnp.zeros((2, parts, cols), f32)
    own = lax.dynamic_update_slice(
        own, jnp.stack([query_gain_grad, key_gain_grad])[:, None, :], (0, w_index, 0)
    ).reshape(2, width)
    table = jnp.concatenate([attn_gain_grad[None], ffn_gain_grad[None], own, router_grad], axis=0)
    count = table.shape[0]
    table = table.reshape(count, owners, parts * final_rows).transpose(1, 0, 2)
    table = lax.all_to_all(table, "expert", split_axis=0, concat_axis=0, tiled=True)
    table = jnp.sum(table, axis=0)
    table = table.reshape(count, parts, final_rows).transpose(1, 0, 2)
    table = jnp.sum(
        lax.all_to_all(table, "wshard", split_axis=0, concat_axis=0, tiled=True), axis=0
    )
    return (
        block_output,
        tokens_grad,
        table[0],
        qkv_sum[0],
        qkv_sum[1],
        qkv_sum[2],
        table[2],
        table[3],
        output_sum,
        table[1],
        table[4:].T,
        gate_weight_grad,
        up_weight_grad,
        down_weight_grad,
    )


def solution(mesh):
    in_specs = (
        P(("expert", "wshard"), None),
        P(("expert", "wshard"), None),
        P(("expert", "wshard"), None),
        P("wshard"),
        P("wshard", None),
        P("wshard", None),
        P("wshard", None),
        P("wshard"),
        P("wshard"),
        P("wshard", None),
        P("wshard"),
        P("wshard", None),
        P("expert", "wshard", None),
        P("expert", "wshard", None),
        P("expert", None, "wshard"),
        P(("expert", "wshard"), None),
    )
    out_specs = (
        P(("expert", "wshard"), None),
        P(("expert", "wshard"), None),
        P(("expert", "wshard")),
        P(("expert", "wshard"), None),
        P(("expert", "wshard"), None),
        P(("expert", "wshard"), None),
        P(("expert", "wshard")),
        P(("expert", "wshard")),
        P(("expert", "wshard"), None),
        P(("expert", "wshard")),
        P(("expert", "wshard"), None),
        P("expert", "wshard", None),
        P("expert", "wshard", None),
        P("expert", None, "wshard"),
    )

    return jax.shard_map(local, mesh=mesh, in_specs=in_specs, out_specs=out_specs, check_vma=False)
```

time: 1260 us -> 950 us (0.75)
  waiting for transfers between devices: 812 us -> 333 us
  other arithmetic: 43.2 us -> 187 us
  blocking collectives: 111 us -> 16.9 us
  local copies, waits for them, and re-layouts: 68.9 us -> 128 us
  starting transfers between devices: 25.7 us -> 68.3 us
  matrix products: 174 us -> 188 us
    reduce_scatter x9 -> x3, waiting for transfers between devices: 533 us -> 0.02 us  [the longest x1 0.02 us: local(): lax.psum_scatter(row_partial, 'expert', scatter_dimension=0, tiled=True)]
    all_gather x6 -> x2, waiting for transfers between devices: 277 us -> 0.03 us  [the longest x1 0.02 us: local(): arrived = lax.all_gather(ffn_in_mixed, 'expert', axis=0, tiled=True)]
    ppermute x0 -> x30, waiting for transfers between devices: none -> 215 us  [swap(): lax.ppermute(values, axis_name, [(i, i ^ mask) for i in range(count)])]
    dot_general x15 -> x6, matrix products: 140 us -> 8.31 us  [the longest x1 2.96 us: local(): jnp.einsum('hbqk,hbkd->hbqd', score_grad, keys, preferred_element_type=f32)]
    concatenate x0 -> x9, other arithmetic: none -> 112 us  [the longest x1 96.7 us: local(): jnp.concatenate([jnp.concatenate([g[0], g[1], u[0], u[1]], axis=1) for g,...]
    all_gather x1, blocking collectives: 80.8 us -> 5.84 us  [local(): small_all = lax.all_gather(small, 'wshard', axis=0)]
    all_to_all x1, waiting for transfers between devices: 0.01 us -> 62 us  [local(): lax.all_to_all(table, 'wshard', split_axis=0, concat_axis=0, tiled=True)]
    dot_general x3 -> x12, matrix products: 12 us -> 71.1 us  [t_dot(): lax.dot_general(a, b, (((0,), (0,)), ((), ())), preferred_element_type=jn...]
  transfers between devices with their start and end apart: 21 -> 44, of which waited for: 14 -> 18; matrix products, arithmetic and copies ran while one was open for 11% -> 40% of each run, Pallas kernels for 0% -> 0%
where the time goes in v2:
time: 950 us; the launch traced here: 937 us
  waiting for transfers between devices  333 us (35%)
  matrix products  188 us (20%)
  other arithmetic  187 us (20%)
  local copies, waits for them, and re-layouts  128 us (13%)
  starting transfers between devices  68.3 us (7%)
  blocking collectives  16.9 us (2%)
  between operations  16.1 us (2%)
    ppermute x30, waiting for transfers between devices, swap(): lax.ppermute(values, axis_name, [(i, i ^ mask) for i in range(count)])  215 us
    concatenate x1, other arithmetic, local(): jnp.concatenate([jnp.concatenate([g[0], g[1], u[0], u[1]], axis=1) for g,...  96.7 us
    dot_general x12, matrix products, t_dot(): lax.dot_general(a, b, (((0,), (0,)), ((), ())), preferred_element_type=jn...  71.1 us
    all_to_all x1, waiting for transfers between devices, local(): lax.all_to_all(table, 'wshard', split_axis=0, concat_axis=0, tiled=True)  62 us
    dot_general x5, matrix products, dot_t(): lax.dot_general(a, b, (((1,), (1,)), ((), ())), preferred_element_type=jn...  57.6 us
    dot_general x12, matrix products, dot(): return jnp.dot(a, b, preferred_element_type=jnp.float32)  51.2 us
    unnamed x263, local copies, waits for them, and re-layouts  42.9 us
    all_to_all x1, waiting for transfers between devices, local(): lax.all_to_all(output_part.reshape(owners, final_rows, width), 'expert',...  41.9 us
  transfers between devices with their start and end apart: 44, of which 18 were waited for; matrix products, arithmetic and copies ran while one was open for 40% of the time, Pallas kernels for 0%

profile of v2, /device:TPU:13, one launch (start us, length us, event | category | flops | bytes accessed | tf_op | source)
XLA Modules:
  0.0 936.8 jit_solution(16308848605561947011)
XLA Ops:
  34.1 14.6 %collective-permute-done.2 = bf16[256,1536]{1,0:T(8,128)(2,1)} collective-permute-done((bf16[256,1536]{1,0:T(8,128)(2,1)}, bf16[256,1536]{1,0:T(8,128)(2,1)}, u32[]{:S(2)}, u32[]{:S(2)}) %collective-permute-start.2) | collective-permute-done | bytes 786464 | tf_op jit(solution)/shard_map/ppermute | solution.py:72
  50.4 15.6 %collective-permute-done.3 = bf16[256,1536]{1,0:T(8,128)(2,1)} collective-permute-done((bf16[256,1536]{1,0:T(8,128)(2,1)}, bf16[256,1536]{1,0:T(8,128)(2,1)}, u32[]{:S(2)}, u32[]{:S(2)}) %collective-permute-start.3) | collective-permute-done | bytes 786464 | tf_op jit(solution)/shard_map/ppermute | solution.py:72
  76.1 34.4 %collective-permute-done.10 = bf16[2,1024,512]{2,1,0:T(8,128)(2,1)} collective-permute-done((bf16[2,1024,512]{2,1,0:T(8,128)(2,1)}, bf16[2,1024,512]{2,1,0:T(8,128)(2,1)}, u32[]{:S(2)}, u32[]{:S(2)}) %collective-permute-start.10) | collective-permute-done | bytes 2097184 | tf_op jit(solution)/shard_map/ppermute | solution.py:72
  117.2 7.6 collective-permute-done.4
  149.9 13.5 %collective-permute-done.8 = bf16[128,2048]{1,0:T(8,128)(2,1)S(1)} collective-permute-done((bf16[128,2048]{1,0:T(8,128)(2,1)}, bf16[128,2048]{1,0:T(8,128)(2,1)S(1)}, u32[]{:S(2)}, u32[]{:S(2)}) %collective-permute-start.8) | collective-permute-done | bytes 524320 | tf_op jit(solution)/shard_map/ppermute | solution.py:72
  176.5 40.1 %collective-permute-done.14 = bf16[2,512,1024]{2,1,0:T(8,128)(2,1)} collective-permute-done((bf16[2,512,1024]{2,1,0:T(8,128)(2,1)}, bf16[2,512,1024]{2,1,0:T(8,128)(2,1)}, u32[]{:S(2)}, u32[]{:S(2)}) %collective-permute-start.14) | collective-permute-done | bytes 2097184 | tf_op jit(solution)/shard_map/ppermute | solution.py:72
  220.3 41.3 %collective-permute-done.15 = bf16[2,512,1024]{2,1,0:T(8,128)(2,1)} collective-permute-done((bf16[2,512,1024]{2,1,0:T(8,128)(2,1)}, bf16[2,512,1024]{2,1,0:T(8,128)(2,1)}, u32[]{:S(2)}, u32[]{:S(2)}) %collective-permute-start.15) | collective-permute-done | bytes 2097184 | tf_op jit(solution)/shard_map/ppermute | solution.py:72
  291.5 96.7 %maximum_maximum_fusion = bf16[2048,4096]{1,0:T(8,128)(2,1)} fusion(bf16[512,1024]{1,0:T(8,128)(2,1)} %get-tuple-element.150, bf16[512,1024]{1,0:T(8,128)(2,1)} %get-tuple-element.149, bf16[512,1024]{1,0:T(8,128)(2,1)} %get-tuple-element.148, bf16[512,1024]{1,0:T(8,128)(2,1)} %get-tuple-element.147, bf16[512,1024]{1,0:T(8,128)(2,1)} %get-tuple-element.146, ...), kind=kLoop, calls=%fused_computation | loop fusion | flops 268435456 | bytes 33554432 | tf_op jit(solution)/shard_map/concatenate | solution.py:257
  388.2 23.5 %fusion.124 = f32[1024,4096]{1,0:T(8,128)} fusion(bf16[1024,2048]{1,0:T(8,128)(2,1)} %all-gather.14.cloned.1.call-done, bf16[2048,4096]{1,0:T(8,128)(2,1)} %maximum_maximum_fusion), kind=kOutput, calls=%fused_computation.355 | convolution fusion | flops 17179869184 | bytes 37748736 | tf_op jit(solution)/shard_map/dot_general | solution.py:59
  414.5 24.3 %multiply_convert_fusion.1 = (bf16[1024,2048]{1,0:T(8,128)(2,1)}, bf16[1024,2048]{1,0:T(8,128)(2,1)}, f32[1024,2048]{1,0:T(8,128)}, bf16[1024,2048]{1,0:T(8,128)(2,1)}) fusion(f32[1024,4096]{1,0:T(8,128)} %fusion.124, f32[1024,1024]{1,0:T(8,128)} %broadcast_in_dim.43, f32[1024,1024]{1,0:T(8,128)S(1)} %broadcast_in_dim.40, ...), kind=kOutput, calls=%fused_computation.10 | convolution fusion | flops 8663334912 | bytes 58720256 | tf_op jit(solution)/shard_map/dot_general | solution.py:63
  438.8 7.9 pad_maximum_fusion.2
  446.7 24.0 %convolution_convert_fusion = bf16[1024,2048]{1,0:T(8,128)(2,1)} fusion(bf16[2048,4096]{1,0:T(8,128)(2,1)} %maximum_maximum_fusion, bf16[1024,2048]{1,0:T(8,128)(2,1)} %get-tuple-element.109, bf16[1024,2048]{1,0:T(8,128)(2,1)} %get-tuple-element.108), kind=kOutput, calls=%fused_computation.24 | convolution fusion | flops 17198743552 | bytes 29360128 | tf_op jit(solution)/shard_map/dot_general | solution.py:63
  470.7 10.4 %fusion.29 = bf16[512,4096]{1,0:T(8,128)(2,1)} fusion(bf16[1024,4096]{1,0:T(8,128)(2,1)} %pad_maximum_fusion.2, bf16[1024,2048]{1,0:T(8,128)(2,1)} %all-gather.14.cloned.1.call-done), kind=kOutput, calls=%fused_computation.79 | convolution fusion | flops 4294967296 | bytes 13631488 | tf_op jit(solution)/shard_map/dot_general | solution.py:67
  510.5 11.8 %reshape.379 = f32[1024,2,1024]{2,1,0:T(2,128)} reshape(f32[1024,2048]{1,0:T(8,128)} %get-tuple-element.110) | data formatting | bytes 16777216 | tf_op jit(solution)/shard_map/reshape | solution.py:290
  538.0 11.7 %add_convert_fusion = bf16[512,4096]{1,0:T(8,128)(2,1)} fusion(bf16[512,4096]{1,0:T(8,128)(2,1)} %collective-permute-done.26, bf16[1024,4096]{1,0:T(8,128)(2,1)} %pad_maximum_fusion.2, bf16[1024,2048]{1,0:T(8,128)(2,1)} %all-gather.14.cloned.1.call-done), kind=kOutput, calls=%fused_computation.8 | convolution fusion | flops 4301258752 | bytes 17825792 | tf_op jit(solution)/shard_map/dot_general | solution.py:67
  562.9 13.4 %convolution_convert_fusion.2 = bf16[1024,2048]{1,0:T(8,128)(2,1)} fusion(bf16[1024,2048]{1,0:T(8,128)(2,1)S(1)} %copy-done.116, bf16[2048,512]{1,0:T(8,128)(2,1)} %bitcast.33, bf16[2048,512]{1,0:T(8,128)(2,1)} %bitcast.32, bf16[2048,512]{1,0:T(8,128)(2,1)} %bitcast.31, bf16[2048,512]{1,0:T(8,128)(2,1)} %bitcast.30), kind=kOutput, calls=%fused_computation.26 | convolution fusion | flops 8625586176 | bytes 16777216 | tf_op jit(solution)/shard_map/dot_general | solution.py:59
  583.6 11.3 %collective-permute-done.19 = bf16[128,2048]{1,0:T(8,128)(2,1)} collective-permute-done((bf16[128,2048]{1,0:T(8,128)(2,1)}, bf16[128,2048]{1,0:T(8,128)(2,1)}, u32[]{:S(2)}, u32[]{:S(2)}) %collective-permute-start.19) | collective-permute-done | bytes 524320 | tf_op jit(solution)/shard_map/ppermute | solution.py:72
  692.6 62.0 %all-to-all-done.3 = f32[4,1,1280]{2,1,0:T(1,128)S(1)} async-done(((f32[4,1,1280]{2,1,0:T(1,128)}), f32[4,1,1280]{2,1,0:T(1,128)S(1)}, u32[]{:S(2)}, u32[]{:S(2)}) %all-to-all-start.3) | async-done | bytes 20512 | tf_op jit(solution)/shard_map/all_to_all | solution.py:413
  779.0 41.9 %all-to-all-done.6 = bf16[8,64,2048]{2,1,0:T(8,128)(2,1)} async-done(((bf16[8,64,2048]{2,1,0:T(8,128)(2,1)}), bf16[8,64,2048]{2,1,0:T(8,128)(2,1)}, u32[]{:S(2)}, u32[]{:S(2)}) %all-to-all-start.6) | async-done | bytes 2097184 | tf_op jit(solution)/shard_map/all_to_all | solution.py:345
  820.9 7.9 all-to-all-start.4
  828.8 11.6 %convert_add_fusion = f32[512,4096]{1,0:T(8,128)} fusion(bf16[512,4096]{1,0:T(8,128)(2,1)} %collective-permute-done.27, f32[512,4096]{1,0:T(8,128)} %fusion.31, bf16[512,4096]{1,0:T(8,128)(2,1)} %collective-permute-done.25), kind=kLoop, calls=%fused_computation.7 | loop fusion | flops 8388608 | bytes 25165824 | tf_op jit(solution)/shard_map/add | solution.py:94
  859.8 29.1 %collective-permute-done.30 = bf16[2048,512]{1,0:T(8,128)(2,1)} collective-permute-done((bf16[2048,512]{1,0:T(8,128)(2,1)}, bf16[2048,512]{1,0:T(8,128)(2,1)}, u32[]{:S(2)}, u32[]{:S(2)}) %collective-permute-start.30) | collective-permute-done | bytes 2097184 | tf_op jit(solution)/shard_map/ppermute | solution.py:72
  900.2 7.1 all-to-all-start.5
  909.5 8.0 all-to-all-done.5
  (509 shorter events, 350.9 us)
Async XLA Ops:
  7.2 59.0 %all-gather.10.cloned.1.call-start = ((), (), s32[]{:S(2)}) async-start(), calls=%async_computation.10 | async-start | bytes 2621440 | tf_op jit(solution)/shard_map/all_gather | solution.py:162
  7.9 158.1 %all-gather.12.cloned.1.call-start = ((), (), s32[]{:S(2)}) async-start(), calls=%async_computation.11 | async-start | bytes 4718592 | tf_op jit(solution)/shard_map/all_gather | solution.py:189
  24.0 50.6 %collective-permute-start.1 = (bf16[256,1536]{1,0:T(8,128)(2,1)}, bf16[256,1536]{1,0:T(8,128)(2,1)}, u32[]{:S(2)}, u32[]{:S(2)}) collective-permute-start(bf16[256,1536]{1,0:T(8,128)(2,1)} %get-tuple-element.176), channel_id=1, source_target_pairs={{0,1},{1,0},{2,3},{3,2},{4,5},{5,4},{6,7},{7,6},{8,9},{9,8},{10,11... | collective-permute-start | bytes 2359304 | tf_op jit(solution)/shard_map/ppermute | solution.py:72
  26.4 88.8 %collective-permute-start = (bf16[256,1536]{1,0:T(8,128)(2,1)}, bf16[256,1536]{1,0:T(8,128)(2,1)}, u32[]{:S(2)}, u32[]{:S(2)}) collective-permute-start(bf16[256,1536]{1,0:T(8,128)(2,1)} %get-tuple-element.175), channel_id=1, source_target_pairs={{0,1},{1,0},{2,3},{3,2},{4,5},{5,4},{6,7},{7,6},{8,9},{9,8},{10,11... | collective-permute-start | bytes 2359304 | tf_op jit(solution)/shard_map/ppermute | solution.py:72
  48.8 61.8 %collective-permute-start.10 = (bf16[2,1024,512]{2,1,0:T(8,128)(2,1)}, bf16[2,1024,512]{2,1,0:T(8,128)(2,1)}, u32[]{:S(2)}, u32[]{:S(2)}) collective-permute-start(bf16[2,1024,512]{2,1,0:T(8,128)(2,1)} %param.32), channel_id=1, source_target_pairs={{0,2},{1,3},{2,0},{3,1},{4,6},{5,7},{6,4},{7,5},{8,10},{9,11},{10,... | collective-permute-start | bytes 6291464 | tf_op jit(solution)/shard_map/ppermute | solution.py:72
  49.2 116.7 %collective-permute-start.9 = (bf16[2,1024,512]{2,1,0:T(8,128)(2,1)}, bf16[2,1024,512]{2,1,0:T(8,128)(2,1)}, u32[]{:S(2)}, u32[]{:S(2)}) collective-permute-start(bf16[2,1024,512]{2,1,0:T(8,128)(2,1)} %param.32), channel_id=1, source_target_pairs={{0,1},{1,0},{2,3},{3,2},{4,5},{5,4},{6,7},{7,6},{8,9},{9,8},{10,11... | collective-permute-start | bytes 6291464 | tf_op jit(solution)/shard_map/ppermute | solution.py:72
  74.6 50.2 %collective-permute-start.4 = (bf16[256,1536]{1,0:T(8,128)(2,1)}, bf16[256,1536]{1,0:T(8,128)(2,1)S(1)}, u32[]{:S(2)}, u32[]{:S(2)}) collective-permute-start(bf16[256,1536]{1,0:T(8,128)(2,1)} %collective-permute-done.2), channel_id=1, source_target_pairs={{0,4},{4,0},{8,12},{12,8},{16,20},{20,16},{24,28},{28,24},{1,5},{5... | collective-permute-start | bytes 2359304 | tf_op jit(solution)/shard_map/ppermute | solution.py:72
  110.6 55.4 %collective-permute-start.11 = (bf16[2,1024,512]{2,1,0:T(8,128)(2,1)}, bf16[2,1024,512]{2,1,0:T(8,128)(2,1)}, u32[]{:S(2)}, u32[]{:S(2)}) collective-permute-start(bf16[2,1024,512]{2,1,0:T(8,128)(2,1)} %collective-permute-done.10), channel_id=1, source_target_pairs={{0,1},{1,0},{2,3},{3,2},{4,5},{5,4},{6,7},{7,6},{8,9},{9,8},{10,11... | collective-permute-start | bytes 6291464 | tf_op jit(solution)/shard_map/ppermute | solution.py:72
  170.2 91.4 %collective-permute-start.15 = (bf16[2,512,1024]{2,1,0:T(8,128)(2,1)}, bf16[2,512,1024]{2,1,0:T(8,128)(2,1)}, u32[]{:S(2)}, u32[]{:S(2)}) collective-permute-start(bf16[2,512,1024]{2,1,0:T(8,128)(2,1)} %param.31), channel_id=1, source_target_pairs={{0,2},{1,3},{2,0},{3,1},{4,6},{5,7},{6,4},{7,5},{8,10},{9,11},{10,... | collective-permute-start | bytes 6291464 | tf_op jit(solution)/shard_map/ppermute | solution.py:72
  171.7 107.3 %collective-permute-start.12 = (bf16[2,512,1024]{2,1,0:T(8,128)(2,1)}, bf16[2,512,1024]{2,1,0:T(8,128)(2,1)}, u32[]{:S(2)}, u32[]{:S(2)}) collective-permute-start(bf16[2,512,1024]{2,1,0:T(8,128)(2,1)} %param.30), channel_id=1, source_target_pairs={{0,1},{1,0},{2,3},{3,2},{4,5},{5,4},{6,7},{7,6},{8,9},{9,8},{10,11... | collective-permute-start | bytes 6291464 | tf_op jit(solution)/shard_map/ppermute | solution.py:72
  173.3 108.7 %collective-permute-start.13 = (bf16[2,512,1024]{2,1,0:T(8,128)(2,1)}, bf16[2,512,1024]{2,1,0:T(8,128)(2,1)}, u32[]{:S(2)}, u32[]{:S(2)}) collective-permute-start(bf16[2,512,1024]{2,1,0:T(8,128)(2,1)} %param.31), channel_id=1, source_target_pairs={{0,1},{1,0},{2,3},{3,2},{4,5},{5,4},{6,7},{7,6},{8,9},{9,8},{10,11... | collective-permute-start | bytes 6291464 | tf_op jit(solution)/shard_map/ppermute | solution.py:72
  216.6 68.6 %collective-permute-start.16 = (bf16[2,512,1024]{2,1,0:T(8,128)(2,1)}, bf16[2,512,1024]{2,1,0:T(8,128)(2,1)}, u32[]{:S(2)}, u32[]{:S(2)}) collective-permute-start(bf16[2,512,1024]{2,1,0:T(8,128)(2,1)} %collective-permute-done.14), channel_id=1, source_target_pairs={{0,1},{1,0},{2,3},{3,2},{4,5},{5,4},{6,7},{7,6},{8,9},{9,8},{10,11... | collective-permute-start | bytes 6291464 | tf_op jit(solution)/shard_map/ppermute | solution.py:72
  269.5 118.7 %all-gather.14.cloned.1.call-start = ((), (), s32[]{:S(2)}) async-start(), calls=%async_computation.12 | async-start | bytes 4718592 | tf_op jit(solution)/shard_map/all_gather | solution.py:270
  272.6 303.7 %reduce-scatter.4.cloned.1.call-start = ((), (), s32[]{:S(2)}) async-start(), calls=%async_computation.13 | async-start | bytes 4718592 | tf_op jit(solution)/shard_map/reduce_scatter | solution.py:299
  481.1 56.8 %collective-permute-start.26 = (bf16[512,4096]{1,0:T(8,128)(2,1)}, bf16[512,4096]{1,0:T(8,128)(2,1)}, u32[]{:S(2)}, u32[]{:S(2)}) collective-permute-start(bf16[512,4096]{1,0:T(8,128)(2,1)} %fusion.29), channel_id=1, source_target_pairs={{0,1},{1,0},{2,3},{3,2},{4,5},{5,4},{6,7},{7,6},{8,9},{9,8},{10,11... | collective-permute-start | bytes 12582920 | tf_op jit(solution)/shard_map/ppermute | solution.py:72
  534.2 364.0 %reduce-scatter.6.cloned.1.call-start = ((), (), s32[]{:S(2)}) async-start(), calls=%async_computation.14 | async-start | bytes 4718592 | tf_op jit(solution)/shard_map/reduce_scatter | solution.py:325
  647.1 181.6 %collective-permute-start.25 = (bf16[512,4096]{1,0:T(8,128)(2,1)}, bf16[512,4096]{1,0:T(8,128)(2,1)}, u32[]{:S(2)}, u32[]{:S(2)}) collective-permute-start(bf16[512,4096]{1,0:T(8,128)(2,1)} %fusion.25), channel_id=1, source_target_pairs={{0,1},{1,0},{2,3},{3,2},{4,5},{5,4},{6,7},{7,6},{8,9},{9,8},{10,11... | collective-permute-start | bytes 12582920 | tf_op jit(solution)/shard_map/ppermute | solution.py:72
  656.7 109.7 %collective-permute-start.29 = (bf16[2048,512]{1,0:T(8,128)(2,1)}, bf16[2048,512]{1,0:T(8,128)(2,1)}, u32[]{:S(2)}, u32[]{:S(2)}) collective-permute-start(bf16[2048,512]{1,0:T(8,128)(2,1)} %convolution_convert_fusion.3), channel_id=1, source_target_pairs={{0,1},{1,0},{2,3},{3,2},{4,5},{5,4},{6,7},{7,6},{8,9},{9,8},{10,11... | collective-permute-start | bytes 6291464 | tf_op jit(solution)/shard_map/ppermute | solution.py:72
  657.1 171.6 %collective-permute-start.27 = (bf16[512,4096]{1,0:T(8,128)(2,1)}, bf16[512,4096]{1,0:T(8,128)(2,1)}, u32[]{:S(2)}, u32[]{:S(2)}) collective-permute-start(bf16[512,4096]{1,0:T(8,128)(2,1)} %add_convert_fusion), channel_id=1, source_target_pairs={{0,2},{1,3},{2,0},{3,1},{4,6},{5,7},{6,4},{7,5},{8,10},{9,11},{10,... | collective-permute-start | bytes 12582920 | tf_op jit(solution)/shard_map/ppermute | solution.py:72
  672.4 225.7 %reduce-scatter.8.cloned.1.call-start = ((), (), s32[]{:S(2)}) async-start(), calls=%async_computation.15 | async-start | bytes 4718592 | tf_op jit(solution)/shard_map/reduce_scatter | solution.py:391
  683.2 71.4 %all-to-all-start.3 = ((f32[4,1,1280]{2,1,0:T(1,128)}), f32[4,1,1280]{2,1,0:T(1,128)S(1)}, u32[]{:S(2)}, u32[]{:S(2)}) async-start(f32[4,1,1280]{2,1,0:T(1,128)} %reshape.404), calls=%async_computation.5 | async-start | bytes 40960 | tf_op jit(solution)/shard_map/all_to_all | solution.py:413
  754.6 66.3 %all-to-all-start.6 = ((bf16[8,64,2048]{2,1,0:T(8,128)(2,1)}), bf16[8,64,2048]{2,1,0:T(8,128)(2,1)}, u32[]{:S(2)}, u32[]{:S(2)}) async-start(bf16[8,64,2048]{2,1,0:T(8,128)(2,1)} %bitcast.229), calls=%async_computation.9 | async-start | bytes 4194304 | tf_op jit(solution)/shard_map/all_to_all | solution.py:345
  820.9 73.5 %all-to-all-start.4 = ((bf16[8,256,512]{2,1,0:T(8,128)(2,1)}), bf16[8,256,512]{2,1,0:T(8,128)(2,1)}, u32[]{:S(2)}, u32[]{:S(2)}) async-start(bf16[8,256,512]{2,1,0:T(8,128)(2,1)} %bitcast.228), calls=%async_computation.7 | async-start | bytes 4194304 | tf_op jit(solution)/shard_map/all_to_all | solution.py:379
  840.4 48.5 %collective-permute-start.30 = (bf16[2048,512]{1,0:T(8,128)(2,1)}, bf16[2048,512]{1,0:T(8,128)(2,1)}, u32[]{:S(2)}, u32[]{:S(2)}) collective-permute-start(bf16[2048,512]{1,0:T(8,128)(2,1)} %convert_add_fusion.2), channel_id=1, source_target_pairs={{0,2},{1,3},{2,0},{3,1},{4,6},{5,7},{6,4},{7,5},{8,10},{9,11},{10,... | collective-permute-start | bytes 6291464 | tf_op jit(solution)/shard_map/ppermute | solution.py:72
  (140 other events, 2120.4 us)
Sparse Core Ops, SparseCore 0:
  9.6 27.9 all-gather.9
  40.3 92.2 all-gather.11
  273.0 69.6 all-gather.13
  488.7 86.5 reduce-scatter.3
  596.6 89.7 reduce-scatter.5
  689.9 111.3 reduce-scatter.7

commit v3 on v2

v3 whole, which is shorter than its diff:
```python
import functools

import jax
import jax.numpy as jnp
from jax import lax
from jax.experimental import pallas as pl
from jax.experimental.pallas import tpu as pltpu
from jax.sharding import PartitionSpec as P


HEADS = 16
HEAD_DIM = 128
EXP_DEV = 2
OWNER = "expert"
SHARD = "wshard"


epsilon = 1e-05
theta_base = 10000.0


def rms_unit(activation):
    inverse = lax.rsqrt(jnp.mean(activation * activation, axis=-1, keepdims=True) + epsilon)
    return (activation * inverse, inverse)


def rms_backward(grad_out, normed, inverse, gain):
    gain_grad = jnp.sum(grad_out * normed, axis=0)
    grad_normed = grad_out * gain
    centred = grad_normed - normed * jnp.mean(grad_normed * normed, axis=-1, keepdims=True)
    return (inverse * centred, gain_grad)


def block_tables(lengths, rows):
    ends = jnp.cumsum(lengths, axis=1)
    row_index = jnp.arange(rows, dtype=jnp.int32)
    passed = (row_index[None, :, None] >= ends[:, None, :]).astype(jnp.int32)
    start = jnp.sum(passed * lengths[:, None, :], axis=2)
    allowed = (row_index[None, None, :] <= row_index[None, :, None]) & (
        row_index[None, None, :] >= start[:, :, None]
    )
    offsets = (row_index[None, :] - start).reshape(-1)
    half_dim = HEAD_DIM // 2
    frequency = theta_base ** (-2.0 * jnp.arange(half_dim, dtype=jnp.float32) / HEAD_DIM)
    angles = offsets.astype(jnp.float32)[:, None] * frequency[None, :]
    return (allowed, jnp.cos(angles), jnp.sin(angles))


def rotate(rows, cosine, sine):
    half_dim = HEAD_DIM // 2
    first = rows[..., :half_dim]
    second = rows[..., half_dim:]
    cosine = cosine[None, :, :]
    sine = sine[None, :, :]
    return jnp.concatenate([first * cosine - second * sine, second * cosine + first * sine], axis=-1)


def softmax_rows(logits):
    row_max = jnp.max(logits, axis=-1, keepdims=True)
    shifted = jnp.exp(logits - row_max)
    return shifted / jnp.sum(shifted, axis=-1, keepdims=True)


def dot(a, b):
    return jnp.dot(a, b, preferred_element_type=jnp.float32)


def dot_t(a, b):
    return lax.dot_general(a, b, (((1,), (1,)), ((), ())), preferred_element_type=jnp.float32)


def t_dot(a, b):
    return lax.dot_general(a, b, (((0,), (0,)), ((), ())), preferred_element_type=jnp.float32)


def swap(values, mask, axis_name=SHARD):
    count = lax.axis_size(axis_name)
    return lax.ppermute(values, axis_name, [(i, i ^ mask) for i in range(count)])


def after(values, *others):
    return lax.optimization_barrier((values, *others))[0]


def bits_of(count):
    return [1 << k for k in range(count.bit_length() - 1)]


def gather_far(shard):
    pieces = {0: shard}
    for bit in reversed(bits_of(lax.axis_size(SHARD))[1:]):
        for mask in list(pieces):
            pieces[mask ^ bit] = swap(pieces[mask], bit)
    return pieces


def gather_near(pieces):
    pieces = dict(pieces)
    for mask in list(pieces):
        pieces[mask ^ 1] = swap(pieces[mask], 1)
    return [pieces[mask] for mask in sorted(pieces)]


def gather_pieces(shard):
    return gather_near(gather_far(shard))


def scatter_stage(blocks, bit):
    masks = sorted(blocks, reverse=True)
    arrived = {m ^ bit: swap(blocks[m].astype(jnp.bfloat16), bit) for m in masks if m & bit}
    return {m: blocks[m] + arrived[m].astype(jnp.float32) for m in arrived}


def scatter_near(blocks):
    return scatter_stage(dict(enumerate(blocks)), 1)


def scatter_far(blocks):
    for bit in bits_of(lax.axis_size(SHARD))[1:]:
        blocks = scatter_stage(blocks, bit)
    return blocks[0]


def scatter_pieces(blocks):
    return scatter_far(scatter_near(blocks))


def block_of(array, index, count, axis):
    size = array.shape[axis] // count
    return lax.dynamic_slice_in_dim(array, index * size, size, axis)


def mixed_order(array, w_index, count):
    return jnp.concatenate(
        [block_of(array, w_index ^ mask, count, array.ndim - 1) for mask in range(count)], axis=-1
    )


def pair_dot(a, b, a_axis, b_axis):
    dims = (((a_axis,), (b_axis,)), ((0, 1), (0, 1)))
    return lax.dot_general(a, b, dims, preferred_element_type=jnp.float32)


def group_sum(values, axis_name):
    return jnp.sum(lax.all_gather(values, axis_name, axis=0), axis=0)


def expert_hidden_kernel(parts, x_ref, cot_ref, weight_ref, *refs):
    gates, ups, downs = refs[:parts], refs[parts : 2 * parts], refs[2 * parts : 3 * parts]
    hidden_ref, gate_grad_ref, up_grad_ref, route_ref = refs[3 * parts :]
    cols = gates[0].shape[0]
    f32 = jnp.float32
    gate_lin = up_lin = back = 0.0
    for m in range(parts):
        x = x_ref[:, m * cols : (m + 1) * cols]
        gate_lin = gate_lin + jnp.dot(x, gates[m][...], preferred_element_type=f32)
        up_lin = up_lin + jnp.dot(x, ups[m][...], preferred_element_type=f32)
        back = back + dot_t(cot_ref[:, m * cols : (m + 1) * cols], downs[m][...])
    weight = weight_ref[...]
    sigmoid = jax.nn.sigmoid(gate_lin)
    swish = gate_lin * sigmoid
    hidden = swish * up_lin
    product = hidden * back
    route = product[:, :128]
    for k in range(1, product.shape[1] // 128):
        route = route + product[:, k * 128 : (k + 1) * 128]
    hidden_ref[...] = (hidden * weight).astype(jnp.bfloat16)
    grad = back * weight
    gate_grad_ref[...] = (grad * up_lin * sigmoid * (1.0 + gate_lin * (1.0 - sigmoid))).astype(
        jnp.bfloat16
    )
    up_grad_ref[...] = (grad * swish).astype(jnp.bfloat16)

    @pl.when(pl.program_id(2) == 0)
    def _():
        route_ref[...] = route

    @pl.when(pl.program_id(2) > 0)
    def _():
        route_ref[...] += route


def row_tile_of(rows):
    return min(rows, 1024)


def expert_hidden(x, cot, weights, gates, ups, downs, tile=256):
    rows, width = x.shape
    parts = len(gates)
    count, cols, ff = gates[0].shape
    row_tile = row_tile_of(rows)
    steps = ff // tile
    row_spec = pl.BlockSpec((row_tile, width), lambda r, e, f: (r, 0))
    in_piece = pl.BlockSpec((None, cols, tile), lambda r, e, f: (e, 0, f))
    out_piece = pl.BlockSpec((None, tile, cols), lambda r, e, f: (e, f, 0))
    wide_spec = pl.BlockSpec((row_tile, tile), lambda r, e, f: (r, e * steps + f))
    wide = jax.ShapeDtypeStruct((rows, count * ff), jnp.bfloat16)
    return pl.pallas_call(
functools.partial(expert_hidden_kernel, parts),
grid=(rows // row_tile, count, steps),
in_specs=[row_spec, row_spec, pl.BlockSpec((None, row_tile, 1), lambda r, e, f: (e, r, 0))]
+ [in_piece] * (2 * parts)
+ [out_piece] * parts,
out_specs=[wide_spec] * 3
+ [pl.BlockSpec((None, row_tile, 128), lambda r, e, f: (e, r, 0))],
out_shape=[wide] * 3 + [jax.ShapeDtypeStruct((count, rows, 128), jnp.float32)],
compiler_params=pltpu.CompilerParams(vmem_limit_bytes=60 * 1024 * 1024),
    )(x, cot, weights, *gates, *ups, *downs)


def back_rows_kernel(parts, gate_grad_ref, up_grad_ref, *refs):
    gates, ups = refs[:parts], refs[parts : 2 * parts]
    out_ref, sum_ref = refs[2 * parts :]
    cols = gates[0].shape[0]
    step = pl.program_id(1) * pl.num_programs(2) + pl.program_id(2)
    last = pl.num_programs(1) * pl.num_programs(2) - 1
    for m in range(parts):
        at = slice(m * cols, (m + 1) * cols)
        part = dot_t(gate_grad_ref[...], gates[m][...]) + dot_t(up_grad_ref[...], ups[m][...])

        @pl.when(step == 0)
        def _():
            sum_ref[:, at] = part

        @pl.when((step > 0) & (step < last))
        def _():
            sum_ref[:, at] += part

        @pl.when(step == last)
        def _():
            out_ref[:, at] = (sum_ref[:, at] + part).astype(jnp.bfloat16)


def back_rows(gate_grad, up_grad, gates, ups, tile=512):
    rows = gate_grad.shape[0]
    parts = len(gates)
    count, cols, ff = gates[0].shape
    row_tile = row_tile_of(rows)
    steps = ff // tile
    wide_spec = pl.BlockSpec((row_tile, tile), lambda r, e, f: (r, e * steps + f))
    piece = pl.BlockSpec((None, cols, tile), lambda r, e, f: (e, 0, f))
    return pl.pallas_call(
functools.partial(back_rows_kernel, parts),
grid=(rows // row_tile, count, steps),
in_specs=[wide_spec] * 2 + [piece] * (2 * parts),
out_specs=pl.BlockSpec((row_tile, parts * cols), lambda r, e, f: (r, 0)),
out_shape=jax.ShapeDtypeStruct((rows, parts * cols), jnp.bfloat16),
scratch_shapes=[pltpu.VMEM((row_tile, parts * cols), jnp.float32)],
compiler_params=pltpu.CompilerParams(vmem_limit_bytes=60 * 1024 * 1024),
    )(gate_grad, up_grad, *gates, *ups)


def local(
    tokens,
    doc_lengths,
    expert_ids,
    attn_gain,
    query_weight,
    key_weight,
    value_weight,
    query_gain,
    key_gain,
    output_weight,
    ffn_gain,
    router_weight,
    gate_weight,
    up_weight,
    down_weight,
    cotangent,
):
    bf16 = jnp.bfloat16
    f32 = jnp.float32
    rows, width = tokens.shape
    owners = lax.axis_size(OWNER)
    parts = lax.axis_size(SHARD)
    w_index = lax.axis_index(SHARD)
    experts = EXP_DEV * owners
    group = parts * rows
    cols = width // parts
    heads = HEADS // parts
    final_rows = width // (owners * parts)
    ff = gate_weight.shape[2]

    e_index = lax.axis_index(OWNER)
    half = cols // 2
    unit = 2 * w_index + e_index % 2
    units = 2 * parts

    tokens_all = lax.all_gather(tokens, SHARD, axis=0, tiled=True)
    docs = doc_lengths.shape[1]
    lengths_row = jnp.zeros((1, cols), bf16).at[:, :docs].set(doc_lengths.astype(bf16))
    small = jnp.concatenate(
        [attn_gain[None, :], ffn_gain[None, :], lengths_row, router_weight.T], axis=0
    )
    small_all = lax.all_gather(small, SHARD, axis=0)
    attn_gain_all = small_all[:, 0, :].reshape(width).astype(f32)
    ffn_gain_all = small_all[:, 1, :].reshape(width).astype(f32)
    lengths_all = small_all[:, 2, :docs].astype(jnp.int32)
    router_t = small_all[:, 3:, :].transpose(1, 0, 2).reshape(experts, width)

    weights_in = after((query_weight, key_weight, value_weight), small_all)
    pieces = [None] * units
    for mask in reversed(range(parts)):
        piece = jnp.concatenate(
            [block_of(weight, w_index ^ mask, parts, 1) for weight in weights_in], axis=1
        )
        for side in range(2):
            pieces[2 * mask + side] = block_of(piece, side ^ (e_index % 2), 2, 0)
    for mask in reversed(range(1, parts)):
        pieces[2 * mask] = swap(pieces[2 * mask], mask)
        if mask == 1:
            pieces[3] = swap(pieces[3], 1)
    for mask in reversed(range(2, parts)):
        pieces[2 * mask + 1] = swap(pieces[2 * mask], 1, OWNER)
    cot_b = mixed_order(cotangent, w_index, parts).astype(bf16)
    cot_all = lax.all_gather(cot_b, OWNER, axis=0, tiled=True)
    down_in = after(down_weight, pieces[4])
    down_pieces = gather_far(down_in)

    unit_all, _ = rms_unit(tokens_all.astype(f32))
    attn_in = (unit_all * attn_gain_all).astype(bf16)
    attn_in_mixed = mixed_order(attn_in, unit, units)
    qkv = 0.0
    for at in [0, 1, 2, 3] + [2 * m for m in range(2, parts)] + [2 * m + 1 for m in range(2, parts)]:
        qkv = qkv + dot(attn_in_mixed[:, at * half : (at + 1) * half], pieces[at])
    query_lin, key_lin, value_lin = (qkv[:, i * cols : (i + 1) * cols] for i in range(3))
    squares = jnp.stack(
        [jnp.sum(query_lin * query_lin, axis=1), jnp.sum(key_lin * key_lin, axis=1)], axis=0
    )
    squares = group_sum(squares, SHARD)
    inverses = lax.rsqrt(squares / width + epsilon)
    query_inverse = inverses[0][:, None]
    key_inverse = inverses[1][:, None]
    query_unit = query_lin * query_inverse
    key_unit = key_lin * key_inverse
    query_gain_f = query_gain.astype(f32)
    key_gain_f = key_gain.astype(f32)
    allowed, cosine, sine = block_tables(lengths_all, rows)
    scale = HEAD_DIM ** (-0.5)

    def by_head(array):
        return jnp.stack(
            [array[:, h * HEAD_DIM : (h + 1) * HEAD_DIM] for h in range(heads)], axis=0
        )

    def by_row(array):
        return jnp.concatenate([array[h] for h in range(heads)], axis=1)

    blocked = (heads, parts, rows, HEAD_DIM)
    whole = (heads, group, HEAD_DIM)
    queries = rotate(by_head(query_unit * query_gain_f), cosine, sine).astype(bf16)
    queries = queries.reshape(blocked)
    keys = rotate(by_head(key_unit * key_gain_f), cosine, sine).astype(bf16).reshape(blocked)
    values = by_head(value_lin).astype(bf16).reshape(blocked)
    scores = pair_dot(queries, keys, 3, 3) * scale
    scores = jnp.where(allowed[None, :, :, :], scores, -1e30)
    row_max = jnp.max(scores, axis=-1, keepdims=True)
    log_total = row_max + jnp.log(jnp.sum(jnp.exp(scores - row_max), axis=-1, keepdims=True))
    probs = jnp.exp(scores - log_total)
    probs_b = probs.astype(bf16)
    mixed = pair_dot(probs_b, values, 3, 2).astype(bf16)
    attn_mix = by_row(mixed.reshape(whole))
    attn_out = dot(attn_mix, output_weight)
    attn_out = scatter_pieces(
        [block_of(attn_out, w_index ^ mask, parts, 0) for mask in range(parts)]
    )
    attn_out, cot_all, down_pieces, *pieces = lax.optimization_barrier(
        (attn_out, cot_all, down_pieces, *pieces)
    )
    down_pieces = gather_near(down_pieces)
    qkv_w = jnp.concatenate(pieces, axis=0)
    qkv_w = jnp.concatenate([block_of(qkv_w, unit ^ k, units, 0) for k in range(units)], axis=0)

    residual = tokens.astype(f32)
    middle = residual + attn_out
    unit_two, inverse_two = rms_unit(middle)
    ffn_in = (unit_two * ffn_gain_all).astype(bf16)
    ffn_in_mixed = mixed_order(ffn_in, w_index, parts)
    gate_in, up_in, ffn_in_mixed, ffn_in = lax.optimization_barrier(
        (gate_weight, up_weight, ffn_in_mixed, ffn_in)
    )
    gate_pieces = gather_pieces(gate_in)
    up_pieces = gather_pieces(up_in)
    router_probs = softmax_rows(dot_t(ffn_in, router_t))
    expert_range = jnp.arange(experts, dtype=jnp.int32)
    named = jnp.any(expert_ids[:, :, None] == expert_range[None, None, :], axis=1)
    route_table = jnp.where(named, router_probs, 0.0)

    arrived = lax.all_gather(ffn_in_mixed, OWNER, axis=0, tiled=True)
    weights = lax.all_to_all(
        route_table.reshape(rows, owners, EXP_DEV).transpose(1, 2, 0),
        OWNER,
        split_axis=0,
        concat_axis=0,
        tiled=True,
    )
    weights = weights.transpose(1, 0, 2).reshape(EXP_DEV, owners * rows, 1)
    hidden_w, gate_grad_b, up_grad_b, route_part = expert_hidden(
        arrived, cot_all, weights, gate_pieces, up_pieces, down_pieces
    )
    row_partial = back_rows(gate_grad_b, up_grad_b, gate_pieces, up_pieces)
    row_grads = lax.psum_scatter(row_partial, OWNER, scatter_dimension=0, tiled=True)
    route_back = jnp.sum(route_part, axis=2)
    route_back = lax.all_to_all(
        route_back.reshape(EXP_DEV, owners, rows).transpose(1, 0, 2),
        OWNER,
        split_axis=0,
        concat_axis=0,
        tiled=True,
    )
    part_of = lambda array, mask: array[:, mask * cols : (mask + 1) * cols]
    order = sorted(range(parts), key=lambda m: (m < parts // 2, -m))

    def ordered_blocks(make):
        blocks = [None] * parts
        for mask in order:
            blocks[mask] = make(mask)
        return blocks

    gate_blocks = ordered_blocks(lambda m: t_dot(part_of(arrived, m), gate_grad_b))
    gate_near = scatter_near(gate_blocks)
    up_blocks = ordered_blocks(lambda m: t_dot(part_of(arrived, m), up_grad_b))
    up_near = scatter_near(up_blocks)
    hidden_w, qkv_w, *_ = lax.optimization_barrier((hidden_w, qkv_w, *gate_blocks, *up_blocks))
    down_blocks = ordered_blocks(lambda m: t_dot(hidden_w, part_of(cot_all, m)))
    down_near = scatter_near(down_blocks)
    gate_sum = scatter_far(gate_near)
    gate_weight_grad = jnp.stack([gate_sum[:, e * ff : (e + 1) * ff] for e in range(EXP_DEV)])
    down_all = jnp.concatenate(
        [piece.reshape(EXP_DEV * ff, cols) for piece in down_pieces], axis=1
    )
    out_partial = dot(hidden_w, down_all).astype(bf16)
    row_grads, out_partial = lax.optimization_barrier((row_grads, out_partial))
    moe_out = lax.psum_scatter(out_partial, OWNER, scatter_dimension=0, tiled=True)

    route_grad = route_back.reshape(experts, rows).T
    prob_grad = jnp.where(named, route_grad, 0.0)
    logit_grad = router_probs * (
        prob_grad - jnp.sum(router_probs * prob_grad, axis=1, keepdims=True)
    )
    logit_grad_b = logit_grad.astype(bf16)
    ffn_in_grad = mixed_order(row_grads, w_index, parts).astype(f32) + dot(logit_grad_b, router_t)
    middle_part, ffn_gain_grad = rms_backward(ffn_in_grad, unit_two, inverse_two, ffn_gain_all)
    middle_grad = cotangent + middle_part
    router_grad = t_dot(logit_grad_b, ffn_in)

    mid_all = jnp.zeros((group, width), bf16)
    mid_pieces = gather_pieces(middle_grad.astype(bf16))
    up_sum = scatter_far(after(up_near, *mid_pieces))
    up_weight_grad = jnp.stack([up_sum[:, e * ff : (e + 1) * ff] for e in range(EXP_DEV)])
    for mask, piece in enumerate(mid_pieces):
        mid_all = lax.dynamic_update_slice(mid_all, piece, ((w_index ^ mask) * rows, 0))
    output_part = t_dot(attn_mix, mid_all).astype(bf16)
    output_sum = lax.all_to_all(
        output_part.reshape(owners, final_rows, width),
        OWNER,
        split_axis=0,
        concat_axis=0,
        tiled=True,
    )
    output_sum = jnp.sum(output_sum.astype(f32), axis=0).astype(bf16)
    mix_grad = by_head(dot_t(mid_all, output_weight).astype(bf16)).reshape(blocked)
    delta = jnp.sum(mix_grad.astype(f32) * mixed.astype(f32), axis=-1, keepdims=True)
    prob_back = pair_dot(mix_grad, values, 3, 3)
    score_grad = (probs * (prob_back - delta)).astype(bf16)
    grad_queries = pair_dot(score_grad, keys, 3, 2)
    grad_keys = pair_dot(score_grad, queries, 2, 2)
    grad_values = pair_dot(probs_b, mix_grad, 2, 2)
    grad_queries = by_row(rotate((grad_queries * scale).reshape(whole), cosine, -sine))
    grad_keys = by_row(rotate((grad_keys * scale).reshape(whole), cosine, -sine))
    query_gain_grad = jnp.sum(grad_queries * query_unit, axis=0)
    key_gain_grad = jnp.sum(grad_keys * key_unit, axis=0)
    grad_queries = grad_queries * query_gain_f
    grad_keys = grad_keys * key_gain_f
    means = jnp.stack(
        [jnp.sum(grad_queries * query_unit, axis=1), jnp.sum(grad_keys * key_unit, axis=1)], axis=0
    )
    means = group_sum(means, SHARD) / width
    query_grad_b = (query_inverse * (grad_queries - query_unit * means[0][:, None])).astype(bf16)
    key_grad_b = (key_inverse * (grad_keys - key_unit * means[1][:, None])).astype(bf16)
    value_grad_b = by_row(grad_values.reshape(whole)).astype(bf16)
    qkv_grad = jnp.concatenate([query_grad_b, key_grad_b, value_grad_b], axis=1)
    attn_in_part = dot_t(qkv_grad, qkv_w)
    attn_in_grad = scatter_pieces(
        [block_of(attn_in_part, w_index ^ mask, parts, 0) for mask in range(parts)]
    )
    value_part = t_dot(attn_in, value_grad_b).astype(bf16).reshape(owners, parts * final_rows, cols)
    down_weight_grad = scatter_far(after(down_near, attn_in_part)).reshape(EXP_DEV, ff, cols)
    value_sum = lax.all_to_all(value_part, OWNER, split_axis=0, concat_axis=0, tiled=True)
    value_sum = jnp.sum(value_sum.astype(f32), axis=0).astype(bf16)
    qk_part = t_dot(attn_in, qkv_grad[:, : 2 * cols]).astype(bf16)

    unit_one, inverse_one = rms_unit(residual)
    input_part, attn_gain_grad = rms_backward(
        attn_in_grad, unit_one, inverse_one, attn_gain_all
    )
    tokens_grad = middle_grad + input_part
    moe_out = after(moe_out, attn_in_part)
    block_output = middle + mixed_order(moe_out, w_index, parts).astype(f32)

    qk_sum = lax.psum_scatter(qk_part, OWNER, scatter_dimension=0, tiled=True)
    qkv_sum = jnp.concatenate([qk_sum, value_sum], axis=1)
    qkv_sum = lax.all_to_all(qkv_sum, SHARD, split_axis=0, concat_axis=0, tiled=True)
    qkv_sum = qkv_sum.reshape(parts, final_rows, 3, cols).transpose(2, 1, 0, 3)
    qkv_sum = qkv_sum.reshape(3, final_rows, width).astype(f32)
    moves = []
    for e in range(owners):
        for w in range(parts):
            moves.append((e * parts + w, w * owners + e))
    output_sum = lax.ppermute(output_sum, (OWNER, SHARD), moves).astype(f32)

    own = jnp.zeros((2, parts, cols), f32)
    own = lax.dynamic_update_slice(
        own, jnp.stack([query_gain_grad, key_gain_grad])[:, None, :], (0, w_index, 0)
    ).reshape(2, width)
    table = jnp.concatenate([attn_gain_grad[None], ffn_gain_grad[None], own, router_grad], axis=0)
    count = table.shape[0]
    table = table.reshape(count, owners, parts * final_rows).transpose(1, 0, 2)
    table = lax.all_to_all(table, OWNER, split_axis=0, concat_axis=0, tiled=True)
    table = jnp.sum(table, axis=0)
    table = table.reshape(count, parts, final_rows).transpose(1, 0, 2)
    table = jnp.sum(
        lax.all_to_all(table, SHARD, split_axis=0, concat_axis=0, tiled=True), axis=0
    )
    return (
        block_output,
        tokens_grad,
        table[0],
        qkv_sum[0],
        qkv_sum[1],
        qkv_sum[2],
        table[2],
        table[3],
        output_sum,
        table[1],
        table[4:].T,
        gate_weight_grad,
        up_weight_grad,
        down_weight_grad,
    )


def solution(mesh):
    rows = P((OWNER, SHARD), None)
    line = P((OWNER, SHARD))
    part = P(SHARD)
    wide = P(SHARD, None)
    into = P(OWNER, SHARD, None)
    back = P(OWNER, None, SHARD)
    in_specs = (rows,) * 3 + (part, wide, wide, wide, part, part, wide, part, wide)
    in_specs = in_specs + (into, into, back, rows)
    out_specs = (rows, rows, line, rows, rows, rows, line, line, rows, line, rows)
    out_specs = out_specs + (into, into, back)

    return jax.shard_map(local, mesh=mesh, in_specs=in_specs, out_specs=out_specs, check_vma=False)
```

time: 950 us -> 779 us (0.82)
  other arithmetic: 187 us -> 88.3 us
  matrix products: 188 us -> 117 us
  Pallas kernels: 0 us -> 64.8 us
  local copies, waits for them, and re-layouts: 128 us -> 85.4 us
  waiting for transfers between devices: 333 us -> 307 us
    concatenate x2 -> x0, other arithmetic: 105 us -> none  [the longest x1 96.7 us: local(): jnp.concatenate([jnp.concatenate([g[0], g[1], u[0], u[1]], axis=1) for g,...]
    all_to_all x5, waiting for transfers between devices: 116 us -> 42.4 us  [the longest x1 29.5 us: local(): lax.all_to_all(output_part.reshape(owners, final_rows, width), OWNER, spl...]
    pallas_call x0 -> x2, Pallas kernels: none -> 64.8 us  [the longest x1 36.5 us: expert_hidden(): pl.pallas_call(functools.partial(expert_hidden_kernel, parts), grid=(rows...]
    dot_general x5 -> x3, matrix products: 57.6 us -> 10.4 us  [dot_t(): lax.dot_general(a, b, (((1,), (1,)), ((), ())), preferred_element_type=jn...]
    squeeze x8 -> x0, local copies, waits for them, and re-layouts: 24.7 us -> none  [the longest x4 12.3 us: local(): g[0]]
    ppermute x30 -> x33, waiting for transfers between devices: 215 us -> 238 us  [swap(): lax.ppermute(values, axis_name, [(i, i ^ mask) for i in range(count)])]
    dot_general x12 -> x11, matrix products: 51.2 us -> 29.7 us  [dot(): return jnp.dot(a, b, preferred_element_type=jnp.float32)]
    reduce_scatter x3, waiting for transfers between devices: 0.02 us -> 20.5 us  [the longest x1 20.5 us: local(): lax.psum_scatter(row_partial, OWNER, scatter_dimension=0, tiled=True)]
  transfers between devices with their start and end apart: 44 -> 47, of which waited for: 18 -> 15; matrix products, arithmetic and copies ran while one was open for 40% -> 33% of each run, Pallas kernels for 0% -> 0%
where the time goes in v3:
time: 779 us; the launch traced here: 767 us
  waiting for transfers between devices  307 us (39%)
  matrix products  117 us (15%)
  other arithmetic  88.3 us (11%)
  local copies, waits for them, and re-layouts  85.4 us (11%)
  starting transfers between devices  69.9 us (9%)
  Pallas kernels  64.8 us (8%)
  blocking collectives  17.9 us (2%)
  between operations  16.4 us (2%)
    ppermute x33, waiting for transfers between devices, swap(): lax.ppermute(values, axis_name, [(i, i ^ mask) for i in range(count)])  238 us
    dot_general x16, matrix products, t_dot(): lax.dot_general(a, b, (((0,), (0,)), ((), ())), preferred_element_type=jn...  68.6 us
    unnamed x227, local copies, waits for them, and re-layouts  39.2 us
    pallas_call x1, Pallas kernels, expert_hidden(): pl.pallas_call(functools.partial(expert_hidden_kernel, parts), grid=(rows...  36.5 us
    dot_general x11, matrix products, dot(): return jnp.dot(a, b, preferred_element_type=jnp.float32)  29.7 us
    all_to_all x1, waiting for transfers between devices, local(): lax.all_to_all(output_part.reshape(owners, final_rows, width), OWNER, spl...  29.5 us
    pallas_call x1, Pallas kernels, back_rows(): pl.pallas_call(functools.partial(back_rows_kernel, parts), grid=(rows //...  28.3 us
    add x6, other arithmetic, scatter_stage(): return {m: blocks[m] + arrived[m].astype(jnp.float32) for m in arrived}  27.6 us
  transfers between devices with their start and end apart: 47, of which 15 were waited for; matrix products, arithmetic and copies ran while one was open for 33% of the time, Pallas kernels for 0%

profile of v3, /device:TPU:13, one launch (start us, length us, event | category | flops | bytes accessed | tf_op | source)
XLA Modules:
  0.0 766.9 jit_solution(12515378550739882124)
XLA Ops:
  12.1 5.8 all-gather.3
  36.0 29.7 %collective-permute-done.2 = bf16[256,1536]{1,0:T(8,128)(2,1)} collective-permute-done((bf16[256,1536]{1,0:T(8,128)(2,1)}, bf16[256,1536]{1,0:T(8,128)(2,1)}, u32[]{:S(2)}, u32[]{:S(2)}) %collective-permute-start.2) | collective-permute-done | bytes 786464 | tf_op jit(solution)/shard_map/ppermute | solution.py:78
  74.4 49.5 %collective-permute-done.5 = bf16[256,1536]{1,0:T(8,128)(2,1)} collective-permute-done((bf16[256,1536]{1,0:T(8,128)(2,1)}, bf16[256,1536]{1,0:T(8,128)(2,1)}, u32[]{:S(2)}, u32[]{:S(2)}) %collective-permute-start.5) | collective-permute-done | bytes 786464 | tf_op jit(solution)/shard_map/ppermute | solution.py:78
  134.8 6.9 all-gather.4
  157.9 12.1 %collective-permute-done.8 = bf16[128,2048]{1,0:T(8,128)(2,1)S(1)} collective-permute-done((bf16[128,2048]{1,0:T(8,128)(2,1)S(1)}, bf16[128,2048]{1,0:T(8,128)(2,1)S(1)}, u32[]{:S(2)}, u32[]{:S(2)}) %collective-permute-start.8) | collective-permute-done | bytes 524320 | tf_op jit(solution)/shard_map/ppermute | solution.py:78
  189.7 35.4 %collective-permute-done.11.refs_2_ = bf16[2,512,1024]{2,1,0:T(8,128)(2,1)} collective-permute-done((bf16[2,512,1024]{2,1,0:T(8,128)(2,1)}, bf16[2,512,1024]{2,1,0:T(8,128)(2,1)}, u32[]{:S(2)}, u32[]{:S(2)}) %collective-permute-start.11) | collective-permute-done | bytes 2097184 | tf_op jit(solution)/shard_map/ppermute | solution.py:78
  226.5 43.5 %collective-permute-done.14.refs_6_ = bf16[2,512,1024]{2,1,0:T(8,128)(2,1)} collective-permute-done((bf16[2,512,1024]{2,1,0:T(8,128)(2,1)}, bf16[2,512,1024]{2,1,0:T(8,128)(2,1)}, u32[]{:S(2)}, u32[]{:S(2)}) %collective-permute-start.14) | collective-permute-done | bytes 2097184 | tf_op jit(solution)/shard_map/ppermute | solution.py:78
  284.5 36.5 %shard_map.263 = (bf16[1024,2048]{1,0:T(8,128)(2,1)}, bf16[1024,2048]{1,0:T(8,128)(2,1)}, bf16[1024,2048]{1,0:T(8,128)(2,1)}, f32[2,1024,128]{2,1,0:T(8,128)}) custom-call(bf16[1024,2048]{1,0:T(8,128)(2,1)} %all-gather.14.cloned.1.call-done.x_ref, bf16[1024,2048]{1,0:T(8,128)(2,1)} %all-gather.12.cloned.1.call-done.cot_ref, f32[2,1024,1]{2,1,0:T(8,128)} %copy.97.weight_ref, ...), custom_call_target="tpu_custom_call" | custom-call | tf_op jit(solution)/shard_map/pallas_call | solution.py:198
  321.0 28.3 %shard_map.264 = bf16[1024,2048]{1,0:T(8,128)(2,1)} custom-call(bf16[1024,2048]{1,0:T(8,128)(2,1)} %get-tuple-element.71.gate_grad_ref, bf16[1024,2048]{1,0:T(8,128)(2,1)} %get-tuple-element.72.up_grad_ref, bf16[2,512,1024]{2,1,0:T(8,128)(2,1)} %refs_0_.1, bf16[2,512,1024]{2,1,0:T(8,128)(2,1)} %collective-permute-done.10.refs_1_, ...), custom_call_target="tpu_custom_call" | custom-call | tf_op jit(solution)/shard_map/pallas_call | solution.py:242
  403.2 14.3 %fusion.11 = bf16[1024,2048]{1,0:T(8,128)(2,1)} fusion(bf16[1024,2048]{1,0:T(8,128)(2,1)} %get-tuple-element.82, bf16[2048,512]{1,0:T(8,128)(2,1)} %bitcast.39, bf16[2048,512]{1,0:T(8,128)(2,1)} %bitcast.38, bf16[2048,512]{1,0:T(8,128)(2,1)} %bitcast.37, bf16[2048,512]{1,0:T(8,128)(2,1)} %bitcast.36), kind=kOutput, calls=%fused_computation.23 | convolution fusion | flops 8625586176 | bytes 16777216 | tf_op jit(solution)/shard_map/dot_general | solution.py:65
  417.6 20.5 %reduce-scatter.4.cloned.1.call-done = bf16[128,2048]{1,0:T(8,128)(2,1)} async-done(((bf16[1024,2048]{1,0:T(8,128)(2,1)}), bf16[128,2048]{1,0:T(8,128)(2,1)}) %reduce-scatter.4.cloned.1.call-update) | async-done | bytes 524304 | tf_op jit(solution)/shard_map/reduce_scatter | solution.py:402
  447.1 9.2 %collective-permute-done.19 = bf16[128,2048]{1,0:T(8,128)(2,1)} collective-permute-done((bf16[128,2048]{1,0:T(8,128)(2,1)}, bf16[128,2048]{1,0:T(8,128)(2,1)}, u32[]{:S(2)}, u32[]{:S(2)}) %collective-permute-start.19) | collective-permute-done | bytes 524320 | tf_op jit(solution)/shard_map/ppermute | solution.py:78
  458.2 6.2 convolution_convert_fusion.2
  503.1 5.8 fusion.135
  523.9 7.0 collective-permute-done.23
  561.2 8.0 %all-to-all-start.6 = ((bf16[8,64,2048]{2,1,0:T(8,128)(2,1)}), bf16[8,64,2048]{2,1,0:T(8,128)(2,1)}, u32[]{:S(2)}, u32[]{:S(2)}) async-start(bf16[8,64,2048]{2,1,0:T(8,128)(2,1)} %bitcast.191), calls=%async_computation.9 | async-start | bytes 4194304 | tf_op jit(solution)/shard_map/all_to_all | solution.py:454
  575.3 6.2 convert_add_fusion.2
  591.6 15.7 %collective-permute-done.27 = bf16[512,2048]{1,0:T(8,128)(2,1)} collective-permute-done((bf16[512,2048]{1,0:T(8,128)(2,1)}, bf16[512,2048]{1,0:T(8,128)(2,1)}, u32[]{:S(2)}, u32[]{:S(2)}) %collective-permute-start.27) | collective-permute-done | bytes 2097184 | tf_op jit(solution)/shard_map/ppermute | solution.py:78
  616.2 29.5 %all-to-all-done.6 = bf16[8,64,2048]{2,1,0:T(8,128)(2,1)} async-done(((bf16[8,64,2048]{2,1,0:T(8,128)(2,1)}), bf16[8,64,2048]{2,1,0:T(8,128)(2,1)}, u32[]{:S(2)}, u32[]{:S(2)}) %all-to-all-start.6) | async-done | bytes 2097184 | tf_op jit(solution)/shard_map/all_to_all | solution.py:454
  645.8 7.3 all-to-all-start.4
  663.7 5.9 convert_add_fusion.3
  669.6 34.5 %collective-permute-done.33 = bf16[2048,512]{1,0:T(8,128)(2,1)} collective-permute-done((bf16[2048,512]{1,0:T(8,128)(2,1)}, bf16[2048,512]{1,0:T(8,128)(2,1)}, u32[]{:S(2)}, u32[]{:S(2)}) %collective-permute-start.33) | collective-permute-done | bytes 2097184 | tf_op jit(solution)/shard_map/ppermute | solution.py:78
  722.1 5.9 collective-permute-done.24
  738.7 8.5 %all-to-all-done.5 = bf16[4,64,1536]{2,1,0:T(8,128)(2,1)} async-done(((bf16[4,64,1536]{2,1,0:T(8,128)(2,1)}), bf16[4,64,1536]{2,1,0:T(8,128)(2,1)}, u32[]{:S(2)}, u32[]{:S(2)}) %all-to-all-start.5) | async-done | bytes 786464 | tf_op jit(solution)/shard_map/all_to_all | solution.py:503
  (472 shorter events, 318.5 us)
Async XLA Ops:
  7.2 60.3 %all-gather.10.cloned.1.call-start = ((), (), s32[]{:S(2)}) async-start(), calls=%async_computation.10 | async-start | bytes 2621440 | tf_op jit(solution)/shard_map/all_gather | solution.py:289
  7.9 164.6 %all-gather.12.cloned.1.call-start = ((), (), s32[]{:S(2)}) async-start(), calls=%async_computation.11 | async-start | bytes 4718592 | tf_op jit(solution)/shard_map/all_gather | solution.py:316
  29.3 97.0 %collective-permute-start.1 = (bf16[256,1536]{1,0:T(8,128)(2,1)}, bf16[256,1536]{1,0:T(8,128)(2,1)}, u32[]{:S(2)}, u32[]{:S(2)}) collective-permute-start(bf16[256,1536]{1,0:T(8,128)(2,1)} %get-tuple-element.160), channel_id=1, source_target_pairs={{0,1},{1,0},{2,3},{3,2},{4,5},{5,4},{6,7},{7,6},{8,9},{9,8},{10,11... | collective-permute-start | bytes 2359304 | tf_op jit(solution)/shard_map/ppermute | solution.py:78
  29.9 98.1 %collective-permute-start = (bf16[256,1536]{1,0:T(8,128)(2,1)}, bf16[256,1536]{1,0:T(8,128)(2,1)}, u32[]{:S(2)}, u32[]{:S(2)}) collective-permute-start(bf16[256,1536]{1,0:T(8,128)(2,1)} %get-tuple-element.159), channel_id=1, source_target_pairs={{0,1},{1,0},{2,3},{3,2},{4,5},{5,4},{6,7},{7,6},{8,9},{9,8},{10,11... | collective-permute-start | bytes 2359304 | tf_op jit(solution)/shard_map/ppermute | solution.py:78
  30.8 253.7 %all-gather.14.cloned.1.call-start = ((), (), s32[]{:S(2)}) async-start(), calls=%async_computation.12 | async-start | bytes 4718592 | tf_op jit(solution)/shard_map/all_gather | solution.py:389
  65.7 106.8 %collective-permute-start.9 = (bf16[2,1024,512]{2,1,0:T(8,128)(2,1)}, bf16[2,1024,512]{2,1,0:T(8,128)(2,1)}, u32[]{:S(2)}, u32[]{:S(2)}) collective-permute-start(bf16[2,1024,512]{2,1,0:T(8,128)(2,1)} %refs_8_), channel_id=1, source_target_pairs={{0,2},{1,3},{2,0},{3,1},{4,6},{5,7},{6,4},{7,5},{8,10},{9,11},{10,... | collective-permute-start | bytes 6291464 | tf_op jit(solution)/shard_map/ppermute | solution.py:78
  66.0 64.0 %collective-permute-start.4 = (bf16[256,1536]{1,0:T(8,128)(2,1)}, bf16[256,1536]{1,0:T(8,128)(2,1)}, u32[]{:S(2)}, u32[]{:S(2)}) collective-permute-start(bf16[256,1536]{1,0:T(8,128)(2,1)} %collective-permute-done.2), channel_id=1, source_target_pairs={{0,4},{4,0},{8,12},{12,8},{16,20},{20,16},{24,28},{28,24},{1,5},{5... | collective-permute-start | bytes 2359304 | tf_op jit(solution)/shard_map/ppermute | solution.py:78
  66.3 57.7 %collective-permute-start.5 = (bf16[256,1536]{1,0:T(8,128)(2,1)}, bf16[256,1536]{1,0:T(8,128)(2,1)}, u32[]{:S(2)}, u32[]{:S(2)}) collective-permute-start(bf16[256,1536]{1,0:T(8,128)(2,1)} %collective-permute-done.3), channel_id=1, source_target_pairs={{0,4},{4,0},{8,12},{12,8},{16,20},{20,16},{24,28},{28,24},{1,5},{5... | collective-permute-start | bytes 2359304 | tf_op jit(solution)/shard_map/ppermute | solution.py:78
  178.8 91.2 %collective-permute-start.14 = (bf16[2,512,1024]{2,1,0:T(8,128)(2,1)}, bf16[2,512,1024]{2,1,0:T(8,128)(2,1)}, u32[]{:S(2)}, u32[]{:S(2)}) collective-permute-start(bf16[2,512,1024]{2,1,0:T(8,128)(2,1)} %refs_4_.1), channel_id=1, source_target_pairs={{0,2},{1,3},{2,0},{3,1},{4,6},{5,7},{6,4},{7,5},{8,10},{9,11},{10,... | collective-permute-start | bytes 6291464 | tf_op jit(solution)/shard_map/ppermute | solution.py:78
  179.2 105.3 %collective-permute-start.13 = (bf16[2,512,1024]{2,1,0:T(8,128)(2,1)}, bf16[2,512,1024]{2,1,0:T(8,128)(2,1)}, u32[]{:S(2)}, u32[]{:S(2)}) collective-permute-start(bf16[2,512,1024]{2,1,0:T(8,128)(2,1)} %refs_4_.1), channel_id=1, source_target_pairs={{0,1},{1,0},{2,3},{3,2},{4,5},{5,4},{6,7},{7,6},{8,9},{9,8},{10,11... | collective-permute-start | bytes 6291464 | tf_op jit(solution)/shard_map/ppermute | solution.py:78
  181.8 101.3 %all-to-all-start = ((f32[8,2,128]{2,1,0:T(2,128)}), f32[8,2,128]{2,1,0:T(2,128)S(1)}, u32[]{:S(2)}, u32[]{:S(2)}) async-start(f32[8,2,128]{2,1,0:T(2,128)} %bitcast.33), calls=%async_computation | async-start | bytes 16384 | tf_op jit(solution)/shard_map/all_to_all | solution.py:390
  187.3 250.7 %reduce-scatter.4.cloned.1.call-start = ((), (), s32[]{:S(2)}) async-start(), calls=%async_computation.13 | async-start | bytes 4718592 | tf_op jit(solution)/shard_map/reduce_scatter | solution.py:402
  187.8 96.7 %collective-permute-start.16 = (bf16[2,1024,512]{2,1,0:T(8,128)(2,1)}, bf16[2,1024,512]{2,1,0:T(8,128)(2,1)}, u32[]{:S(2)}, u32[]{:S(2)}) collective-permute-start(bf16[2,1024,512]{2,1,0:T(8,128)(2,1)} %refs_8_), channel_id=1, source_target_pairs={{0,1},{1,0},{2,3},{3,2},{4,5},{5,4},{6,7},{7,6},{8,9},{9,8},{10,11... | collective-permute-start | bytes 6291464 | tf_op jit(solution)/shard_map/ppermute | solution.py:78
  189.6 94.9 %collective-permute-start.17 = (bf16[2,1024,512]{2,1,0:T(8,128)(2,1)}, bf16[2,1024,512]{2,1,0:T(8,128)(2,1)}, u32[]{:S(2)}, u32[]{:S(2)}) collective-permute-start(bf16[2,1024,512]{2,1,0:T(8,128)(2,1)} %collective-permute-done.9.refs_10_), channel_id=1, source_target_pairs={{0,1},{1,0},{2,3},{3,2},{4,5},{5,4},{6,7},{7,6},{8,9},{9,8},{10,11... | collective-permute-start | bytes 6291464 | tf_op jit(solution)/shard_map/ppermute | solution.py:78
  225.1 59.4 %collective-permute-start.12 = (bf16[2,512,1024]{2,1,0:T(8,128)(2,1)}, bf16[2,512,1024]{2,1,0:T(8,128)(2,1)}, u32[]{:S(2)}, u32[]{:S(2)}) collective-permute-start(bf16[2,512,1024]{2,1,0:T(8,128)(2,1)} %collective-permute-done.11.refs_2_), channel_id=1, source_target_pairs={{0,1},{1,0},{2,3},{3,2},{4,5},{5,4},{6,7},{7,6},{8,9},{9,8},{10,11... | collective-permute-start | bytes 6291464 | tf_op jit(solution)/shard_map/ppermute | solution.py:78
  403.2 326.6 %reduce-scatter.6.cloned.1.call-start = ((), (), s32[]{:S(2)}) async-start(), calls=%async_computation.14 | async-start | bytes 4718592 | tf_op jit(solution)/shard_map/reduce_scatter | solution.py:434
  445.2 95.2 %collective-permute-start.26 = (bf16[512,2048]{1,0:T(8,128)(2,1)}, bf16[512,2048]{1,0:T(8,128)(2,1)}, u32[]{:S(2)}, u32[]{:S(2)}) collective-permute-start(bf16[512,2048]{1,0:T(8,128)(2,1)} %fusion.40), channel_id=1, source_target_pairs={{0,1},{1,0},{2,3},{3,2},{4,5},{5,4},{6,7},{7,6},{8,9},{9,8},{10,11... | collective-permute-start | bytes 6291464 | tf_op jit(solution)/shard_map/ppermute | solution.py:78
  446.6 113.2 %collective-permute-start.29 = (bf16[512,2048]{1,0:T(8,128)(2,1)}, bf16[512,2048]{1,0:T(8,128)(2,1)}, u32[]{:S(2)}, u32[]{:S(2)}) collective-permute-start(bf16[512,2048]{1,0:T(8,128)(2,1)} %fusion.38), channel_id=1, source_target_pairs={{0,1},{1,0},{2,3},{3,2},{4,5},{5,4},{6,7},{7,6},{8,9},{9,8},{10,11... | collective-permute-start | bytes 6291464 | tf_op jit(solution)/shard_map/ppermute | solution.py:78
  464.4 265.4 %reduce-scatter.8.cloned.1.call-start = ((), (), s32[]{:S(2)}) async-start(), calls=%async_computation.15 | async-start | bytes 4718592 | tf_op jit(solution)/shard_map/reduce_scatter | solution.py:501
  515.7 58.6 %collective-permute-start.31 = (bf16[2048,512]{1,0:T(8,128)(2,1)}, bf16[2048,512]{1,0:T(8,128)(2,1)}, u32[]{:S(2)}, u32[]{:S(2)}) collective-permute-start(bf16[2048,512]{1,0:T(8,128)(2,1)} %convolution_convert_fusion.2), channel_id=1, source_target_pairs={{0,1},{1,0},{2,3},{3,2},{4,5},{5,4},{6,7},{7,6},{8,9},{9,8},{10,11... | collective-permute-start | bytes 6291464 | tf_op jit(solution)/shard_map/ppermute | solution.py:78
  523.1 68.5 %collective-permute-start.25 = (bf16[512,2048]{1,0:T(8,128)(2,1)}, bf16[512,2048]{1,0:T(8,128)(2,1)}, u32[]{:S(2)}, u32[]{:S(2)}) collective-permute-start(bf16[512,2048]{1,0:T(8,128)(2,1)} %fusion.48), channel_id=1, source_target_pairs={{0,1},{1,0},{2,3},{3,2},{4,5},{5,4},{6,7},{7,6},{8,9},{9,8},{10,11... | collective-permute-start | bytes 6291464 | tf_op jit(solution)/shard_map/ppermute | solution.py:78
  530.9 56.2 %collective-permute-start.28 = (bf16[512,2048]{1,0:T(8,128)(2,1)}, bf16[512,2048]{1,0:T(8,128)(2,1)}, u32[]{:S(2)}, u32[]{:S(2)}) collective-permute-start(bf16[512,2048]{1,0:T(8,128)(2,1)} %fusion.46), channel_id=1, source_target_pairs={{0,1},{1,0},{2,3},{3,2},{4,5},{5,4},{6,7},{7,6},{8,9},{9,8},{10,11... | collective-permute-start | bytes 6291464 | tf_op jit(solution)/shard_map/ppermute | solution.py:78
  561.2 84.6 %all-to-all-start.6 = ((bf16[8,64,2048]{2,1,0:T(8,128)(2,1)}), bf16[8,64,2048]{2,1,0:T(8,128)(2,1)}, u32[]{:S(2)}, u32[]{:S(2)}) async-start(bf16[8,64,2048]{2,1,0:T(8,128)(2,1)} %bitcast.191), calls=%async_computation.9 | async-start | bytes 4194304 | tf_op jit(solution)/shard_map/all_to_all | solution.py:454
  645.8 74.4 %all-to-all-start.4 = ((bf16[8,256,512]{2,1,0:T(8,128)(2,1)}), bf16[8,256,512]{2,1,0:T(8,128)(2,1)}, u32[]{:S(2)}, u32[]{:S(2)}) async-start(bf16[8,256,512]{2,1,0:T(8,128)(2,1)} %bitcast.190), calls=%async_computation.7 | async-start | bytes 4194304 | tf_op jit(solution)/shard_map/all_to_all | solution.py:489
  (125 other events, 2930.3 us)
Sparse Core Ops, SparseCore 0:
  9.6 29.1 all-gather.9
  41.5 92.2 all-gather.11
  176.7 71.2 all-gather.13
  349.5 88.5 reduce-scatter.3
  464.5 90.7 reduce-scatter.5
  558.8 155.5 reduce-scatter.7

commit v4 on v3

--- a/solution.py
+++ b/solution.py
@@ -141,8 +141,48 @@
     return lax.dot_general(a, b, dims, preferred_element_type=jnp.float32)
 
 
-def group_sum(values, axis_name):
-    return jnp.sum(lax.all_gather(values, axis_name, axis=0), axis=0)
+def group_sum(values):
+    count = lax.axis_size(SHARD)
+    blocks = values.reshape(values.shape[0], count, -1)
+    total = blocks
+    for mask in reversed(range(1, count)):
+        arrived = swap(blocks, mask)
+        total = total + jnp.stack([arrived[:, m ^ mask] for m in range(count)], axis=1)
+    return total.reshape(values.shape)
+
+
+def owner_scatter(values):
+    owners = lax.axis_size(OWNER)
+    index = lax.axis_index(OWNER)
+    if owners > 8:
+        return lax.psum_scatter(values, OWNER, scatter_dimension=0, tiled=True)[0]
+    pairs = values.reshape(owners // 2, 2, *values.shape[1:])
+    away = lax.dynamic_index_in_dim(pairs, 1 - index % 2, 1, keepdims=False)
+    kept = lax.dynamic_index_in_dim(pairs, index % 2, 1, keepdims=False)
+    arrived = swap(away, 1, OWNER)
+    near = (kept.astype(jnp.float32) + arrived.astype(jnp.float32)).astype(jnp.bfloat16)
+    total = 0.0
+    for mask in reversed(range(owners // 2)):
+        part = lax.dynamic_index_in_dim(near, (index // 2) ^ mask, 0, keepdims=False)
+        if mask:
+            part = swap(part, 2 * mask, OWNER)
+        total = total + part.astype(jnp.float32)
+    return total.astype(jnp.bfloat16)
+
+
+def place_kernel(heads_ref, values_ref, query_ref, key_ref, value_ref):
+    parts, _, cols = values_ref.shape
+    for p in range(parts):
+        at = slice(p * cols, (p + 1) * cols)
+        query_ref[:, at] = heads_ref[p, :, :cols].astype(jnp.float32)
+        key_ref[:, at] = heads_ref[p, :, cols:].astype(jnp.float32)
+        value_ref[:, at] = values_ref[p].astype(jnp.float32)
+
+
+def place(heads, values):
+    parts, rows, cols = values.shape
+    shape = jax.ShapeDtypeStruct((rows, parts * cols), jnp.float32)
+    return pl.pallas_call(place_kernel, out_shape=[shape] * 3)(heads, values)
 
 
 def expert_hidden_kernel(parts, x_ref, cot_ref, weight_ref, *refs):
@@ -286,7 +326,8 @@
     unit = 2 * w_index + e_index % 2
     units = 2 * parts
 
-    tokens_all = lax.all_gather(tokens, SHARD, axis=0, tiled=True)
+    cot_b = mixed_order(cotangent, w_index, parts).astype(bf16)
+    cot_all = lax.all_gather(cot_b, OWNER, axis=0, tiled=True)
     docs = doc_lengths.shape[1]
     lengths_row = jnp.zeros((1, cols), bf16).at[:, :docs].set(doc_lengths.astype(bf16))
     small = jnp.concatenate(
@@ -296,9 +337,14 @@
     attn_gain_all = small_all[:, 0, :].reshape(width).astype(f32)
     ffn_gain_all = small_all[:, 1, :].reshape(width).astype(f32)
     lengths_all = small_all[:, 2, :docs].astype(jnp.int32)
+    lengths_all = jnp.concatenate([block_of(lengths_all, w_index ^ m, parts, 0) for m in range(parts)])
     router_t = small_all[:, 3:, :].transpose(1, 0, 2).reshape(experts, width)
 
-    weights_in = after((query_weight, key_weight, value_weight), small_all)
+    *weights_in, tokens_in, _ = lax.optimization_barrier(
+        (query_weight, key_weight, value_weight, tokens, small_all)
+    )
+    tokens_far = gather_far(tokens_in)
+    tokens_all = jnp.concatenate(gather_near(tokens_far), axis=0)
     pieces = [None] * units
     for mask in reversed(range(parts)):
         piece = jnp.concatenate(
@@ -312,8 +358,6 @@
             pieces[3] = swap(pieces[3], 1)
     for mask in reversed(range(2, parts)):
         pieces[2 * mask + 1] = swap(pieces[2 * mask], 1, OWNER)
-    cot_b = mixed_order(cotangent, w_index, parts).astype(bf16)
-    cot_all = lax.all_gather(cot_b, OWNER, axis=0, tiled=True)
     down_in = after(down_weight, pieces[4])
     down_pieces = gather_far(down_in)
 
@@ -327,7 +371,7 @@
     squares = jnp.stack(
         [jnp.sum(query_lin * query_lin, axis=1), jnp.sum(key_lin * key_lin, axis=1)], axis=0
     )
-    squares = group_sum(squares, SHARD)
+    squares = group_sum(squares)
     inverses = lax.rsqrt(squares / width + epsilon)
     query_inverse = inverses[0][:, None]
     key_inverse = inverses[1][:, None]
@@ -361,9 +405,7 @@
     mixed = pair_dot(probs_b, values, 3, 2).astype(bf16)
     attn_mix = by_row(mixed.reshape(whole))
     attn_out = dot(attn_mix, output_weight)
-    attn_out = scatter_pieces(
-        [block_of(attn_out, w_index ^ mask, parts, 0) for mask in range(parts)]
-    )
+    attn_out = scatter_pieces([attn_out[mask * rows : (mask + 1) * rows] for mask in range(parts)])
     attn_out, cot_all, down_pieces, *pieces = lax.optimization_barrier(
         (attn_out, cot_all, down_pieces, *pieces)
     )
@@ -430,8 +472,8 @@
         [piece.reshape(EXP_DEV * ff, cols) for piece in down_pieces], axis=1
     )
     out_partial = dot(hidden_w, down_all).astype(bf16)
-    row_grads, out_partial = lax.optimization_barrier((row_grads, out_partial))
-    moe_out = lax.psum_scatter(out_partial, OWNER, scatter_dimension=0, tiled=True)
+    moe_out = owner_scatter(out_partial.reshape(owners, rows, width))
+    row_grads, route_back = lax.optimization_barrier((row_grads, route_back))
 
     route_grad = route_back.reshape(experts, rows).T
     prob_grad = jnp.where(named, route_grad, 0.0)
@@ -444,21 +486,10 @@
     middle_grad = cotangent + middle_part
     router_grad = t_dot(logit_grad_b, ffn_in)
 
-    mid_all = jnp.zeros((group, width), bf16)
     mid_pieces = gather_pieces(middle_grad.astype(bf16))
-    up_sum = scatter_far(after(up_near, *mid_pieces))
-    up_weight_grad = jnp.stack([up_sum[:, e * ff : (e + 1) * ff] for e in range(EXP_DEV)])
-    for mask, piece in enumerate(mid_pieces):
-        mid_all = lax.dynamic_update_slice(mid_all, piece, ((w_index ^ mask) * rows, 0))
+    mid_all = jnp.concatenate(mid_pieces, axis=0)
     output_part = t_dot(attn_mix, mid_all).astype(bf16)
-    output_sum = lax.all_to_all(
-        output_part.reshape(owners, final_rows, width),
-        OWNER,
-        split_axis=0,
-        concat_axis=0,
-        tiled=True,
-    )
-    output_sum = jnp.sum(output_sum.astype(f32), axis=0).astype(bf16)
+    output_sum = owner_scatter(output_part.reshape(owners, final_rows, width))
     mix_grad = by_head(dot_t(mid_all, output_weight).astype(bf16)).reshape(blocked)
     delta = jnp.sum(mix_grad.astype(f32) * mixed.astype(f32), axis=-1, keepdims=True)
     prob_back = pair_dot(mix_grad, values, 3, 3)
@@ -475,20 +506,23 @@
     means = jnp.stack(
         [jnp.sum(grad_queries * query_unit, axis=1), jnp.sum(grad_keys * key_unit, axis=1)], axis=0
     )
-    means = group_sum(means, SHARD) / width
+    means = group_sum(means) / width
+    up_sum = scatter_far(after(up_near, means))
+    up_weight_grad = jnp.stack([up_sum[:, e * ff : (e + 1) * ff] for e in range(EXP_DEV)])
     query_grad_b = (query_inverse * (grad_queries - query_unit * means[0][:, None])).astype(bf16)
     key_grad_b = (key_inverse * (grad_keys - key_unit * means[1][:, None])).astype(bf16)
     value_grad_b = by_row(grad_values.reshape(whole)).astype(bf16)
     qkv_grad = jnp.concatenate([query_grad_b, key_grad_b, value_grad_b], axis=1)
     attn_in_part = dot_t(qkv_grad, qkv_w)
     attn_in_grad = scatter_pieces(
-        [block_of(attn_in_part, w_index ^ mask, parts, 0) for mask in range(parts)]
+        [attn_in_part[mask * rows : (mask + 1) * rows] for mask in range(parts)]
     )
     value_part = t_dot(attn_in, value_grad_b).astype(bf16).reshape(owners, parts * final_rows, cols)
     down_weight_grad = scatter_far(after(down_near, attn_in_part)).reshape(EXP_DEV, ff, cols)
-    value_sum = lax.all_to_all(value_part, OWNER, split_axis=0, concat_axis=0, tiled=True)
-    value_sum = jnp.sum(value_sum.astype(f32), axis=0).astype(bf16)
-    qk_part = t_dot(attn_in, qkv_grad[:, : 2 * cols]).astype(bf16)
+    value_sum = owner_scatter(value_part).reshape(parts, final_rows, cols)
+    value_sum = lax.all_to_all(value_sum, SHARD, split_axis=0, concat_axis=0, tiled=True)
+    qk_part = t_dot(attn_in, qkv_grad[:, : 2 * cols])
+    qk_part = qk_part.astype(bf16)
 
     unit_one, inverse_one = rms_unit(residual)
     input_part, attn_gain_grad = rms_backward(
@@ -499,10 +533,9 @@
     block_output = middle + mixed_order(moe_out, w_index, parts).astype(f32)
 
     qk_sum = lax.psum_scatter(qk_part, OWNER, scatter_dimension=0, tiled=True)
-    qkv_sum = jnp.concatenate([qk_sum, value_sum], axis=1)
-    qkv_sum = lax.all_to_all(qkv_sum, SHARD, split_axis=0, concat_axis=0, tiled=True)
-    qkv_sum = qkv_sum.reshape(parts, final_rows, 3, cols).transpose(2, 1, 0, 3)
-    qkv_sum = qkv_sum.reshape(3, final_rows, width).astype(f32)
+    qk_sum = qk_sum.reshape(parts, final_rows, 2 * cols)
+    qk_sum = lax.all_to_all(qk_sum, SHARD, split_axis=0, concat_axis=0, tiled=True)
+    qkv_sum = place(qk_sum, value_sum)
     moves = []
     for e in range(owners):
         for w in range(parts):

time: 779 us -> 748 us (0.960)
  local copies, waits for them, and re-layouts: 85.4 us -> 58.3 us
  starting transfers between devices: 69.9 us -> 92 us
  matrix products: 117 us -> 102 us
  blocking collectives: 17.9 us -> 5.84 us
  waiting for transfers between devices: 307 us -> 318 us
  other arithmetic: 88.3 us -> 79.1 us
    ppermute x33 -> x54, waiting for transfers between devices: 238 us -> 315 us  [swap(): lax.ppermute(values, axis_name, [(i, i ^ mask) for i in range(count)])]
    all_to_all x3 -> x2, waiting for transfers between devices: 38.1 us -> 2.99 us  [the longest x1 2.99 us: local(): lax.all_to_all(qk_sum, SHARD, split_axis=0, concat_axis=0, tiled=True)]
    ppermute x33 -> x54, starting transfers between devices: 25.2 us -> 56.9 us  [swap(): lax.ppermute(values, axis_name, [(i, i ^ mask) for i in range(count)])]
    reduce_scatter x1, waiting for transfers between devices: 20.5 us -> 0.01 us  [local(): lax.psum_scatter(row_partial, OWNER, scatter_dimension=0, tiled=True)]
    unnamed x227 -> x232, local copies, waits for them, and re-layouts: 39.2 us -> 23.3 us
    all_gather x2 -> x0, blocking collectives: 12.1 us -> none  [group_sum(): return jnp.sum(lax.all_gather(values, axis_name, axis=0), axis=0)]
    convert_element_type x0 -> x8, other arithmetic: none -> 10.1 us  [the longest x3 4.48 us: owner_scatter(): (kept.astype(jnp.float32) + arrived.astype(jnp.float32)).astype(jnp.bfloa...]
    all_to_all x3 -> x2, starting transfers between devices: 20.1 us -> 12.5 us  [the longest x1 8.57 us: local(): lax.all_to_all(value_sum, SHARD, split_axis=0, concat_axis=0, tiled=True)]
  transfers between devices with their start and end apart: 47 -> 65, of which waited for: 15 -> 23; matrix products, arithmetic and copies ran while one was open for 33% -> 28% of each run, Pallas kernels for 0% -> 0%
where the time goes in v4:
time: 748 us; the launch traced here: 738 us
  waiting for transfers between devices  318 us (43%)
  matrix products  102 us (14%)
  starting transfers between devices  92 us (12%)
  other arithmetic  79.1 us (11%)
  Pallas kernels  67.1 us (9%)
  local copies, waits for them, and re-layouts  58.3 us (8%)
  between operations  16.1 us (2%)
    ppermute x54, waiting for transfers between devices, swap(): lax.ppermute(values, axis_name, [(i, i ^ mask) for i in range(count)])  315 us
    dot_general x16, matrix products, t_dot(): lax.dot_general(a, b, (((0,), (0,)), ((), ())), preferred_element_type=jn...  65.8 us
    ppermute x54, starting transfers between devices, swap(): lax.ppermute(values, axis_name, [(i, i ^ mask) for i in range(count)])  56.9 us
    pallas_call x1, Pallas kernels, expert_hidden(): pl.pallas_call(functools.partial(expert_hidden_kernel, parts), grid=(rows...  36.5 us
    pallas_call x1, Pallas kernels, back_rows(): pl.pallas_call(functools.partial(back_rows_kernel, parts), grid=(rows //...  28.3 us
    unnamed x232, local copies, waits for them, and re-layouts  23.3 us
    add x6, other arithmetic, scatter_stage(): return {m: blocks[m] + arrived[m].astype(jnp.float32) for m in arrived}  23.1 us
    dot_general x11, matrix products, dot(): return jnp.dot(a, b, preferred_element_type=jnp.float32)  22 us
  transfers between devices with their start and end apart: 65, of which 23 were waited for; matrix products, arithmetic and copies ran while one was open for 28% of the time, Pallas kernels for 0%

profile of v4, /device:TPU:13, one launch (start us, length us, event | category | flops | bytes accessed | tf_op | source)
XLA Modules:
  0.0 738.1 jit_solution(5775314019129610888)
XLA Ops:
  11.3 5.8 all-gather.1
  41.6 6.3 collective-permute-done.5
  50.5 15.2 %collective-permute-done.6 = bf16[256,1536]{1,0:T(8,128)(2,1)} collective-permute-done((bf16[256,1536]{1,0:T(8,128)(2,1)}, bf16[256,1536]{1,0:T(8,128)(2,1)}, u32[]{:S(2)}, u32[]{:S(2)}) %collective-permute-start.6) | collective-permute-done | bytes 786464 | tf_op jit(solution)/shard_map/ppermute | solution.py:78
  77.5 34.4 %collective-permute-done.8 = bf16[256,1536]{1,0:T(8,128)(2,1)S(1)} collective-permute-done((bf16[256,1536]{1,0:T(8,128)(2,1)}, bf16[256,1536]{1,0:T(8,128)(2,1)S(1)}, u32[]{:S(2)}, u32[]{:S(2)}) %collective-permute-start.8) | collective-permute-done | bytes 786464 | tf_op jit(solution)/shard_map/ppermute | solution.py:78
  126.5 12.6 %collective-permute-done.14 = bf16[128,2048]{1,0:T(8,128)(2,1)S(1)} collective-permute-done((bf16[128,2048]{1,0:T(8,128)(2,1)S(1)}, bf16[128,2048]{1,0:T(8,128)(2,1)S(1)}, u32[]{:S(2)}, u32[]{:S(2)}) %collective-permute-start.14) | collective-permute-done | bytes 524320 | tf_op jit(solution)/shard_map/ppermute | solution.py:78
  163.2 29.6 %collective-permute-done.17.refs_2_ = bf16[2,512,1024]{2,1,0:T(8,128)(2,1)} collective-permute-done((bf16[2,512,1024]{2,1,0:T(8,128)(2,1)}, bf16[2,512,1024]{2,1,0:T(8,128)(2,1)}, u32[]{:S(2)}, u32[]{:S(2)}) %collective-permute-start.17) | collective-permute-done | bytes 2097184 | tf_op jit(solution)/shard_map/ppermute | solution.py:78
  196.5 41.2 %collective-permute-done.20.refs_6_ = bf16[2,512,1024]{2,1,0:T(8,128)(2,1)} collective-permute-done((bf16[2,512,1024]{2,1,0:T(8,128)(2,1)}, bf16[2,512,1024]{2,1,0:T(8,128)(2,1)}, u32[]{:S(2)}, u32[]{:S(2)}) %collective-permute-start.20) | collective-permute-done | bytes 2097184 | tf_op jit(solution)/shard_map/ppermute | solution.py:78
  248.8 36.5 %shard_map.263 = (bf16[1024,2048]{1,0:T(8,128)(2,1)}, bf16[1024,2048]{1,0:T(8,128)(2,1)}, bf16[1024,2048]{1,0:T(8,128)(2,1)}, f32[2,1024,128]{2,1,0:T(8,128)}) custom-call(bf16[1024,2048]{1,0:T(8,128)(2,1)} %all-gather.7.cloned.1.call-done.x_ref, bf16[1024,2048]{1,0:T(8,128)(2,1)} %all-gather.5.cloned.1.call-done.cot_ref, f32[2,1024,1]{2,1,0:T(8,128)} %copy.87.weight_ref, ...), custom_call_target="tpu_custom_call" | custom-call | tf_op jit(solution)/shard_map/pallas_call | solution.py:238
  285.3 28.3 %shard_map.264 = bf16[1024,2048]{1,0:T(8,128)(2,1)} custom-call(bf16[1024,2048]{1,0:T(8,128)(2,1)} %get-tuple-element.85.gate_grad_ref, bf16[1024,2048]{1,0:T(8,128)(2,1)} %get-tuple-element.86.up_grad_ref, bf16[2,512,1024]{2,1,0:T(8,128)(2,1)} %refs_0_.1, bf16[2,512,1024]{2,1,0:T(8,128)(2,1)} %collective-permute-done.16.refs_1_, ...), custom_call_target="tpu_custom_call" | custom-call | tf_op jit(solution)/shard_map/pallas_call | solution.py:282
  313.7 6.3 fusion.48
  349.6 12.3 %fusion.12 = bf16[1024,2048]{1,0:T(8,128)(2,1)S(1)} fusion(bf16[1024,2048]{1,0:T(8,128)(2,1)} %get-tuple-element.87, bf16[2048,512]{1,0:T(8,128)(2,1)} %bitcast.43, bf16[2048,512]{1,0:T(8,128)(2,1)} %bitcast.42, bf16[2048,512]{1,0:T(8,128)(2,1)} %bitcast.41, bf16[2048,512]{1,0:T(8,128)(2,1)S(1)} %bitcast.275), kind=kOutput, calls=%fused_computation.25 | convolution fusion | flops 8625586176 | bytes 16777216 | tf_op jit(solution)/shard_map/dot_general | solution.py:65
  366.9 6.2 convolution_convert_fusion.2
  376.5 5.5 all-to-all-start.1
  387.2 34.4 %collective-permute-done.24 = bf16[4,128,2048]{2,1,0:T(8,128)(2,1)} collective-permute-done((bf16[4,128,2048]{2,1,0:T(8,128)(2,1)}, bf16[4,128,2048]{2,1,0:T(8,128)(2,1)}, u32[]{:S(2)}, u32[]{:S(2)}) %collective-permute-start.24) | collective-permute-done | bytes 2097184 | tf_op jit(solution)/shard_map/ppermute | solution.py:78
  430.1 6.1 convert_add_fusion.3
  450.9 9.7 %collective-permute-done.25 = bf16[128,2048]{1,0:T(8,128)(2,1)S(1)} collective-permute-done((bf16[128,2048]{1,0:T(8,128)(2,1)S(1)}, bf16[128,2048]{1,0:T(8,128)(2,1)S(1)}, u32[]{:S(2)}, u32[]{:S(2)}) %collective-permute-start.25) | collective-permute-done | bytes 524320 | tf_op jit(solution)/shard_map/ppermute | solution.py:78
  461.4 20.0 %collective-permute-done.26 = bf16[128,2048]{1,0:T(8,128)(2,1)S(1)} collective-permute-done((bf16[128,2048]{1,0:T(8,128)(2,1)S(1)}, bf16[128,2048]{1,0:T(8,128)(2,1)S(1)}, u32[]{:S(2)}, u32[]{:S(2)}) %collective-permute-start.26) | collective-permute-done | bytes 524320 | tf_op jit(solution)/shard_map/ppermute | solution.py:78
  541.7 5.7 fusion.163
  551.7 6.6 collective-permute-done.41
  562.4 28.3 %collective-permute-done.37 = bf16[4,256,512]{2,1,0:T(8,128)(2,1)S(1)} collective-permute-done((bf16[4,256,512]{2,1,0:T(8,128)(2,1)S(1)}, bf16[4,256,512]{2,1,0:T(8,128)(2,1)S(1)}, u32[]{:S(2)}, u32[]{:S(2)}) %collective-permute-start.37) | collective-permute-done | bytes 1048608 | tf_op jit(solution)/shard_map/ppermute | solution.py:78
  597.6 53.8 %collective-permute-done.36 = bf16[128,2048]{1,0:T(8,128)(2,1)S(1)} collective-permute-done((bf16[128,2048]{1,0:T(8,128)(2,1)S(1)}, bf16[128,2048]{1,0:T(8,128)(2,1)S(1)}, u32[]{:S(2)}, u32[]{:S(2)}) %collective-permute-start.36) | collective-permute-done | bytes 524320 | tf_op jit(solution)/shard_map/ppermute | solution.py:78
  681.6 6.8 collective-permute-done.38
  694.2 8.6 %all-to-all-start.5 = ((bf16[4,64,512]{2,1,0:T(8,128)(2,1)}), bf16[4,64,512]{2,1,0:T(8,128)(2,1)S(1)}, u32[]{:S(2)}, u32[]{:S(2)}) async-start(bf16[4,64,512]{2,1,0:T(8,128)(2,1)} %bitcast.94), calls=%async_computation.7 | async-start | bytes 524288 | tf_op jit(solution)/shard_map/all_to_all | solution.py:523
  706.1 5.8 convert_add_fusion.4
  (522 shorter events, 296.1 us)
Async XLA Ops:
  7.2 133.0 %all-gather.5.cloned.1.call-start = ((), (), s32[]{:S(2)}) async-start(), calls=%async_computation.8 | async-start | bytes 4718592 | tf_op jit(solution)/shard_map/all_gather | solution.py:330
  20.9 227.9 %all-gather.7.cloned.1.call-start = ((), (), s32[]{:S(2)}) async-start(), calls=%async_computation.9 | async-start | bytes 4718592 | tf_op jit(solution)/shard_map/all_gather | solution.py:431
  49.3 90.9 %collective-permute-start.15 = (bf16[2,1024,512]{2,1,0:T(8,128)(2,1)S(1)}, bf16[2,1024,512]{2,1,0:T(8,128)(2,1)}, u32[]{:S(2)}, u32[]{:S(2)}) collective-permute-start(bf16[2,1024,512]{2,1,0:T(8,128)(2,1)S(1)} %copy-done.46), channel_id=1, source_target_pairs={{0,2},{1,3},{2,0},{3,1},{4,6},{5,7},{6,4},{7,5},{8,10},{9,11},{10,... | collective-permute-start | bytes 6291464 | tf_op jit(solution)/shard_map/ppermute | solution.py:78
  148.3 89.3 %collective-permute-start.20 = (bf16[2,512,1024]{2,1,0:T(8,128)(2,1)}, bf16[2,512,1024]{2,1,0:T(8,128)(2,1)}, u32[]{:S(2)}, u32[]{:S(2)}) collective-permute-start(bf16[2,512,1024]{2,1,0:T(8,128)(2,1)} %refs_4_.1), channel_id=1, source_target_pairs={{0,2},{1,3},{2,0},{3,1},{4,6},{5,7},{6,4},{7,5},{8,10},{9,11},{10,... | collective-permute-start | bytes 6291464 | tf_op jit(solution)/shard_map/ppermute | solution.py:78
  149.4 99.3 %collective-permute-start.19 = (bf16[2,512,1024]{2,1,0:T(8,128)(2,1)}, bf16[2,512,1024]{2,1,0:T(8,128)(2,1)}, u32[]{:S(2)}, u32[]{:S(2)}) collective-permute-start(bf16[2,512,1024]{2,1,0:T(8,128)(2,1)} %refs_4_.1), channel_id=1, source_target_pairs={{0,1},{1,0},{2,3},{3,2},{4,5},{5,4},{6,7},{7,6},{8,9},{9,8},{10,11... | collective-permute-start | bytes 6291464 | tf_op jit(solution)/shard_map/ppermute | solution.py:78
  151.7 95.8 %all-to-all-start = ((f32[8,2,128]{2,1,0:T(2,128)}), f32[8,2,128]{2,1,0:T(2,128)S(1)}, u32[]{:S(2)}, u32[]{:S(2)}) async-start(f32[8,2,128]{2,1,0:T(2,128)} %bitcast.37), calls=%async_computation | async-start | bytes 16384 | tf_op jit(solution)/shard_map/all_to_all | solution.py:432
  157.2 325.4 %reduce-scatter.3.cloned.1.call-start = ((), (), s32[]{:S(2)}) async-start(), calls=%async_computation.10 | async-start | bytes 4718592 | tf_op jit(solution)/shard_map/reduce_scatter | solution.py:444
  157.2 91.6 %collective-permute-start.22 = (bf16[2,1024,512]{2,1,0:T(8,128)(2,1)}, bf16[2,1024,512]{2,1,0:T(8,128)(2,1)}, u32[]{:S(2)}, u32[]{:S(2)}) collective-permute-start(bf16[2,1024,512]{2,1,0:T(8,128)(2,1)} %refs_8_), channel_id=1, source_target_pairs={{0,1},{1,0},{2,3},{3,2},{4,5},{5,4},{6,7},{7,6},{8,9},{9,8},{10,11... | collective-permute-start | bytes 6291464 | tf_op jit(solution)/shard_map/ppermute | solution.py:78
  192.7 56.0 %collective-permute-start.23 = (bf16[2,1024,512]{2,1,0:T(8,128)(2,1)}, bf16[2,1024,512]{2,1,0:T(8,128)(2,1)}, u32[]{:S(2)}, u32[]{:S(2)}) collective-permute-start(bf16[2,1024,512]{2,1,0:T(8,128)(2,1)} %collective-permute-done.15.refs_10_), channel_id=1, source_target_pairs={{0,1},{1,0},{2,3},{3,2},{4,5},{5,4},{6,7},{7,6},{8,9},{9,8},{10,11... | collective-permute-start | bytes 6291464 | tf_op jit(solution)/shard_map/ppermute | solution.py:78
  196.5 52.3 %collective-permute-start.18 = (bf16[2,512,1024]{2,1,0:T(8,128)(2,1)}, bf16[2,512,1024]{2,1,0:T(8,128)(2,1)}, u32[]{:S(2)}, u32[]{:S(2)}) collective-permute-start(bf16[2,512,1024]{2,1,0:T(8,128)(2,1)} %collective-permute-done.17.refs_2_), channel_id=1, source_target_pairs={{0,1},{1,0},{2,3},{3,2},{4,5},{5,4},{6,7},{7,6},{8,9},{9,8},{10,11... | collective-permute-start | bytes 6291464 | tf_op jit(solution)/shard_map/ppermute | solution.py:78
  365.4 56.2 %collective-permute-start.24 = (bf16[4,128,2048]{2,1,0:T(8,128)(2,1)}, bf16[4,128,2048]{2,1,0:T(8,128)(2,1)}, u32[]{:S(2)}, u32[]{:S(2)}) collective-permute-start(bf16[4,128,2048]{2,1,0:T(8,128)(2,1)} %dynamic-slice_bitcast_fusion), channel_id=1, source_target_pairs={{0,4},{4,0},{8,12},{12,8},{16,20},{20,16},{24,28},{28,24},{1,5},{5... | collective-permute-start | bytes 6291464 | tf_op jit(solution)/shard_map/ppermute | solution.py:78
  366.6 58.3 %collective-permute-start.47 = (bf16[512,2048]{1,0:T(8,128)(2,1)}, bf16[512,2048]{1,0:T(8,128)(2,1)}, u32[]{:S(2)}, u32[]{:S(2)}) collective-permute-start(bf16[512,2048]{1,0:T(8,128)(2,1)} %fusion.48), channel_id=1, source_target_pairs={{0,1},{1,0},{2,3},{3,2},{4,5},{5,4},{6,7},{7,6},{8,9},{9,8},{10,11... | collective-permute-start | bytes 6291464 | tf_op jit(solution)/shard_map/ppermute | solution.py:78
  373.1 55.8 %collective-permute-start.52 = (bf16[2048,512]{1,0:T(8,128)(2,1)}, bf16[2048,512]{1,0:T(8,128)(2,1)}, u32[]{:S(2)}, u32[]{:S(2)}) collective-permute-start(bf16[2048,512]{1,0:T(8,128)(2,1)} %convolution_convert_fusion.2), channel_id=1, source_target_pairs={{0,1},{1,0},{2,3},{3,2},{4,5},{5,4},{6,7},{7,6},{8,9},{9,8},{10,11... | collective-permute-start | bytes 6291464 | tf_op jit(solution)/shard_map/ppermute | solution.py:78
  373.8 67.3 %collective-permute-start.49 = (bf16[512,2048]{1,0:T(8,128)(2,1)}, bf16[512,2048]{1,0:T(8,128)(2,1)}, u32[]{:S(2)}, u32[]{:S(2)}) collective-permute-start(bf16[512,2048]{1,0:T(8,128)(2,1)} %fusion.54), channel_id=1, source_target_pairs={{0,1},{1,0},{2,3},{3,2},{4,5},{5,4},{6,7},{7,6},{8,9},{9,8},{10,11... | collective-permute-start | bytes 6291464 | tf_op jit(solution)/shard_map/ppermute | solution.py:78
  374.1 72.8 %collective-permute-start.50 = (bf16[512,2048]{1,0:T(8,128)(2,1)}, bf16[512,2048]{1,0:T(8,128)(2,1)}, u32[]{:S(2)}, u32[]{:S(2)}) collective-permute-start(bf16[512,2048]{1,0:T(8,128)(2,1)} %fusion.46), channel_id=1, source_target_pairs={{0,1},{1,0},{2,3},{3,2},{4,5},{5,4},{6,7},{7,6},{8,9},{9,8},{10,11... | collective-permute-start | bytes 6291464 | tf_op jit(solution)/shard_map/ppermute | solution.py:78
  376.5 106.1 %all-to-all-start.1 = ((f32[8,2,128]{2,1,0:T(2,128)}), f32[8,2,128]{2,1,0:T(2,128)S(1)}, u32[]{:S(2)}, u32[]{:S(2)}) async-start(f32[8,2,128]{2,1,0:T(2,128)} %bitcast.52), calls=%async_computation.2 | async-start | bytes 16384 | tf_op jit(solution)/shard_map/all_to_all | solution.py:446
  382.0 334.3 %reduce-scatter.5.cloned.1.call-start = ((), (), s32[]{:S(2)}) async-start(), calls=%async_computation.11 | async-start | bytes 4718592 | tf_op jit(solution)/shard_map/reduce_scatter | solution.py:535
  424.9 62.7 %collective-permute-start.46 = (bf16[512,2048]{1,0:T(8,128)(2,1)}, bf16[512,2048]{1,0:T(8,128)(2,1)}, u32[]{:S(2)}, u32[]{:S(2)}) collective-permute-start(bf16[512,2048]{1,0:T(8,128)(2,1)} %fusion.56), channel_id=1, source_target_pairs={{0,1},{1,0},{2,3},{3,2},{4,5},{5,4},{6,7},{7,6},{8,9},{9,8},{10,11... | collective-permute-start | bytes 6291464 | tf_op jit(solution)/shard_map/ppermute | solution.py:78
  428.9 58.7 %collective-permute-start.48 = (bf16[512,2048]{1,0:T(8,128)(2,1)}, bf16[512,2048]{1,0:T(8,128)(2,1)}, u32[]{:S(2)}, u32[]{:S(2)}) collective-permute-start(bf16[512,2048]{1,0:T(8,128)(2,1)} %add_convert_fusion), channel_id=1, source_target_pairs={{0,2},{1,3},{2,0},{3,1},{4,6},{5,7},{6,4},{7,5},{8,10},{9,11},{10,... | collective-permute-start | bytes 6291464 | tf_op jit(solution)/shard_map/ppermute | solution.py:78
  548.3 157.9 %collective-permute-start.51 = (bf16[512,2048]{1,0:T(8,128)(2,1)}, bf16[512,2048]{1,0:T(8,128)(2,1)}, u32[]{:S(2)}, u32[]{:S(2)}) collective-permute-start(bf16[512,2048]{1,0:T(8,128)(2,1)} %convert_add_fusion.5), channel_id=1, source_target_pairs={{0,2},{1,3},{2,0},{3,1},{4,6},{5,7},{6,4},{7,5},{8,10},{9,11},{10,... | collective-permute-start | bytes 6291464 | tf_op jit(solution)/shard_map/ppermute | solution.py:78
  550.5 161.4 %collective-permute-start.54 = (bf16[2048,512]{1,0:T(8,128)(2,1)}, bf16[2048,512]{1,0:T(8,128)(2,1)}, u32[]{:S(2)}, u32[]{:S(2)}) collective-permute-start(bf16[2048,512]{1,0:T(8,128)(2,1)} %convert_add_fusion.2), channel_id=1, source_target_pairs={{0,2},{1,3},{2,0},{3,1},{4,6},{5,7},{6,4},{7,5},{8,10},{9,11},{10,... | collective-permute-start | bytes 6291464 | tf_op jit(solution)/shard_map/ppermute | solution.py:78
  558.3 93.1 %collective-permute-start.36 = (bf16[128,2048]{1,0:T(8,128)(2,1)S(1)}, bf16[128,2048]{1,0:T(8,128)(2,1)S(1)}, u32[]{:S(2)}, u32[]{:S(2)}) collective-permute-start(bf16[128,2048]{1,0:T(8,128)(2,1)S(1)} %fusion.33), channel_id=1, source_target_pairs={{0,2},{1,3},{2,0},{3,1},{4,6},{5,7},{6,4},{7,5},{8,10},{9,11},{10,... | collective-permute-start | bytes 1572872 | tf_op jit(solution)/shard_map/ppermute | solution.py:78
  590.7 72.3 %collective-permute-start.42 = (bf16[64,2048]{1,0:T(8,128)(2,1)}, bf16[64,2048]{1,0:T(8,128)(2,1)}, u32[]{:S(2)}, u32[]{:S(2)}) collective-permute-start(bf16[64,2048]{1,0:T(8,128)(2,1)} %get-tuple-element.169), channel_id=1, source_target_pairs={{0,24},{4,28},{8,16},{12,20},{16,8},{20,12},{24,0},{28,4},{1,25},{... | collective-permute-start | bytes 786440 | tf_op jit(solution)/shard_map/ppermute | solution.py:78
  594.0 70.1 %collective-permute-start.44 = (bf16[64,2048]{1,0:T(8,128)(2,1)}, bf16[64,2048]{1,0:T(8,128)(2,1)}, u32[]{:S(2)}, u32[]{:S(2)}) collective-permute-start(bf16[64,2048]{1,0:T(8,128)(2,1)} %get-tuple-element.170), channel_id=1, source_target_pairs={{0,8},{4,12},{8,0},{12,4},{16,24},{20,28},{24,16},{28,20},{1,9},{5... | collective-permute-start | bytes 786440 | tf_op jit(solution)/shard_map/ppermute | solution.py:78
  (147 other events, 2491.2 us)
Sparse Core Ops, SparseCore 0:
  21.1 78.5 all-gather.4
  144.9 70.7 all-gather.6
  313.8 94.6 reduce-scatter.2
  534.3 98.8 reduce-scatter.4

commit v5 on v4

--- a/solution.py
+++ b/solution.py
@@ -170,19 +170,16 @@
     return total.astype(jnp.bfloat16)
 
 
-def place_kernel(heads_ref, values_ref, query_ref, key_ref, value_ref):
+def place_kernel(values_ref, out_ref):
     parts, _, cols = values_ref.shape
     for p in range(parts):
-        at = slice(p * cols, (p + 1) * cols)
-        query_ref[:, at] = heads_ref[p, :, :cols].astype(jnp.float32)
-        key_ref[:, at] = heads_ref[p, :, cols:].astype(jnp.float32)
-        value_ref[:, at] = values_ref[p].astype(jnp.float32)
-
-
-def place(heads, values):
+        out_ref[:, p * cols : (p + 1) * cols] = values_ref[p].astype(jnp.float32)
+
+
+def place(values):
     parts, rows, cols = values.shape
     shape = jax.ShapeDtypeStruct((rows, parts * cols), jnp.float32)
-    return pl.pallas_call(place_kernel, out_shape=[shape] * 3)(heads, values)
+    return pl.pallas_call(place_kernel, out_shape=shape)(values)
 
 
 def expert_hidden_kernel(parts, x_ref, cot_ref, weight_ref, *refs):
@@ -326,8 +323,6 @@
     unit = 2 * w_index + e_index % 2
     units = 2 * parts
 
-    cot_b = mixed_order(cotangent, w_index, parts).astype(bf16)
-    cot_all = lax.all_gather(cot_b, OWNER, axis=0, tiled=True)
     docs = doc_lengths.shape[1]
     lengths_row = jnp.zeros((1, cols), bf16).at[:, :docs].set(doc_lengths.astype(bf16))
     small = jnp.concatenate(
@@ -358,6 +353,9 @@
             pieces[3] = swap(pieces[3], 1)
     for mask in reversed(range(2, parts)):
         pieces[2 * mask + 1] = swap(pieces[2 * mask], 1, OWNER)
+    cot_b = mixed_order(cotangent, w_index, parts).astype(bf16)
+    cot_b = after(cot_b, *pieces[5:])
+    cot_all = lax.all_gather(cot_b, OWNER, axis=0, tiled=True)
     down_in = after(down_weight, pieces[4])
     down_pieces = gather_far(down_in)
 
@@ -396,7 +394,8 @@
     queries = queries.reshape(blocked)
     keys = rotate(by_head(key_unit * key_gain_f), cosine, sine).astype(bf16).reshape(blocked)
     values = by_head(value_lin).astype(bf16).reshape(blocked)
-    scores = pair_dot(queries, keys, 3, 3) * scale
+    scores = pair_dot(queries, keys, 3, 3)
+    scores = scores * scale
     scores = jnp.where(allowed[None, :, :, :], scores, -1e30)
     row_max = jnp.max(scores, axis=-1, keepdims=True)
     log_total = row_max + jnp.log(jnp.sum(jnp.exp(scores - row_max), axis=-1, keepdims=True))
@@ -406,12 +405,12 @@
     attn_mix = by_row(mixed.reshape(whole))
     attn_out = dot(attn_mix, output_weight)
     attn_out = scatter_pieces([attn_out[mask * rows : (mask + 1) * rows] for mask in range(parts)])
-    attn_out, cot_all, down_pieces, *pieces = lax.optimization_barrier(
-        (attn_out, cot_all, down_pieces, *pieces)
-    )
+    attn_out, down_pieces, *pieces = lax.optimization_barrier((attn_out, down_pieces, *pieces))
     down_pieces = gather_near(down_pieces)
     qkv_w = jnp.concatenate(pieces, axis=0)
-    qkv_w = jnp.concatenate([block_of(qkv_w, unit ^ k, units, 0) for k in range(units)], axis=0)
+    qkv_w = jnp.concatenate(
+        [block_of(qkv_w, unit ^ k, units, 0) for k in range(units)], axis=0
+    )
 
     residual = tokens.astype(f32)
     middle = residual + attn_out
@@ -421,7 +420,8 @@
     gate_in, up_in, ffn_in_mixed, ffn_in = lax.optimization_barrier(
         (gate_weight, up_weight, ffn_in_mixed, ffn_in)
     )
-    gate_pieces = gather_pieces(gate_in)
+    gate_far = gather_far(gate_in)
+    gate_pieces = gather_near(gate_far)
     up_pieces = gather_pieces(up_in)
     router_probs = softmax_rows(dot_t(ffn_in, router_t))
     expert_range = jnp.arange(experts, dtype=jnp.int32)
@@ -440,8 +440,13 @@
     hidden_w, gate_grad_b, up_grad_b, route_part = expert_hidden(
         arrived, cot_all, weights, gate_pieces, up_pieces, down_pieces
     )
-    row_partial = back_rows(gate_grad_b, up_grad_b, gate_pieces, up_pieces)
-    row_grads = lax.psum_scatter(row_partial, OWNER, scatter_dimension=0, tiled=True)
+    row_grads = []
+    for at in (0, parts // 2):
+        chosen = slice(at, at + parts // 2)
+        row_partial = back_rows(gate_grad_b, up_grad_b, gate_pieces[chosen], up_pieces[chosen])
+        row_grads.append(owner_scatter(row_partial.reshape(owners, rows, width // 2)))
+    row_grads = jnp.concatenate(row_grads, axis=1)
+    gate_grad_b, up_grad_b, _ = lax.optimization_barrier((gate_grad_b, up_grad_b, row_partial))
     route_back = jnp.sum(route_part, axis=2)
     route_back = lax.all_to_all(
         route_back.reshape(EXP_DEV, owners, rows).transpose(1, 0, 2),
@@ -472,7 +477,7 @@
         [piece.reshape(EXP_DEV * ff, cols) for piece in down_pieces], axis=1
     )
     out_partial = dot(hidden_w, down_all).astype(bf16)
-    moe_out = owner_scatter(out_partial.reshape(owners, rows, width))
+    moe_out = lax.psum_scatter(out_partial, OWNER, scatter_dimension=0, tiled=True)
     row_grads, route_back = lax.optimization_barrier((row_grads, route_back))
 
     route_grad = route_back.reshape(experts, rows).T
@@ -507,7 +512,7 @@
         [jnp.sum(grad_queries * query_unit, axis=1), jnp.sum(grad_keys * key_unit, axis=1)], axis=0
     )
     means = group_sum(means) / width
-    up_sum = scatter_far(after(up_near, means))
+    up_sum = scatter_far(up_near)
     up_weight_grad = jnp.stack([up_sum[:, e * ff : (e + 1) * ff] for e in range(EXP_DEV)])
     query_grad_b = (query_inverse * (grad_queries - query_unit * means[0][:, None])).astype(bf16)
     key_grad_b = (key_inverse * (grad_keys - key_unit * means[1][:, None])).astype(bf16)
@@ -517,12 +522,14 @@
     attn_in_grad = scatter_pieces(
         [attn_in_part[mask * rows : (mask + 1) * rows] for mask in range(parts)]
     )
-    value_part = t_dot(attn_in, value_grad_b).astype(bf16).reshape(owners, parts * final_rows, cols)
+    placed = []
+    for grad in (value_grad_b, query_grad_b, key_grad_b):
+        part = t_dot(attn_in, grad)
+        part = part.astype(bf16).reshape(owners, parts * final_rows, cols)
+        total = owner_scatter(part).reshape(parts, final_rows, cols)
+        total = lax.all_to_all(total, SHARD, split_axis=0, concat_axis=0, tiled=True)
+        placed.append(place(total))
     down_weight_grad = scatter_far(after(down_near, attn_in_part)).reshape(EXP_DEV, ff, cols)
-    value_sum = owner_scatter(value_part).reshape(parts, final_rows, cols)
-    value_sum = lax.all_to_all(value_sum, SHARD, split_axis=0, concat_axis=0, tiled=True)
-    qk_part = t_dot(attn_in, qkv_grad[:, : 2 * cols])
-    qk_part = qk_part.astype(bf16)
 
     unit_one, inverse_one = rms_unit(residual)
     input_part, attn_gain_grad = rms_backward(
@@ -532,10 +539,6 @@
     moe_out = after(moe_out, attn_in_part)
     block_output = middle + mixed_order(moe_out, w_index, parts).astype(f32)
 
-    qk_sum = lax.psum_scatter(qk_part, OWNER, scatter_dimension=0, tiled=True)
-    qk_sum = qk_sum.reshape(parts, final_rows, 2 * cols)
-    qk_sum = lax.all_to_all(qk_sum, SHARD, split_axis=0, concat_axis=0, tiled=True)
-    qkv_sum = place(qk_sum, value_sum)
     moves = []
     for e in range(owners):
         for w in range(parts):
@@ -559,9 +562,9 @@
         block_output,
         tokens_grad,
         table[0],
-        qkv_sum[0],
-        qkv_sum[1],
-        qkv_sum[2],
+        placed[1],
+        placed[2],
+        placed[0],
         table[2],
         table[3],
         output_sum,

time: 748 us -> 860 us (1.15)
  waiting for transfers between devices: 318 us -> 402 us
  starting transfers between devices: 92 us -> 113 us
    all_to_all x2 -> x3, waiting for transfers between devices: 2.99 us -> 49 us  [local(): lax.all_to_all(total, SHARD, split_axis=0, concat_axis=0, tiled=True)]
    ppermute x54 -> x66, waiting for transfers between devices: 315 us -> 338 us  [swap(): lax.ppermute(values, axis_name, [(i, i ^ mask) for i in range(count)])]
    add x6 -> x4, other arithmetic: 23.1 us -> 7.51 us  [scatter_stage(): return {m: blocks[m] + arrived[m].astype(jnp.float32) for m in arrived}]
    ppermute x54 -> x66, starting transfers between devices: 56.9 us -> 72.1 us  [swap(): lax.ppermute(values, axis_name, [(i, i ^ mask) for i in range(count)])]
    all_gather x1, waiting for transfers between devices: 0.02 us -> 15.2 us  [local(): arrived = lax.all_gather(ffn_in_mixed, OWNER, axis=0, tiled=True)]
    pallas_call x1 -> x2, Pallas kernels: 28.3 us -> 30.7 us  [back_rows(): pl.pallas_call(functools.partial(back_rows_kernel, parts), grid=(rows //...]
    dot_general x16 -> x17, matrix products: 65.8 us -> 67.4 us  [t_dot(): lax.dot_general(a, b, (((0,), (0,)), ((), ())), preferred_element_type=jn...]
    unnamed x232 -> x302, local copies, waits for them, and re-layouts: 23.3 us -> 22.3 us
  transfers between devices with their start and end apart: 65 -> 77, of which waited for: 23 -> 31; matrix products, arithmetic and copies ran while one was open for 28% -> 26% of each run, Pallas kernels for 0% -> 2%
where the time goes in v5:
time: 860 us; the launch traced here: 849 us
  waiting for transfers between devices  402 us (47%)
  starting transfers between devices  113 us (13%)
  matrix products  107 us (12%)
  other arithmetic  73.2 us (9%)
  Pallas kernels  72.5 us (8%)
  local copies, waits for them, and re-layouts  59 us (7%)
  between operations  16.7 us (2%)
    ppermute x66, waiting for transfers between devices, swap(): lax.ppermute(values, axis_name, [(i, i ^ mask) for i in range(count)])  338 us
    ppermute x66, starting transfers between devices, swap(): lax.ppermute(values, axis_name, [(i, i ^ mask) for i in range(count)])  72.1 us
    dot_general x17, matrix products, t_dot(): lax.dot_general(a, b, (((0,), (0,)), ((), ())), preferred_element_type=jn...  67.4 us
    all_to_all x3, waiting for transfers between devices, local(): lax.all_to_all(total, SHARD, split_axis=0, concat_axis=0, tiled=True)  49 us
    pallas_call x1, Pallas kernels, expert_hidden(): pl.pallas_call(functools.partial(expert_hidden_kernel, parts), grid=(rows...  36.5 us
    pallas_call x2, Pallas kernels, back_rows(): pl.pallas_call(functools.partial(back_rows_kernel, parts), grid=(rows //...  30.7 us
    dot_general x11, matrix products, dot(): return jnp.dot(a, b, preferred_element_type=jnp.float32)  26.1 us
    unnamed x302, local copies, waits for them, and re-layouts  22.3 us
  transfers between devices with their start and end apart: 77, of which 31 were waited for; matrix products, arithmetic and copies ran while one was open for 26% of the time, Pallas kernels for 2%

profile of v5, /device:TPU:13, one launch (start us, length us, event | category | flops | bytes accessed | tf_op | source)
XLA Modules:
  0.0 849.0 jit_solution(9427927471546304387)
XLA Ops:
  38.0 9.7 %collective-permute-done.5 = bf16[256,1536]{1,0:T(8,128)(2,1)} collective-permute-done((bf16[256,1536]{1,0:T(8,128)(2,1)}, bf16[256,1536]{1,0:T(8,128)(2,1)}, u32[]{:S(2)}, u32[]{:S(2)}) %collective-permute-start.5) | collective-permute-done | bytes 786464 | tf_op jit(solution)/shard_map/ppermute | solution.py:78
  50.5 14.9 %collective-permute-done.6 = bf16[256,1536]{1,0:T(8,128)(2,1)} collective-permute-done((bf16[256,1536]{1,0:T(8,128)(2,1)}, bf16[256,1536]{1,0:T(8,128)(2,1)}, u32[]{:S(2)}, u32[]{:S(2)}) %collective-permute-start.6) | collective-permute-done | bytes 786464 | tf_op jit(solution)/shard_map/ppermute | solution.py:78
  77.7 24.3 %collective-permute-done.8 = bf16[256,1536]{1,0:T(8,128)(2,1)S(1)} collective-permute-done((bf16[256,1536]{1,0:T(8,128)(2,1)}, bf16[256,1536]{1,0:T(8,128)(2,1)S(1)}, u32[]{:S(2)}, u32[]{:S(2)}) %collective-permute-start.8) | collective-permute-done | bytes 786464 | tf_op jit(solution)/shard_map/ppermute | solution.py:78
  122.0 12.6 %collective-permute-done.14 = bf16[128,2048]{1,0:T(8,128)(2,1)S(1)} collective-permute-done((bf16[128,2048]{1,0:T(8,128)(2,1)S(1)}, bf16[128,2048]{1,0:T(8,128)(2,1)S(1)}, u32[]{:S(2)}, u32[]{:S(2)}) %collective-permute-start.14) | collective-permute-done | bytes 524320 | tf_op jit(solution)/shard_map/ppermute | solution.py:78
  158.3 27.6 %collective-permute-done.17.refs_2_.refs_0_ = bf16[2,512,1024]{2,1,0:T(8,128)(2,1)} collective-permute-done((bf16[2,512,1024]{2,1,0:T(8,128)(2,1)}, bf16[2,512,1024]{2,1,0:T(8,128)(2,1)}, u32[]{:S(2)}, u32[]{:S(2)}) %collective-permute-start.17) | collective-permute-done | bytes 2097184 | tf_op jit(solution)/shard_map/ppermute | solution.py:78
  189.7 41.2 %collective-permute-done.20.refs_6_.refs_2_ = bf16[2,512,1024]{2,1,0:T(8,128)(2,1)} collective-permute-done((bf16[2,512,1024]{2,1,0:T(8,128)(2,1)}, bf16[2,512,1024]{2,1,0:T(8,128)(2,1)}, u32[]{:S(2)}, u32[]{:S(2)}) %collective-permute-start.20) | collective-permute-done | bytes 2097184 | tf_op jit(solution)/shard_map/ppermute | solution.py:78
  238.1 15.2 %all-gather.5.cloned.1.call-done.x_ref = bf16[1024,2048]{1,0:T(8,128)(2,1)} async-done(((bf16[128,2048]{1,0:T(8,128)(2,1)}), bf16[1024,2048]{1,0:T(8,128)(2,1)}) %all-gather.5.cloned.1.call-update) | async-done | bytes 4194320 | tf_op jit(solution)/shard_map/all_gather | solution.py:431
  253.3 36.5 %shard_map.263 = (bf16[1024,2048]{1,0:T(8,128)(2,1)}, bf16[1024,2048]{1,0:T(8,128)(2,1)}, bf16[1024,2048]{1,0:T(8,128)(2,1)}, f32[2,1024,128]{2,1,0:T(8,128)}) custom-call(bf16[1024,2048]{1,0:T(8,128)(2,1)} %all-gather.5.cloned.1.call-done.x_ref, bf16[1024,2048]{1,0:T(8,128)(2,1)} %all-gather.7.cloned.1.call-done.cot_ref, f32[2,1024,1]{2,1,0:T(8,128)} %copy.100.weight_ref, ...), custom_call_target="tpu_custom_call" | custom-call | tf_op jit(solution)/shard_map/pallas_call | solution.py:235
  289.8 15.3 %shard_map.264 = bf16[1024,1024]{1,0:T(8,128)(2,1)} custom-call(bf16[1024,2048]{1,0:T(8,128)(2,1)} %get-tuple-element.84.gate_grad_ref, bf16[1024,2048]{1,0:T(8,128)(2,1)} %get-tuple-element.85.up_grad_ref, bf16[2,512,1024]{2,1,0:T(8,128)(2,1)} %collective-permute-done.17.refs_2_.refs_0_, bf16[2,512,1024]{2,1,0:T(8,128)(2,1)} %collective-permute-done.18.refs_3_.refs_1_, ...), custom_call_target="tpu_custom_call" | custom-call | tf_op jit(solution)/shard_map/pallas_call | solution.py:279
  315.5 15.4 %shard_map.265 = bf16[1024,1024]{1,0:T(8,128)(2,1)} custom-call(bf16[1024,2048]{1,0:T(8,128)(2,1)} %get-tuple-element.84.gate_grad_ref, bf16[1024,2048]{1,0:T(8,128)(2,1)} %get-tuple-element.85.up_grad_ref, bf16[2,512,1024]{2,1,0:T(8,128)(2,1)} %refs_0_.1, bf16[2,512,1024]{2,1,0:T(8,128)(2,1)} %collective-permute-done.16.refs_1_, ...), custom_call_target="tpu_custom_call" | custom-call | tf_op jit(solution)/shard_map/pallas_call | solution.py:279
  333.8 6.9 fusion.53
  359.5 18.7 %collective-permute-done.28 = bf16[4,128,1024]{2,1,0:T(8,128)(2,1)S(1)} collective-permute-done((bf16[4,128,1024]{2,1,0:T(8,128)(2,1)}, bf16[4,128,1024]{2,1,0:T(8,128)(2,1)S(1)}, u32[]{:S(2)}, u32[]{:S(2)}) %collective-permute-start.28) | collective-permute-done | bytes 1048608 | tf_op jit(solution)/shard_map/ppermute | solution.py:78
  392.3 8.7 %collective-permute-done.30 = bf16[128,1024]{1,0:T(8,128)(2,1)S(1)} collective-permute-done((bf16[128,1024]{1,0:T(8,128)(2,1)S(1)}, bf16[128,1024]{1,0:T(8,128)(2,1)S(1)}, u32[]{:S(2)}, u32[]{:S(2)}) %collective-permute-start.30) | collective-permute-done | bytes 262176 | tf_op jit(solution)/shard_map/ppermute | solution.py:78
  435.3 13.2 %fusion.11 = bf16[1024,2048]{1,0:T(8,128)(2,1)} fusion(bf16[1024,2048]{1,0:T(8,128)(2,1)S(1)} %copy-done.136, bf16[2048,512]{1,0:T(8,128)(2,1)} %bitcast.43, bf16[2048,512]{1,0:T(8,128)(2,1)} %bitcast.42, bf16[2048,512]{1,0:T(8,128)(2,1)} %bitcast.41, bf16[2048,512]{1,0:T(8,128)(2,1)} %bitcast.40), kind=kOutput, calls=%fused_computation.22 | convolution fusion | flops 8625586176 | bytes 16777216 | tf_op jit(solution)/shard_map/dot_general | solution.py:65
  512.9 11.3 %collective-permute-done.53 = bf16[4,64,2048]{2,1,0:T(8,128)(2,1)} collective-permute-done((bf16[4,64,2048]{2,1,0:T(8,128)(2,1)}, bf16[4,64,2048]{2,1,0:T(8,128)(2,1)}, u32[]{:S(2)}, u32[]{:S(2)}) %collective-permute-start.53) | collective-permute-done | bytes 1048608 | tf_op jit(solution)/shard_map/ppermute | solution.py:78
  526.9 25.4 %collective-permute-done.49 = bf16[4,256,512]{2,1,0:T(8,128)(2,1)S(1)} collective-permute-done((bf16[4,256,512]{2,1,0:T(8,128)(2,1)}, bf16[4,256,512]{2,1,0:T(8,128)(2,1)S(1)}, u32[]{:S(2)}, u32[]{:S(2)}) %collective-permute-start.49) | collective-permute-done | bytes 1048608 | tf_op jit(solution)/shard_map/ppermute | solution.py:78
  556.7 8.2 collective-permute-done.40
  582.5 16.3 %collective-permute-done.45 = bf16[4,256,512]{2,1,0:T(8,128)(2,1)} collective-permute-done((bf16[4,256,512]{2,1,0:T(8,128)(2,1)}, bf16[4,256,512]{2,1,0:T(8,128)(2,1)}, u32[]{:S(2)}, u32[]{:S(2)}) %collective-permute-start.45) | collective-permute-done | bytes 1048608 | tf_op jit(solution)/shard_map/ppermute | solution.py:78
  617.6 9.5 %collective-permute-done.51 = bf16[256,512]{1,0:T(8,128)(2,1)S(1)} collective-permute-done((bf16[256,512]{1,0:T(8,128)(2,1)S(1)}, bf16[256,512]{1,0:T(8,128)(2,1)S(1)}, u32[]{:S(2)}, u32[]{:S(2)}) %collective-permute-start.51) | collective-permute-done | bytes 262176 | tf_op jit(solution)/shard_map/ppermute | solution.py:78
  632.2 12.8 %collective-permute-done.42 = bf16[256,512]{1,0:T(8,128)(2,1)S(1)} collective-permute-done((bf16[256,512]{1,0:T(8,128)(2,1)S(1)}, bf16[256,512]{1,0:T(8,128)(2,1)S(1)}, u32[]{:S(2)}, u32[]{:S(2)}) %collective-permute-start.42) | collective-permute-done | bytes 262176 | tf_op jit(solution)/shard_map/ppermute | solution.py:78
  655.4 6.9 all-to-all-start.3
  678.0 42.5 %all-to-all-done.6.values_ref = bf16[4,64,512]{2,1,0:T(8,128)(2,1)S(1)} async-done(((bf16[4,64,512]{2,1,0:T(8,128)(2,1)}), bf16[4,64,512]{2,1,0:T(8,128)(2,1)S(1)}, u32[]{:S(2)}, u32[]{:S(2)}) %all-to-all-start.6) | async-done | bytes 262176 | tf_op jit(solution)/shard_map/all_to_all | solution.py:530
  763.0 29.3 %collective-permute-done.60 = bf16[512,2048]{1,0:T(8,128)(2,1)S(1)} collective-permute-done((bf16[512,2048]{1,0:T(8,128)(2,1)}, bf16[512,2048]{1,0:T(8,128)(2,1)S(1)}, u32[]{:S(2)}, u32[]{:S(2)}) %collective-permute-start.60) | collective-permute-done | bytes 2097184 | tf_op jit(solution)/shard_map/ppermute | solution.py:78
  796.1 41.1 %collective-permute-done.66 = bf16[2048,512]{1,0:T(8,128)(2,1)S(1)} collective-permute-done((bf16[2048,512]{1,0:T(8,128)(2,1)S(1)}, bf16[2048,512]{1,0:T(8,128)(2,1)S(1)}, u32[]{:S(2)}, u32[]{:S(2)}) %collective-permute-start.66) | collective-permute-done | bytes 2097184 | tf_op jit(solution)/shard_map/ppermute | solution.py:78
  (630 shorter events, 369.0 us)
Async XLA Ops:
  7.2 230.9 %all-gather.7.cloned.1.call-start = ((), (), s32[]{:S(2)}) async-start(), calls=%async_computation.9 | async-start | bytes 4718592 | tf_op jit(solution)/shard_map/all_gather | solution.py:358
  49.3 85.5 %collective-permute-start.15 = (bf16[2,1024,512]{2,1,0:T(8,128)(2,1)}, bf16[2,1024,512]{2,1,0:T(8,128)(2,1)}, u32[]{:S(2)}, u32[]{:S(2)}) collective-permute-start(bf16[2,1024,512]{2,1,0:T(8,128)(2,1)} %refs_8_), channel_id=1, source_target_pairs={{0,2},{1,3},{2,0},{3,1},{4,6},{5,7},{6,4},{7,5},{8,10},{9,11},{10,... | collective-permute-start | bytes 6291464 | tf_op jit(solution)/shard_map/ppermute | solution.py:78
  108.5 144.8 %all-gather.5.cloned.1.call-start = ((), (), s32[]{:S(2)}) async-start(), calls=%async_computation.8 | async-start | bytes 4718592 | tf_op jit(solution)/shard_map/all_gather | solution.py:431
  140.1 49.6 %collective-permute-start.16 = (bf16[2,512,1024]{2,1,0:T(8,128)(2,1)}, bf16[2,512,1024]{2,1,0:T(8,128)(2,1)}, u32[]{:S(2)}, u32[]{:S(2)}) collective-permute-start(bf16[2,512,1024]{2,1,0:T(8,128)(2,1)} %refs_0_.1), channel_id=1, source_target_pairs={{0,1},{1,0},{2,3},{3,2},{4,5},{5,4},{6,7},{7,6},{8,9},{9,8},{10,11... | collective-permute-start | bytes 6291464 | tf_op jit(solution)/shard_map/ppermute | solution.py:78
  141.5 89.3 %collective-permute-start.20 = (bf16[2,512,1024]{2,1,0:T(8,128)(2,1)}, bf16[2,512,1024]{2,1,0:T(8,128)(2,1)}, u32[]{:S(2)}, u32[]{:S(2)}) collective-permute-start(bf16[2,512,1024]{2,1,0:T(8,128)(2,1)} %refs_2_), channel_id=1, source_target_pairs={{0,2},{1,3},{2,0},{3,1},{4,6},{5,7},{6,4},{7,5},{8,10},{9,11},{10,... | collective-permute-start | bytes 6291464 | tf_op jit(solution)/shard_map/ppermute | solution.py:78
  142.6 95.4 %collective-permute-start.19 = (bf16[2,512,1024]{2,1,0:T(8,128)(2,1)}, bf16[2,512,1024]{2,1,0:T(8,128)(2,1)}, u32[]{:S(2)}, u32[]{:S(2)}) collective-permute-start(bf16[2,512,1024]{2,1,0:T(8,128)(2,1)} %refs_2_), channel_id=1, source_target_pairs={{0,1},{1,0},{2,3},{3,2},{4,5},{5,4},{6,7},{7,6},{8,9},{9,8},{10,11... | collective-permute-start | bytes 6291464 | tf_op jit(solution)/shard_map/ppermute | solution.py:78
  145.0 91.7 %all-to-all-start = ((f32[8,2,128]{2,1,0:T(2,128)}), f32[8,2,128]{2,1,0:T(2,128)S(1)}, u32[]{:S(2)}, u32[]{:S(2)}) async-start(f32[8,2,128]{2,1,0:T(2,128)} %bitcast.397), calls=%async_computation | async-start | bytes 16384 | tf_op jit(solution)/shard_map/all_to_all | solution.py:432
  151.1 86.9 %collective-permute-start.22 = (bf16[2,1024,512]{2,1,0:T(8,128)(2,1)}, bf16[2,1024,512]{2,1,0:T(8,128)(2,1)}, u32[]{:S(2)}, u32[]{:S(2)}) collective-permute-start(bf16[2,1024,512]{2,1,0:T(8,128)(2,1)} %refs_8_), channel_id=1, source_target_pairs={{0,1},{1,0},{2,3},{3,2},{4,5},{5,4},{6,7},{7,6},{8,9},{9,8},{10,11... | collective-permute-start | bytes 6291464 | tf_op jit(solution)/shard_map/ppermute | solution.py:78
  185.9 52.1 %collective-permute-start.23 = (bf16[2,1024,512]{2,1,0:T(8,128)(2,1)}, bf16[2,1024,512]{2,1,0:T(8,128)(2,1)}, u32[]{:S(2)}, u32[]{:S(2)}) collective-permute-start(bf16[2,1024,512]{2,1,0:T(8,128)(2,1)} %collective-permute-done.15.refs_10_), channel_id=1, source_target_pairs={{0,1},{1,0},{2,3},{3,2},{4,5},{5,4},{6,7},{7,6},{8,9},{9,8},{10,11... | collective-permute-start | bytes 6291464 | tf_op jit(solution)/shard_map/ppermute | solution.py:78
  189.7 48.4 %collective-permute-start.18 = (bf16[2,512,1024]{2,1,0:T(8,128)(2,1)}, bf16[2,512,1024]{2,1,0:T(8,128)(2,1)}, u32[]{:S(2)}, u32[]{:S(2)}) collective-permute-start(bf16[2,512,1024]{2,1,0:T(8,128)(2,1)} %collective-permute-done.17.refs_2_.refs_0_), channel_id=1, source_target_pairs={{0,1},{1,0},{2,3},{3,2},{4,5},{5,4},{6,7},{7,6},{8,9},{9,8},{10,11... | collective-permute-start | bytes 6291464 | tf_op jit(solution)/shard_map/ppermute | solution.py:78
  307.2 94.8 %all-to-all-start.1 = ((f32[8,2,128]{2,1,0:T(2,128)}), f32[8,2,128]{2,1,0:T(2,128)S(1)}, u32[]{:S(2)}, u32[]{:S(2)}) async-start(f32[8,2,128]{2,1,0:T(2,128)} %bitcast.395), calls=%async_computation.2 | async-start | bytes 16384 | tf_op jit(solution)/shard_map/all_to_all | solution.py:451
  313.2 526.6 %reduce-scatter.2.cloned.1.call-start = ((), (), s32[]{:S(2)}) async-start(), calls=%async_computation.10 | async-start | bytes 4718592 | tf_op jit(solution)/shard_map/reduce_scatter | solution.py:480
  454.9 289.9 %collective-permute-start.64 = (bf16[2048,512]{1,0:T(8,128)(2,1)}, bf16[2048,512]{1,0:T(8,128)(2,1)}, u32[]{:S(2)}, u32[]{:S(2)}) collective-permute-start(bf16[2048,512]{1,0:T(8,128)(2,1)} %convolution_convert_fusion.1), channel_id=1, source_target_pairs={{0,1},{1,0},{2,3},{3,2},{4,5},{5,4},{6,7},{7,6},{8,9},{9,8},{10,11... | collective-permute-start | bytes 6291464 | tf_op jit(solution)/shard_map/ppermute | solution.py:78
  492.0 60.3 %collective-permute-start.49 = (bf16[4,256,512]{2,1,0:T(8,128)(2,1)}, bf16[4,256,512]{2,1,0:T(8,128)(2,1)S(1)}, u32[]{:S(2)}, u32[]{:S(2)}) collective-permute-start(bf16[4,256,512]{2,1,0:T(8,128)(2,1)} %dynamic-slice_bitcast_fusion.1), channel_id=1, source_target_pairs={{0,4},{4,0},{8,12},{12,8},{16,20},{20,16},{24,28},{28,24},{1,5},{5... | collective-permute-start | bytes 3145736 | tf_op jit(solution)/shard_map/ppermute | solution.py:78
  511.3 64.0 %collective-permute-start.41 = (bf16[4,256,512]{2,1,0:T(8,128)(2,1)}, bf16[4,256,512]{2,1,0:T(8,128)(2,1)}, u32[]{:S(2)}, u32[]{:S(2)}) collective-permute-start(bf16[4,256,512]{2,1,0:T(8,128)(2,1)} %dynamic-slice_bitcast_fusion.3), channel_id=1, source_target_pairs={{0,4},{4,0},{8,12},{12,8},{16,20},{20,16},{24,28},{28,24},{1,5},{5... | collective-permute-start | bytes 3145736 | tf_op jit(solution)/shard_map/ppermute | solution.py:78
  511.6 87.2 %collective-permute-start.45 = (bf16[4,256,512]{2,1,0:T(8,128)(2,1)}, bf16[4,256,512]{2,1,0:T(8,128)(2,1)}, u32[]{:S(2)}, u32[]{:S(2)}) collective-permute-start(bf16[4,256,512]{2,1,0:T(8,128)(2,1)} %dynamic-slice_bitcast_fusion.2), channel_id=1, source_target_pairs={{0,4},{4,0},{8,12},{12,8},{16,20},{20,16},{24,28},{28,24},{1,5},{5... | collective-permute-start | bytes 3145736 | tf_op jit(solution)/shard_map/ppermute | solution.py:78
  567.5 87.1 %all-to-all-start.2 = ((f32[8,20,256]{2,1,0:T(8,128)}), f32[8,20,256]{2,1,0:T(8,128)S(1)}, u32[]{:S(2)}, u32[]{:S(2)}) async-start(f32[8,20,256]{2,1,0:T(8,128)} %maximum_bitcast_fusion), calls=%async_computation.3 | async-start | bytes 393216 | tf_op jit(solution)/shard_map/all_to_all | solution.py:555
  604.7 146.1 %collective-permute-start.65 = (bf16[2048,512]{1,0:T(8,128)(2,1)}, bf16[2048,512]{1,0:T(8,128)(2,1)}, u32[]{:S(2)}, u32[]{:S(2)}) collective-permute-start(bf16[2048,512]{1,0:T(8,128)(2,1)} %convolution_convert_fusion), channel_id=1, source_target_pairs={{0,1},{1,0},{2,3},{3,2},{4,5},{5,4},{6,7},{7,6},{8,9},{9,8},{10,11... | collective-permute-start | bytes 6291464 | tf_op jit(solution)/shard_map/ppermute | solution.py:78
  664.4 92.3 %collective-permute-start.61 = (bf16[512,2048]{1,0:T(8,128)(2,1)}, bf16[512,2048]{1,0:T(8,128)(2,1)}, u32[]{:S(2)}, u32[]{:S(2)}) collective-permute-start(bf16[512,2048]{1,0:T(8,128)(2,1)} %fusion.59), channel_id=1, source_target_pairs={{0,1},{1,0},{2,3},{3,2},{4,5},{5,4},{6,7},{7,6},{8,9},{9,8},{10,11... | collective-permute-start | bytes 6291464 | tf_op jit(solution)/shard_map/ppermute | solution.py:78
  665.4 91.3 %collective-permute-start.63 = (bf16[512,2048]{1,0:T(8,128)(2,1)}, bf16[512,2048]{1,0:T(8,128)(2,1)}, u32[]{:S(2)}, u32[]{:S(2)}) collective-permute-start(bf16[512,2048]{1,0:T(8,128)(2,1)} %add_convert_fusion), channel_id=1, source_target_pairs={{0,2},{1,3},{2,0},{3,1},{4,6},{5,7},{6,4},{7,5},{8,10},{9,11},{10,... | collective-permute-start | bytes 6291464 | tf_op jit(solution)/shard_map/ppermute | solution.py:78
  666.7 75.4 %collective-permute-start.57 = (bf16[64,2048]{1,0:T(8,128)(2,1)}, bf16[64,2048]{1,0:T(8,128)(2,1)}, u32[]{:S(2)}, u32[]{:S(2)}) collective-permute-start(bf16[64,2048]{1,0:T(8,128)(2,1)} %fusion.80), channel_id=1, source_target_pairs={{0,0},{1,8},{2,16},{3,24},{4,1},{5,9},{6,17},{7,25},{8,2},{9,10},{... | collective-permute-start | bytes 786440 | tf_op jit(solution)/shard_map/ppermute | solution.py:546
  669.6 50.9 %all-to-all-start.6 = ((bf16[4,64,512]{2,1,0:T(8,128)(2,1)}), bf16[4,64,512]{2,1,0:T(8,128)(2,1)S(1)}, u32[]{:S(2)}, u32[]{:S(2)}) async-start(bf16[4,64,512]{2,1,0:T(8,128)(2,1)} %bitcast.116), calls=%async_computation.7 | async-start | bytes 524288 | tf_op jit(solution)/shard_map/all_to_all | solution.py:530
  744.8 47.4 %collective-permute-start.60 = (bf16[512,2048]{1,0:T(8,128)(2,1)}, bf16[512,2048]{1,0:T(8,128)(2,1)S(1)}, u32[]{:S(2)}, u32[]{:S(2)}) collective-permute-start(bf16[512,2048]{1,0:T(8,128)(2,1)} %add_convert_fusion.1), channel_id=1, source_target_pairs={{0,2},{1,3},{2,0},{3,1},{4,6},{5,7},{6,4},{7,5},{8,10},{9,11},{10,... | collective-permute-start | bytes 6291464 | tf_op jit(solution)/shard_map/ppermute | solution.py:78
  755.4 81.8 %collective-permute-start.66 = (bf16[2048,512]{1,0:T(8,128)(2,1)S(1)}, bf16[2048,512]{1,0:T(8,128)(2,1)S(1)}, u32[]{:S(2)}, u32[]{:S(2)}) collective-permute-start(bf16[2048,512]{1,0:T(8,128)(2,1)S(1)} %convert_add_fusion.1), channel_id=1, source_target_pairs={{0,2},{1,3},{2,0},{3,1},{4,6},{5,7},{6,4},{7,5},{8,10},{9,11},{10,... | collective-permute-start | bytes 6291464 | tf_op jit(solution)/shard_map/ppermute | solution.py:78
  (194 other events, 2751.2 us)
Sparse Core Ops, SparseCore 0:
  108.6 70.5 all-gather.6
  181.9 71.3 all-gather.4
  448.7 103.8 reduce-scatter.1

commit v6 on v4

--- a/solution.py
+++ b/solution.py
@@ -326,8 +326,6 @@
     unit = 2 * w_index + e_index % 2
     units = 2 * parts
 
-    cot_b = mixed_order(cotangent, w_index, parts).astype(bf16)
-    cot_all = lax.all_gather(cot_b, OWNER, axis=0, tiled=True)
     docs = doc_lengths.shape[1]
     lengths_row = jnp.zeros((1, cols), bf16).at[:, :docs].set(doc_lengths.astype(bf16))
     small = jnp.concatenate(
@@ -358,8 +356,12 @@
             pieces[3] = swap(pieces[3], 1)
     for mask in reversed(range(2, parts)):
         pieces[2 * mask + 1] = swap(pieces[2 * mask], 1, OWNER)
-    down_in = after(down_weight, pieces[4])
-    down_pieces = gather_far(down_in)
+    cot_b = mixed_order(cotangent, w_index, parts).astype(bf16)
+    cot_all = lax.all_gather(cot_b, OWNER, axis=0, tiled=True)
+    down_first = after(down_weight[:1], pieces[4])
+    down_first = gather_far(down_first)
+    down_second = after(down_weight[1:], pieces[4])
+    down_second = gather_far(down_second)
 
     unit_all, _ = rms_unit(tokens_all.astype(f32))
     attn_in = (unit_all * attn_gain_all).astype(bf16)
@@ -406,12 +408,11 @@
     attn_mix = by_row(mixed.reshape(whole))
     attn_out = dot(attn_mix, output_weight)
     attn_out = scatter_pieces([attn_out[mask * rows : (mask + 1) * rows] for mask in range(parts)])
-    attn_out, cot_all, down_pieces, *pieces = lax.optimization_barrier(
-        (attn_out, cot_all, down_pieces, *pieces)
-    )
-    down_pieces = gather_near(down_pieces)
+    attn_out, *pieces = lax.optimization_barrier((attn_out, *pieces))
     qkv_w = jnp.concatenate(pieces, axis=0)
-    qkv_w = jnp.concatenate([block_of(qkv_w, unit ^ k, units, 0) for k in range(units)], axis=0)
+    qkv_w = jnp.concatenate(
+        [block_of(qkv_w, unit ^ k, units, 0) for k in range(units)], axis=0
+    )
 
     residual = tokens.astype(f32)
     middle = residual + attn_out
@@ -421,8 +422,8 @@
     gate_in, up_in, ffn_in_mixed, ffn_in = lax.optimization_barrier(
         (gate_weight, up_weight, ffn_in_mixed, ffn_in)
     )
-    gate_pieces = gather_pieces(gate_in)
-    up_pieces = gather_pieces(up_in)
+    gate_far = gather_far(gate_in)
+    up_far = gather_far(up_in)
     router_probs = softmax_rows(dot_t(ffn_in, router_t))
     expert_range = jnp.arange(experts, dtype=jnp.int32)
     named = jnp.any(expert_ids[:, :, None] == expert_range[None, None, :], axis=1)
@@ -437,6 +438,12 @@
         tiled=True,
     )
     weights = weights.transpose(1, 0, 2).reshape(EXP_DEV, owners * rows, 1)
+    gate_pieces = gather_near(gate_far)
+    up_pieces = gather_near(
+        {m: after(p, weights, gate_pieces[-1]) if m else p for m, p in up_far.items()}
+    )
+    down_far = {m: jnp.concatenate([down_first[m], down_second[m]]) for m in down_first if m}
+    down_pieces = gather_near({0: down_weight, **down_far})
     hidden_w, gate_grad_b, up_grad_b, route_part = expert_hidden(
         arrived, cot_all, weights, gate_pieces, up_pieces, down_pieces
     )

time: 748 us -> 801 us (1.071)
  waiting for transfers between devices: 318 us -> 356 us
  local copies, waits for them, and re-layouts: 58.3 us -> 81.6 us
    ppermute x54 -> x55, waiting for transfers between devices: 315 us -> 353 us  [swap(): lax.ppermute(values, axis_name, [(i, i ^ mask) for i in range(count)])]
    unnamed x232 -> x231, local copies, waits for them, and re-layouts: 23.3 us -> 38.6 us
    ppermute x54 -> x55, starting transfers between devices: 56.9 us -> 51.9 us  [swap(): lax.ppermute(values, axis_name, [(i, i ^ mask) for i in range(count)])]
  transfers between devices with their start and end apart: 65 -> 66, of which waited for: 23 -> 23; matrix products, arithmetic and copies ran while one was open for 28% -> 29% of each run, Pallas kernels for 0% -> 0%
where the time goes in v6:
time: 801 us; the launch traced here: 791 us
  waiting for transfers between devices  356 us (44%)
  matrix products  101 us (13%)
  starting transfers between devices  88 us (11%)
  local copies, waits for them, and re-layouts  81.6 us (10%)
  other arithmetic  75.6 us (9%)
  Pallas kernels  67.1 us (8%)
  between operations  16.2 us (2%)
    ppermute x55, waiting for transfers between devices, swap(): lax.ppermute(values, axis_name, [(i, i ^ mask) for i in range(count)])  353 us
    dot_general x16, matrix products, t_dot(): lax.dot_general(a, b, (((0,), (0,)), ((), ())), preferred_element_type=jn...  66.2 us
    ppermute x55, starting transfers between devices, swap(): lax.ppermute(values, axis_name, [(i, i ^ mask) for i in range(count)])  51.9 us
    unnamed x231, local copies, waits for them, and re-layouts  38.6 us
    pallas_call x1, Pallas kernels, expert_hidden(): pl.pallas_call(functools.partial(expert_hidden_kernel, parts), grid=(rows...  36.5 us
    pallas_call x1, Pallas kernels, back_rows(): pl.pallas_call(functools.partial(back_rows_kernel, parts), grid=(rows //...  28.4 us
    add x6, other arithmetic, scatter_stage(): return {m: blocks[m] + arrived[m].astype(jnp.float32) for m in arrived}  22.1 us
    dot_general x11, matrix products, dot(): return jnp.dot(a, b, preferred_element_type=jnp.float32)  21.4 us
  transfers between devices with their start and end apart: 66, of which 23 were waited for; matrix products, arithmetic and copies ran while one was open for 29% of the time, Pallas kernels for 0%

profile of v6, /device:TPU:13, one launch (start us, length us, event | category | flops | bytes accessed | tf_op | source)
XLA Modules:
  0.0 791.4 jit_solution(14201236744533289977)
XLA Ops:
  41.8 6.0 collective-permute-done.5
  48.1 17.2 %collective-permute-done.6 = bf16[256,1536]{1,0:T(8,128)(2,1)} collective-permute-done((bf16[256,1536]{1,0:T(8,128)(2,1)}, bf16[256,1536]{1,0:T(8,128)(2,1)}, u32[]{:S(2)}, u32[]{:S(2)}) %collective-permute-start.6) | collective-permute-done | bytes 786464 | tf_op jit(solution)/shard_map/ppermute | solution.py:78
  75.8 29.4 %collective-permute-done.8 = bf16[256,1536]{1,0:T(8,128)(2,1)S(1)} collective-permute-done((bf16[256,1536]{1,0:T(8,128)(2,1)}, bf16[256,1536]{1,0:T(8,128)(2,1)S(1)}, u32[]{:S(2)}, u32[]{:S(2)}) %collective-permute-start.8) | collective-permute-done | bytes 786464 | tf_op jit(solution)/shard_map/ppermute | solution.py:78
  121.7 12.8 %collective-permute-done.14 = bf16[128,2048]{1,0:T(8,128)(2,1)S(1)} collective-permute-done((bf16[128,2048]{1,0:T(8,128)(2,1)S(1)}, bf16[128,2048]{1,0:T(8,128)(2,1)S(1)}, u32[]{:S(2)}, u32[]{:S(2)}) %collective-permute-start.14) | collective-permute-done | bytes 524320 | tf_op jit(solution)/shard_map/ppermute | solution.py:78
  143.4 62.5 %collective-permute-done.22 = bf16[1,1024,512]{2,1,0:T(8,128)(2,1)} collective-permute-done((bf16[1,1024,512]{2,1,0:T(8,128)(2,1)}, bf16[1,1024,512]{2,1,0:T(8,128)(2,1)}, u32[]{:S(2)}, u32[]{:S(2)}) %collective-permute-start.22) | collective-permute-done | bytes 1048608 | tf_op jit(solution)/shard_map/ppermute | solution.py:78
  208.2 20.2 %collective-permute-done.23 = bf16[1,1024,512]{2,1,0:T(8,128)(2,1)} collective-permute-done((bf16[1,1024,512]{2,1,0:T(8,128)(2,1)}, bf16[1,1024,512]{2,1,0:T(8,128)(2,1)}, u32[]{:S(2)}, u32[]{:S(2)}) %collective-permute-start.23) | collective-permute-done | bytes 1048608 | tf_op jit(solution)/shard_map/ppermute | solution.py:78
  234.7 6.1 all-to-all-start
  252.2 27.9 %collective-permute-done.19.refs_6_ = bf16[2,512,1024]{2,1,0:T(8,128)(2,1)} collective-permute-done((bf16[2,512,1024]{2,1,0:T(8,128)(2,1)}, bf16[2,512,1024]{2,1,0:T(8,128)(2,1)}, u32[]{:S(2)}, u32[]{:S(2)}) %collective-permute-start.19) | collective-permute-done | bytes 2097184 | tf_op jit(solution)/shard_map/ppermute | solution.py:78
  301.8 36.5 %shard_map.263 = (bf16[1024,2048]{1,0:T(8,128)(2,1)}, bf16[1024,2048]{1,0:T(8,128)(2,1)}, bf16[1024,2048]{1,0:T(8,128)(2,1)}, f32[2,1024,128]{2,1,0:T(8,128)}) custom-call(bf16[1024,2048]{1,0:T(8,128)(2,1)} %all-gather.5.cloned.1.call-done.x_ref, bf16[1024,2048]{1,0:T(8,128)(2,1)} %all-gather.7.cloned.1.call-done.cot_ref, f32[2,1024,1]{2,1,0:T(8,128)} %copy.87.weight_ref, ...), custom_call_target="tpu_custom_call" | custom-call | tf_op jit(solution)/shard_map/pallas_call | solution.py:238
  338.3 28.4 %shard_map.264 = bf16[1024,2048]{1,0:T(8,128)(2,1)} custom-call(bf16[1024,2048]{1,0:T(8,128)(2,1)} %get-tuple-element.83.gate_grad_ref, bf16[1024,2048]{1,0:T(8,128)(2,1)} %get-tuple-element.84.up_grad_ref, bf16[2,512,1024]{2,1,0:T(8,128)(2,1)} %refs_0_.1, bf16[2,512,1024]{2,1,0:T(8,128)(2,1)} %collective-permute-done.15.refs_1_, ...), custom_call_target="tpu_custom_call" | custom-call | tf_op jit(solution)/shard_map/pallas_call | solution.py:282
  366.7 6.3 fusion.54
  402.8 11.7 %fusion.12 = bf16[1024,2048]{1,0:T(8,128)(2,1)S(1)} fusion(bf16[1024,2048]{1,0:T(8,128)(2,1)S(1)} %copy-done.97, bf16[2048,512]{1,0:T(8,128)(2,1)} %bitcast.44, bf16[2048,512]{1,0:T(8,128)(2,1)} %bitcast.43, bf16[2048,512]{1,0:T(8,128)(2,1)} %bitcast.42, bf16[2048,512]{1,0:T(8,128)(2,1)} %bitcast.41), kind=kOutput, calls=%fused_computation.25 | convolution fusion | flops 8625586176 | bytes 16777216 | tf_op jit(solution)/shard_map/dot_general | solution.py:65
  418.6 6.2 convolution_convert_fusion.2
  428.1 6.0 all-to-all-start.1
  439.3 35.7 %collective-permute-done.25 = bf16[4,128,2048]{2,1,0:T(8,128)(2,1)} collective-permute-done((bf16[4,128,2048]{2,1,0:T(8,128)(2,1)}, bf16[4,128,2048]{2,1,0:T(8,128)(2,1)}, u32[]{:S(2)}, u32[]{:S(2)}) %collective-permute-start.25) | collective-permute-done | bytes 2097184 | tf_op jit(solution)/shard_map/ppermute | solution.py:78
  483.7 6.1 convert_add_fusion.3
  504.7 9.7 %collective-permute-done.26 = bf16[128,2048]{1,0:T(8,128)(2,1)S(1)} collective-permute-done((bf16[128,2048]{1,0:T(8,128)(2,1)S(1)}, bf16[128,2048]{1,0:T(8,128)(2,1)S(1)}, u32[]{:S(2)}, u32[]{:S(2)}) %collective-permute-start.26) | collective-permute-done | bytes 524320 | tf_op jit(solution)/shard_map/ppermute | solution.py:78
  515.1 20.0 %collective-permute-done.27 = bf16[128,2048]{1,0:T(8,128)(2,1)S(1)} collective-permute-done((bf16[128,2048]{1,0:T(8,128)(2,1)S(1)}, bf16[128,2048]{1,0:T(8,128)(2,1)S(1)}, u32[]{:S(2)}, u32[]{:S(2)}) %collective-permute-start.27) | collective-permute-done | bytes 524320 | tf_op jit(solution)/shard_map/ppermute | solution.py:78
  605.0 6.5 collective-permute-done.42
  615.6 28.2 %collective-permute-done.38 = bf16[4,256,512]{2,1,0:T(8,128)(2,1)S(1)} collective-permute-done((bf16[4,256,512]{2,1,0:T(8,128)(2,1)S(1)}, bf16[4,256,512]{2,1,0:T(8,128)(2,1)S(1)}, u32[]{:S(2)}, u32[]{:S(2)}) %collective-permute-start.38) | collective-permute-done | bytes 1048608 | tf_op jit(solution)/shard_map/ppermute | solution.py:78
  650.8 53.9 %collective-permute-done.37 = bf16[128,2048]{1,0:T(8,128)(2,1)S(1)} collective-permute-done((bf16[128,2048]{1,0:T(8,128)(2,1)S(1)}, bf16[128,2048]{1,0:T(8,128)(2,1)S(1)}, u32[]{:S(2)}, u32[]{:S(2)}) %collective-permute-start.37) | collective-permute-done | bytes 524320 | tf_op jit(solution)/shard_map/ppermute | solution.py:78
  734.9 6.7 collective-permute-done.39
  747.6 8.6 %all-to-all-start.5 = ((bf16[4,64,512]{2,1,0:T(8,128)(2,1)}), bf16[4,64,512]{2,1,0:T(8,128)(2,1)S(1)}, u32[]{:S(2)}, u32[]{:S(2)}) async-start(bf16[4,64,512]{2,1,0:T(8,128)(2,1)} %bitcast.95), calls=%async_computation.7 | async-start | bytes 524288 | tf_op jit(solution)/shard_map/all_to_all | solution.py:530
  759.4 5.8 convert_add_fusion.4
  (525 shorter events, 316.7 us)
Async XLA Ops:
  7.2 294.6 %all-gather.7.cloned.1.call-start = ((), (), s32[]{:S(2)}) async-start(), calls=%async_computation.9 | async-start | bytes 4718592 | tf_op jit(solution)/shard_map/all_gather | solution.py:360
  20.9 280.9 %all-gather.5.cloned.1.call-start = ((), (), s32[]{:S(2)}) async-start(), calls=%async_computation.8 | async-start | bytes 4718592 | tf_op jit(solution)/shard_map/all_gather | solution.py:432
  47.8 57.9 %collective-permute-start.7 = (bf16[256,1536]{1,0:T(8,128)(2,1)}, bf16[256,1536]{1,0:T(8,128)(2,1)S(1)}, u32[]{:S(2)}, u32[]{:S(2)}) collective-permute-start(bf16[256,1536]{1,0:T(8,128)(2,1)} %collective-permute-done.5), channel_id=1, source_target_pairs={{0,4},{4,0},{8,12},{12,8},{16,20},{20,16},{24,28},{28,24},{1,5},{5... | collective-permute-start | bytes 2359304 | tf_op jit(solution)/shard_map/ppermute | solution.py:78
  136.9 96.1 %collective-permute-start.16 = (bf16[2,512,1024]{2,1,0:T(8,128)(2,1)}, bf16[2,512,1024]{2,1,0:T(8,128)(2,1)}, u32[]{:S(2)}, u32[]{:S(2)}) collective-permute-start(bf16[2,512,1024]{2,1,0:T(8,128)(2,1)} %refs_0_.1), channel_id=1, source_target_pairs={{0,2},{1,3},{2,0},{3,1},{4,6},{5,7},{6,4},{7,5},{8,10},{9,11},{10,... | collective-permute-start | bytes 6291464 | tf_op jit(solution)/shard_map/ppermute | solution.py:78
  140.0 66.0 %collective-permute-start.22 = (bf16[1,1024,512]{2,1,0:T(8,128)(2,1)}, bf16[1,1024,512]{2,1,0:T(8,128)(2,1)}, u32[]{:S(2)}, u32[]{:S(2)}) collective-permute-start(bf16[1,1024,512]{2,1,0:T(8,128)(2,1)} %get-tuple-element.72), channel_id=1, source_target_pairs={{0,2},{1,3},{2,0},{3,1},{4,6},{5,7},{6,4},{7,5},{8,10},{9,11},{10,... | collective-permute-start | bytes 3145736 | tf_op jit(solution)/shard_map/ppermute | solution.py:78
  141.4 87.0 %collective-permute-start.23 = (bf16[1,1024,512]{2,1,0:T(8,128)(2,1)}, bf16[1,1024,512]{2,1,0:T(8,128)(2,1)}, u32[]{:S(2)}, u32[]{:S(2)}) collective-permute-start(bf16[1,1024,512]{2,1,0:T(8,128)(2,1)} %get-tuple-element.73), channel_id=1, source_target_pairs={{0,2},{1,3},{2,0},{3,1},{4,6},{5,7},{6,4},{7,5},{8,10},{9,11},{10,... | collective-permute-start | bytes 3145736 | tf_op jit(solution)/shard_map/ppermute | solution.py:78
  141.5 160.3 %collective-permute-start.21 = (bf16[2,1024,512]{2,1,0:T(8,128)(2,1)}, bf16[2,1024,512]{2,1,0:T(8,128)(2,1)}, u32[]{:S(2)}, u32[]{:S(2)}) collective-permute-start(bf16[2,1024,512]{2,1,0:T(8,128)(2,1)} %refs_8_.1), channel_id=1, source_target_pairs={{0,1},{1,0},{2,3},{3,2},{4,5},{5,4},{6,7},{7,6},{8,9},{9,8},{10,11... | collective-permute-start | bytes 6291464 | tf_op jit(solution)/shard_map/ppermute | solution.py:78
  230.7 71.0 %collective-permute-start.24 = (bf16[2,1024,512]{2,1,0:T(8,128)(2,1)}, bf16[2,1024,512]{2,1,0:T(8,128)(2,1)}, u32[]{:S(2)}, u32[]{:S(2)}) collective-permute-start(bf16[2,1024,512]{2,1,0:T(8,128)(2,1)} %constant_dynamic-update-slice_fusion.refs_10_), channel_id=1, source_target_pairs={{0,1},{1,0},{2,3},{3,2},{4,5},{5,4},{6,7},{7,6},{8,9},{9,8},{10,11... | collective-permute-start | bytes 6291464 | tf_op jit(solution)/shard_map/ppermute | solution.py:78
  233.0 68.8 %collective-permute-start.15 = (bf16[2,512,1024]{2,1,0:T(8,128)(2,1)}, bf16[2,512,1024]{2,1,0:T(8,128)(2,1)}, u32[]{:S(2)}, u32[]{:S(2)}) collective-permute-start(bf16[2,512,1024]{2,1,0:T(8,128)(2,1)} %refs_0_.1), channel_id=1, source_target_pairs={{0,1},{1,0},{2,3},{3,2},{4,5},{5,4},{6,7},{7,6},{8,9},{9,8},{10,11... | collective-permute-start | bytes 6291464 | tf_op jit(solution)/shard_map/ppermute | solution.py:78
  240.8 295.5 %reduce-scatter.3.cloned.1.call-start = ((), (), s32[]{:S(2)}) async-start(), calls=%async_computation.10 | async-start | bytes 4718592 | tf_op jit(solution)/shard_map/reduce_scatter | solution.py:451
  418.1 57.0 %collective-permute-start.25 = (bf16[4,128,2048]{2,1,0:T(8,128)(2,1)}, bf16[4,128,2048]{2,1,0:T(8,128)(2,1)}, u32[]{:S(2)}, u32[]{:S(2)}) collective-permute-start(bf16[4,128,2048]{2,1,0:T(8,128)(2,1)} %dynamic-slice_bitcast_fusion), channel_id=1, source_target_pairs={{0,4},{4,0},{8,12},{12,8},{16,20},{20,16},{24,28},{28,24},{1,5},{5... | collective-permute-start | bytes 6291464 | tf_op jit(solution)/shard_map/ppermute | solution.py:78
  418.1 60.5 %collective-permute-start.48 = (bf16[512,2048]{1,0:T(8,128)(2,1)}, bf16[512,2048]{1,0:T(8,128)(2,1)}, u32[]{:S(2)}, u32[]{:S(2)}) collective-permute-start(bf16[512,2048]{1,0:T(8,128)(2,1)} %fusion.54), channel_id=1, source_target_pairs={{0,1},{1,0},{2,3},{3,2},{4,5},{5,4},{6,7},{7,6},{8,9},{9,8},{10,11... | collective-permute-start | bytes 6291464 | tf_op jit(solution)/shard_map/ppermute | solution.py:78
  424.8 57.7 %collective-permute-start.53 = (bf16[2048,512]{1,0:T(8,128)(2,1)}, bf16[2048,512]{1,0:T(8,128)(2,1)}, u32[]{:S(2)}, u32[]{:S(2)}) collective-permute-start(bf16[2048,512]{1,0:T(8,128)(2,1)} %convolution_convert_fusion.2), channel_id=1, source_target_pairs={{0,1},{1,0},{2,3},{3,2},{4,5},{5,4},{6,7},{7,6},{8,9},{9,8},{10,11... | collective-permute-start | bytes 6291464 | tf_op jit(solution)/shard_map/ppermute | solution.py:78
  425.4 69.5 %collective-permute-start.50 = (bf16[512,2048]{1,0:T(8,128)(2,1)}, bf16[512,2048]{1,0:T(8,128)(2,1)}, u32[]{:S(2)}, u32[]{:S(2)}) collective-permute-start(bf16[512,2048]{1,0:T(8,128)(2,1)} %fusion.60), channel_id=1, source_target_pairs={{0,1},{1,0},{2,3},{3,2},{4,5},{5,4},{6,7},{7,6},{8,9},{9,8},{10,11... | collective-permute-start | bytes 6291464 | tf_op jit(solution)/shard_map/ppermute | solution.py:78
  425.8 74.8 %collective-permute-start.51 = (bf16[512,2048]{1,0:T(8,128)(2,1)}, bf16[512,2048]{1,0:T(8,128)(2,1)}, u32[]{:S(2)}, u32[]{:S(2)}) collective-permute-start(bf16[512,2048]{1,0:T(8,128)(2,1)} %fusion.52), channel_id=1, source_target_pairs={{0,1},{1,0},{2,3},{3,2},{4,5},{5,4},{6,7},{7,6},{8,9},{9,8},{10,11... | collective-permute-start | bytes 6291464 | tf_op jit(solution)/shard_map/ppermute | solution.py:78
  428.1 108.2 %all-to-all-start.1 = ((f32[8,2,128]{2,1,0:T(2,128)}), f32[8,2,128]{2,1,0:T(2,128)S(1)}, u32[]{:S(2)}, u32[]{:S(2)}) async-start(f32[8,2,128]{2,1,0:T(2,128)} %bitcast.53), calls=%async_computation.2 | async-start | bytes 16384 | tf_op jit(solution)/shard_map/all_to_all | solution.py:453
  434.1 335.6 %reduce-scatter.5.cloned.1.call-start = ((), (), s32[]{:S(2)}) async-start(), calls=%async_computation.11 | async-start | bytes 4718592 | tf_op jit(solution)/shard_map/reduce_scatter | solution.py:542
  478.5 62.7 %collective-permute-start.47 = (bf16[512,2048]{1,0:T(8,128)(2,1)}, bf16[512,2048]{1,0:T(8,128)(2,1)}, u32[]{:S(2)}, u32[]{:S(2)}) collective-permute-start(bf16[512,2048]{1,0:T(8,128)(2,1)} %fusion.62), channel_id=1, source_target_pairs={{0,1},{1,0},{2,3},{3,2},{4,5},{5,4},{6,7},{7,6},{8,9},{9,8},{10,11... | collective-permute-start | bytes 6291464 | tf_op jit(solution)/shard_map/ppermute | solution.py:78
  482.5 58.8 %collective-permute-start.49 = (bf16[512,2048]{1,0:T(8,128)(2,1)}, bf16[512,2048]{1,0:T(8,128)(2,1)}, u32[]{:S(2)}, u32[]{:S(2)}) collective-permute-start(bf16[512,2048]{1,0:T(8,128)(2,1)} %add_convert_fusion), channel_id=1, source_target_pairs={{0,2},{1,3},{2,0},{3,1},{4,6},{5,7},{6,4},{7,5},{8,10},{9,11},{10,... | collective-permute-start | bytes 6291464 | tf_op jit(solution)/shard_map/ppermute | solution.py:78
  601.6 157.8 %collective-permute-start.52 = (bf16[512,2048]{1,0:T(8,128)(2,1)}, bf16[512,2048]{1,0:T(8,128)(2,1)}, u32[]{:S(2)}, u32[]{:S(2)}) collective-permute-start(bf16[512,2048]{1,0:T(8,128)(2,1)} %convert_add_fusion.5), channel_id=1, source_target_pairs={{0,2},{1,3},{2,0},{3,1},{4,6},{5,7},{6,4},{7,5},{8,10},{9,11},{10,... | collective-permute-start | bytes 6291464 | tf_op jit(solution)/shard_map/ppermute | solution.py:78
  603.9 161.4 %collective-permute-start.55 = (bf16[2048,512]{1,0:T(8,128)(2,1)}, bf16[2048,512]{1,0:T(8,128)(2,1)}, u32[]{:S(2)}, u32[]{:S(2)}) collective-permute-start(bf16[2048,512]{1,0:T(8,128)(2,1)} %convert_add_fusion.2), channel_id=1, source_target_pairs={{0,2},{1,3},{2,0},{3,1},{4,6},{5,7},{6,4},{7,5},{8,10},{9,11},{10,... | collective-permute-start | bytes 6291464 | tf_op jit(solution)/shard_map/ppermute | solution.py:78
  611.5 93.3 %collective-permute-start.37 = (bf16[128,2048]{1,0:T(8,128)(2,1)S(1)}, bf16[128,2048]{1,0:T(8,128)(2,1)S(1)}, u32[]{:S(2)}, u32[]{:S(2)}) collective-permute-start(bf16[128,2048]{1,0:T(8,128)(2,1)S(1)} %fusion.43), channel_id=1, source_target_pairs={{0,2},{1,3},{2,0},{3,1},{4,6},{5,7},{6,4},{7,5},{8,10},{9,11},{10,... | collective-permute-start | bytes 1572872 | tf_op jit(solution)/shard_map/ppermute | solution.py:78
  643.8 72.5 %collective-permute-start.43 = (bf16[64,2048]{1,0:T(8,128)(2,1)}, bf16[64,2048]{1,0:T(8,128)(2,1)}, u32[]{:S(2)}, u32[]{:S(2)}) collective-permute-start(bf16[64,2048]{1,0:T(8,128)(2,1)} %get-tuple-element.169), channel_id=1, source_target_pairs={{0,24},{4,28},{8,16},{12,20},{16,8},{20,12},{24,0},{28,4},{1,25},{... | collective-permute-start | bytes 786440 | tf_op jit(solution)/shard_map/ppermute | solution.py:78
  647.2 70.3 %collective-permute-start.45 = (bf16[64,2048]{1,0:T(8,128)(2,1)}, bf16[64,2048]{1,0:T(8,128)(2,1)}, u32[]{:S(2)}, u32[]{:S(2)}) collective-permute-start(bf16[64,2048]{1,0:T(8,128)(2,1)} %get-tuple-element.170), channel_id=1, source_target_pairs={{0,8},{4,12},{8,0},{12,4},{16,24},{20,28},{24,16},{28,20},{1,9},{5... | collective-permute-start | bytes 786440 | tf_op jit(solution)/shard_map/ppermute | solution.py:78
  (147 other events, 2396.6 us)
Sparse Core Ops, SparseCore 0:
  21.1 92.4 all-gather.6
  137.0 70.5 all-gather.4
  366.8 95.9 reduce-scatter.2
  587.5 98.9 reduce-scatter.4

commit v7 on v6

--- a/solution.py
+++ b/solution.py
@@ -358,10 +358,8 @@
         pieces[2 * mask + 1] = swap(pieces[2 * mask], 1, OWNER)
     cot_b = mixed_order(cotangent, w_index, parts).astype(bf16)
     cot_all = lax.all_gather(cot_b, OWNER, axis=0, tiled=True)
-    down_first = after(down_weight[:1], pieces[4])
-    down_first = gather_far(down_first)
-    down_second = after(down_weight[1:], pieces[4])
-    down_second = gather_far(down_second)
+    down_in = after(down_weight, pieces[4])
+    down_far = gather_far(down_in)
 
     unit_all, _ = rms_unit(tokens_all.astype(f32))
     attn_in = (unit_all * attn_gain_all).astype(bf16)
@@ -442,8 +440,7 @@
     up_pieces = gather_near(
         {m: after(p, weights, gate_pieces[-1]) if m else p for m, p in up_far.items()}
     )
-    down_far = {m: jnp.concatenate([down_first[m], down_second[m]]) for m in down_first if m}
-    down_pieces = gather_near({0: down_weight, **down_far})
+    down_pieces = gather_near({m: after(p, attn_out) if m else p for m, p in down_far.items()})
     hidden_w, gate_grad_b, up_grad_b, route_part = expert_hidden(
         arrived, cot_all, weights, gate_pieces, up_pieces, down_pieces
     )
@@ -478,9 +475,10 @@
     down_all = jnp.concatenate(
         [piece.reshape(EXP_DEV * ff, cols) for piece in down_pieces], axis=1
     )
-    out_partial = dot(hidden_w, down_all).astype(bf16)
-    moe_out = owner_scatter(out_partial.reshape(owners, rows, width))
+    out_partial = dot(hidden_w, down_all)
+    out_partial = out_partial.astype(bf16)
     row_grads, route_back = lax.optimization_barrier((row_grads, route_back))
+    moe_out = lax.psum_scatter(out_partial, OWNER, scatter_dimension=0, tiled=True)
 
     route_grad = route_back.reshape(experts, rows).T
     prob_grad = jnp.where(named, route_grad, 0.0)

time: 801 us -> 752 us (0.939)
  waiting for transfers between devices: 356 us -> 315 us
  starting transfers between devices: 88 us -> 79.7 us
    ppermute x55 -> x50, waiting for transfers between devices: 353 us -> 312 us  [swap(): lax.ppermute(values, axis_name, [(i, i ^ mask) for i in range(count)])]
    ppermute x55 -> x50, starting transfers between devices: 51.9 us -> 45.9 us  [swap(): lax.ppermute(values, axis_name, [(i, i ^ mask) for i in range(count)])]
    unnamed x231 -> x244, local copies, waits for them, and re-layouts: 38.6 us -> 39.3 us
  transfers between devices with their start and end apart: 66 -> 62, of which waited for: 23 -> 19; matrix products, arithmetic and copies ran while one was open for 29% -> 33% of each run, Pallas kernels for 0% -> 0%
where the time goes in v7:
time: 752 us; the launch traced here: 742 us
  waiting for transfers between devices  315 us (42%)
  matrix products  104 us (14%)
  starting transfers between devices  79.7 us (11%)
  local copies, waits for them, and re-layouts  78.8 us (10%)
  other arithmetic  75.5 us (10%)
  Pallas kernels  67 us (9%)
  between operations  16 us (2%)
    ppermute x50, waiting for transfers between devices, swap(): lax.ppermute(values, axis_name, [(i, i ^ mask) for i in range(count)])  312 us
    dot_general x16, matrix products, t_dot(): lax.dot_general(a, b, (((0,), (0,)), ((), ())), preferred_element_type=jn...  64 us
    ppermute x50, starting transfers between devices, swap(): lax.ppermute(values, axis_name, [(i, i ^ mask) for i in range(count)])  45.9 us
    unnamed x244, local copies, waits for them, and re-layouts  39.3 us
    pallas_call x1, Pallas kernels, expert_hidden(): pl.pallas_call(functools.partial(expert_hidden_kernel, parts), grid=(rows...  36.5 us
    pallas_call x1, Pallas kernels, back_rows(): pl.pallas_call(functools.partial(back_rows_kernel, parts), grid=(rows //...  28.2 us
    add x6, other arithmetic, scatter_stage(): return {m: blocks[m] + arrived[m].astype(jnp.float32) for m in arrived}  22.1 us
    dot_general x11, matrix products, dot(): return jnp.dot(a, b, preferred_element_type=jnp.float32)  22 us
  transfers between devices with their start and end apart: 62, of which 19 were waited for; matrix products, arithmetic and copies ran while one was open for 33% of the time, Pallas kernels for 0%

profile of v7, /device:TPU:13, one launch (start us, length us, event | category | flops | bytes accessed | tf_op | source)
XLA Modules:
  0.0 741.6 jit_solution(11804020173098612457)
XLA Ops:
  11.3 5.8 all-gather.1
  41.8 6.0 collective-permute-done.5
  48.1 17.2 %collective-permute-done.6 = bf16[256,1536]{1,0:T(8,128)(2,1)} collective-permute-done((bf16[256,1536]{1,0:T(8,128)(2,1)}, bf16[256,1536]{1,0:T(8,128)(2,1)}, u32[]{:S(2)}, u32[]{:S(2)}) %collective-permute-start.6) | collective-permute-done | bytes 786464 | tf_op jit(solution)/shard_map/ppermute | solution.py:78
  75.8 29.4 %collective-permute-done.8 = bf16[256,1536]{1,0:T(8,128)(2,1)S(1)} collective-permute-done((bf16[256,1536]{1,0:T(8,128)(2,1)}, bf16[256,1536]{1,0:T(8,128)(2,1)S(1)}, u32[]{:S(2)}, u32[]{:S(2)}) %collective-permute-start.8) | collective-permute-done | bytes 786464 | tf_op jit(solution)/shard_map/ppermute | solution.py:78
  121.7 12.8 %collective-permute-done.14 = bf16[128,2048]{1,0:T(8,128)(2,1)S(1)} collective-permute-done((bf16[128,2048]{1,0:T(8,128)(2,1)S(1)}, bf16[128,2048]{1,0:T(8,128)(2,1)S(1)}, u32[]{:S(2)}, u32[]{:S(2)}) %collective-permute-start.14) | collective-permute-done | bytes 524320 | tf_op jit(solution)/shard_map/ppermute | solution.py:78
  139.6 44.9 %collective-permute-done.16.refs_2_ = bf16[2,512,1024]{2,1,0:T(8,128)(2,1)} collective-permute-done((bf16[2,512,1024]{2,1,0:T(8,128)(2,1)}, bf16[2,512,1024]{2,1,0:T(8,128)(2,1)}, u32[]{:S(2)}, u32[]{:S(2)}) %collective-permute-start.16) | collective-permute-done | bytes 2097184 | tf_op jit(solution)/shard_map/ppermute | solution.py:78
  192.0 5.9 all-to-all-start
  206.2 23.3 %collective-permute-done.22.refs_10_ = bf16[2,1024,512]{2,1,0:T(8,128)(2,1)} collective-permute-done((bf16[2,1024,512]{2,1,0:T(8,128)(2,1)}, bf16[2,1024,512]{2,1,0:T(8,128)(2,1)}, u32[]{:S(2)}, u32[]{:S(2)}) %collective-permute-start.22) | collective-permute-done | bytes 2097184 | tf_op jit(solution)/shard_map/ppermute | solution.py:78
  232.7 41.6 %collective-permute-done.19.refs_6_ = bf16[2,512,1024]{2,1,0:T(8,128)(2,1)} collective-permute-done((bf16[2,512,1024]{2,1,0:T(8,128)(2,1)}, bf16[2,512,1024]{2,1,0:T(8,128)(2,1)}, u32[]{:S(2)}, u32[]{:S(2)}) %collective-permute-start.19) | collective-permute-done | bytes 2097184 | tf_op jit(solution)/shard_map/ppermute | solution.py:78
  295.6 36.5 %shard_map.263 = (bf16[1024,2048]{1,0:T(8,128)(2,1)}, bf16[1024,2048]{1,0:T(8,128)(2,1)}, bf16[1024,2048]{1,0:T(8,128)(2,1)}, f32[2,1024,128]{2,1,0:T(8,128)}) custom-call(bf16[1024,2048]{1,0:T(8,128)(2,1)} %all-gather.5.cloned.1.call-done.x_ref, bf16[1024,2048]{1,0:T(8,128)(2,1)} %all-gather.7.cloned.1.call-done.cot_ref, f32[2,1024,1]{2,1,0:T(8,128)} %copy.84.weight_ref, ...), custom_call_target="tpu_custom_call" | custom-call | tf_op jit(solution)/shard_map/pallas_call | solution.py:238
  332.1 28.2 %shard_map.264 = bf16[1024,2048]{1,0:T(8,128)(2,1)} custom-call(bf16[1024,2048]{1,0:T(8,128)(2,1)} %get-tuple-element.83.gate_grad_ref, bf16[1024,2048]{1,0:T(8,128)(2,1)} %get-tuple-element.84.up_grad_ref, bf16[2,512,1024]{2,1,0:T(8,128)(2,1)} %refs_0_.1, bf16[2,512,1024]{2,1,0:T(8,128)(2,1)} %collective-permute-done.15.refs_1_, ...), custom_call_target="tpu_custom_call" | custom-call | tf_op jit(solution)/shard_map/pallas_call | solution.py:282
  367.8 5.7 all-to-all-start.1
  374.0 6.4 fusion.58
  419.3 12.3 %fusion.11 = bf16[1024,2048]{1,0:T(8,128)(2,1)} fusion(bf16[1024,2048]{1,0:T(8,128)(2,1)S(1)} %copy-done.104, bf16[2048,512]{1,0:T(8,128)(2,1)} %bitcast.44, bf16[2048,512]{1,0:T(8,128)(2,1)} %bitcast.43, bf16[2048,512]{1,0:T(8,128)(2,1)} %bitcast.42, bf16[2048,512]{1,0:T(8,128)(2,1)S(1)} %bitcast.256), kind=kOutput, calls=%fused_computation.23 | convolution fusion | flops 8625586176 | bytes 16777216 | tf_op jit(solution)/shard_map/dot_general | solution.py:65
  438.1 6.2 convert_add_fusion.2
  444.2 5.6 convert_add_fusion.1
  462.2 21.8 %collective-permute-done.44 = bf16[512,2048]{1,0:T(8,128)(2,1)} collective-permute-done((bf16[512,2048]{1,0:T(8,128)(2,1)}, bf16[512,2048]{1,0:T(8,128)(2,1)}, u32[]{:S(2)}, u32[]{:S(2)}) %collective-permute-start.44) | collective-permute-done | bytes 2097184 | tf_op jit(solution)/shard_map/ppermute | solution.py:78
  490.1 5.1 collective-permute-done.25
  541.2 8.3 %fusion.167 = (bf16[512,2048]{1,0:T(8,128)(2,1)}, f32[512,2048]{1,0:T(8,128)}) fusion(bf16[512,1536]{1,0:T(8,128)(2,1)S(1)} %constant_dynamic-update-slice_fusion.8, bf16[2048,1536]{1,0:T(8,128)(2,1)} %dynamic-slice_dynamic-update-slice_fusion), kind=kOutput, calls=%fused_computation.389 | convolution fusion | flops 3222274048 | bytes 14155776 | tf_op jit(solution)/shard_map/dot_general | solution.py:69
  558.9 24.5 %collective-permute-done.33 = bf16[4,256,512]{2,1,0:T(8,128)(2,1)} collective-permute-done((bf16[4,256,512]{2,1,0:T(8,128)(2,1)}, bf16[4,256,512]{2,1,0:T(8,128)(2,1)}, u32[]{:S(2)}, u32[]{:S(2)}) %collective-permute-start.33) | collective-permute-done | bytes 1048608 | tf_op jit(solution)/shard_map/ppermute | solution.py:78
  590.6 65.8 %collective-permute-done.32 = bf16[128,2048]{1,0:T(8,128)(2,1)S(1)} collective-permute-done((bf16[128,2048]{1,0:T(8,128)(2,1)S(1)}, bf16[128,2048]{1,0:T(8,128)(2,1)S(1)}, u32[]{:S(2)}, u32[]{:S(2)}) %collective-permute-start.32) | collective-permute-done | bytes 524320 | tf_op jit(solution)/shard_map/ppermute | solution.py:78
  669.8 7.6 %collective-permute-done.39 = bf16[64,2048]{1,0:T(8,128)(2,1)} collective-permute-done((bf16[64,2048]{1,0:T(8,128)(2,1)}, bf16[64,2048]{1,0:T(8,128)(2,1)}, u32[]{:S(2)}, u32[]{:S(2)}) %collective-permute-start.39) | collective-permute-done | bytes 262176 | tf_op jit(solution)/shard_map/ppermute | solution.py:78
  699.0 8.0 %all-to-all-start.5 = ((bf16[4,64,512]{2,1,0:T(8,128)(2,1)}), bf16[4,64,512]{2,1,0:T(8,128)(2,1)S(1)}, u32[]{:S(2)}, u32[]{:S(2)}) async-start(bf16[4,64,512]{2,1,0:T(8,128)(2,1)} %bitcast.88), calls=%async_computation.8 | async-start | bytes 524288 | tf_op jit(solution)/shard_map/all_to_all | solution.py:528
  710.3 5.9 convert_add_fusion.3
  (525 shorter events, 290.9 us)
Async XLA Ops:
  7.2 288.3 %all-gather.7.cloned.1.call-start = ((), (), s32[]{:S(2)}) async-start(), calls=%async_computation.10 | async-start | bytes 4718592 | tf_op jit(solution)/shard_map/all_gather | solution.py:360
  21.0 274.6 %all-gather.5.cloned.1.call-start = ((), (), s32[]{:S(2)}) async-start(), calls=%async_computation.9 | async-start | bytes 4718592 | tf_op jit(solution)/shard_map/all_gather | solution.py:430
  47.9 57.9 %collective-permute-start.7 = (bf16[256,1536]{1,0:T(8,128)(2,1)}, bf16[256,1536]{1,0:T(8,128)(2,1)S(1)}, u32[]{:S(2)}, u32[]{:S(2)}) collective-permute-start(bf16[256,1536]{1,0:T(8,128)(2,1)} %collective-permute-done.5), channel_id=1, source_target_pairs={{0,4},{4,0},{8,12},{12,8},{16,20},{20,16},{24,28},{28,24},{1,5},{5... | collective-permute-start | bytes 2359304 | tf_op jit(solution)/shard_map/ppermute | solution.py:78
  137.9 46.6 %collective-permute-start.16 = (bf16[2,512,1024]{2,1,0:T(8,128)(2,1)}, bf16[2,512,1024]{2,1,0:T(8,128)(2,1)}, u32[]{:S(2)}, u32[]{:S(2)}) collective-permute-start(bf16[2,512,1024]{2,1,0:T(8,128)(2,1)} %refs_0_.1), channel_id=1, source_target_pairs={{0,2},{1,3},{2,0},{3,1},{4,6},{5,7},{6,4},{7,5},{8,10},{9,11},{10,... | collective-permute-start | bytes 6291464 | tf_op jit(solution)/shard_map/ppermute | solution.py:78
  138.0 91.4 %collective-permute-start.22 = (bf16[2,1024,512]{2,1,0:T(8,128)(2,1)}, bf16[2,1024,512]{2,1,0:T(8,128)(2,1)}, u32[]{:S(2)}, u32[]{:S(2)}) collective-permute-start(bf16[2,1024,512]{2,1,0:T(8,128)(2,1)} %refs_8_), channel_id=1, source_target_pairs={{0,2},{1,3},{2,0},{3,1},{4,6},{5,7},{6,4},{7,5},{8,10},{9,11},{10,... | collective-permute-start | bytes 6291464 | tf_op jit(solution)/shard_map/ppermute | solution.py:78
  139.4 134.9 %collective-permute-start.19 = (bf16[2,512,1024]{2,1,0:T(8,128)(2,1)}, bf16[2,512,1024]{2,1,0:T(8,128)(2,1)}, u32[]{:S(2)}, u32[]{:S(2)}) collective-permute-start(bf16[2,512,1024]{2,1,0:T(8,128)(2,1)} %refs_4_.1), channel_id=1, source_target_pairs={{0,2},{1,3},{2,0},{3,1},{4,6},{5,7},{6,4},{7,5},{8,10},{9,11},{10,... | collective-permute-start | bytes 6291464 | tf_op jit(solution)/shard_map/ppermute | solution.py:78
  184.5 91.7 %collective-permute-start.17 = (bf16[2,512,1024]{2,1,0:T(8,128)(2,1)}, bf16[2,512,1024]{2,1,0:T(8,128)(2,1)}, u32[]{:S(2)}, u32[]{:S(2)}) collective-permute-start(bf16[2,512,1024]{2,1,0:T(8,128)(2,1)} %collective-permute-done.16.refs_2_), channel_id=1, source_target_pairs={{0,1},{1,0},{2,3},{3,2},{4,5},{5,4},{6,7},{7,6},{8,9},{9,8},{10,11... | collective-permute-start | bytes 6291464 | tf_op jit(solution)/shard_map/ppermute | solution.py:78
  189.5 106.0 %collective-permute-start.21 = (bf16[2,1024,512]{2,1,0:T(8,128)(2,1)}, bf16[2,1024,512]{2,1,0:T(8,128)(2,1)}, u32[]{:S(2)}, u32[]{:S(2)}) collective-permute-start(bf16[2,1024,512]{2,1,0:T(8,128)(2,1)} %refs_8_), channel_id=1, source_target_pairs={{0,1},{1,0},{2,3},{3,2},{4,5},{5,4},{6,7},{7,6},{8,9},{9,8},{10,11... | collective-permute-start | bytes 6291464 | tf_op jit(solution)/shard_map/ppermute | solution.py:78
  189.5 105.9 %collective-permute-start.15 = (bf16[2,512,1024]{2,1,0:T(8,128)(2,1)}, bf16[2,512,1024]{2,1,0:T(8,128)(2,1)}, u32[]{:S(2)}, u32[]{:S(2)}) collective-permute-start(bf16[2,512,1024]{2,1,0:T(8,128)(2,1)} %refs_0_.1), channel_id=1, source_target_pairs={{0,1},{1,0},{2,3},{3,2},{4,5},{5,4},{6,7},{7,6},{8,9},{9,8},{10,11... | collective-permute-start | bytes 6291464 | tf_op jit(solution)/shard_map/ppermute | solution.py:78
  192.0 84.2 %all-to-all-start = ((f32[8,2,128]{2,1,0:T(2,128)}), f32[8,2,128]{2,1,0:T(2,128)S(1)}, u32[]{:S(2)}, u32[]{:S(2)}) async-start(f32[8,2,128]{2,1,0:T(2,128)} %bitcast.37), calls=%async_computation | async-start | bytes 16384 | tf_op jit(solution)/shard_map/all_to_all | solution.py:431
  197.9 260.2 %reduce-scatter.6.cloned.1.call-start = ((), (), s32[]{:S(2)}) async-start(), calls=%async_computation.12 | async-start | bytes 4718592 | tf_op jit(solution)/shard_map/reduce_scatter | solution.py:448
  229.4 66.0 %collective-permute-start.18 = (bf16[2,512,1024]{2,1,0:T(8,128)(2,1)}, bf16[2,512,1024]{2,1,0:T(8,128)(2,1)}, u32[]{:S(2)}, u32[]{:S(2)}) collective-permute-start(bf16[2,512,1024]{2,1,0:T(8,128)(2,1)} %refs_4_.1), channel_id=1, source_target_pairs={{0,1},{1,0},{2,3},{3,2},{4,5},{5,4},{6,7},{7,6},{8,9},{9,8},{10,11... | collective-permute-start | bytes 6291464 | tf_op jit(solution)/shard_map/ppermute | solution.py:78
  367.8 90.2 %all-to-all-start.1 = ((f32[8,2,128]{2,1,0:T(2,128)}), f32[8,2,128]{2,1,0:T(2,128)S(1)}, u32[]{:S(2)}, u32[]{:S(2)}) async-start(f32[8,2,128]{2,1,0:T(2,128)} %bitcast.46), calls=%async_computation.3 | async-start | bytes 16384 | tf_op jit(solution)/shard_map/all_to_all | solution.py:450
  373.5 176.0 %reduce-scatter.4.cloned.1.call-start = ((), (), s32[]{:S(2)}) async-start(), calls=%async_computation.11 | async-start | bytes 4718592 | tf_op jit(solution)/shard_map/reduce_scatter | solution.py:481
  380.4 69.5 %collective-permute-start.45 = (bf16[512,2048]{1,0:T(8,128)(2,1)}, bf16[512,2048]{1,0:T(8,128)(2,1)}, u32[]{:S(2)}, u32[]{:S(2)}) collective-permute-start(bf16[512,2048]{1,0:T(8,128)(2,1)} %fusion.58), channel_id=1, source_target_pairs={{0,1},{1,0},{2,3},{3,2},{4,5},{5,4},{6,7},{7,6},{8,9},{9,8},{10,11... | collective-permute-start | bytes 6291464 | tf_op jit(solution)/shard_map/ppermute | solution.py:78
  385.1 69.1 %collective-permute-start.46 = (bf16[512,2048]{1,0:T(8,128)(2,1)}, bf16[512,2048]{1,0:T(8,128)(2,1)}, u32[]{:S(2)}, u32[]{:S(2)}) collective-permute-start(bf16[512,2048]{1,0:T(8,128)(2,1)} %fusion.50), channel_id=1, source_target_pairs={{0,1},{1,0},{2,3},{3,2},{4,5},{5,4},{6,7},{7,6},{8,9},{9,8},{10,11... | collective-permute-start | bytes 6291464 | tf_op jit(solution)/shard_map/ppermute | solution.py:78
  431.6 289.0 %reduce-scatter.8.cloned.1.call-start = ((), (), s32[]{:S(2)}) async-start(), calls=%async_computation.13 | async-start | bytes 4718592 | tf_op jit(solution)/shard_map/reduce_scatter | solution.py:540
  437.1 46.9 %collective-permute-start.44 = (bf16[512,2048]{1,0:T(8,128)(2,1)}, bf16[512,2048]{1,0:T(8,128)(2,1)}, u32[]{:S(2)}, u32[]{:S(2)}) collective-permute-start(bf16[512,2048]{1,0:T(8,128)(2,1)} %add_convert_fusion), channel_id=1, source_target_pairs={{0,2},{1,3},{2,0},{3,1},{4,6},{5,7},{6,4},{7,5},{8,10},{9,11},{10,... | collective-permute-start | bytes 6291464 | tf_op jit(solution)/shard_map/ppermute | solution.py:78
  539.9 43.5 %collective-permute-start.33 = (bf16[4,256,512]{2,1,0:T(8,128)(2,1)}, bf16[4,256,512]{2,1,0:T(8,128)(2,1)}, u32[]{:S(2)}, u32[]{:S(2)}) collective-permute-start(bf16[4,256,512]{2,1,0:T(8,128)(2,1)} %dynamic-slice_bitcast_fusion.1), channel_id=1, source_target_pairs={{0,4},{4,0},{8,12},{12,8},{16,20},{20,16},{24,28},{28,24},{1,5},{5... | collective-permute-start | bytes 3145736 | tf_op jit(solution)/shard_map/ppermute | solution.py:78
  553.3 157.0 %collective-permute-start.47 = (bf16[512,2048]{1,0:T(8,128)(2,1)}, bf16[512,2048]{1,0:T(8,128)(2,1)}, u32[]{:S(2)}, u32[]{:S(2)}) collective-permute-start(bf16[512,2048]{1,0:T(8,128)(2,1)} %convert_add_fusion.4), channel_id=1, source_target_pairs={{0,2},{1,3},{2,0},{3,1},{4,6},{5,7},{6,4},{7,5},{8,10},{9,11},{10,... | collective-permute-start | bytes 6291464 | tf_op jit(solution)/shard_map/ppermute | solution.py:78
  554.6 161.6 %collective-permute-start.50 = (bf16[2048,512]{1,0:T(8,128)(2,1)}, bf16[2048,512]{1,0:T(8,128)(2,1)}, u32[]{:S(2)}, u32[]{:S(2)}) collective-permute-start(bf16[2048,512]{1,0:T(8,128)(2,1)} %convert_add_fusion.1), channel_id=1, source_target_pairs={{0,2},{1,3},{2,0},{3,1},{4,6},{5,7},{6,4},{7,5},{8,10},{9,11},{10,... | collective-permute-start | bytes 6291464 | tf_op jit(solution)/shard_map/ppermute | solution.py:78
  556.0 100.5 %collective-permute-start.32 = (bf16[128,2048]{1,0:T(8,128)(2,1)S(1)}, bf16[128,2048]{1,0:T(8,128)(2,1)S(1)}, u32[]{:S(2)}, u32[]{:S(2)}) collective-permute-start(bf16[128,2048]{1,0:T(8,128)(2,1)S(1)} %fusion.42), channel_id=1, source_target_pairs={{0,2},{1,3},{2,0},{3,1},{4,6},{5,7},{6,4},{7,5},{8,10},{9,11},{10,... | collective-permute-start | bytes 1572872 | tf_op jit(solution)/shard_map/ppermute | solution.py:78
  583.4 83.2 %collective-permute-start.38 = (bf16[64,2048]{1,0:T(8,128)(2,1)}, bf16[64,2048]{1,0:T(8,128)(2,1)}, u32[]{:S(2)}, u32[]{:S(2)}) collective-permute-start(bf16[64,2048]{1,0:T(8,128)(2,1)} %get-tuple-element.164), channel_id=1, source_target_pairs={{0,24},{4,28},{8,16},{12,20},{16,8},{20,12},{24,0},{28,4},{1,25},{... | collective-permute-start | bytes 786440 | tf_op jit(solution)/shard_map/ppermute | solution.py:78
  588.1 79.7 %collective-permute-start.40 = (bf16[64,2048]{1,0:T(8,128)(2,1)}, bf16[64,2048]{1,0:T(8,128)(2,1)}, u32[]{:S(2)}, u32[]{:S(2)}) collective-permute-start(bf16[64,2048]{1,0:T(8,128)(2,1)} %get-tuple-element.165), channel_id=1, source_target_pairs={{0,8},{4,12},{8,0},{12,4},{16,24},{20,28},{24,16},{28,20},{1,9},{5... | collective-permute-start | bytes 786440 | tf_op jit(solution)/shard_map/ppermute | solution.py:78
  (150 other events, 2218.3 us)
Sparse Core Ops, SparseCore 0:
  21.1 92.4 all-gather.6
  138.0 70.7 all-gather.4
  360.5 88.4 reduce-scatter.5
  453.0 87.9 reduce-scatter.3
  544.5 101.0 reduce-scatter.7

commit v8 on v7

--- a/solution.py
+++ b/solution.py
@@ -153,21 +153,14 @@
 
 def owner_scatter(values):
     owners = lax.axis_size(OWNER)
-    index = lax.axis_index(OWNER)
-    if owners > 8:
-        return lax.psum_scatter(values, OWNER, scatter_dimension=0, tiled=True)[0]
-    pairs = values.reshape(owners // 2, 2, *values.shape[1:])
-    away = lax.dynamic_index_in_dim(pairs, 1 - index % 2, 1, keepdims=False)
-    kept = lax.dynamic_index_in_dim(pairs, index % 2, 1, keepdims=False)
-    arrived = swap(away, 1, OWNER)
-    near = (kept.astype(jnp.float32) + arrived.astype(jnp.float32)).astype(jnp.bfloat16)
-    total = 0.0
-    for mask in reversed(range(owners // 2)):
-        part = lax.dynamic_index_in_dim(near, (index // 2) ^ mask, 0, keepdims=False)
-        if mask:
-            part = swap(part, 2 * mask, OWNER)
-        total = total + part.astype(jnp.float32)
-    return total.astype(jnp.bfloat16)
+    values = values.reshape([2] * len(bits_of(owners)) + list(values.shape[1:]))
+    for axis, bit in reversed(list(enumerate(reversed(bits_of(owners))))):
+        index = (lax.axis_index(OWNER) // bit) % 2
+        away = lax.dynamic_index_in_dim(values, 1 - index, axis, keepdims=False)
+        kept = lax.dynamic_index_in_dim(values, index, axis, keepdims=False)
+        arrived = swap(away, bit, OWNER)
+        values = (kept.astype(jnp.float32) + arrived.astype(jnp.float32)).astype(jnp.bfloat16)
+    return values
 
 
 def place_kernel(heads_ref, values_ref, query_ref, key_ref, value_ref):
@@ -478,7 +471,7 @@
     out_partial = dot(hidden_w, down_all)
     out_partial = out_partial.astype(bf16)
     row_grads, route_back = lax.optimization_barrier((row_grads, route_back))
-    moe_out = lax.psum_scatter(out_partial, OWNER, scatter_dimension=0, tiled=True)
+    moe_out = owner_scatter(out_partial.reshape(owners, rows, width))
 
     route_grad = route_back.reshape(experts, rows).T
     prob_grad = jnp.where(named, route_grad, 0.0)

time: 752 us -> 813 us (1.081)
  waiting for transfers between devices: 315 us -> 377 us
  matrix products: 104 us -> 95.7 us
    ppermute x50 -> x51, waiting for transfers between devices: 312 us -> 365 us  [swap(): lax.ppermute(values, axis_name, [(i, i ^ mask) for i in range(count)])]
    dynamic_slice x0 -> x6, local copies, waits for them, and re-layouts: none -> 9.61 us  [the longest x3 5.03 us: owner_scatter(): away = lax.dynamic_index_in_dim(values, 1 - index, axis, keepdims=False)]
    convert_element_type x2 -> x9, other arithmetic: 3.18 us -> 11.6 us  [owner_scatter(): (kept.astype(jnp.float32) + arrived.astype(jnp.float32)).astype(jnp.bfloa...]
    ppermute x50 -> x51, starting transfers between devices: 45.9 us -> 39.9 us  [swap(): lax.ppermute(values, axis_name, [(i, i ^ mask) for i in range(count)])]
    unnamed x244 -> x264, local copies, waits for them, and re-layouts: 39.3 us -> 35 us
  transfers between devices with their start and end apart: 62 -> 62, of which waited for: 19 -> 24; matrix products, arithmetic and copies ran while one was open for 33% -> 29% of each run, Pallas kernels for 0% -> 0%
where the time goes in v8:
time: 813 us; the launch traced here: 807 us
  waiting for transfers between devices  377 us (46%)
  matrix products  95.7 us (12%)
  other arithmetic  82.5 us (10%)
  local copies, waits for them, and re-layouts  81.8 us (10%)
  starting transfers between devices  80.2 us (10%)
  Pallas kernels  67.4 us (8%)
  between operations  16.2 us (2%)
    ppermute x51, waiting for transfers between devices, swap(): lax.ppermute(values, axis_name, [(i, i ^ mask) for i in range(count)])  365 us
    dot_general x16, matrix products, t_dot(): lax.dot_general(a, b, (((0,), (0,)), ((), ())), preferred_element_type=jn...  59 us
    ppermute x51, starting transfers between devices, swap(): lax.ppermute(values, axis_name, [(i, i ^ mask) for i in range(count)])  39.9 us
    pallas_call x1, Pallas kernels, expert_hidden(): pl.pallas_call(functools.partial(expert_hidden_kernel, parts), grid=(rows...  36.5 us
    unnamed x264, local copies, waits for them, and re-layouts  35 us
    pallas_call x1, Pallas kernels, back_rows(): pl.pallas_call(functools.partial(back_rows_kernel, parts), grid=(rows //...  28.6 us
    add x6, other arithmetic, scatter_stage(): return {m: blocks[m] + arrived[m].astype(jnp.float32) for m in arrived}  22.2 us
    dot_general x11, matrix products, dot(): return jnp.dot(a, b, preferred_element_type=jnp.float32)  22 us
  transfers between devices with their start and end apart: 62, of which 24 were waited for; matrix products, arithmetic and copies ran while one was open for 29% of the time, Pallas kernels for 0%

profile of v8, /device:TPU:13, one launch (start us, length us, event | category | flops | bytes accessed | tf_op | source)
XLA Modules:
  0.0 806.7 jit_solution(692647852324907601)
XLA Ops:
  41.8 6.0 collective-permute-done.5
  48.1 17.2 %collective-permute-done.6 = bf16[256,1536]{1,0:T(8,128)(2,1)} collective-permute-done((bf16[256,1536]{1,0:T(8,128)(2,1)}, bf16[256,1536]{1,0:T(8,128)(2,1)}, u32[]{:S(2)}, u32[]{:S(2)}) %collective-permute-start.6) | collective-permute-done | bytes 786464 | tf_op jit(solution)/shard_map/ppermute | solution.py:78
  75.8 29.4 %collective-permute-done.8 = bf16[256,1536]{1,0:T(8,128)(2,1)S(1)} collective-permute-done((bf16[256,1536]{1,0:T(8,128)(2,1)}, bf16[256,1536]{1,0:T(8,128)(2,1)S(1)}, u32[]{:S(2)}, u32[]{:S(2)}) %collective-permute-start.8) | collective-permute-done | bytes 786464 | tf_op jit(solution)/shard_map/ppermute | solution.py:78
  121.7 12.8 %collective-permute-done.14 = bf16[128,2048]{1,0:T(8,128)(2,1)S(1)} collective-permute-done((bf16[128,2048]{1,0:T(8,128)(2,1)S(1)}, bf16[128,2048]{1,0:T(8,128)(2,1)S(1)}, u32[]{:S(2)}, u32[]{:S(2)}) %collective-permute-start.14) | collective-permute-done | bytes 524320 | tf_op jit(solution)/shard_map/ppermute | solution.py:78
  140.2 43.3 %collective-permute-done.16.refs_2_ = bf16[2,512,1024]{2,1,0:T(8,128)(2,1)} collective-permute-done((bf16[2,512,1024]{2,1,0:T(8,128)(2,1)}, bf16[2,512,1024]{2,1,0:T(8,128)(2,1)}, u32[]{:S(2)}, u32[]{:S(2)}) %collective-permute-start.16) | collective-permute-done | bytes 2097184 | tf_op jit(solution)/shard_map/ppermute | solution.py:78
  205.8 22.6 %collective-permute-done.22.refs_10_ = bf16[2,1024,512]{2,1,0:T(8,128)(2,1)} collective-permute-done((bf16[2,1024,512]{2,1,0:T(8,128)(2,1)}, bf16[2,1024,512]{2,1,0:T(8,128)(2,1)}, u32[]{:S(2)}, u32[]{:S(2)}) %collective-permute-start.22) | collective-permute-done | bytes 2097184 | tf_op jit(solution)/shard_map/ppermute | solution.py:78
  231.7 41.6 %collective-permute-done.19.refs_6_ = bf16[2,512,1024]{2,1,0:T(8,128)(2,1)} collective-permute-done((bf16[2,512,1024]{2,1,0:T(8,128)(2,1)}, bf16[2,512,1024]{2,1,0:T(8,128)(2,1)}, u32[]{:S(2)}, u32[]{:S(2)}) %collective-permute-start.19) | collective-permute-done | bytes 2097184 | tf_op jit(solution)/shard_map/ppermute | solution.py:78
  295.5 36.5 %shard_map.263 = (bf16[1024,2048]{1,0:T(8,128)(2,1)}, bf16[1024,2048]{1,0:T(8,128)(2,1)}, bf16[1024,2048]{1,0:T(8,128)(2,1)}, f32[2,1024,128]{2,1,0:T(8,128)}) custom-call(bf16[1024,2048]{1,0:T(8,128)(2,1)} %all-gather.5.cloned.1.call-done.x_ref, bf16[1024,2048]{1,0:T(8,128)(2,1)} %all-gather.7.cloned.1.call-done.cot_ref, f32[2,1024,1]{2,1,0:T(8,128)} %copy.98.weight_ref, ...), custom_call_target="tpu_custom_call" | custom-call | tf_op jit(solution)/shard_map/pallas_call | solution.py:231
  332.0 28.6 %shard_map.264 = bf16[1024,2048]{1,0:T(8,128)(2,1)} custom-call(bf16[1024,2048]{1,0:T(8,128)(2,1)} %get-tuple-element.83.gate_grad_ref, bf16[1024,2048]{1,0:T(8,128)(2,1)} %get-tuple-element.84.up_grad_ref, bf16[2,512,1024]{2,1,0:T(8,128)(2,1)} %refs_0_.1, bf16[2,512,1024]{2,1,0:T(8,128)(2,1)} %collective-permute-done.15.refs_1_, ...), custom_call_target="tpu_custom_call" | custom-call | tf_op jit(solution)/shard_map/pallas_call | solution.py:275
  360.7 6.4 fusion.57
  396.4 12.3 %fusion.12 = bf16[1024,2048]{1,0:T(8,128)(2,1)S(1)} fusion(bf16[1024,2048]{1,0:T(8,128)(2,1)} %get-tuple-element.85, bf16[2048,512]{1,0:T(8,128)(2,1)} %bitcast.44, bf16[2048,512]{1,0:T(8,128)(2,1)} %bitcast.43, bf16[2048,512]{1,0:T(8,128)(2,1)} %bitcast.42, bf16[2048,512]{1,0:T(8,128)(2,1)S(1)} %bitcast.280), kind=kOutput, calls=%fused_computation.25 | convolution fusion | flops 8625586176 | bytes 16777216 | tf_op jit(solution)/shard_map/dot_general | solution.py:65
  415.9 6.2 all-to-all-start.1
  430.4 38.5 %collective-permute-done.24 = bf16[2,2,128,2048]{3,2,0,1:T(8,128)(2,1)} collective-permute-done((bf16[2,2,128,2048]{3,2,0,1:T(8,128)(2,1)}, bf16[2,2,128,2048]{3,2,0,1:T(8,128)(2,1)}, u32[]{:S(2)}, u32[]{:S(2)}) %collective-permute-start.24) | collective-permute-done | bytes 2097184 | tf_op jit(solution)/shard_map/ppermute | solution.py:78
  490.2 15.9 %collective-permute-done.25 = bf16[2,128,2048]{2,1,0:T(8,128)(2,1)S(1)} collective-permute-done((bf16[2,128,2048]{2,1,0:T(8,128)(2,1)S(1)}, bf16[2,128,2048]{2,1,0:T(8,128)(2,1)S(1)}, u32[]{:S(2)}, u32[]{:S(2)}) %collective-permute-start.25) | collective-permute-done | bytes 1048608 | tf_op jit(solution)/shard_map/ppermute | solution.py:78
  512.2 18.2 %collective-permute-done.26 = bf16[128,2048]{1,0:T(8,128)(2,1)S(1)} collective-permute-done((bf16[128,2048]{1,0:T(8,128)(2,1)S(1)}, bf16[128,2048]{1,0:T(8,128)(2,1)S(1)}, u32[]{:S(2)}, u32[]{:S(2)}) %collective-permute-start.26) | collective-permute-done | bytes 524320 | tf_op jit(solution)/shard_map/ppermute | solution.py:78
  541.0 6.3 collective-permute-done.28
  599.6 6.1 fusion.172
  612.8 19.8 %collective-permute-done.36 = bf16[2,2,256,512]{3,2,0,1:T(8,128)(2,1)} collective-permute-done((bf16[2,2,256,512]{3,2,0,1:T(8,128)(2,1)}, bf16[2,2,256,512]{3,2,0,1:T(8,128)(2,1)}, u32[]{:S(2)}, u32[]{:S(2)}) %collective-permute-start.36) | collective-permute-done | bytes 1048608 | tf_op jit(solution)/shard_map/ppermute | solution.py:78
  636.6 73.0 %collective-permute-done.35 = bf16[128,2048]{1,0:T(8,128)(2,1)S(1)} collective-permute-done((bf16[128,2048]{1,0:T(8,128)(2,1)S(1)}, bf16[128,2048]{1,0:T(8,128)(2,1)S(1)}, u32[]{:S(2)}, u32[]{:S(2)}) %collective-permute-start.35) | collective-permute-done | bytes 524320 | tf_op jit(solution)/shard_map/ppermute | solution.py:78
  710.9 6.4 all-to-all-start.2
  723.3 6.8 all-to-all-start.3
  740.8 12.9 %collective-permute-done.41 = bf16[64,2048]{1,0:T(8,128)(2,1)S(1)} collective-permute-done((bf16[64,2048]{1,0:T(8,128)(2,1)S(1)}, bf16[64,2048]{1,0:T(8,128)(2,1)S(1)}, u32[]{:S(2)}, u32[]{:S(2)}) %collective-permute-start.41) | collective-permute-done | bytes 262176 | tf_op jit(solution)/shard_map/ppermute | solution.py:78
  760.1 6.2 all-to-all-start.5
  783.1 6.0 all-to-all-start.4
  (557 shorter events, 311.6 us)
Async XLA Ops:
  7.2 288.3 %all-gather.7.cloned.1.call-start = ((), (), s32[]{:S(2)}) async-start(), calls=%async_computation.9 | async-start | bytes 4718592 | tf_op jit(solution)/shard_map/all_gather | solution.py:353
  20.9 274.6 %all-gather.5.cloned.1.call-start = ((), (), s32[]{:S(2)}) async-start(), calls=%async_computation.8 | async-start | bytes 4718592 | tf_op jit(solution)/shard_map/all_gather | solution.py:423
  47.8 57.9 %collective-permute-start.7 = (bf16[256,1536]{1,0:T(8,128)(2,1)}, bf16[256,1536]{1,0:T(8,128)(2,1)S(1)}, u32[]{:S(2)}, u32[]{:S(2)}) collective-permute-start(bf16[256,1536]{1,0:T(8,128)(2,1)} %collective-permute-done.5), channel_id=1, source_target_pairs={{0,4},{4,0},{8,12},{12,8},{16,20},{20,16},{24,28},{28,24},{1,5},{5... | collective-permute-start | bytes 2359304 | tf_op jit(solution)/shard_map/ppermute | solution.py:78
  137.1 91.3 %collective-permute-start.22 = (bf16[2,1024,512]{2,1,0:T(8,128)(2,1)}, bf16[2,1024,512]{2,1,0:T(8,128)(2,1)}, u32[]{:S(2)}, u32[]{:S(2)}) collective-permute-start(bf16[2,1024,512]{2,1,0:T(8,128)(2,1)} %refs_8_), channel_id=1, source_target_pairs={{0,2},{1,3},{2,0},{3,1},{4,6},{5,7},{6,4},{7,5},{8,10},{9,11},{10,... | collective-permute-start | bytes 6291464 | tf_op jit(solution)/shard_map/ppermute | solution.py:78
  138.6 156.9 %collective-permute-start.21 = (bf16[2,1024,512]{2,1,0:T(8,128)(2,1)}, bf16[2,1024,512]{2,1,0:T(8,128)(2,1)}, u32[]{:S(2)}, u32[]{:S(2)}) collective-permute-start(bf16[2,1024,512]{2,1,0:T(8,128)(2,1)} %refs_8_), channel_id=1, source_target_pairs={{0,1},{1,0},{2,3},{3,2},{4,5},{5,4},{6,7},{7,6},{8,9},{9,8},{10,11... | collective-permute-start | bytes 6291464 | tf_op jit(solution)/shard_map/ppermute | solution.py:78
  140.1 155.3 %collective-permute-start.15 = (bf16[2,512,1024]{2,1,0:T(8,128)(2,1)}, bf16[2,512,1024]{2,1,0:T(8,128)(2,1)}, u32[]{:S(2)}, u32[]{:S(2)}) collective-permute-start(bf16[2,512,1024]{2,1,0:T(8,128)(2,1)} %refs_0_.1), channel_id=1, source_target_pairs={{0,1},{1,0},{2,3},{3,2},{4,5},{5,4},{6,7},{7,6},{8,9},{9,8},{10,11... | collective-permute-start | bytes 6291464 | tf_op jit(solution)/shard_map/ppermute | solution.py:78
  140.1 133.2 %collective-permute-start.19 = (bf16[2,512,1024]{2,1,0:T(8,128)(2,1)}, bf16[2,512,1024]{2,1,0:T(8,128)(2,1)}, u32[]{:S(2)}, u32[]{:S(2)}) collective-permute-start(bf16[2,512,1024]{2,1,0:T(8,128)(2,1)} %refs_4_.1), channel_id=1, source_target_pairs={{0,2},{1,3},{2,0},{3,1},{4,6},{5,7},{6,4},{7,5},{8,10},{9,11},{10,... | collective-permute-start | bytes 6291464 | tf_op jit(solution)/shard_map/ppermute | solution.py:78
  183.5 91.7 %collective-permute-start.17 = (bf16[2,512,1024]{2,1,0:T(8,128)(2,1)}, bf16[2,512,1024]{2,1,0:T(8,128)(2,1)}, u32[]{:S(2)}, u32[]{:S(2)}) collective-permute-start(bf16[2,512,1024]{2,1,0:T(8,128)(2,1)} %collective-permute-done.16.refs_2_), channel_id=1, source_target_pairs={{0,1},{1,0},{2,3},{3,2},{4,5},{5,4},{6,7},{7,6},{8,9},{9,8},{10,11... | collective-permute-start | bytes 6291464 | tf_op jit(solution)/shard_map/ppermute | solution.py:78
  188.7 86.5 %all-to-all-start = ((f32[8,2,128]{2,1,0:T(2,128)}), f32[8,2,128]{2,1,0:T(2,128)S(1)}, u32[]{:S(2)}, u32[]{:S(2)}) async-start(f32[8,2,128]{2,1,0:T(2,128)} %bitcast.37), calls=%async_computation | async-start | bytes 16384 | tf_op jit(solution)/shard_map/all_to_all | solution.py:424
  194.4 336.9 %reduce-scatter.3.cloned.1.call-start = ((), (), s32[]{:S(2)}) async-start(), calls=%async_computation.10 | async-start | bytes 4718592 | tf_op jit(solution)/shard_map/reduce_scatter | solution.py:441
  228.4 67.0 %collective-permute-start.18 = (bf16[2,512,1024]{2,1,0:T(8,128)(2,1)}, bf16[2,512,1024]{2,1,0:T(8,128)(2,1)}, u32[]{:S(2)}, u32[]{:S(2)}) collective-permute-start(bf16[2,512,1024]{2,1,0:T(8,128)(2,1)} %refs_4_.1), channel_id=1, source_target_pairs={{0,1},{1,0},{2,3},{3,2},{4,5},{5,4},{6,7},{7,6},{8,9},{9,8},{10,11... | collective-permute-start | bytes 6291464 | tf_op jit(solution)/shard_map/ppermute | solution.py:78
  412.2 56.8 %collective-permute-start.24 = (bf16[2,2,128,2048]{3,2,0,1:T(8,128)(2,1)}, bf16[2,2,128,2048]{3,2,0,1:T(8,128)(2,1)}, u32[]{:S(2)}, u32[]{:S(2)}) collective-permute-start(bf16[2,2,128,2048]{3,2,0,1:T(8,128)(2,1)} %bitcast.261), channel_id=1, source_target_pairs={{0,4},{4,0},{8,12},{12,8},{16,20},{20,16},{24,28},{28,24},{1,5},{5... | collective-permute-start | bytes 6291464 | tf_op jit(solution)/shard_map/ppermute | solution.py:78
  412.2 60.2 %collective-permute-start.44 = (bf16[512,2048]{1,0:T(8,128)(2,1)}, bf16[512,2048]{1,0:T(8,128)(2,1)}, u32[]{:S(2)}, u32[]{:S(2)}) collective-permute-start(bf16[512,2048]{1,0:T(8,128)(2,1)} %fusion.57), channel_id=1, source_target_pairs={{0,1},{1,0},{2,3},{3,2},{4,5},{5,4},{6,7},{7,6},{8,9},{9,8},{10,11... | collective-permute-start | bytes 6291464 | tf_op jit(solution)/shard_map/ppermute | solution.py:78
  413.2 72.8 %collective-permute-start.46 = (bf16[512,2048]{1,0:T(8,128)(2,1)}, bf16[512,2048]{1,0:T(8,128)(2,1)}, u32[]{:S(2)}, u32[]{:S(2)}) collective-permute-start(bf16[512,2048]{1,0:T(8,128)(2,1)} %fusion.63), channel_id=1, source_target_pairs={{0,1},{1,0},{2,3},{3,2},{4,5},{5,4},{6,7},{7,6},{8,9},{9,8},{10,11... | collective-permute-start | bytes 6291464 | tf_op jit(solution)/shard_map/ppermute | solution.py:78
  413.2 94.9 %collective-permute-start.47 = (bf16[512,2048]{1,0:T(8,128)(2,1)}, bf16[512,2048]{1,0:T(8,128)(2,1)}, u32[]{:S(2)}, u32[]{:S(2)}) collective-permute-start(bf16[512,2048]{1,0:T(8,128)(2,1)} %fusion.55), channel_id=1, source_target_pairs={{0,1},{1,0},{2,3},{3,2},{4,5},{5,4},{6,7},{7,6},{8,9},{9,8},{10,11... | collective-permute-start | bytes 6291464 | tf_op jit(solution)/shard_map/ppermute | solution.py:78
  415.9 115.4 %all-to-all-start.1 = ((f32[8,2,128]{2,1,0:T(2,128)}), f32[8,2,128]{2,1,0:T(2,128)S(1)}, u32[]{:S(2)}, u32[]{:S(2)}) async-start(f32[8,2,128]{2,1,0:T(2,128)} %bitcast.53), calls=%async_computation.2 | async-start | bytes 16384 | tf_op jit(solution)/shard_map/all_to_all | solution.py:443
  422.1 361.0 %reduce-scatter.5.cloned.1.call-start = ((), (), s32[]{:S(2)}) async-start(), calls=%async_computation.11 | async-start | bytes 4718592 | tf_op jit(solution)/shard_map/reduce_scatter | solution.py:533
  427.3 48.9 %collective-permute-start.49 = (bf16[2048,512]{1,0:T(8,128)(2,1)S(1)}, bf16[2048,512]{1,0:T(8,128)(2,1)S(1)}, u32[]{:S(2)}, u32[]{:S(2)}) collective-permute-start(bf16[2048,512]{1,0:T(8,128)(2,1)S(1)} %convolution_convert_fusion.2), channel_id=1, source_target_pairs={{0,1},{1,0},{2,3},{3,2},{4,5},{5,4},{6,7},{7,6},{8,9},{9,8},{10,11... | collective-permute-start | bytes 6291464 | tf_op jit(solution)/shard_map/ppermute | solution.py:78
  472.4 63.0 %collective-permute-start.43 = (bf16[512,2048]{1,0:T(8,128)(2,1)}, bf16[512,2048]{1,0:T(8,128)(2,1)}, u32[]{:S(2)}, u32[]{:S(2)}) collective-permute-start(bf16[512,2048]{1,0:T(8,128)(2,1)} %fusion.65), channel_id=1, source_target_pairs={{0,1},{1,0},{2,3},{3,2},{4,5},{5,4},{6,7},{7,6},{8,9},{9,8},{10,11... | collective-permute-start | bytes 6291464 | tf_op jit(solution)/shard_map/ppermute | solution.py:78
  476.2 59.1 %collective-permute-start.45 = (bf16[512,2048]{1,0:T(8,128)(2,1)}, bf16[512,2048]{1,0:T(8,128)(2,1)}, u32[]{:S(2)}, u32[]{:S(2)}) collective-permute-start(bf16[512,2048]{1,0:T(8,128)(2,1)} %add_convert_fusion), channel_id=1, source_target_pairs={{0,2},{1,3},{2,0},{3,1},{4,6},{5,7},{6,4},{7,5},{8,10},{9,11},{10,... | collective-permute-start | bytes 6291464 | tf_op jit(solution)/shard_map/ppermute | solution.py:78
  606.3 166.5 %collective-permute-start.48 = (bf16[512,2048]{1,0:T(8,128)(2,1)}, bf16[512,2048]{1,0:T(8,128)(2,1)}, u32[]{:S(2)}, u32[]{:S(2)}) collective-permute-start(bf16[512,2048]{1,0:T(8,128)(2,1)} %convert_add_fusion.5), channel_id=1, source_target_pairs={{0,2},{1,3},{2,0},{3,1},{4,6},{5,7},{6,4},{7,5},{8,10},{9,11},{10,... | collective-permute-start | bytes 6291464 | tf_op jit(solution)/shard_map/ppermute | solution.py:78
  608.5 170.2 %collective-permute-start.51 = (bf16[2048,512]{1,0:T(8,128)(2,1)}, bf16[2048,512]{1,0:T(8,128)(2,1)}, u32[]{:S(2)}, u32[]{:S(2)}) collective-permute-start(bf16[2048,512]{1,0:T(8,128)(2,1)} %convert_add_fusion.2), channel_id=1, source_target_pairs={{0,2},{1,3},{2,0},{3,1},{4,6},{5,7},{6,4},{7,5},{8,10},{9,11},{10,... | collective-permute-start | bytes 6291464 | tf_op jit(solution)/shard_map/ppermute | solution.py:78
  609.1 100.5 %collective-permute-start.35 = (bf16[128,2048]{1,0:T(8,128)(2,1)S(1)}, bf16[128,2048]{1,0:T(8,128)(2,1)S(1)}, u32[]{:S(2)}, u32[]{:S(2)}) collective-permute-start(bf16[128,2048]{1,0:T(8,128)(2,1)S(1)} %fusion.44), channel_id=1, source_target_pairs={{0,2},{1,3},{2,0},{3,1},{4,6},{5,7},{6,4},{7,5},{8,10},{9,11},{10,... | collective-permute-start | bytes 1572872 | tf_op jit(solution)/shard_map/ppermute | solution.py:78
  632.6 103.0 %collective-permute-start.40 = (bf16[2,64,2048]{2,1,0:T(8,128)(2,1)}, bf16[2,64,2048]{2,1,0:T(8,128)(2,1)}, u32[]{:S(2)}, u32[]{:S(2)}) collective-permute-start(bf16[2,64,2048]{2,1,0:T(8,128)(2,1)} %dynamic-slice_bitcast_fusion.1), channel_id=1, source_target_pairs={{0,8},{4,12},{8,0},{12,4},{16,24},{20,28},{24,16},{28,20},{1,9},{5... | collective-permute-start | bytes 1572872 | tf_op jit(solution)/shard_map/ppermute | solution.py:78
  (160 other events, 2393.8 us)
Sparse Core Ops, SparseCore 0:
  21.1 92.4 all-gather.6
  137.0 70.6 all-gather.4
  360.8 95.7 reduce-scatter.2
  599.7 101.2 reduce-scatter.4

commit v9 on v8

--- a/solution.py
+++ b/solution.py
@@ -151,31 +151,56 @@
     return total.reshape(values.shape)
 
 
+def owner_bits():
+    return bits_of(lax.axis_size(OWNER))[::-1]
+
+
+def owner_split(values):
+    return values.reshape([2] * len(owner_bits()) + list(values.shape[1:]))
+
+
+def owner_stage(values, left, bit):
+    index = (lax.axis_index(OWNER) // bit) % 2
+    axis = left.index(bit)
+    away = lax.dynamic_index_in_dim(values, 1 - index, axis, keepdims=False)
+    kept = lax.dynamic_index_in_dim(values, index, axis, keepdims=False)
+    arrived = swap(away, bit, OWNER)
+    total = kept.astype(jnp.float32) + arrived.astype(jnp.float32)
+    return total.astype(jnp.bfloat16), [b for b in left if b != bit]
+
+
 def owner_scatter(values):
-    owners = lax.axis_size(OWNER)
-    values = values.reshape([2] * len(bits_of(owners)) + list(values.shape[1:]))
-    for axis, bit in reversed(list(enumerate(reversed(bits_of(owners))))):
-        index = (lax.axis_index(OWNER) // bit) % 2
-        away = lax.dynamic_index_in_dim(values, 1 - index, axis, keepdims=False)
-        kept = lax.dynamic_index_in_dim(values, index, axis, keepdims=False)
-        arrived = swap(away, bit, OWNER)
-        values = (kept.astype(jnp.float32) + arrived.astype(jnp.float32)).astype(jnp.bfloat16)
+    values, left = owner_split(values), owner_bits()
+    for bit in left[::-1]:
+        values, left = owner_stage(values, left, bit)
     return values
 
 
-def place_kernel(heads_ref, values_ref, query_ref, key_ref, value_ref):
+def owner_scatter_pair(first, second):
+    first, second = owner_split(first), owner_split(second)
+    left, left_two = owner_bits(), owner_bits()
+    order = left[::-1]
+    for bit, bit_two in zip(order, order[1:] + order[:1]):
+        first, left = owner_stage(first, left, bit)
+        second, left_two = owner_stage(second, left_two, bit_two)
+        first, second = lax.optimization_barrier((first, second))
+    return first, second
+
+
+def place_kernel(values_ref, *out_refs):
     parts, _, cols = values_ref.shape
-    for p in range(parts):
-        at = slice(p * cols, (p + 1) * cols)
-        query_ref[:, at] = heads_ref[p, :, :cols].astype(jnp.float32)
-        key_ref[:, at] = heads_ref[p, :, cols:].astype(jnp.float32)
-        value_ref[:, at] = values_ref[p].astype(jnp.float32)
-
-
-def place(heads, values):
+    cols = cols // 3
+    for k in range(3):
+        for p in range(parts):
+            out_refs[k][:, p * cols : (p + 1) * cols] = values_ref[
+                p, :, k * cols : (k + 1) * cols
+            ].astype(jnp.float32)
+
+
+def place(values):
     parts, rows, cols = values.shape
-    shape = jax.ShapeDtypeStruct((rows, parts * cols), jnp.float32)
-    return pl.pallas_call(place_kernel, out_shape=[shape] * 3)(heads, values)
+    shape = jax.ShapeDtypeStruct((rows, parts * cols // 3), jnp.float32)
+    return pl.pallas_call(place_kernel, out_shape=[shape] * 3)(values)
 
 
 def expert_hidden_kernel(parts, x_ref, cot_ref, weight_ref, *refs):
@@ -511,16 +536,19 @@
     key_grad_b = (key_inverse * (grad_keys - key_unit * means[1][:, None])).astype(bf16)
     value_grad_b = by_row(grad_values.reshape(whole)).astype(bf16)
     qkv_grad = jnp.concatenate([query_grad_b, key_grad_b, value_grad_b], axis=1)
+    query_part = t_dot(attn_in, query_grad_b)
+    key_part = t_dot(attn_in, key_grad_b)
+    query_part, key_part = query_part.astype(bf16), key_part.astype(bf16)
+    qkv_grad = after(qkv_grad, query_part, key_part)
     attn_in_part = dot_t(qkv_grad, qkv_w)
     attn_in_grad = scatter_pieces(
         [attn_in_part[mask * rows : (mask + 1) * rows] for mask in range(parts)]
     )
     value_part = t_dot(attn_in, value_grad_b).astype(bf16).reshape(owners, parts * final_rows, cols)
     down_weight_grad = scatter_far(after(down_near, attn_in_part)).reshape(EXP_DEV, ff, cols)
-    value_sum = owner_scatter(value_part).reshape(parts, final_rows, cols)
-    value_sum = lax.all_to_all(value_sum, SHARD, split_axis=0, concat_axis=0, tiled=True)
-    qk_part = t_dot(attn_in, qkv_grad[:, : 2 * cols])
-    qk_part = qk_part.astype(bf16)
+    value_sum = owner_scatter(value_part)
+    cut = (owners, parts * final_rows, cols)
+    query_sum, key_sum = owner_scatter_pair(query_part.reshape(cut), key_part.reshape(cut))
 
     unit_one, inverse_one = rms_unit(residual)
     input_part, attn_gain_grad = rms_backward(
@@ -530,10 +558,10 @@
     moe_out = after(moe_out, attn_in_part)
     block_output = middle + mixed_order(moe_out, w_index, parts).astype(f32)
 
-    qk_sum = lax.psum_scatter(qk_part, OWNER, scatter_dimension=0, tiled=True)
-    qk_sum = qk_sum.reshape(parts, final_rows, 2 * cols)
-    qk_sum = lax.all_to_all(qk_sum, SHARD, split_axis=0, concat_axis=0, tiled=True)
-    qkv_sum = place(qk_sum, value_sum)
+    qkv_sum = jnp.concatenate([query_sum, key_sum, value_sum], axis=1)
+    qkv_sum = qkv_sum.reshape(parts, final_rows, 3 * cols)
+    qkv_sum = lax.all_to_all(qkv_sum, SHARD, split_axis=0, concat_axis=0, tiled=True)
+    qkv_sum = place(qkv_sum)
     moves = []
     for e in range(owners):
         for w in range(parts):

time: 813 us -> 850 us (1.046)
  waiting for transfers between devices: 377 us -> 411 us
    ppermute x51 -> x57, waiting for transfers between devices: 365 us -> 390 us  [swap(): lax.ppermute(values, axis_name, [(i, i ^ mask) for i in range(count)])]
    all_to_all x1, waiting for transfers between devices: 2.96 us -> 17 us  [local(): lax.all_to_all(table, OWNER, split_axis=0, concat_axis=0, tiled=True)]
    ppermute x51 -> x57, starting transfers between devices: 39.9 us -> 50.5 us  [swap(): lax.ppermute(values, axis_name, [(i, i ^ mask) for i in range(count)])]
    dot_general x16 -> x17, matrix products: 59 us -> 57.4 us  [t_dot(): lax.dot_general(a, b, (((0,), (0,)), ((), ())), preferred_element_type=jn...]
    unnamed x264 -> x270, local copies, waits for them, and re-layouts: 35 us -> 35.3 us
  transfers between devices with their start and end apart: 62 -> 66, of which waited for: 24 -> 24; matrix products, arithmetic and copies ran while one was open for 29% -> 27% of each run, Pallas kernels for 0% -> 0%
where the time goes in v9:
time: 850 us; the launch traced here: 840 us
  waiting for transfers between devices  411 us (48%)
  matrix products  93.5 us (11%)
  starting transfers between devices  84 us (10%)
  other arithmetic  81.3 us (10%)
  local copies, waits for them, and re-layouts  80.9 us (10%)
  Pallas kernels  67.4 us (8%)
  between operations  16.3 us (2%)
    ppermute x57, waiting for transfers between devices, swap(): lax.ppermute(values, axis_name, [(i, i ^ mask) for i in range(count)])  390 us
    dot_general x17, matrix products, t_dot(): lax.dot_general(a, b, (((0,), (0,)), ((), ())), preferred_element_type=jn...  57.4 us
    ppermute x57, starting transfers between devices, swap(): lax.ppermute(values, axis_name, [(i, i ^ mask) for i in range(count)])  50.5 us
    pallas_call x1, Pallas kernels, expert_hidden(): pl.pallas_call(functools.partial(expert_hidden_kernel, parts), grid=(rows...  36.5 us
    unnamed x270, local copies, waits for them, and re-layouts  35.3 us
    pallas_call x1, Pallas kernels, back_rows(): pl.pallas_call(functools.partial(back_rows_kernel, parts), grid=(rows //...  28.6 us
    dot_general x11, matrix products, dot(): return jnp.dot(a, b, preferred_element_type=jnp.float32)  22 us
    add x6, other arithmetic, scatter_stage(): return {m: blocks[m] + arrived[m].astype(jnp.float32) for m in arrived}  20 us
  transfers between devices with their start and end apart: 66, of which 24 were waited for; matrix products, arithmetic and copies ran while one was open for 27% of the time, Pallas kernels for 0%

profile of v9, /device:TPU:13, one launch (start us, length us, event | category | flops | bytes accessed | tf_op | source)
XLA Modules:
  0.0 840.0 jit_solution(17047503347789522800)
XLA Ops:
  11.3 5.8 all-gather.1
  41.8 6.0 collective-permute-done.5
  48.1 17.2 %collective-permute-done.6 = bf16[256,1536]{1,0:T(8,128)(2,1)} collective-permute-done((bf16[256,1536]{1,0:T(8,128)(2,1)}, bf16[256,1536]{1,0:T(8,128)(2,1)}, u32[]{:S(2)}, u32[]{:S(2)}) %collective-permute-start.6) | collective-permute-done | bytes 786464 | tf_op jit(solution)/shard_map/ppermute | solution.py:78
  75.8 29.4 %collective-permute-done.8 = bf16[256,1536]{1,0:T(8,128)(2,1)S(1)} collective-permute-done((bf16[256,1536]{1,0:T(8,128)(2,1)}, bf16[256,1536]{1,0:T(8,128)(2,1)S(1)}, u32[]{:S(2)}, u32[]{:S(2)}) %collective-permute-start.8) | collective-permute-done | bytes 786464 | tf_op jit(solution)/shard_map/ppermute | solution.py:78
  121.7 12.8 %collective-permute-done.14 = bf16[128,2048]{1,0:T(8,128)(2,1)S(1)} collective-permute-done((bf16[128,2048]{1,0:T(8,128)(2,1)S(1)}, bf16[128,2048]{1,0:T(8,128)(2,1)S(1)}, u32[]{:S(2)}, u32[]{:S(2)}) %collective-permute-start.14) | collective-permute-done | bytes 524320 | tf_op jit(solution)/shard_map/ppermute | solution.py:78
  140.3 43.3 %collective-permute-done.16.refs_2_ = bf16[2,512,1024]{2,1,0:T(8,128)(2,1)} collective-permute-done((bf16[2,512,1024]{2,1,0:T(8,128)(2,1)}, bf16[2,512,1024]{2,1,0:T(8,128)(2,1)}, u32[]{:S(2)}, u32[]{:S(2)}) %collective-permute-start.16) | collective-permute-done | bytes 2097184 | tf_op jit(solution)/shard_map/ppermute | solution.py:78
  205.8 22.6 %collective-permute-done.22.refs_10_ = bf16[2,1024,512]{2,1,0:T(8,128)(2,1)} collective-permute-done((bf16[2,1024,512]{2,1,0:T(8,128)(2,1)}, bf16[2,1024,512]{2,1,0:T(8,128)(2,1)}, u32[]{:S(2)}, u32[]{:S(2)}) %collective-permute-start.22) | collective-permute-done | bytes 2097184 | tf_op jit(solution)/shard_map/ppermute | solution.py:78
  231.8 41.6 %collective-permute-done.19.refs_6_ = bf16[2,512,1024]{2,1,0:T(8,128)(2,1)} collective-permute-done((bf16[2,512,1024]{2,1,0:T(8,128)(2,1)}, bf16[2,512,1024]{2,1,0:T(8,128)(2,1)}, u32[]{:S(2)}, u32[]{:S(2)}) %collective-permute-start.19) | collective-permute-done | bytes 2097184 | tf_op jit(solution)/shard_map/ppermute | solution.py:78
  295.5 36.5 %shard_map.263 = (bf16[1024,2048]{1,0:T(8,128)(2,1)}, bf16[1024,2048]{1,0:T(8,128)(2,1)}, bf16[1024,2048]{1,0:T(8,128)(2,1)}, f32[2,1024,128]{2,1,0:T(8,128)}) custom-call(bf16[1024,2048]{1,0:T(8,128)(2,1)} %all-gather.5.cloned.1.call-done.x_ref, bf16[1024,2048]{1,0:T(8,128)(2,1)} %all-gather.7.cloned.1.call-done.cot_ref, f32[2,1024,1]{2,1,0:T(8,128)} %copy.110.weight_ref, ...), custom_call_target="tpu_custom_call" | custom-call | tf_op jit(solution)/shard_map/pallas_call | solution.py:256
  332.0 28.6 %shard_map.264 = bf16[1024,2048]{1,0:T(8,128)(2,1)} custom-call(bf16[1024,2048]{1,0:T(8,128)(2,1)} %get-tuple-element.90.gate_grad_ref, bf16[1024,2048]{1,0:T(8,128)(2,1)} %get-tuple-element.91.up_grad_ref, bf16[2,512,1024]{2,1,0:T(8,128)(2,1)} %refs_0_.1, bf16[2,512,1024]{2,1,0:T(8,128)(2,1)} %collective-permute-done.15.refs_1_, ...), custom_call_target="tpu_custom_call" | custom-call | tf_op jit(solution)/shard_map/pallas_call | solution.py:300
  360.7 6.4 fusion.58
  396.5 12.3 %fusion.12 = bf16[1024,2048]{1,0:T(8,128)(2,1)S(1)} fusion(bf16[1024,2048]{1,0:T(8,128)(2,1)} %get-tuple-element.92, bf16[2048,512]{1,0:T(8,128)(2,1)} %bitcast.44, bf16[2048,512]{1,0:T(8,128)(2,1)} %bitcast.43, bf16[2048,512]{1,0:T(8,128)(2,1)} %bitcast.42, bf16[2048,512]{1,0:T(8,128)(2,1)S(1)} %bitcast.320), kind=kOutput, calls=%fused_computation.25 | convolution fusion | flops 8625586176 | bytes 16777216 | tf_op jit(solution)/shard_map/dot_general | solution.py:65
  415.9 6.4 all-to-all-start.1
  430.5 38.5 %collective-permute-done.24 = bf16[2,2,128,2048]{3,2,0,1:T(8,128)(2,1)} collective-permute-done((bf16[2,2,128,2048]{3,2,0,1:T(8,128)(2,1)}, bf16[2,2,128,2048]{3,2,0,1:T(8,128)(2,1)}, u32[]{:S(2)}, u32[]{:S(2)}) %collective-permute-start.24) | collective-permute-done | bytes 2097184 | tf_op jit(solution)/shard_map/ppermute | solution.py:78
  490.3 15.8 %collective-permute-done.25 = bf16[2,128,2048]{2,1,0:T(8,128)(2,1)S(1)} collective-permute-done((bf16[2,128,2048]{2,1,0:T(8,128)(2,1)S(1)}, bf16[2,128,2048]{2,1,0:T(8,128)(2,1)S(1)}, u32[]{:S(2)}, u32[]{:S(2)}) %collective-permute-start.25) | collective-permute-done | bytes 1048608 | tf_op jit(solution)/shard_map/ppermute | solution.py:78
  512.4 18.1 %collective-permute-done.26 = bf16[128,2048]{1,0:T(8,128)(2,1)S(1)} collective-permute-done((bf16[128,2048]{1,0:T(8,128)(2,1)S(1)}, bf16[128,2048]{1,0:T(8,128)(2,1)S(1)}, u32[]{:S(2)}, u32[]{:S(2)}) %collective-permute-start.26) | collective-permute-done | bytes 524320 | tf_op jit(solution)/shard_map/ppermute | solution.py:78
  541.1 6.4 collective-permute-done.28
  606.3 18.9 %collective-permute-done.42 = bf16[2,2,256,512]{3,2,0,1:T(8,128)(2,1)S(1)} collective-permute-done((bf16[2,2,256,512]{3,2,0,1:T(8,128)(2,1)S(1)}, bf16[2,2,256,512]{3,2,0,1:T(8,128)(2,1)S(1)}, u32[]{:S(2)}, u32[]{:S(2)}) %collective-permute-start.42) | collective-permute-done | bytes 1048608 | tf_op jit(solution)/shard_map/ppermute | solution.py:78
  631.0 16.7 %collective-permute-done.36 = bf16[2,2,256,512]{3,2,0,1:T(8,128)(2,1)S(1)} collective-permute-done((bf16[2,2,256,512]{3,2,0,1:T(8,128)(2,1)S(1)}, bf16[2,2,256,512]{3,2,0,1:T(8,128)(2,1)S(1)}, u32[]{:S(2)}, u32[]{:S(2)}) %collective-permute-start.36) | collective-permute-done | bytes 1048608 | tf_op jit(solution)/shard_map/ppermute | solution.py:78
  651.4 76.6 %collective-permute-done.35 = bf16[128,2048]{1,0:T(8,128)(2,1)S(1)} collective-permute-done((bf16[128,2048]{1,0:T(8,128)(2,1)S(1)}, bf16[128,2048]{1,0:T(8,128)(2,1)S(1)}, u32[]{:S(2)}, u32[]{:S(2)}) %collective-permute-start.35) | collective-permute-done | bytes 524320 | tf_op jit(solution)/shard_map/ppermute | solution.py:78
  739.1 17.0 %all-to-all-done.2 = f32[8,20,256]{2,1,0:T(8,128)S(1)} async-done(((f32[8,20,256]{2,1,0:T(8,128)}), f32[8,20,256]{2,1,0:T(8,128)S(1)}, u32[]{:S(2)}, u32[]{:S(2)}) %all-to-all-start.2) | async-done | bytes 163872 | tf_op jit(solution)/shard_map/all_to_all | solution.py:578
  775.9 13.2 %collective-permute-done.38 = bf16[2,256,512]{2,1,0:T(8,128)(2,1)S(1)} collective-permute-done((bf16[2,256,512]{2,1,0:T(8,128)(2,1)}, bf16[2,256,512]{2,1,0:T(8,128)(2,1)S(1)}, u32[]{:S(2)}, u32[]{:S(2)}) %collective-permute-start.38) | collective-permute-done | bytes 524320 | tf_op jit(solution)/shard_map/ppermute | solution.py:78
  796.2 8.0 collective-permute-done.40
  805.2 9.7 %all-to-all-start.4 = ((bf16[4,64,1536]{2,1,0:T(8,128)(2,1)}), bf16[4,64,1536]{2,1,0:T(8,128)(2,1)S(1)}, u32[]{:S(2)}, u32[]{:S(2)}) async-start(bf16[4,64,1536]{2,1,0:T(8,128)(2,1)} %bitcast.319), calls=%async_computation.5 | async-start | bytes 1572864 | tf_op jit(solution)/shard_map/all_to_all | solution.py:563
  (585 shorter events, 316.0 us)
Async XLA Ops:
  7.2 288.3 %all-gather.7.cloned.1.call-start = ((), (), s32[]{:S(2)}) async-start(), calls=%async_computation.7 | async-start | bytes 4718592 | tf_op jit(solution)/shard_map/all_gather | solution.py:378
  20.9 274.6 %all-gather.5.cloned.1.call-start = ((), (), s32[]{:S(2)}) async-start(), calls=%async_computation.6 | async-start | bytes 4718592 | tf_op jit(solution)/shard_map/all_gather | solution.py:448
  47.8 57.9 %collective-permute-start.7 = (bf16[256,1536]{1,0:T(8,128)(2,1)}, bf16[256,1536]{1,0:T(8,128)(2,1)S(1)}, u32[]{:S(2)}, u32[]{:S(2)}) collective-permute-start(bf16[256,1536]{1,0:T(8,128)(2,1)} %collective-permute-done.5), channel_id=1, source_target_pairs={{0,4},{4,0},{8,12},{12,8},{16,20},{20,16},{24,28},{28,24},{1,5},{5... | collective-permute-start | bytes 2359304 | tf_op jit(solution)/shard_map/ppermute | solution.py:78
  137.1 91.3 %collective-permute-start.22 = (bf16[2,1024,512]{2,1,0:T(8,128)(2,1)}, bf16[2,1024,512]{2,1,0:T(8,128)(2,1)}, u32[]{:S(2)}, u32[]{:S(2)}) collective-permute-start(bf16[2,1024,512]{2,1,0:T(8,128)(2,1)} %refs_8_), channel_id=1, source_target_pairs={{0,2},{1,3},{2,0},{3,1},{4,6},{5,7},{6,4},{7,5},{8,10},{9,11},{10,... | collective-permute-start | bytes 6291464 | tf_op jit(solution)/shard_map/ppermute | solution.py:78
  138.6 156.8 %collective-permute-start.21 = (bf16[2,1024,512]{2,1,0:T(8,128)(2,1)}, bf16[2,1024,512]{2,1,0:T(8,128)(2,1)}, u32[]{:S(2)}, u32[]{:S(2)}) collective-permute-start(bf16[2,1024,512]{2,1,0:T(8,128)(2,1)} %refs_8_), channel_id=1, source_target_pairs={{0,1},{1,0},{2,3},{3,2},{4,5},{5,4},{6,7},{7,6},{8,9},{9,8},{10,11... | collective-permute-start | bytes 6291464 | tf_op jit(solution)/shard_map/ppermute | solution.py:78
  140.2 155.3 %collective-permute-start.15 = (bf16[2,512,1024]{2,1,0:T(8,128)(2,1)}, bf16[2,512,1024]{2,1,0:T(8,128)(2,1)}, u32[]{:S(2)}, u32[]{:S(2)}) collective-permute-start(bf16[2,512,1024]{2,1,0:T(8,128)(2,1)} %refs_0_.1), channel_id=1, source_target_pairs={{0,1},{1,0},{2,3},{3,2},{4,5},{5,4},{6,7},{7,6},{8,9},{9,8},{10,11... | collective-permute-start | bytes 6291464 | tf_op jit(solution)/shard_map/ppermute | solution.py:78
  140.2 133.2 %collective-permute-start.19 = (bf16[2,512,1024]{2,1,0:T(8,128)(2,1)}, bf16[2,512,1024]{2,1,0:T(8,128)(2,1)}, u32[]{:S(2)}, u32[]{:S(2)}) collective-permute-start(bf16[2,512,1024]{2,1,0:T(8,128)(2,1)} %refs_4_.1), channel_id=1, source_target_pairs={{0,2},{1,3},{2,0},{3,1},{4,6},{5,7},{6,4},{7,5},{8,10},{9,11},{10,... | collective-permute-start | bytes 6291464 | tf_op jit(solution)/shard_map/ppermute | solution.py:78
  183.5 91.7 %collective-permute-start.17 = (bf16[2,512,1024]{2,1,0:T(8,128)(2,1)}, bf16[2,512,1024]{2,1,0:T(8,128)(2,1)}, u32[]{:S(2)}, u32[]{:S(2)}) collective-permute-start(bf16[2,512,1024]{2,1,0:T(8,128)(2,1)} %collective-permute-done.16.refs_2_), channel_id=1, source_target_pairs={{0,1},{1,0},{2,3},{3,2},{4,5},{5,4},{6,7},{7,6},{8,9},{9,8},{10,11... | collective-permute-start | bytes 6291464 | tf_op jit(solution)/shard_map/ppermute | solution.py:78
  188.8 86.5 %all-to-all-start = ((f32[8,2,128]{2,1,0:T(2,128)}), f32[8,2,128]{2,1,0:T(2,128)S(1)}, u32[]{:S(2)}, u32[]{:S(2)}) async-start(f32[8,2,128]{2,1,0:T(2,128)} %bitcast.37), calls=%async_computation | async-start | bytes 16384 | tf_op jit(solution)/shard_map/all_to_all | solution.py:449
  194.4 337.0 %reduce-scatter.2.cloned.1.call-start = ((), (), s32[]{:S(2)}) async-start(), calls=%async_computation.8 | async-start | bytes 4718592 | tf_op jit(solution)/shard_map/reduce_scatter | solution.py:466
  228.5 67.0 %collective-permute-start.18 = (bf16[2,512,1024]{2,1,0:T(8,128)(2,1)}, bf16[2,512,1024]{2,1,0:T(8,128)(2,1)}, u32[]{:S(2)}, u32[]{:S(2)}) collective-permute-start(bf16[2,512,1024]{2,1,0:T(8,128)(2,1)} %refs_4_.1), channel_id=1, source_target_pairs={{0,1},{1,0},{2,3},{3,2},{4,5},{5,4},{6,7},{7,6},{8,9},{9,8},{10,11... | collective-permute-start | bytes 6291464 | tf_op jit(solution)/shard_map/ppermute | solution.py:78
  412.2 56.8 %collective-permute-start.24 = (bf16[2,2,128,2048]{3,2,0,1:T(8,128)(2,1)}, bf16[2,2,128,2048]{3,2,0,1:T(8,128)(2,1)}, u32[]{:S(2)}, u32[]{:S(2)}) collective-permute-start(bf16[2,2,128,2048]{3,2,0,1:T(8,128)(2,1)} %bitcast.299), channel_id=1, source_target_pairs={{0,4},{4,0},{8,12},{12,8},{16,20},{20,16},{24,28},{28,24},{1,5},{5... | collective-permute-start | bytes 6291464 | tf_op jit(solution)/shard_map/ppermute | solution.py:78
  412.2 60.1 %collective-permute-start.50 = (bf16[512,2048]{1,0:T(8,128)(2,1)}, bf16[512,2048]{1,0:T(8,128)(2,1)}, u32[]{:S(2)}, u32[]{:S(2)}) collective-permute-start(bf16[512,2048]{1,0:T(8,128)(2,1)} %fusion.58), channel_id=1, source_target_pairs={{0,1},{1,0},{2,3},{3,2},{4,5},{5,4},{6,7},{7,6},{8,9},{9,8},{10,11... | collective-permute-start | bytes 6291464 | tf_op jit(solution)/shard_map/ppermute | solution.py:78
  413.2 72.8 %collective-permute-start.52 = (bf16[512,2048]{1,0:T(8,128)(2,1)}, bf16[512,2048]{1,0:T(8,128)(2,1)}, u32[]{:S(2)}, u32[]{:S(2)}) collective-permute-start(bf16[512,2048]{1,0:T(8,128)(2,1)} %fusion.64), channel_id=1, source_target_pairs={{0,1},{1,0},{2,3},{3,2},{4,5},{5,4},{6,7},{7,6},{8,9},{9,8},{10,11... | collective-permute-start | bytes 6291464 | tf_op jit(solution)/shard_map/ppermute | solution.py:78
  413.3 94.9 %collective-permute-start.53 = (bf16[512,2048]{1,0:T(8,128)(2,1)}, bf16[512,2048]{1,0:T(8,128)(2,1)}, u32[]{:S(2)}, u32[]{:S(2)}) collective-permute-start(bf16[512,2048]{1,0:T(8,128)(2,1)} %fusion.56), channel_id=1, source_target_pairs={{0,1},{1,0},{2,3},{3,2},{4,5},{5,4},{6,7},{7,6},{8,9},{9,8},{10,11... | collective-permute-start | bytes 6291464 | tf_op jit(solution)/shard_map/ppermute | solution.py:78
  415.9 115.5 %all-to-all-start.1 = ((f32[8,2,128]{2,1,0:T(2,128)}), f32[8,2,128]{2,1,0:T(2,128)S(1)}, u32[]{:S(2)}, u32[]{:S(2)}) async-start(f32[8,2,128]{2,1,0:T(2,128)} %bitcast.53), calls=%async_computation.2 | async-start | bytes 16384 | tf_op jit(solution)/shard_map/all_to_all | solution.py:468
  472.4 63.0 %collective-permute-start.49 = (bf16[512,2048]{1,0:T(8,128)(2,1)}, bf16[512,2048]{1,0:T(8,128)(2,1)}, u32[]{:S(2)}, u32[]{:S(2)}) collective-permute-start(bf16[512,2048]{1,0:T(8,128)(2,1)} %fusion.66), channel_id=1, source_target_pairs={{0,1},{1,0},{2,3},{3,2},{4,5},{5,4},{6,7},{7,6},{8,9},{9,8},{10,11... | collective-permute-start | bytes 6291464 | tf_op jit(solution)/shard_map/ppermute | solution.py:78
  476.3 59.1 %collective-permute-start.51 = (bf16[512,2048]{1,0:T(8,128)(2,1)}, bf16[512,2048]{1,0:T(8,128)(2,1)}, u32[]{:S(2)}, u32[]{:S(2)}) collective-permute-start(bf16[512,2048]{1,0:T(8,128)(2,1)} %add_convert_fusion), channel_id=1, source_target_pairs={{0,2},{1,3},{2,0},{3,1},{4,6},{5,7},{6,4},{7,5},{8,10},{9,11},{10,... | collective-permute-start | bytes 6291464 | tf_op jit(solution)/shard_map/ppermute | solution.py:78
  597.3 50.5 %collective-permute-start.36 = (bf16[2,2,256,512]{3,2,0,1:T(8,128)(2,1)S(1)}, bf16[2,2,256,512]{3,2,0,1:T(8,128)(2,1)S(1)}, u32[]{:S(2)}, u32[]{:S(2)}) collective-permute-start(bf16[2,2,256,512]{3,2,0,1:T(8,128)(2,1)S(1)} %bitcast.327), channel_id=1, source_target_pairs={{0,4},{4,0},{8,12},{12,8},{16,20},{20,16},{24,28},{28,24},{1,5},{5... | collective-permute-start | bytes 3145736 | tf_op jit(solution)/shard_map/ppermute | solution.py:78
  625.2 193.0 %collective-permute-start.54 = (bf16[512,2048]{1,0:T(8,128)(2,1)}, bf16[512,2048]{1,0:T(8,128)(2,1)}, u32[]{:S(2)}, u32[]{:S(2)}) collective-permute-start(bf16[512,2048]{1,0:T(8,128)(2,1)} %convert_add_fusion.5), channel_id=1, source_target_pairs={{0,2},{1,3},{2,0},{3,1},{4,6},{5,7},{6,4},{7,5},{8,10},{9,11},{10,... | collective-permute-start | bytes 6291464 | tf_op jit(solution)/shard_map/ppermute | solution.py:78
  626.6 197.8 %collective-permute-start.57 = (bf16[2048,512]{1,0:T(8,128)(2,1)}, bf16[2048,512]{1,0:T(8,128)(2,1)}, u32[]{:S(2)}, u32[]{:S(2)}) collective-permute-start(bf16[2048,512]{1,0:T(8,128)(2,1)} %convert_add_fusion.2), channel_id=1, source_target_pairs={{0,2},{1,3},{2,0},{3,1},{4,6},{5,7},{6,4},{7,5},{8,10},{9,11},{10,... | collective-permute-start | bytes 6291464 | tf_op jit(solution)/shard_map/ppermute | solution.py:78
  630.5 97.5 %collective-permute-start.35 = (bf16[128,2048]{1,0:T(8,128)(2,1)S(1)}, bf16[128,2048]{1,0:T(8,128)(2,1)S(1)}, u32[]{:S(2)}, u32[]{:S(2)}) collective-permute-start(bf16[128,2048]{1,0:T(8,128)(2,1)S(1)} %fusion.46), channel_id=1, source_target_pairs={{0,2},{1,3},{2,0},{3,1},{4,6},{5,7},{6,4},{7,5},{8,10},{9,11},{10,... | collective-permute-start | bytes 1572872 | tf_op jit(solution)/shard_map/ppermute | solution.py:78
  647.8 120.2 %collective-permute-start.46 = (bf16[2,64,2048]{2,1,0:T(8,128)(2,1)}, bf16[2,64,2048]{2,1,0:T(8,128)(2,1)}, u32[]{:S(2)}, u32[]{:S(2)}) collective-permute-start(bf16[2,64,2048]{2,1,0:T(8,128)(2,1)} %dynamic-slice_bitcast_fusion.2), channel_id=1, source_target_pairs={{0,8},{4,12},{8,0},{12,4},{16,24},{20,28},{24,16},{28,20},{1,9},{5... | collective-permute-start | bytes 1572872 | tf_op jit(solution)/shard_map/ppermute | solution.py:78
  651.1 120.0 %collective-permute-start.43 = (bf16[2,256,512]{2,1,0:T(8,128)(2,1)}, bf16[2,256,512]{2,1,0:T(8,128)(2,1)}, u32[]{:S(2)}, u32[]{:S(2)}) collective-permute-start(bf16[2,256,512]{2,1,0:T(8,128)(2,1)} %dynamic-slice_bitcast_fusion.3), channel_id=1, source_target_pairs={{0,8},{4,12},{8,0},{12,4},{16,24},{20,28},{24,16},{28,20},{1,9},{5... | collective-permute-start | bytes 1572872 | tf_op jit(solution)/shard_map/ppermute | solution.py:78
  (167 other events, 2604.5 us)
Sparse Core Ops, SparseCore 0:
  21.0 92.4 all-gather.6
  137.1 70.6 all-gather.4
  360.8 95.6 reduce-scatter.1

commit v10 on v9

--- a/solution.py
+++ b/solution.py
@@ -174,17 +174,6 @@
     for bit in left[::-1]:
         values, left = owner_stage(values, left, bit)
     return values
-
-
-def owner_scatter_pair(first, second):
-    first, second = owner_split(first), owner_split(second)
-    left, left_two = owner_bits(), owner_bits()
-    order = left[::-1]
-    for bit, bit_two in zip(order, order[1:] + order[:1]):
-        first, left = owner_stage(first, left, bit)
-        second, left_two = owner_stage(second, left_two, bit_two)
-        first, second = lax.optimization_barrier((first, second))
-    return first, second
 
 
 def place_kernel(values_ref, *out_refs):
@@ -548,7 +537,8 @@
     down_weight_grad = scatter_far(after(down_near, attn_in_part)).reshape(EXP_DEV, ff, cols)
     value_sum = owner_scatter(value_part)
     cut = (owners, parts * final_rows, cols)
-    query_sum, key_sum = owner_scatter_pair(query_part.reshape(cut), key_part.reshape(cut))
+    query_sum = owner_scatter(query_part.reshape(cut))
+    key_sum = owner_scatter(key_part.reshape(cut))
 
     unit_one, inverse_one = rms_unit(residual)
     input_part, attn_gain_grad = rms_backward(

time: 850 us -> 809 us (0.952)
  waiting for transfers between devices: 411 us -> 366 us
    ppermute x57, waiting for transfers between devices: 390 us -> 346 us  [swap(): lax.ppermute(values, axis_name, [(i, i ^ mask) for i in range(count)])]
    all_to_all x1, waiting for transfers between devices: 1.27 us -> 18.5 us  [local(): lax.all_to_all(table, SHARD, split_axis=0, concat_axis=0, tiled=True)]
    all_to_all x1, waiting for transfers between devices: 17 us -> 0.01 us  [local(): lax.all_to_all(table, OWNER, split_axis=0, concat_axis=0, tiled=True)]
    unnamed x270 -> x276, local copies, waits for them, and re-layouts: 35.3 us -> 36.2 us
  transfers between devices with their start and end apart: 66 -> 66, of which waited for: 24 -> 24; matrix products, arithmetic and copies ran while one was open for 27% -> 29% of each run, Pallas kernels for 0% -> 0%
where the time goes in v10:
time: 809 us; the launch traced here: 801 us
  waiting for transfers between devices  366 us (45%)
  matrix products  93.6 us (12%)
  local copies, waits for them, and re-layouts  85.9 us (11%)
  other arithmetic  83.6 us (10%)
  starting transfers between devices  82.7 us (10%)
  Pallas kernels  67.4 us (8%)
  between operations  16.3 us (2%)
    ppermute x57, waiting for transfers between devices, swap(): lax.ppermute(values, axis_name, [(i, i ^ mask) for i in range(count)])  346 us
    dot_general x17, matrix products, t_dot(): lax.dot_general(a, b, (((0,), (0,)), ((), ())), preferred_element_type=jn...  57.4 us
    ppermute x57, starting transfers between devices, swap(): lax.ppermute(values, axis_name, [(i, i ^ mask) for i in range(count)])  46.7 us
    pallas_call x1, Pallas kernels, expert_hidden(): pl.pallas_call(functools.partial(expert_hidden_kernel, parts), grid=(rows...  36.5 us
    unnamed x276, local copies, waits for them, and re-layouts  36.2 us
    pallas_call x1, Pallas kernels, back_rows(): pl.pallas_call(functools.partial(back_rows_kernel, parts), grid=(rows //...  28.6 us
    dot_general x11, matrix products, dot(): return jnp.dot(a, b, preferred_element_type=jnp.float32)  22 us
    add x6, other arithmetic, scatter_stage(): return {m: blocks[m] + arrived[m].astype(jnp.float32) for m in arrived}  20.1 us
  transfers between devices with their start and end apart: 66, of which 24 were waited for; matrix products, arithmetic and copies ran while one was open for 29% of the time, Pallas kernels for 0%

profile of v10, /device:TPU:13, one launch (start us, length us, event | category | flops | bytes accessed | tf_op | source)
XLA Modules:
  0.0 800.9 jit_solution(4914608422067901821)
XLA Ops:
  11.3 5.8 all-gather.1
  41.8 6.0 collective-permute-done.5
  48.1 17.2 %collective-permute-done.6 = bf16[256,1536]{1,0:T(8,128)(2,1)} collective-permute-done((bf16[256,1536]{1,0:T(8,128)(2,1)}, bf16[256,1536]{1,0:T(8,128)(2,1)}, u32[]{:S(2)}, u32[]{:S(2)}) %collective-permute-start.6) | collective-permute-done | bytes 786464 | tf_op jit(solution)/shard_map/ppermute | solution.py:78
  75.8 29.4 %collective-permute-done.8 = bf16[256,1536]{1,0:T(8,128)(2,1)S(1)} collective-permute-done((bf16[256,1536]{1,0:T(8,128)(2,1)}, bf16[256,1536]{1,0:T(8,128)(2,1)S(1)}, u32[]{:S(2)}, u32[]{:S(2)}) %collective-permute-start.8) | collective-permute-done | bytes 786464 | tf_op jit(solution)/shard_map/ppermute | solution.py:78
  121.7 12.8 %collective-permute-done.14 = bf16[128,2048]{1,0:T(8,128)(2,1)S(1)} collective-permute-done((bf16[128,2048]{1,0:T(8,128)(2,1)S(1)}, bf16[128,2048]{1,0:T(8,128)(2,1)S(1)}, u32[]{:S(2)}, u32[]{:S(2)}) %collective-permute-start.14) | collective-permute-done | bytes 524320 | tf_op jit(solution)/shard_map/ppermute | solution.py:78
  140.3 43.2 %collective-permute-done.16.refs_2_ = bf16[2,512,1024]{2,1,0:T(8,128)(2,1)} collective-permute-done((bf16[2,512,1024]{2,1,0:T(8,128)(2,1)}, bf16[2,512,1024]{2,1,0:T(8,128)(2,1)}, u32[]{:S(2)}, u32[]{:S(2)}) %collective-permute-start.16) | collective-permute-done | bytes 2097184 | tf_op jit(solution)/shard_map/ppermute | solution.py:78
  205.8 22.7 %collective-permute-done.22.refs_10_ = bf16[2,1024,512]{2,1,0:T(8,128)(2,1)} collective-permute-done((bf16[2,1024,512]{2,1,0:T(8,128)(2,1)}, bf16[2,1024,512]{2,1,0:T(8,128)(2,1)}, u32[]{:S(2)}, u32[]{:S(2)}) %collective-permute-start.22) | collective-permute-done | bytes 2097184 | tf_op jit(solution)/shard_map/ppermute | solution.py:78
  231.7 41.6 %collective-permute-done.19.refs_6_ = bf16[2,512,1024]{2,1,0:T(8,128)(2,1)} collective-permute-done((bf16[2,512,1024]{2,1,0:T(8,128)(2,1)}, bf16[2,512,1024]{2,1,0:T(8,128)(2,1)}, u32[]{:S(2)}, u32[]{:S(2)}) %collective-permute-start.19) | collective-permute-done | bytes 2097184 | tf_op jit(solution)/shard_map/ppermute | solution.py:78
  295.5 36.5 %shard_map.263 = (bf16[1024,2048]{1,0:T(8,128)(2,1)}, bf16[1024,2048]{1,0:T(8,128)(2,1)}, bf16[1024,2048]{1,0:T(8,128)(2,1)}, f32[2,1024,128]{2,1,0:T(8,128)}) custom-call(bf16[1024,2048]{1,0:T(8,128)(2,1)} %all-gather.5.cloned.1.call-done.x_ref, bf16[1024,2048]{1,0:T(8,128)(2,1)} %all-gather.7.cloned.1.call-done.cot_ref, f32[2,1024,1]{2,1,0:T(8,128)} %copy.114.weight_ref, ...), custom_call_target="tpu_custom_call" | custom-call | tf_op jit(solution)/shard_map/pallas_call | solution.py:245
  332.0 28.6 %shard_map.264 = bf16[1024,2048]{1,0:T(8,128)(2,1)} custom-call(bf16[1024,2048]{1,0:T(8,128)(2,1)} %get-tuple-element.84.gate_grad_ref, bf16[1024,2048]{1,0:T(8,128)(2,1)} %get-tuple-element.85.up_grad_ref, bf16[2,512,1024]{2,1,0:T(8,128)(2,1)} %refs_0_.1, bf16[2,512,1024]{2,1,0:T(8,128)(2,1)} %collective-permute-done.15.refs_1_, ...), custom_call_target="tpu_custom_call" | custom-call | tf_op jit(solution)/shard_map/pallas_call | solution.py:289
  360.7 6.4 fusion.58
  396.5 12.3 %fusion.12 = bf16[1024,2048]{1,0:T(8,128)(2,1)S(1)} fusion(bf16[1024,2048]{1,0:T(8,128)(2,1)} %get-tuple-element.86, bf16[2048,512]{1,0:T(8,128)(2,1)} %bitcast.44, bf16[2048,512]{1,0:T(8,128)(2,1)} %bitcast.43, bf16[2048,512]{1,0:T(8,128)(2,1)} %bitcast.42, bf16[2048,512]{1,0:T(8,128)(2,1)S(1)} %bitcast.321), kind=kOutput, calls=%fused_computation.25 | convolution fusion | flops 8625586176 | bytes 16777216 | tf_op jit(solution)/shard_map/dot_general | solution.py:65
  415.9 6.4 all-to-all-start.1
  430.5 38.5 %collective-permute-done.24 = bf16[2,2,128,2048]{3,2,0,1:T(8,128)(2,1)} collective-permute-done((bf16[2,2,128,2048]{3,2,0,1:T(8,128)(2,1)}, bf16[2,2,128,2048]{3,2,0,1:T(8,128)(2,1)}, u32[]{:S(2)}, u32[]{:S(2)}) %collective-permute-start.24) | collective-permute-done | bytes 2097184 | tf_op jit(solution)/shard_map/ppermute | solution.py:78
  490.3 15.9 %collective-permute-done.25 = bf16[2,128,2048]{2,1,0:T(8,128)(2,1)S(1)} collective-permute-done((bf16[2,128,2048]{2,1,0:T(8,128)(2,1)S(1)}, bf16[2,128,2048]{2,1,0:T(8,128)(2,1)S(1)}, u32[]{:S(2)}, u32[]{:S(2)}) %collective-permute-start.25) | collective-permute-done | bytes 1048608 | tf_op jit(solution)/shard_map/ppermute | solution.py:78
  512.4 18.0 %collective-permute-done.26 = bf16[128,2048]{1,0:T(8,128)(2,1)S(1)} collective-permute-done((bf16[128,2048]{1,0:T(8,128)(2,1)S(1)}, bf16[128,2048]{1,0:T(8,128)(2,1)S(1)}, u32[]{:S(2)}, u32[]{:S(2)}) %collective-permute-start.26) | collective-permute-done | bytes 524320 | tf_op jit(solution)/shard_map/ppermute | solution.py:78
  541.1 6.3 collective-permute-done.28
  612.4 12.8 %collective-permute-done.42 = bf16[2,2,256,512]{3,2,0,1:T(8,128)(2,1)S(1)} collective-permute-done((bf16[2,2,256,512]{3,2,0,1:T(8,128)(2,1)S(1)}, bf16[2,2,256,512]{3,2,0,1:T(8,128)(2,1)S(1)}, u32[]{:S(2)}, u32[]{:S(2)}) %collective-permute-start.42) | collective-permute-done | bytes 1048608 | tf_op jit(solution)/shard_map/ppermute | solution.py:78
  628.8 40.1 %collective-permute-done.35 = bf16[128,2048]{1,0:T(8,128)(2,1)S(1)} collective-permute-done((bf16[128,2048]{1,0:T(8,128)(2,1)S(1)}, bf16[128,2048]{1,0:T(8,128)(2,1)S(1)}, u32[]{:S(2)}, u32[]{:S(2)}) %collective-permute-start.35) | collective-permute-done | bytes 524320 | tf_op jit(solution)/shard_map/ppermute | solution.py:78
  688.2 6.1 all-to-all-start.3
  696.1 18.5 %all-to-all-done.3 = f32[4,1,1280]{2,1,0:T(1,128)S(1)} async-done(((f32[4,1,1280]{2,1,0:T(1,128)}), f32[4,1,1280]{2,1,0:T(1,128)S(1)}, u32[]{:S(2)}, u32[]{:S(2)}) %all-to-all-start.3) | async-done | bytes 20512 | tf_op jit(solution)/shard_map/all_to_all | solution.py:572
  724.5 14.8 %collective-permute-done.37 = bf16[2,256,512]{2,1,0:T(8,128)(2,1)S(1)} collective-permute-done((bf16[2,256,512]{2,1,0:T(8,128)(2,1)}, bf16[2,256,512]{2,1,0:T(8,128)(2,1)S(1)}, u32[]{:S(2)}, u32[]{:S(2)}) %collective-permute-start.37) | collective-permute-done | bytes 524320 | tf_op jit(solution)/shard_map/ppermute | solution.py:78
  742.0 12.9 %collective-permute-done.44 = bf16[256,512]{1,0:T(8,128)(2,1)S(1)} collective-permute-done((bf16[256,512]{1,0:T(8,128)(2,1)S(1)}, bf16[256,512]{1,0:T(8,128)(2,1)S(1)}, u32[]{:S(2)}, u32[]{:S(2)}) %collective-permute-start.44) | collective-permute-done | bytes 262176 | tf_op jit(solution)/shard_map/ppermute | solution.py:78
  767.2 9.7 %all-to-all-start.4 = ((bf16[4,64,1536]{2,1,0:T(8,128)(2,1)}), bf16[4,64,1536]{2,1,0:T(8,128)(2,1)S(1)}, u32[]{:S(2)}, u32[]{:S(2)}) async-start(bf16[4,64,1536]{2,1,0:T(8,128)(2,1)} %bitcast.320), calls=%async_computation.5 | async-start | bytes 1572864 | tf_op jit(solution)/shard_map/all_to_all | solution.py:553
  (592 shorter events, 322.2 us)
Async XLA Ops:
  7.2 288.3 %all-gather.7.cloned.1.call-start = ((), (), s32[]{:S(2)}) async-start(), calls=%async_computation.7 | async-start | bytes 4718592 | tf_op jit(solution)/shard_map/all_gather | solution.py:367
  20.9 274.6 %all-gather.5.cloned.1.call-start = ((), (), s32[]{:S(2)}) async-start(), calls=%async_computation.6 | async-start | bytes 4718592 | tf_op jit(solution)/shard_map/all_gather | solution.py:437
  47.9 57.9 %collective-permute-start.7 = (bf16[256,1536]{1,0:T(8,128)(2,1)}, bf16[256,1536]{1,0:T(8,128)(2,1)S(1)}, u32[]{:S(2)}, u32[]{:S(2)}) collective-permute-start(bf16[256,1536]{1,0:T(8,128)(2,1)} %collective-permute-done.5), channel_id=1, source_target_pairs={{0,4},{4,0},{8,12},{12,8},{16,20},{20,16},{24,28},{28,24},{1,5},{5... | collective-permute-start | bytes 2359304 | tf_op jit(solution)/shard_map/ppermute | solution.py:78
  137.1 91.3 %collective-permute-start.22 = (bf16[2,1024,512]{2,1,0:T(8,128)(2,1)}, bf16[2,1024,512]{2,1,0:T(8,128)(2,1)}, u32[]{:S(2)}, u32[]{:S(2)}) collective-permute-start(bf16[2,1024,512]{2,1,0:T(8,128)(2,1)} %refs_8_), channel_id=1, source_target_pairs={{0,2},{1,3},{2,0},{3,1},{4,6},{5,7},{6,4},{7,5},{8,10},{9,11},{10,... | collective-permute-start | bytes 6291464 | tf_op jit(solution)/shard_map/ppermute | solution.py:78
  138.6 156.9 %collective-permute-start.21 = (bf16[2,1024,512]{2,1,0:T(8,128)(2,1)}, bf16[2,1024,512]{2,1,0:T(8,128)(2,1)}, u32[]{:S(2)}, u32[]{:S(2)}) collective-permute-start(bf16[2,1024,512]{2,1,0:T(8,128)(2,1)} %refs_8_), channel_id=1, source_target_pairs={{0,1},{1,0},{2,3},{3,2},{4,5},{5,4},{6,7},{7,6},{8,9},{9,8},{10,11... | collective-permute-start | bytes 6291464 | tf_op jit(solution)/shard_map/ppermute | solution.py:78
  140.2 155.3 %collective-permute-start.15 = (bf16[2,512,1024]{2,1,0:T(8,128)(2,1)}, bf16[2,512,1024]{2,1,0:T(8,128)(2,1)}, u32[]{:S(2)}, u32[]{:S(2)}) collective-permute-start(bf16[2,512,1024]{2,1,0:T(8,128)(2,1)} %refs_0_.1), channel_id=1, source_target_pairs={{0,1},{1,0},{2,3},{3,2},{4,5},{5,4},{6,7},{7,6},{8,9},{9,8},{10,11... | collective-permute-start | bytes 6291464 | tf_op jit(solution)/shard_map/ppermute | solution.py:78
  140.2 133.2 %collective-permute-start.19 = (bf16[2,512,1024]{2,1,0:T(8,128)(2,1)}, bf16[2,512,1024]{2,1,0:T(8,128)(2,1)}, u32[]{:S(2)}, u32[]{:S(2)}) collective-permute-start(bf16[2,512,1024]{2,1,0:T(8,128)(2,1)} %refs_4_.1), channel_id=1, source_target_pairs={{0,2},{1,3},{2,0},{3,1},{4,6},{5,7},{6,4},{7,5},{8,10},{9,11},{10,... | collective-permute-start | bytes 6291464 | tf_op jit(solution)/shard_map/ppermute | solution.py:78
  183.5 91.7 %collective-permute-start.17 = (bf16[2,512,1024]{2,1,0:T(8,128)(2,1)}, bf16[2,512,1024]{2,1,0:T(8,128)(2,1)}, u32[]{:S(2)}, u32[]{:S(2)}) collective-permute-start(bf16[2,512,1024]{2,1,0:T(8,128)(2,1)} %collective-permute-done.16.refs_2_), channel_id=1, source_target_pairs={{0,1},{1,0},{2,3},{3,2},{4,5},{5,4},{6,7},{7,6},{8,9},{9,8},{10,11... | collective-permute-start | bytes 6291464 | tf_op jit(solution)/shard_map/ppermute | solution.py:78
  188.7 86.5 %all-to-all-start = ((f32[8,2,128]{2,1,0:T(2,128)}), f32[8,2,128]{2,1,0:T(2,128)S(1)}, u32[]{:S(2)}, u32[]{:S(2)}) async-start(f32[8,2,128]{2,1,0:T(2,128)} %bitcast.37), calls=%async_computation | async-start | bytes 16384 | tf_op jit(solution)/shard_map/all_to_all | solution.py:438
  194.4 337.0 %reduce-scatter.2.cloned.1.call-start = ((), (), s32[]{:S(2)}) async-start(), calls=%async_computation.8 | async-start | bytes 4718592 | tf_op jit(solution)/shard_map/reduce_scatter | solution.py:455
  228.4 67.0 %collective-permute-start.18 = (bf16[2,512,1024]{2,1,0:T(8,128)(2,1)}, bf16[2,512,1024]{2,1,0:T(8,128)(2,1)}, u32[]{:S(2)}, u32[]{:S(2)}) collective-permute-start(bf16[2,512,1024]{2,1,0:T(8,128)(2,1)} %refs_4_.1), channel_id=1, source_target_pairs={{0,1},{1,0},{2,3},{3,2},{4,5},{5,4},{6,7},{7,6},{8,9},{9,8},{10,11... | collective-permute-start | bytes 6291464 | tf_op jit(solution)/shard_map/ppermute | solution.py:78
  412.2 56.7 %collective-permute-start.24 = (bf16[2,2,128,2048]{3,2,0,1:T(8,128)(2,1)}, bf16[2,2,128,2048]{3,2,0,1:T(8,128)(2,1)}, u32[]{:S(2)}, u32[]{:S(2)}) collective-permute-start(bf16[2,2,128,2048]{3,2,0,1:T(8,128)(2,1)} %bitcast.299), channel_id=1, source_target_pairs={{0,4},{4,0},{8,12},{12,8},{16,20},{20,16},{24,28},{28,24},{1,5},{5... | collective-permute-start | bytes 6291464 | tf_op jit(solution)/shard_map/ppermute | solution.py:78
  412.3 60.1 %collective-permute-start.50 = (bf16[512,2048]{1,0:T(8,128)(2,1)}, bf16[512,2048]{1,0:T(8,128)(2,1)}, u32[]{:S(2)}, u32[]{:S(2)}) collective-permute-start(bf16[512,2048]{1,0:T(8,128)(2,1)} %fusion.58), channel_id=1, source_target_pairs={{0,1},{1,0},{2,3},{3,2},{4,5},{5,4},{6,7},{7,6},{8,9},{9,8},{10,11... | collective-permute-start | bytes 6291464 | tf_op jit(solution)/shard_map/ppermute | solution.py:78
  413.2 72.8 %collective-permute-start.52 = (bf16[512,2048]{1,0:T(8,128)(2,1)}, bf16[512,2048]{1,0:T(8,128)(2,1)}, u32[]{:S(2)}, u32[]{:S(2)}) collective-permute-start(bf16[512,2048]{1,0:T(8,128)(2,1)} %fusion.64), channel_id=1, source_target_pairs={{0,1},{1,0},{2,3},{3,2},{4,5},{5,4},{6,7},{7,6},{8,9},{9,8},{10,11... | collective-permute-start | bytes 6291464 | tf_op jit(solution)/shard_map/ppermute | solution.py:78
  413.3 94.9 %collective-permute-start.53 = (bf16[512,2048]{1,0:T(8,128)(2,1)}, bf16[512,2048]{1,0:T(8,128)(2,1)}, u32[]{:S(2)}, u32[]{:S(2)}) collective-permute-start(bf16[512,2048]{1,0:T(8,128)(2,1)} %fusion.56), channel_id=1, source_target_pairs={{0,1},{1,0},{2,3},{3,2},{4,5},{5,4},{6,7},{7,6},{8,9},{9,8},{10,11... | collective-permute-start | bytes 6291464 | tf_op jit(solution)/shard_map/ppermute | solution.py:78
  415.9 115.4 %all-to-all-start.1 = ((f32[8,2,128]{2,1,0:T(2,128)}), f32[8,2,128]{2,1,0:T(2,128)S(1)}, u32[]{:S(2)}, u32[]{:S(2)}) async-start(f32[8,2,128]{2,1,0:T(2,128)} %bitcast.53), calls=%async_computation.2 | async-start | bytes 16384 | tf_op jit(solution)/shard_map/all_to_all | solution.py:457
  427.4 48.9 %collective-permute-start.55 = (bf16[2048,512]{1,0:T(8,128)(2,1)S(1)}, bf16[2048,512]{1,0:T(8,128)(2,1)S(1)}, u32[]{:S(2)}, u32[]{:S(2)}) collective-permute-start(bf16[2048,512]{1,0:T(8,128)(2,1)S(1)} %convolution_convert_fusion.1), channel_id=1, source_target_pairs={{0,1},{1,0},{2,3},{3,2},{4,5},{5,4},{6,7},{7,6},{8,9},{9,8},{10,11... | collective-permute-start | bytes 6291464 | tf_op jit(solution)/shard_map/ppermute | solution.py:78
  472.4 63.0 %collective-permute-start.49 = (bf16[512,2048]{1,0:T(8,128)(2,1)}, bf16[512,2048]{1,0:T(8,128)(2,1)}, u32[]{:S(2)}, u32[]{:S(2)}) collective-permute-start(bf16[512,2048]{1,0:T(8,128)(2,1)} %fusion.66), channel_id=1, source_target_pairs={{0,1},{1,0},{2,3},{3,2},{4,5},{5,4},{6,7},{7,6},{8,9},{9,8},{10,11... | collective-permute-start | bytes 6291464 | tf_op jit(solution)/shard_map/ppermute | solution.py:78
  476.3 59.1 %collective-permute-start.51 = (bf16[512,2048]{1,0:T(8,128)(2,1)}, bf16[512,2048]{1,0:T(8,128)(2,1)}, u32[]{:S(2)}, u32[]{:S(2)}) collective-permute-start(bf16[512,2048]{1,0:T(8,128)(2,1)} %add_convert_fusion), channel_id=1, source_target_pairs={{0,2},{1,3},{2,0},{3,1},{4,6},{5,7},{6,4},{7,5},{8,10},{9,11},{10,... | collective-permute-start | bytes 6291464 | tf_op jit(solution)/shard_map/ppermute | solution.py:78
  597.9 79.1 %collective-permute-start.39 = (bf16[2,2,256,512]{3,2,0,1:T(8,128)(2,1)}, bf16[2,2,256,512]{3,2,0,1:T(8,128)(2,1)}, u32[]{:S(2)}, u32[]{:S(2)}) collective-permute-start(bf16[2,2,256,512]{3,2,0,1:T(8,128)(2,1)} %bitcast.302), channel_id=1, source_target_pairs={{0,4},{4,0},{8,12},{12,8},{16,20},{20,16},{24,28},{28,24},{1,5},{5... | collective-permute-start | bytes 3145736 | tf_op jit(solution)/shard_map/ppermute | solution.py:78
  600.5 83.2 %collective-permute-start.36 = (bf16[2,2,256,512]{3,2,0,1:T(8,128)(2,1)}, bf16[2,2,256,512]{3,2,0,1:T(8,128)(2,1)}, u32[]{:S(2)}, u32[]{:S(2)}) collective-permute-start(bf16[2,2,256,512]{3,2,0,1:T(8,128)(2,1)} %bitcast.303), channel_id=1, source_target_pairs={{0,4},{4,0},{8,12},{12,8},{16,20},{20,16},{24,28},{28,24},{1,5},{5... | collective-permute-start | bytes 3145736 | tf_op jit(solution)/shard_map/ppermute | solution.py:78
  610.3 168.9 %collective-permute-start.54 = (bf16[512,2048]{1,0:T(8,128)(2,1)}, bf16[512,2048]{1,0:T(8,128)(2,1)}, u32[]{:S(2)}, u32[]{:S(2)}) collective-permute-start(bf16[512,2048]{1,0:T(8,128)(2,1)} %convert_add_fusion.5), channel_id=1, source_target_pairs={{0,2},{1,3},{2,0},{3,1},{4,6},{5,7},{6,4},{7,5},{8,10},{9,11},{10,... | collective-permute-start | bytes 6291464 | tf_op jit(solution)/shard_map/ppermute | solution.py:78
  627.6 157.8 %collective-permute-start.57 = (bf16[2048,512]{1,0:T(8,128)(2,1)}, bf16[2048,512]{1,0:T(8,128)(2,1)}, u32[]{:S(2)}, u32[]{:S(2)}) collective-permute-start(bf16[2048,512]{1,0:T(8,128)(2,1)} %convert_add_fusion.2), channel_id=1, source_target_pairs={{0,2},{1,3},{2,0},{3,1},{4,6},{5,7},{6,4},{7,5},{8,10},{9,11},{10,... | collective-permute-start | bytes 6291464 | tf_op jit(solution)/shard_map/ppermute | solution.py:78
  668.9 48.1 %collective-permute-start.46 = (bf16[2,64,2048]{2,1,0:T(8,128)(2,1)}, bf16[2,64,2048]{2,1,0:T(8,128)(2,1)}, u32[]{:S(2)}, u32[]{:S(2)}) collective-permute-start(bf16[2,64,2048]{2,1,0:T(8,128)(2,1)} %dynamic-slice_bitcast_fusion.1), channel_id=1, source_target_pairs={{0,8},{4,12},{8,0},{12,4},{16,24},{20,28},{24,16},{28,20},{1,9},{5... | collective-permute-start | bytes 1572872 | tf_op jit(solution)/shard_map/ppermute | solution.py:78
  (170 other events, 2343.2 us)
Sparse Core Ops, SparseCore 0:
  21.0 92.4 all-gather.6
  137.0 70.7 all-gather.4
  360.8 95.6 reduce-scatter.1

commit v11 on v10

--- a/solution.py
+++ b/solution.py
@@ -165,8 +165,8 @@
     away = lax.dynamic_index_in_dim(values, 1 - index, axis, keepdims=False)
     kept = lax.dynamic_index_in_dim(values, index, axis, keepdims=False)
     arrived = swap(away, bit, OWNER)
-    total = kept.astype(jnp.float32) + arrived.astype(jnp.float32)
-    return total.astype(jnp.bfloat16), [b for b in left if b != bit]
+    total = (kept.astype(jnp.float32) + arrived.astype(jnp.float32)).astype(jnp.bfloat16)
+    return total, [b for b in left if b != bit]
 
 
 def owner_scatter(values):
@@ -225,6 +225,47 @@
     @pl.when(pl.program_id(2) > 0)
     def _():
         route_ref[...] += route
+
+
+def attend_back_kernel(
+    grad_ref, query_ref, key_ref, value_ref, mix_ref, probs_ref, cos_ref, sin_ref, *out_refs
+):
+    query_out, key_out, value_out = out_refs
+    f32, bf16 = jnp.float32, jnp.bfloat16
+    scale = HEAD_DIM ** (-0.5)
+    cosine = cos_ref[...]
+    sine = sin_ref[...]
+    for h in range(query_ref.shape[0]):
+        at = slice(h * HEAD_DIM, (h + 1) * HEAD_DIM)
+        grad = grad_ref[:, at]
+        probs = probs_ref[h]
+        delta = jnp.sum(grad.astype(f32) * mix_ref[h].astype(f32), axis=1, keepdims=True)
+        score = probs * (dot_t(grad, value_ref[h]) - delta)
+        query = jnp.dot(score.astype(bf16), key_ref[h], preferred_element_type=f32) * scale
+        key = jnp.dot(score.T.astype(bf16), query_ref[h], preferred_element_type=f32) * scale
+        value = jnp.dot(probs.T.astype(bf16), grad, preferred_element_type=f32)
+        query = query * cosine + pltpu.roll(query, HEAD_DIM // 2, 1) * sine
+        key = key * cosine + pltpu.roll(key, HEAD_DIM // 2, 1) * sine
+        query_out[:, at] = query
+        key_out[:, at] = key
+        value_out[:, at] = value.astype(bf16)
+
+
+def attend_back(grad, queries, keys, values, mixed, probs, cosine, sine):
+    heads, blocks, rows, _ = queries.shape
+    cols = grad.shape[1]
+    head = pl.BlockSpec((heads, None, rows, HEAD_DIM), lambda b: (0, b, 0, 0))
+    line = pl.BlockSpec((rows, cols), lambda b: (b, 0))
+    table = pl.BlockSpec((rows, HEAD_DIM), lambda b: (b, 0))
+    wide = jax.ShapeDtypeStruct(grad.shape, jnp.float32)
+    return pl.pallas_call(
+        attend_back_kernel,
+        grid=(blocks,),
+        in_specs=[line] + [head] * 4
+        + [pl.BlockSpec((heads, None, rows, rows), lambda b: (0, b, 0, 0)), table, table],
+        out_specs=[line] * 3,
+        out_shape=[wide, wide, jax.ShapeDtypeStruct(grad.shape, jnp.bfloat16)],
+    )(grad, queries, keys, values, mixed, probs, cosine, sine)
 
 
 def row_tile_of(rows):
@@ -502,15 +543,17 @@
     mid_all = jnp.concatenate(mid_pieces, axis=0)
     output_part = t_dot(attn_mix, mid_all).astype(bf16)
     output_sum = owner_scatter(output_part.reshape(owners, final_rows, width))
-    mix_grad = by_head(dot_t(mid_all, output_weight).astype(bf16)).reshape(blocked)
-    delta = jnp.sum(mix_grad.astype(f32) * mixed.astype(f32), axis=-1, keepdims=True)
-    prob_back = pair_dot(mix_grad, values, 3, 3)
-    score_grad = (probs * (prob_back - delta)).astype(bf16)
-    grad_queries = pair_dot(score_grad, keys, 3, 2)
-    grad_keys = pair_dot(score_grad, queries, 2, 2)
-    grad_values = pair_dot(probs_b, mix_grad, 2, 2)
-    grad_queries = by_row(rotate((grad_queries * scale).reshape(whole), cosine, -sine))
-    grad_keys = by_row(rotate((grad_keys * scale).reshape(whole), cosine, -sine))
+    mix_grad = dot_t(mid_all, output_weight).astype(bf16)
+    grad_queries, grad_keys, value_grad_b = attend_back(
+        mix_grad,
+        queries,
+        keys,
+        values,
+        mixed,
+        probs,
+        jnp.concatenate([cosine, cosine], axis=1),
+        jnp.concatenate([sine, -sine], axis=1),
+    )
     query_gain_grad = jnp.sum(grad_queries * query_unit, axis=0)
     key_gain_grad = jnp.sum(grad_keys * key_unit, axis=0)
     grad_queries = grad_queries * query_gain_f
@@ -523,7 +566,6 @@
     up_weight_grad = jnp.stack([up_sum[:, e * ff : (e + 1) * ff] for e in range(EXP_DEV)])
     query_grad_b = (query_inverse * (grad_queries - query_unit * means[0][:, None])).astype(bf16)
     key_grad_b = (key_inverse * (grad_keys - key_unit * means[1][:, None])).astype(bf16)
-    value_grad_b = by_row(grad_values.reshape(whole)).astype(bf16)
     qkv_grad = jnp.concatenate([query_grad_b, key_grad_b, value_grad_b], axis=1)
     query_part = t_dot(attn_in, query_grad_b)
     key_part = t_dot(attn_in, key_grad_b)

time: 809 us -> 799 us (0.988)
  local copies, waits for them, and re-layouts: 85.9 us -> 76.9 us
    unnamed x276 -> x235, local copies, waits for them, and re-layouts: 36.2 us -> 35.3 us
  transfers between devices with their start and end apart: 66 -> 66, of which waited for: 24 -> 24; matrix products, arithmetic and copies ran while one was open for 29% -> 30% of each run, Pallas kernels for 0% -> 0%
where the time goes in v11:
time: 799 us; the launch traced here: 791 us
  waiting for transfers between devices  361 us (45%)
  matrix products  90.6 us (11%)
  other arithmetic  83.7 us (10%)
  starting transfers between devices  82.5 us (10%)
  local copies, waits for them, and re-layouts  76.9 us (10%)
  Pallas kernels  74.5 us (9%)
  between operations  16.1 us (2%)
    ppermute x57, waiting for transfers between devices, swap(): lax.ppermute(values, axis_name, [(i, i ^ mask) for i in range(count)])  341 us
    dot_general x17, matrix products, t_dot(): lax.dot_general(a, b, (((0,), (0,)), ((), ())), preferred_element_type=jn...  58.8 us
    ppermute x57, starting transfers between devices, swap(): lax.ppermute(values, axis_name, [(i, i ^ mask) for i in range(count)])  46.4 us
    pallas_call x1, Pallas kernels, expert_hidden(): pl.pallas_call(functools.partial(expert_hidden_kernel, parts), grid=(rows...  36.5 us
    unnamed x235, local copies, waits for them, and re-layouts  35.3 us
    pallas_call x1, Pallas kernels, back_rows(): pl.pallas_call(functools.partial(back_rows_kernel, parts), grid=(rows //...  28.6 us
    dot_general x11, matrix products, dot(): return jnp.dot(a, b, preferred_element_type=jnp.float32)  22 us
    add x6, other arithmetic, scatter_stage(): return {m: blocks[m] + arrived[m].astype(jnp.float32) for m in arrived}  19.6 us
  transfers between devices with their start and end apart: 66, of which 24 were waited for; matrix products, arithmetic and copies ran while one was open for 30% of the time, Pallas kernels for 0%

profile of v11, /device:TPU:13, one launch (start us, length us, event | category | flops | bytes accessed | tf_op | source)
XLA Modules:
  0.0 791.1 jit_solution(7841414559106959201)
XLA Ops:
  11.3 5.8 all-gather.1
  48.1 17.2 %collective-permute-done.6 = bf16[256,1536]{1,0:T(8,128)(2,1)} collective-permute-done((bf16[256,1536]{1,0:T(8,128)(2,1)}, bf16[256,1536]{1,0:T(8,128)(2,1)}, u32[]{:S(2)}, u32[]{:S(2)}) %collective-permute-start.6) | collective-permute-done | bytes 786464 | tf_op jit(solution)/shard_map/ppermute | solution.py:78
  75.8 29.4 %collective-permute-done.8 = bf16[256,1536]{1,0:T(8,128)(2,1)S(1)} collective-permute-done((bf16[256,1536]{1,0:T(8,128)(2,1)}, bf16[256,1536]{1,0:T(8,128)(2,1)S(1)}, u32[]{:S(2)}, u32[]{:S(2)}) %collective-permute-start.8) | collective-permute-done | bytes 786464 | tf_op jit(solution)/shard_map/ppermute | solution.py:78
  123.0 12.8 %collective-permute-done.14 = bf16[128,2048]{1,0:T(8,128)(2,1)S(1)} collective-permute-done((bf16[128,2048]{1,0:T(8,128)(2,1)S(1)}, bf16[128,2048]{1,0:T(8,128)(2,1)S(1)}, u32[]{:S(2)}, u32[]{:S(2)}) %collective-permute-start.14) | collective-permute-done | bytes 524320 | tf_op jit(solution)/shard_map/ppermute | solution.py:78
  143.2 42.3 %collective-permute-done.16.refs_2_ = bf16[2,512,1024]{2,1,0:T(8,128)(2,1)} collective-permute-done((bf16[2,512,1024]{2,1,0:T(8,128)(2,1)}, bf16[2,512,1024]{2,1,0:T(8,128)(2,1)}, u32[]{:S(2)}, u32[]{:S(2)}) %collective-permute-start.16) | collective-permute-done | bytes 2097184 | tf_op jit(solution)/shard_map/ppermute | solution.py:78
  207.8 22.6 %collective-permute-done.22.refs_10_ = bf16[2,1024,512]{2,1,0:T(8,128)(2,1)} collective-permute-done((bf16[2,1024,512]{2,1,0:T(8,128)(2,1)}, bf16[2,1024,512]{2,1,0:T(8,128)(2,1)}, u32[]{:S(2)}, u32[]{:S(2)}) %collective-permute-start.22) | collective-permute-done | bytes 2097184 | tf_op jit(solution)/shard_map/ppermute | solution.py:78
  233.7 41.6 %collective-permute-done.19.refs_6_ = bf16[2,512,1024]{2,1,0:T(8,128)(2,1)} collective-permute-done((bf16[2,512,1024]{2,1,0:T(8,128)(2,1)}, bf16[2,512,1024]{2,1,0:T(8,128)(2,1)}, u32[]{:S(2)}, u32[]{:S(2)}) %collective-permute-start.19) | collective-permute-done | bytes 2097184 | tf_op jit(solution)/shard_map/ppermute | solution.py:78
  297.6 36.5 %shard_map.263 = (bf16[1024,2048]{1,0:T(8,128)(2,1)}, bf16[1024,2048]{1,0:T(8,128)(2,1)}, bf16[1024,2048]{1,0:T(8,128)(2,1)}, f32[2,1024,128]{2,1,0:T(8,128)}) custom-call(bf16[1024,2048]{1,0:T(8,128)(2,1)} %all-gather.5.cloned.1.call-done.x_ref, bf16[1024,2048]{1,0:T(8,128)(2,1)} %all-gather.7.cloned.1.call-done.cot_ref, f32[2,1024,1]{2,1,0:T(8,128)} %copy.90.weight_ref, ...), custom_call_target="tpu_custom_call" | custom-call | tf_op jit(solution)/shard_map/pallas_call | solution.py:286
  334.1 28.6 %shard_map.264 = bf16[1024,2048]{1,0:T(8,128)(2,1)} custom-call(bf16[1024,2048]{1,0:T(8,128)(2,1)} %get-tuple-element.87.gate_grad_ref, bf16[1024,2048]{1,0:T(8,128)(2,1)} %get-tuple-element.88.up_grad_ref, bf16[2,512,1024]{2,1,0:T(8,128)(2,1)} %refs_0_.1, bf16[2,512,1024]{2,1,0:T(8,128)(2,1)} %collective-permute-done.15.refs_1_, ...), custom_call_target="tpu_custom_call" | custom-call | tf_op jit(solution)/shard_map/pallas_call | solution.py:330
  362.8 6.3 fusion.55
  398.5 12.3 %fusion.12 = bf16[1024,2048]{1,0:T(8,128)(2,1)S(1)} fusion(bf16[1024,2048]{1,0:T(8,128)(2,1)} %get-tuple-element.89, bf16[2048,512]{1,0:T(8,128)(2,1)} %bitcast.44, bf16[2048,512]{1,0:T(8,128)(2,1)} %bitcast.43, bf16[2048,512]{1,0:T(8,128)(2,1)} %bitcast.42, bf16[2048,512]{1,0:T(8,128)(2,1)S(1)} %bitcast.286), kind=kOutput, calls=%fused_computation.25 | convolution fusion | flops 8625586176 | bytes 16777216 | tf_op jit(solution)/shard_map/dot_general | solution.py:65
  422.9 6.3 all-to-all-start.1
  437.4 33.7 %collective-permute-done.24 = bf16[2,2,128,2048]{3,2,0,1:T(8,128)(2,1)} collective-permute-done((bf16[2,2,128,2048]{3,2,0,1:T(8,128)(2,1)}, bf16[2,2,128,2048]{3,2,0,1:T(8,128)(2,1)}, u32[]{:S(2)}, u32[]{:S(2)}) %collective-permute-start.24) | collective-permute-done | bytes 2097184 | tf_op jit(solution)/shard_map/ppermute | solution.py:78
  492.4 15.8 %collective-permute-done.25 = bf16[2,128,2048]{2,1,0:T(8,128)(2,1)S(1)} collective-permute-done((bf16[2,128,2048]{2,1,0:T(8,128)(2,1)S(1)}, bf16[2,128,2048]{2,1,0:T(8,128)(2,1)S(1)}, u32[]{:S(2)}, u32[]{:S(2)}) %collective-permute-start.25) | collective-permute-done | bytes 1048608 | tf_op jit(solution)/shard_map/ppermute | solution.py:78
  514.4 18.2 %collective-permute-done.26 = bf16[128,2048]{1,0:T(8,128)(2,1)S(1)} collective-permute-done((bf16[128,2048]{1,0:T(8,128)(2,1)S(1)}, bf16[128,2048]{1,0:T(8,128)(2,1)S(1)}, u32[]{:S(2)}, u32[]{:S(2)}) %collective-permute-start.26) | collective-permute-done | bytes 524320 | tf_op jit(solution)/shard_map/ppermute | solution.py:78
  543.3 6.4 collective-permute-done.28
  557.3 7.1 shard_map.265
  601.3 21.0 %collective-permute-done.42 = bf16[2,2,256,512]{3,2,0,1:T(8,128)(2,1)S(1)} collective-permute-done((bf16[2,2,256,512]{3,2,0,1:T(8,128)(2,1)S(1)}, bf16[2,2,256,512]{3,2,0,1:T(8,128)(2,1)S(1)}, u32[]{:S(2)}, u32[]{:S(2)}) %collective-permute-start.42) | collective-permute-done | bytes 1048608 | tf_op jit(solution)/shard_map/ppermute | solution.py:78
  625.8 33.3 %collective-permute-done.35 = bf16[128,2048]{1,0:T(8,128)(2,1)S(1)} collective-permute-done((bf16[128,2048]{1,0:T(8,128)(2,1)S(1)}, bf16[128,2048]{1,0:T(8,128)(2,1)S(1)}, u32[]{:S(2)}, u32[]{:S(2)}) %collective-permute-start.35) | collective-permute-done | bytes 524320 | tf_op jit(solution)/shard_map/ppermute | solution.py:78
  678.3 6.1 all-to-all-start.3
  686.3 18.4 %all-to-all-done.3 = f32[4,1,1280]{2,1,0:T(1,128)S(1)} async-done(((f32[4,1,1280]{2,1,0:T(1,128)}), f32[4,1,1280]{2,1,0:T(1,128)S(1)}, u32[]{:S(2)}, u32[]{:S(2)}) %all-to-all-start.3) | async-done | bytes 20512 | tf_op jit(solution)/shard_map/all_to_all | solution.py:614
  714.7 14.8 %collective-permute-done.37 = bf16[2,256,512]{2,1,0:T(8,128)(2,1)S(1)} collective-permute-done((bf16[2,256,512]{2,1,0:T(8,128)(2,1)}, bf16[2,256,512]{2,1,0:T(8,128)(2,1)S(1)}, u32[]{:S(2)}, u32[]{:S(2)}) %collective-permute-start.37) | collective-permute-done | bytes 524320 | tf_op jit(solution)/shard_map/ppermute | solution.py:78
  732.2 12.9 %collective-permute-done.44 = bf16[256,512]{1,0:T(8,128)(2,1)S(1)} collective-permute-done((bf16[256,512]{1,0:T(8,128)(2,1)S(1)}, bf16[256,512]{1,0:T(8,128)(2,1)S(1)}, u32[]{:S(2)}, u32[]{:S(2)}) %collective-permute-start.44) | collective-permute-done | bytes 262176 | tf_op jit(solution)/shard_map/ppermute | solution.py:78
  757.4 9.7 %all-to-all-start.4 = ((bf16[4,64,1536]{2,1,0:T(8,128)(2,1)}), bf16[4,64,1536]{2,1,0:T(8,128)(2,1)S(1)}, u32[]{:S(2)}, u32[]{:S(2)}) async-start(bf16[4,64,1536]{2,1,0:T(8,128)(2,1)} %bitcast.285), calls=%async_computation.5 | async-start | bytes 1572864 | tf_op jit(solution)/shard_map/all_to_all | solution.py:595
  (544 shorter events, 315.9 us)
Async XLA Ops:
  7.2 290.4 %all-gather.7.cloned.1.call-start = ((), (), s32[]{:S(2)}) async-start(), calls=%async_computation.7 | async-start | bytes 4718592 | tf_op jit(solution)/shard_map/all_gather | solution.py:408
  21.0 276.7 %all-gather.5.cloned.1.call-start = ((), (), s32[]{:S(2)}) async-start(), calls=%async_computation.6 | async-start | bytes 4718592 | tf_op jit(solution)/shard_map/all_gather | solution.py:478
  47.8 57.9 %collective-permute-start.7 = (bf16[256,1536]{1,0:T(8,128)(2,1)}, bf16[256,1536]{1,0:T(8,128)(2,1)S(1)}, u32[]{:S(2)}, u32[]{:S(2)}) collective-permute-start(bf16[256,1536]{1,0:T(8,128)(2,1)} %collective-permute-done.5), channel_id=1, source_target_pairs={{0,4},{4,0},{8,12},{12,8},{16,20},{20,16},{24,28},{28,24},{1,5},{5... | collective-permute-start | bytes 2359304 | tf_op jit(solution)/shard_map/ppermute | solution.py:78
  138.9 46.6 %collective-permute-start.16 = (bf16[2,512,1024]{2,1,0:T(8,128)(2,1)}, bf16[2,512,1024]{2,1,0:T(8,128)(2,1)}, u32[]{:S(2)}, u32[]{:S(2)}) collective-permute-start(bf16[2,512,1024]{2,1,0:T(8,128)(2,1)} %refs_0_.1), channel_id=1, source_target_pairs={{0,2},{1,3},{2,0},{3,1},{4,6},{5,7},{6,4},{7,5},{8,10},{9,11},{10,... | collective-permute-start | bytes 6291464 | tf_op jit(solution)/shard_map/ppermute | solution.py:78
  140.0 90.4 %collective-permute-start.22 = (bf16[2,1024,512]{2,1,0:T(8,128)(2,1)}, bf16[2,1024,512]{2,1,0:T(8,128)(2,1)}, u32[]{:S(2)}, u32[]{:S(2)}) collective-permute-start(bf16[2,1024,512]{2,1,0:T(8,128)(2,1)} %refs_8_), channel_id=1, source_target_pairs={{0,2},{1,3},{2,0},{3,1},{4,6},{5,7},{6,4},{7,5},{8,10},{9,11},{10,... | collective-permute-start | bytes 6291464 | tf_op jit(solution)/shard_map/ppermute | solution.py:78
  141.5 156.0 %collective-permute-start.21 = (bf16[2,1024,512]{2,1,0:T(8,128)(2,1)}, bf16[2,1024,512]{2,1,0:T(8,128)(2,1)}, u32[]{:S(2)}, u32[]{:S(2)}) collective-permute-start(bf16[2,1024,512]{2,1,0:T(8,128)(2,1)} %refs_8_), channel_id=1, source_target_pairs={{0,1},{1,0},{2,3},{3,2},{4,5},{5,4},{6,7},{7,6},{8,9},{9,8},{10,11... | collective-permute-start | bytes 6291464 | tf_op jit(solution)/shard_map/ppermute | solution.py:78
  143.1 154.5 %collective-permute-start.15 = (bf16[2,512,1024]{2,1,0:T(8,128)(2,1)}, bf16[2,512,1024]{2,1,0:T(8,128)(2,1)}, u32[]{:S(2)}, u32[]{:S(2)}) collective-permute-start(bf16[2,512,1024]{2,1,0:T(8,128)(2,1)} %refs_0_.1), channel_id=1, source_target_pairs={{0,1},{1,0},{2,3},{3,2},{4,5},{5,4},{6,7},{7,6},{8,9},{9,8},{10,11... | collective-permute-start | bytes 6291464 | tf_op jit(solution)/shard_map/ppermute | solution.py:78
  143.1 132.3 %collective-permute-start.19 = (bf16[2,512,1024]{2,1,0:T(8,128)(2,1)}, bf16[2,512,1024]{2,1,0:T(8,128)(2,1)}, u32[]{:S(2)}, u32[]{:S(2)}) collective-permute-start(bf16[2,512,1024]{2,1,0:T(8,128)(2,1)} %refs_4_.1), channel_id=1, source_target_pairs={{0,2},{1,3},{2,0},{3,1},{4,6},{5,7},{6,4},{7,5},{8,10},{9,11},{10,... | collective-permute-start | bytes 6291464 | tf_op jit(solution)/shard_map/ppermute | solution.py:78
  185.5 91.7 %collective-permute-start.17 = (bf16[2,512,1024]{2,1,0:T(8,128)(2,1)}, bf16[2,512,1024]{2,1,0:T(8,128)(2,1)}, u32[]{:S(2)}, u32[]{:S(2)}) collective-permute-start(bf16[2,512,1024]{2,1,0:T(8,128)(2,1)} %collective-permute-done.16.refs_2_), channel_id=1, source_target_pairs={{0,1},{1,0},{2,3},{3,2},{4,5},{5,4},{6,7},{7,6},{8,9},{9,8},{10,11... | collective-permute-start | bytes 6291464 | tf_op jit(solution)/shard_map/ppermute | solution.py:78
  190.8 86.5 %all-to-all-start = ((f32[8,2,128]{2,1,0:T(2,128)}), f32[8,2,128]{2,1,0:T(2,128)S(1)}, u32[]{:S(2)}, u32[]{:S(2)}) async-start(f32[8,2,128]{2,1,0:T(2,128)} %bitcast.37), calls=%async_computation | async-start | bytes 16384 | tf_op jit(solution)/shard_map/all_to_all | solution.py:479
  196.4 337.1 %reduce-scatter.2.cloned.1.call-start = ((), (), s32[]{:S(2)}) async-start(), calls=%async_computation.8 | async-start | bytes 4718592 | tf_op jit(solution)/shard_map/reduce_scatter | solution.py:496
  230.4 67.1 %collective-permute-start.18 = (bf16[2,512,1024]{2,1,0:T(8,128)(2,1)}, bf16[2,512,1024]{2,1,0:T(8,128)(2,1)}, u32[]{:S(2)}, u32[]{:S(2)}) collective-permute-start(bf16[2,512,1024]{2,1,0:T(8,128)(2,1)} %refs_4_.1), channel_id=1, source_target_pairs={{0,1},{1,0},{2,3},{3,2},{4,5},{5,4},{6,7},{7,6},{8,9},{9,8},{10,11... | collective-permute-start | bytes 6291464 | tf_op jit(solution)/shard_map/ppermute | solution.py:78
  414.4 56.7 %collective-permute-start.24 = (bf16[2,2,128,2048]{3,2,0,1:T(8,128)(2,1)}, bf16[2,2,128,2048]{3,2,0,1:T(8,128)(2,1)}, u32[]{:S(2)}, u32[]{:S(2)}) collective-permute-start(bf16[2,2,128,2048]{3,2,0,1:T(8,128)(2,1)} %bitcast.274), channel_id=1, source_target_pairs={{0,4},{4,0},{8,12},{12,8},{16,20},{20,16},{24,28},{28,24},{1,5},{5... | collective-permute-start | bytes 6291464 | tf_op jit(solution)/shard_map/ppermute | solution.py:78
  418.5 55.9 %collective-permute-start.50 = (bf16[512,2048]{1,0:T(8,128)(2,1)}, bf16[512,2048]{1,0:T(8,128)(2,1)}, u32[]{:S(2)}, u32[]{:S(2)}) collective-permute-start(bf16[512,2048]{1,0:T(8,128)(2,1)} %fusion.55), channel_id=1, source_target_pairs={{0,1},{1,0},{2,3},{3,2},{4,5},{5,4},{6,7},{7,6},{8,9},{9,8},{10,11... | collective-permute-start | bytes 6291464 | tf_op jit(solution)/shard_map/ppermute | solution.py:78
  420.2 67.9 %collective-permute-start.52 = (bf16[512,2048]{1,0:T(8,128)(2,1)}, bf16[512,2048]{1,0:T(8,128)(2,1)}, u32[]{:S(2)}, u32[]{:S(2)}) collective-permute-start(bf16[512,2048]{1,0:T(8,128)(2,1)} %fusion.61), channel_id=1, source_target_pairs={{0,1},{1,0},{2,3},{3,2},{4,5},{5,4},{6,7},{7,6},{8,9},{9,8},{10,11... | collective-permute-start | bytes 6291464 | tf_op jit(solution)/shard_map/ppermute | solution.py:78
  420.2 90.1 %collective-permute-start.53 = (bf16[512,2048]{1,0:T(8,128)(2,1)}, bf16[512,2048]{1,0:T(8,128)(2,1)}, u32[]{:S(2)}, u32[]{:S(2)}) collective-permute-start(bf16[512,2048]{1,0:T(8,128)(2,1)} %fusion.53), channel_id=1, source_target_pairs={{0,1},{1,0},{2,3},{3,2},{4,5},{5,4},{6,7},{7,6},{8,9},{9,8},{10,11... | collective-permute-start | bytes 6291464 | tf_op jit(solution)/shard_map/ppermute | solution.py:78
  422.9 110.6 %all-to-all-start.1 = ((f32[8,2,128]{2,1,0:T(2,128)}), f32[8,2,128]{2,1,0:T(2,128)S(1)}, u32[]{:S(2)}, u32[]{:S(2)}) async-start(f32[8,2,128]{2,1,0:T(2,128)} %bitcast.53), calls=%async_computation.2 | async-start | bytes 16384 | tf_op jit(solution)/shard_map/all_to_all | solution.py:498
  474.5 63.1 %collective-permute-start.49 = (bf16[512,2048]{1,0:T(8,128)(2,1)}, bf16[512,2048]{1,0:T(8,128)(2,1)}, u32[]{:S(2)}, u32[]{:S(2)}) collective-permute-start(bf16[512,2048]{1,0:T(8,128)(2,1)} %fusion.63), channel_id=1, source_target_pairs={{0,1},{1,0},{2,3},{3,2},{4,5},{5,4},{6,7},{7,6},{8,9},{9,8},{10,11... | collective-permute-start | bytes 6291464 | tf_op jit(solution)/shard_map/ppermute | solution.py:78
  478.4 59.2 %collective-permute-start.51 = (bf16[512,2048]{1,0:T(8,128)(2,1)}, bf16[512,2048]{1,0:T(8,128)(2,1)}, u32[]{:S(2)}, u32[]{:S(2)}) collective-permute-start(bf16[512,2048]{1,0:T(8,128)(2,1)} %add_convert_fusion), channel_id=1, source_target_pairs={{0,2},{1,3},{2,0},{3,1},{4,6},{5,7},{6,4},{7,5},{8,10},{9,11},{10,... | collective-permute-start | bytes 6291464 | tf_op jit(solution)/shard_map/ppermute | solution.py:78
  588.3 78.9 %collective-permute-start.39 = (bf16[2,2,256,512]{3,2,0,1:T(8,128)(2,1)}, bf16[2,2,256,512]{3,2,0,1:T(8,128)(2,1)}, u32[]{:S(2)}, u32[]{:S(2)}) collective-permute-start(bf16[2,2,256,512]{3,2,0,1:T(8,128)(2,1)} %bitcast.277), channel_id=1, source_target_pairs={{0,4},{4,0},{8,12},{12,8},{16,20},{20,16},{24,28},{28,24},{1,5},{5... | collective-permute-start | bytes 3145736 | tf_op jit(solution)/shard_map/ppermute | solution.py:78
  590.9 83.0 %collective-permute-start.36 = (bf16[2,2,256,512]{3,2,0,1:T(8,128)(2,1)}, bf16[2,2,256,512]{3,2,0,1:T(8,128)(2,1)}, u32[]{:S(2)}, u32[]{:S(2)}) collective-permute-start(bf16[2,2,256,512]{3,2,0,1:T(8,128)(2,1)} %bitcast.278), channel_id=1, source_target_pairs={{0,4},{4,0},{8,12},{12,8},{16,20},{20,16},{24,28},{28,24},{1,5},{5... | collective-permute-start | bytes 3145736 | tf_op jit(solution)/shard_map/ppermute | solution.py:78
  600.4 168.9 %collective-permute-start.54 = (bf16[512,2048]{1,0:T(8,128)(2,1)}, bf16[512,2048]{1,0:T(8,128)(2,1)}, u32[]{:S(2)}, u32[]{:S(2)}) collective-permute-start(bf16[512,2048]{1,0:T(8,128)(2,1)} %convert_add_fusion.5), channel_id=1, source_target_pairs={{0,2},{1,3},{2,0},{3,1},{4,6},{5,7},{6,4},{7,5},{8,10},{9,11},{10,... | collective-permute-start | bytes 6291464 | tf_op jit(solution)/shard_map/ppermute | solution.py:78
  624.5 151.0 %collective-permute-start.57 = (bf16[2048,512]{1,0:T(8,128)(2,1)}, bf16[2048,512]{1,0:T(8,128)(2,1)}, u32[]{:S(2)}, u32[]{:S(2)}) collective-permute-start(bf16[2048,512]{1,0:T(8,128)(2,1)} %convert_add_fusion.2), channel_id=1, source_target_pairs={{0,2},{1,3},{2,0},{3,1},{4,6},{5,7},{6,4},{7,5},{8,10},{9,11},{10,... | collective-permute-start | bytes 6291464 | tf_op jit(solution)/shard_map/ppermute | solution.py:78
  659.1 48.1 %collective-permute-start.46 = (bf16[2,64,2048]{2,1,0:T(8,128)(2,1)}, bf16[2,64,2048]{2,1,0:T(8,128)(2,1)}, u32[]{:S(2)}, u32[]{:S(2)}) collective-permute-start(bf16[2,64,2048]{2,1,0:T(8,128)(2,1)} %dynamic-slice_bitcast_fusion.1), channel_id=1, source_target_pairs={{0,8},{4,12},{8,0},{12,4},{16,24},{20,28},{24,16},{28,20},{1,9},{5... | collective-permute-start | bytes 1572872 | tf_op jit(solution)/shard_map/ppermute | solution.py:78
  (151 other events, 2660.8 us)
Sparse Core Ops, SparseCore 0:
  21.1 92.4 all-gather.6
  139.0 70.6 all-gather.4
  362.9 95.5 reduce-scatter.1

commit v12 on v11

--- a/solution.py
+++ b/solution.py
@@ -169,9 +169,9 @@
     return total, [b for b in left if b != bit]
 
 
-def owner_scatter(values):
+def owner_scatter(values, turn=0):
     values, left = owner_split(values), owner_bits()
-    for bit in left[::-1]:
+    for bit in left[::-1][turn:] + left[::-1][:turn]:
         values, left = owner_stage(values, left, bit)
     return values
 
@@ -542,7 +542,7 @@
     mid_pieces = gather_pieces(middle_grad.astype(bf16))
     mid_all = jnp.concatenate(mid_pieces, axis=0)
     output_part = t_dot(attn_mix, mid_all).astype(bf16)
-    output_sum = owner_scatter(output_part.reshape(owners, final_rows, width))
+    output_sum = owner_scatter(output_part.reshape(owners, final_rows, width), turn=1)
     mix_grad = dot_t(mid_all, output_weight).astype(bf16)
     grad_queries, grad_keys, value_grad_b = attend_back(
         mix_grad,

time: 799 us -> 794 us (level)
    all_to_all x1, waiting for transfers between devices: 0.01 us -> 11.7 us  [local(): lax.all_to_all(table, OWNER, split_axis=0, concat_axis=0, tiled=True)]
    all_to_all x1, waiting for transfers between devices: 18.4 us -> 9.12 us  [local(): lax.all_to_all(table, SHARD, split_axis=0, concat_axis=0, tiled=True)]
    unnamed x235 -> x231, local copies, waits for them, and re-layouts: 35.3 us -> 36.1 us
  transfers between devices with their start and end apart: 66 -> 66, of which waited for: 24 -> 25; matrix products, arithmetic and copies ran while one was open for 30% -> 30% of each run, Pallas kernels for 0% -> 0%
where the time goes in v12:
time: 794 us; the launch traced here: 786 us
  waiting for transfers between devices  357 us (45%)
  matrix products  90.6 us (11%)
  other arithmetic  83.8 us (11%)
  starting transfers between devices  80.5 us (10%)
  local copies, waits for them, and re-layouts  76.9 us (10%)
  Pallas kernels  74.5 us (9%)
  between operations  16 us (2%)
    ppermute x57, waiting for transfers between devices, swap(): lax.ppermute(values, axis_name, [(i, i ^ mask) for i in range(count)])  334 us
    dot_general x17, matrix products, t_dot(): lax.dot_general(a, b, (((0,), (0,)), ((), ())), preferred_element_type=jn...  58.8 us
    ppermute x57, starting transfers between devices, swap(): lax.ppermute(values, axis_name, [(i, i ^ mask) for i in range(count)])  50.7 us
    pallas_call x1, Pallas kernels, expert_hidden(): pl.pallas_call(functools.partial(expert_hidden_kernel, parts), grid=(rows...  36.5 us
    unnamed x231, local copies, waits for them, and re-layouts  36.1 us
    pallas_call x1, Pallas kernels, back_rows(): pl.pallas_call(functools.partial(back_rows_kernel, parts), grid=(rows //...  28.6 us
    dot_general x11, matrix products, dot(): return jnp.dot(a, b, preferred_element_type=jnp.float32)  22 us
    add x6, other arithmetic, scatter_stage(): return {m: blocks[m] + arrived[m].astype(jnp.float32) for m in arrived}  19.5 us
  transfers between devices with their start and end apart: 66, of which 25 were waited for; matrix products, arithmetic and copies ran while one was open for 30% of the time, Pallas kernels for 0%

profile of v12, /device:TPU:13, one launch (start us, length us, event | category | flops | bytes accessed | tf_op | source)
XLA Modules:
  0.0 785.7 jit_solution(1983976568813497599)
XLA Ops:
  11.3 5.8 all-gather.1
  42.0 5.8 collective-permute-done.5
  48.1 17.2 %collective-permute-done.6 = bf16[256,1536]{1,0:T(8,128)(2,1)} collective-permute-done((bf16[256,1536]{1,0:T(8,128)(2,1)}, bf16[256,1536]{1,0:T(8,128)(2,1)}, u32[]{:S(2)}, u32[]{:S(2)}) %collective-permute-start.6) | collective-permute-done | bytes 786464 | tf_op jit(solution)/shard_map/ppermute | solution.py:78
  75.8 29.4 %collective-permute-done.8 = bf16[256,1536]{1,0:T(8,128)(2,1)S(1)} collective-permute-done((bf16[256,1536]{1,0:T(8,128)(2,1)}, bf16[256,1536]{1,0:T(8,128)(2,1)S(1)}, u32[]{:S(2)}, u32[]{:S(2)}) %collective-permute-start.8) | collective-permute-done | bytes 786464 | tf_op jit(solution)/shard_map/ppermute | solution.py:78
  123.0 12.8 %collective-permute-done.14 = bf16[128,2048]{1,0:T(8,128)(2,1)S(1)} collective-permute-done((bf16[128,2048]{1,0:T(8,128)(2,1)S(1)}, bf16[128,2048]{1,0:T(8,128)(2,1)S(1)}, u32[]{:S(2)}, u32[]{:S(2)}) %collective-permute-start.14) | collective-permute-done | bytes 524320 | tf_op jit(solution)/shard_map/ppermute | solution.py:78
  143.2 42.3 %collective-permute-done.16.refs_2_ = bf16[2,512,1024]{2,1,0:T(8,128)(2,1)} collective-permute-done((bf16[2,512,1024]{2,1,0:T(8,128)(2,1)}, bf16[2,512,1024]{2,1,0:T(8,128)(2,1)}, u32[]{:S(2)}, u32[]{:S(2)}) %collective-permute-start.16) | collective-permute-done | bytes 2097184 | tf_op jit(solution)/shard_map/ppermute | solution.py:78
  207.8 22.7 %collective-permute-done.22.refs_10_ = bf16[2,1024,512]{2,1,0:T(8,128)(2,1)} collective-permute-done((bf16[2,1024,512]{2,1,0:T(8,128)(2,1)}, bf16[2,1024,512]{2,1,0:T(8,128)(2,1)}, u32[]{:S(2)}, u32[]{:S(2)}) %collective-permute-start.22) | collective-permute-done | bytes 2097184 | tf_op jit(solution)/shard_map/ppermute | solution.py:78
  233.8 41.6 %collective-permute-done.19.refs_6_ = bf16[2,512,1024]{2,1,0:T(8,128)(2,1)} collective-permute-done((bf16[2,512,1024]{2,1,0:T(8,128)(2,1)}, bf16[2,512,1024]{2,1,0:T(8,128)(2,1)}, u32[]{:S(2)}, u32[]{:S(2)}) %collective-permute-start.19) | collective-permute-done | bytes 2097184 | tf_op jit(solution)/shard_map/ppermute | solution.py:78
  297.7 36.5 %shard_map.263 = (bf16[1024,2048]{1,0:T(8,128)(2,1)}, bf16[1024,2048]{1,0:T(8,128)(2,1)}, bf16[1024,2048]{1,0:T(8,128)(2,1)}, f32[2,1024,128]{2,1,0:T(8,128)}) custom-call(bf16[1024,2048]{1,0:T(8,128)(2,1)} %all-gather.5.cloned.1.call-done.x_ref, bf16[1024,2048]{1,0:T(8,128)(2,1)} %all-gather.7.cloned.1.call-done.cot_ref, f32[2,1024,1]{2,1,0:T(8,128)} %copy.86.weight_ref, ...), custom_call_target="tpu_custom_call" | custom-call | tf_op jit(solution)/shard_map/pallas_call | solution.py:286
  334.2 28.6 %shard_map.264 = bf16[1024,2048]{1,0:T(8,128)(2,1)} custom-call(bf16[1024,2048]{1,0:T(8,128)(2,1)} %get-tuple-element.87.gate_grad_ref, bf16[1024,2048]{1,0:T(8,128)(2,1)} %get-tuple-element.88.up_grad_ref, bf16[2,512,1024]{2,1,0:T(8,128)(2,1)} %refs_0_.1, bf16[2,512,1024]{2,1,0:T(8,128)(2,1)} %collective-permute-done.15.refs_1_, ...), custom_call_target="tpu_custom_call" | custom-call | tf_op jit(solution)/shard_map/pallas_call | solution.py:330
  362.9 6.3 fusion.55
  398.7 12.3 %fusion.12 = bf16[1024,2048]{1,0:T(8,128)(2,1)S(1)} fusion(bf16[1024,2048]{1,0:T(8,128)(2,1)} %get-tuple-element.89, bf16[2048,512]{1,0:T(8,128)(2,1)} %bitcast.44, bf16[2048,512]{1,0:T(8,128)(2,1)} %bitcast.43, bf16[2048,512]{1,0:T(8,128)(2,1)} %bitcast.42, bf16[2048,512]{1,0:T(8,128)(2,1)S(1)} %bitcast.285), kind=kOutput, calls=%fused_computation.25 | convolution fusion | flops 8625586176 | bytes 16777216 | tf_op jit(solution)/shard_map/dot_general | solution.py:65
  423.0 6.5 all-to-all-start.1
  437.7 33.5 %collective-permute-done.24 = bf16[2,2,128,2048]{3,2,0,1:T(8,128)(2,1)} collective-permute-done((bf16[2,2,128,2048]{3,2,0,1:T(8,128)(2,1)}, bf16[2,2,128,2048]{3,2,0,1:T(8,128)(2,1)}, u32[]{:S(2)}, u32[]{:S(2)}) %collective-permute-start.24) | collective-permute-done | bytes 2097184 | tf_op jit(solution)/shard_map/ppermute | solution.py:78
  492.5 15.8 %collective-permute-done.25 = bf16[2,128,2048]{2,1,0:T(8,128)(2,1)S(1)} collective-permute-done((bf16[2,128,2048]{2,1,0:T(8,128)(2,1)S(1)}, bf16[2,128,2048]{2,1,0:T(8,128)(2,1)S(1)}, u32[]{:S(2)}, u32[]{:S(2)}) %collective-permute-start.25) | collective-permute-done | bytes 1048608 | tf_op jit(solution)/shard_map/ppermute | solution.py:78
  514.2 18.4 %collective-permute-done.26 = bf16[128,2048]{1,0:T(8,128)(2,1)S(1)} collective-permute-done((bf16[128,2048]{1,0:T(8,128)(2,1)S(1)}, bf16[128,2048]{1,0:T(8,128)(2,1)S(1)}, u32[]{:S(2)}, u32[]{:S(2)}) %collective-permute-start.26) | collective-permute-done | bytes 524320 | tf_op jit(solution)/shard_map/ppermute | solution.py:78
  543.4 6.3 collective-permute-done.28
  557.3 7.1 shard_map.265
  608.1 50.9 %collective-permute-done.35 = bf16[128,2048]{1,0:T(8,128)(2,1)S(1)} collective-permute-done((bf16[128,2048]{1,0:T(8,128)(2,1)S(1)}, bf16[128,2048]{1,0:T(8,128)(2,1)S(1)}, u32[]{:S(2)}, u32[]{:S(2)}) %collective-permute-start.35) | collective-permute-done | bytes 524320 | tf_op jit(solution)/shard_map/ppermute | solution.py:78
  677.7 11.7 %all-to-all-done.2 = f32[8,20,256]{2,1,0:T(8,128)S(1)} async-done(((f32[8,20,256]{2,1,0:T(8,128)}), f32[8,20,256]{2,1,0:T(8,128)S(1)}, u32[]{:S(2)}, u32[]{:S(2)}) %all-to-all-start.2) | async-done | bytes 163872 | tf_op jit(solution)/shard_map/all_to_all | solution.py:610
  696.1 9.1 %all-to-all-done.3 = f32[4,1,1280]{2,1,0:T(1,128)S(1)} async-done(((f32[4,1,1280]{2,1,0:T(1,128)}), f32[4,1,1280]{2,1,0:T(1,128)S(1)}, u32[]{:S(2)}, u32[]{:S(2)}) %all-to-all-start.3) | async-done | bytes 20512 | tf_op jit(solution)/shard_map/all_to_all | solution.py:614
  715.3 10.4 %collective-permute-done.37 = bf16[2,256,512]{2,1,0:T(8,128)(2,1)S(1)} collective-permute-done((bf16[2,256,512]{2,1,0:T(8,128)(2,1)}, bf16[2,256,512]{2,1,0:T(8,128)(2,1)S(1)}, u32[]{:S(2)}, u32[]{:S(2)}) %collective-permute-start.37) | collective-permute-done | bytes 524320 | tf_op jit(solution)/shard_map/ppermute | solution.py:78
  732.2 14.0 %collective-permute-done.41 = bf16[256,512]{1,0:T(8,128)(2,1)S(1)} collective-permute-done((bf16[256,512]{1,0:T(8,128)(2,1)S(1)}, bf16[256,512]{1,0:T(8,128)(2,1)S(1)}, u32[]{:S(2)}, u32[]{:S(2)}) %collective-permute-start.41) | collective-permute-done | bytes 262176 | tf_op jit(solution)/shard_map/ppermute | solution.py:78
  752.9 7.9 %all-to-all-start.4 = ((bf16[4,64,1536]{2,1,0:T(8,128)(2,1)}), bf16[4,64,1536]{2,1,0:T(8,128)(2,1)S(1)}, u32[]{:S(2)}, u32[]{:S(2)}) async-start(bf16[4,64,1536]{2,1,0:T(8,128)(2,1)} %bitcast.284), calls=%async_computation.5 | async-start | bytes 1572864 | tf_op jit(solution)/shard_map/all_to_all | solution.py:595
  (539 shorter events, 316.5 us)
Async XLA Ops:
  7.2 290.5 %all-gather.7.cloned.1.call-start = ((), (), s32[]{:S(2)}) async-start(), calls=%async_computation.7 | async-start | bytes 4718592 | tf_op jit(solution)/shard_map/all_gather | solution.py:408
  21.0 276.7 %all-gather.5.cloned.1.call-start = ((), (), s32[]{:S(2)}) async-start(), calls=%async_computation.6 | async-start | bytes 4718592 | tf_op jit(solution)/shard_map/all_gather | solution.py:478
  47.8 57.9 %collective-permute-start.7 = (bf16[256,1536]{1,0:T(8,128)(2,1)}, bf16[256,1536]{1,0:T(8,128)(2,1)S(1)}, u32[]{:S(2)}, u32[]{:S(2)}) collective-permute-start(bf16[256,1536]{1,0:T(8,128)(2,1)} %collective-permute-done.5), channel_id=1, source_target_pairs={{0,4},{4,0},{8,12},{12,8},{16,20},{20,16},{24,28},{28,24},{1,5},{5... | collective-permute-start | bytes 2359304 | tf_op jit(solution)/shard_map/ppermute | solution.py:78
  140.0 90.4 %collective-permute-start.22 = (bf16[2,1024,512]{2,1,0:T(8,128)(2,1)}, bf16[2,1024,512]{2,1,0:T(8,128)(2,1)}, u32[]{:S(2)}, u32[]{:S(2)}) collective-permute-start(bf16[2,1024,512]{2,1,0:T(8,128)(2,1)} %refs_8_), channel_id=1, source_target_pairs={{0,2},{1,3},{2,0},{3,1},{4,6},{5,7},{6,4},{7,5},{8,10},{9,11},{10,... | collective-permute-start | bytes 6291464 | tf_op jit(solution)/shard_map/ppermute | solution.py:78
  141.5 156.1 %collective-permute-start.21 = (bf16[2,1024,512]{2,1,0:T(8,128)(2,1)}, bf16[2,1024,512]{2,1,0:T(8,128)(2,1)}, u32[]{:S(2)}, u32[]{:S(2)}) collective-permute-start(bf16[2,1024,512]{2,1,0:T(8,128)(2,1)} %refs_8_), channel_id=1, source_target_pairs={{0,1},{1,0},{2,3},{3,2},{4,5},{5,4},{6,7},{7,6},{8,9},{9,8},{10,11... | collective-permute-start | bytes 6291464 | tf_op jit(solution)/shard_map/ppermute | solution.py:78
  143.1 154.5 %collective-permute-start.15 = (bf16[2,512,1024]{2,1,0:T(8,128)(2,1)}, bf16[2,512,1024]{2,1,0:T(8,128)(2,1)}, u32[]{:S(2)}, u32[]{:S(2)}) collective-permute-start(bf16[2,512,1024]{2,1,0:T(8,128)(2,1)} %refs_0_.1), channel_id=1, source_target_pairs={{0,1},{1,0},{2,3},{3,2},{4,5},{5,4},{6,7},{7,6},{8,9},{9,8},{10,11... | collective-permute-start | bytes 6291464 | tf_op jit(solution)/shard_map/ppermute | solution.py:78
  143.1 132.3 %collective-permute-start.19 = (bf16[2,512,1024]{2,1,0:T(8,128)(2,1)}, bf16[2,512,1024]{2,1,0:T(8,128)(2,1)}, u32[]{:S(2)}, u32[]{:S(2)}) collective-permute-start(bf16[2,512,1024]{2,1,0:T(8,128)(2,1)} %refs_4_.1), channel_id=1, source_target_pairs={{0,2},{1,3},{2,0},{3,1},{4,6},{5,7},{6,4},{7,5},{8,10},{9,11},{10,... | collective-permute-start | bytes 6291464 | tf_op jit(solution)/shard_map/ppermute | solution.py:78
  185.5 91.7 %collective-permute-start.17 = (bf16[2,512,1024]{2,1,0:T(8,128)(2,1)}, bf16[2,512,1024]{2,1,0:T(8,128)(2,1)}, u32[]{:S(2)}, u32[]{:S(2)}) collective-permute-start(bf16[2,512,1024]{2,1,0:T(8,128)(2,1)} %collective-permute-done.16.refs_2_), channel_id=1, source_target_pairs={{0,1},{1,0},{2,3},{3,2},{4,5},{5,4},{6,7},{7,6},{8,9},{9,8},{10,11... | collective-permute-start | bytes 6291464 | tf_op jit(solution)/shard_map/ppermute | solution.py:78
  190.8 86.5 %all-to-all-start = ((f32[8,2,128]{2,1,0:T(2,128)}), f32[8,2,128]{2,1,0:T(2,128)S(1)}, u32[]{:S(2)}, u32[]{:S(2)}) async-start(f32[8,2,128]{2,1,0:T(2,128)} %bitcast.37), calls=%async_computation | async-start | bytes 16384 | tf_op jit(solution)/shard_map/all_to_all | solution.py:479
  196.5 337.1 %reduce-scatter.2.cloned.1.call-start = ((), (), s32[]{:S(2)}) async-start(), calls=%async_computation.8 | async-start | bytes 4718592 | tf_op jit(solution)/shard_map/reduce_scatter | solution.py:496
  230.5 67.1 %collective-permute-start.18 = (bf16[2,512,1024]{2,1,0:T(8,128)(2,1)}, bf16[2,512,1024]{2,1,0:T(8,128)(2,1)}, u32[]{:S(2)}, u32[]{:S(2)}) collective-permute-start(bf16[2,512,1024]{2,1,0:T(8,128)(2,1)} %refs_4_.1), channel_id=1, source_target_pairs={{0,1},{1,0},{2,3},{3,2},{4,5},{5,4},{6,7},{7,6},{8,9},{9,8},{10,11... | collective-permute-start | bytes 6291464 | tf_op jit(solution)/shard_map/ppermute | solution.py:78
  414.5 56.7 %collective-permute-start.24 = (bf16[2,2,128,2048]{3,2,0,1:T(8,128)(2,1)}, bf16[2,2,128,2048]{3,2,0,1:T(8,128)(2,1)}, u32[]{:S(2)}, u32[]{:S(2)}) collective-permute-start(bf16[2,2,128,2048]{3,2,0,1:T(8,128)(2,1)} %bitcast.274), channel_id=1, source_target_pairs={{0,4},{4,0},{8,12},{12,8},{16,20},{20,16},{24,28},{28,24},{1,5},{5... | collective-permute-start | bytes 6291464 | tf_op jit(solution)/shard_map/ppermute | solution.py:78
  418.6 55.9 %collective-permute-start.50 = (bf16[512,2048]{1,0:T(8,128)(2,1)}, bf16[512,2048]{1,0:T(8,128)(2,1)}, u32[]{:S(2)}, u32[]{:S(2)}) collective-permute-start(bf16[512,2048]{1,0:T(8,128)(2,1)} %fusion.55), channel_id=1, source_target_pairs={{0,1},{1,0},{2,3},{3,2},{4,5},{5,4},{6,7},{7,6},{8,9},{9,8},{10,11... | collective-permute-start | bytes 6291464 | tf_op jit(solution)/shard_map/ppermute | solution.py:78
  420.3 67.9 %collective-permute-start.52 = (bf16[512,2048]{1,0:T(8,128)(2,1)}, bf16[512,2048]{1,0:T(8,128)(2,1)}, u32[]{:S(2)}, u32[]{:S(2)}) collective-permute-start(bf16[512,2048]{1,0:T(8,128)(2,1)} %fusion.61), channel_id=1, source_target_pairs={{0,1},{1,0},{2,3},{3,2},{4,5},{5,4},{6,7},{7,6},{8,9},{9,8},{10,11... | collective-permute-start | bytes 6291464 | tf_op jit(solution)/shard_map/ppermute | solution.py:78
  420.3 90.0 %collective-permute-start.53 = (bf16[512,2048]{1,0:T(8,128)(2,1)}, bf16[512,2048]{1,0:T(8,128)(2,1)}, u32[]{:S(2)}, u32[]{:S(2)}) collective-permute-start(bf16[512,2048]{1,0:T(8,128)(2,1)} %fusion.53), channel_id=1, source_target_pairs={{0,1},{1,0},{2,3},{3,2},{4,5},{5,4},{6,7},{7,6},{8,9},{9,8},{10,11... | collective-permute-start | bytes 6291464 | tf_op jit(solution)/shard_map/ppermute | solution.py:78
  423.0 110.6 %all-to-all-start.1 = ((f32[8,2,128]{2,1,0:T(2,128)}), f32[8,2,128]{2,1,0:T(2,128)S(1)}, u32[]{:S(2)}, u32[]{:S(2)}) async-start(f32[8,2,128]{2,1,0:T(2,128)} %bitcast.53), calls=%async_computation.2 | async-start | bytes 16384 | tf_op jit(solution)/shard_map/all_to_all | solution.py:498
  474.6 63.1 %collective-permute-start.49 = (bf16[512,2048]{1,0:T(8,128)(2,1)}, bf16[512,2048]{1,0:T(8,128)(2,1)}, u32[]{:S(2)}, u32[]{:S(2)}) collective-permute-start(bf16[512,2048]{1,0:T(8,128)(2,1)} %fusion.63), channel_id=1, source_target_pairs={{0,1},{1,0},{2,3},{3,2},{4,5},{5,4},{6,7},{7,6},{8,9},{9,8},{10,11... | collective-permute-start | bytes 6291464 | tf_op jit(solution)/shard_map/ppermute | solution.py:78
  478.4 59.2 %collective-permute-start.51 = (bf16[512,2048]{1,0:T(8,128)(2,1)}, bf16[512,2048]{1,0:T(8,128)(2,1)}, u32[]{:S(2)}, u32[]{:S(2)}) collective-permute-start(bf16[512,2048]{1,0:T(8,128)(2,1)} %add_convert_fusion), channel_id=1, source_target_pairs={{0,2},{1,3},{2,0},{3,1},{4,6},{5,7},{6,4},{7,5},{8,10},{9,11},{10,... | collective-permute-start | bytes 6291464 | tf_op jit(solution)/shard_map/ppermute | solution.py:78
  587.6 79.6 %collective-permute-start.39 = (bf16[2,2,256,512]{3,2,0,1:T(8,128)(2,1)}, bf16[2,2,256,512]{3,2,0,1:T(8,128)(2,1)}, u32[]{:S(2)}, u32[]{:S(2)}) collective-permute-start(bf16[2,2,256,512]{3,2,0,1:T(8,128)(2,1)} %bitcast.276), channel_id=1, source_target_pairs={{0,4},{4,0},{8,12},{12,8},{16,20},{20,16},{24,28},{28,24},{1,5},{5... | collective-permute-start | bytes 3145736 | tf_op jit(solution)/shard_map/ppermute | solution.py:78
  590.7 83.3 %collective-permute-start.36 = (bf16[2,2,256,512]{3,2,0,1:T(8,128)(2,1)}, bf16[2,2,256,512]{3,2,0,1:T(8,128)(2,1)}, u32[]{:S(2)}, u32[]{:S(2)}) collective-permute-start(bf16[2,2,256,512]{3,2,0,1:T(8,128)(2,1)} %bitcast.277), channel_id=1, source_target_pairs={{0,4},{4,0},{8,12},{12,8},{16,20},{20,16},{24,28},{28,24},{1,5},{5... | collective-permute-start | bytes 3145736 | tf_op jit(solution)/shard_map/ppermute | solution.py:78
  601.0 162.8 %collective-permute-start.54 = (bf16[512,2048]{1,0:T(8,128)(2,1)}, bf16[512,2048]{1,0:T(8,128)(2,1)}, u32[]{:S(2)}, u32[]{:S(2)}) collective-permute-start(bf16[512,2048]{1,0:T(8,128)(2,1)} %convert_add_fusion.5), channel_id=1, source_target_pairs={{0,2},{1,3},{2,0},{3,1},{4,6},{5,7},{6,4},{7,5},{8,10},{9,11},{10,... | collective-permute-start | bytes 6291464 | tf_op jit(solution)/shard_map/ppermute | solution.py:78
  603.6 55.4 %collective-permute-start.35 = (bf16[128,2048]{1,0:T(8,128)(2,1)S(1)}, bf16[128,2048]{1,0:T(8,128)(2,1)S(1)}, u32[]{:S(2)}, u32[]{:S(2)}) collective-permute-start(bf16[128,2048]{1,0:T(8,128)(2,1)S(1)} %fusion.44), channel_id=1, source_target_pairs={{0,2},{1,3},{2,0},{3,1},{4,6},{5,7},{6,4},{7,5},{8,10},{9,11},{10,... | collective-permute-start | bytes 1572872 | tf_op jit(solution)/shard_map/ppermute | solution.py:78
  606.7 163.4 %collective-permute-start.57 = (bf16[2048,512]{1,0:T(8,128)(2,1)}, bf16[2048,512]{1,0:T(8,128)(2,1)}, u32[]{:S(2)}, u32[]{:S(2)}) collective-permute-start(bf16[2048,512]{1,0:T(8,128)(2,1)} %convert_add_fusion.2), channel_id=1, source_target_pairs={{0,2},{1,3},{2,0},{3,1},{4,6},{5,7},{6,4},{7,5},{8,10},{9,11},{10,... | collective-permute-start | bytes 6291464 | tf_op jit(solution)/shard_map/ppermute | solution.py:78
  659.0 48.7 %collective-permute-start.46 = (bf16[2,64,2048]{2,1,0:T(8,128)(2,1)}, bf16[2,64,2048]{2,1,0:T(8,128)(2,1)}, u32[]{:S(2)}, u32[]{:S(2)}) collective-permute-start(bf16[2,64,2048]{2,1,0:T(8,128)(2,1)} %dynamic-slice_bitcast_fusion.2), channel_id=1, source_target_pairs={{0,16},{4,20},{8,24},{12,28},{16,0},{20,4},{24,8},{28,12},{1,17},{... | collective-permute-start | bytes 1572872 | tf_op jit(solution)/shard_map/ppermute | solution.py:78
  (149 other events, 2615.2 us)
Sparse Core Ops, SparseCore 0:
  21.1 92.4 all-gather.6
  139.1 70.6 all-gather.4
  363.0 95.5 reduce-scatter.1

commit v13 on v12

--- a/solution.py
+++ b/solution.py
@@ -583,9 +583,7 @@
     key_sum = owner_scatter(key_part.reshape(cut))
 
     unit_one, inverse_one = rms_unit(residual)
-    input_part, attn_gain_grad = rms_backward(
-        attn_in_grad, unit_one, inverse_one, attn_gain_all
-    )
+    input_part, attn_gain_grad = rms_backward(attn_in_grad, unit_one, inverse_one, attn_gain_all)
     tokens_grad = middle_grad + input_part
     moe_out = after(moe_out, attn_in_part)
     block_output = middle + mixed_order(moe_out, w_index, parts).astype(f32)
@@ -610,9 +608,8 @@
     table = lax.all_to_all(table, OWNER, split_axis=0, concat_axis=0, tiled=True)
     table = jnp.sum(table, axis=0)
     table = table.reshape(count, parts, final_rows).transpose(1, 0, 2)
-    table = jnp.sum(
-        lax.all_to_all(table, SHARD, split_axis=0, concat_axis=0, tiled=True), axis=0
-    )
+    table = lax.all_to_all(table, SHARD, split_axis=0, concat_axis=0, tiled=True)
+    table = jnp.sum(table, axis=0)
     return (
         block_output,
         tokens_grad,

time: 794 us -> 794 us (level)
  no operation moved by 1% of the time
where the time goes in v13:
time: 794 us; the launch traced here: 786 us
  waiting for transfers between devices  357 us (45%)
  matrix products  90.6 us (11%)
  other arithmetic  83.8 us (11%)
  starting transfers between devices  80.5 us (10%)
  local copies, waits for them, and re-layouts  76.9 us (10%)
  Pallas kernels  74.5 us (9%)
  between operations  16 us (2%)
    ppermute x57, waiting for transfers between devices, swap(): lax.ppermute(values, axis_name, [(i, i ^ mask) for i in range(count)])  334 us
    dot_general x17, matrix products, t_dot(): lax.dot_general(a, b, (((0,), (0,)), ((), ())), preferred_element_type=jn...  58.8 us
    ppermute x57, starting transfers between devices, swap(): lax.ppermute(values, axis_name, [(i, i ^ mask) for i in range(count)])  50.7 us
    pallas_call x1, Pallas kernels, expert_hidden(): pl.pallas_call(functools.partial(expert_hidden_kernel, parts), grid=(rows...  36.5 us
    unnamed x231, local copies, waits for them, and re-layouts  36.1 us
    pallas_call x1, Pallas kernels, back_rows(): pl.pallas_call(functools.partial(back_rows_kernel, parts), grid=(rows //...  28.6 us
    dot_general x11, matrix products, dot(): return jnp.dot(a, b, preferred_element_type=jnp.float32)  22 us
    add x6, other arithmetic, scatter_stage(): return {m: blocks[m] + arrived[m].astype(jnp.float32) for m in arrived}  19.5 us
  transfers between devices with their start and end apart: 66, of which 25 were waited for; matrix products, arithmetic and copies ran while one was open for 30% of the time, Pallas kernels for 0%

profile of v13, /device:TPU:13, one launch (start us, length us, event | category | flops | bytes accessed | tf_op | source)
XLA Modules:
  0.0 785.7 jit_solution(1983976568813497599)
XLA Ops:
  11.3 5.8 all-gather.1
  42.0 5.8 collective-permute-done.5
  48.1 17.2 %collective-permute-done.6 = bf16[256,1536]{1,0:T(8,128)(2,1)} collective-permute-done((bf16[256,1536]{1,0:T(8,128)(2,1)}, bf16[256,1536]{1,0:T(8,128)(2,1)}, u32[]{:S(2)}, u32[]{:S(2)}) %collective-permute-start.6) | collective-permute-done | bytes 786464 | tf_op jit(solution)/shard_map/ppermute | solution.py:78
  75.8 29.4 %collective-permute-done.8 = bf16[256,1536]{1,0:T(8,128)(2,1)S(1)} collective-permute-done((bf16[256,1536]{1,0:T(8,128)(2,1)}, bf16[256,1536]{1,0:T(8,128)(2,1)S(1)}, u32[]{:S(2)}, u32[]{:S(2)}) %collective-permute-start.8) | collective-permute-done | bytes 786464 | tf_op jit(solution)/shard_map/ppermute | solution.py:78
  123.0 12.8 %collective-permute-done.14 = bf16[128,2048]{1,0:T(8,128)(2,1)S(1)} collective-permute-done((bf16[128,2048]{1,0:T(8,128)(2,1)S(1)}, bf16[128,2048]{1,0:T(8,128)(2,1)S(1)}, u32[]{:S(2)}, u32[]{:S(2)}) %collective-permute-start.14) | collective-permute-done | bytes 524320 | tf_op jit(solution)/shard_map/ppermute | solution.py:78
  143.2 42.3 %collective-permute-done.16.refs_2_ = bf16[2,512,1024]{2,1,0:T(8,128)(2,1)} collective-permute-done((bf16[2,512,1024]{2,1,0:T(8,128)(2,1)}, bf16[2,512,1024]{2,1,0:T(8,128)(2,1)}, u32[]{:S(2)}, u32[]{:S(2)}) %collective-permute-start.16) | collective-permute-done | bytes 2097184 | tf_op jit(solution)/shard_map/ppermute | solution.py:78
  207.8 22.7 %collective-permute-done.22.refs_10_ = bf16[2,1024,512]{2,1,0:T(8,128)(2,1)} collective-permute-done((bf16[2,1024,512]{2,1,0:T(8,128)(2,1)}, bf16[2,1024,512]{2,1,0:T(8,128)(2,1)}, u32[]{:S(2)}, u32[]{:S(2)}) %collective-permute-start.22) | collective-permute-done | bytes 2097184 | tf_op jit(solution)/shard_map/ppermute | solution.py:78
  233.8 41.6 %collective-permute-done.19.refs_6_ = bf16[2,512,1024]{2,1,0:T(8,128)(2,1)} collective-permute-done((bf16[2,512,1024]{2,1,0:T(8,128)(2,1)}, bf16[2,512,1024]{2,1,0:T(8,128)(2,1)}, u32[]{:S(2)}, u32[]{:S(2)}) %collective-permute-start.19) | collective-permute-done | bytes 2097184 | tf_op jit(solution)/shard_map/ppermute | solution.py:78
  297.7 36.5 %shard_map.263 = (bf16[1024,2048]{1,0:T(8,128)(2,1)}, bf16[1024,2048]{1,0:T(8,128)(2,1)}, bf16[1024,2048]{1,0:T(8,128)(2,1)}, f32[2,1024,128]{2,1,0:T(8,128)}) custom-call(bf16[1024,2048]{1,0:T(8,128)(2,1)} %all-gather.5.cloned.1.call-done.x_ref, bf16[1024,2048]{1,0:T(8,128)(2,1)} %all-gather.7.cloned.1.call-done.cot_ref, f32[2,1024,1]{2,1,0:T(8,128)} %copy.86.weight_ref, ...), custom_call_target="tpu_custom_call" | custom-call | tf_op jit(solution)/shard_map/pallas_call | solution.py:286
  334.2 28.6 %shard_map.264 = bf16[1024,2048]{1,0:T(8,128)(2,1)} custom-call(bf16[1024,2048]{1,0:T(8,128)(2,1)} %get-tuple-element.87.gate_grad_ref, bf16[1024,2048]{1,0:T(8,128)(2,1)} %get-tuple-element.88.up_grad_ref, bf16[2,512,1024]{2,1,0:T(8,128)(2,1)} %refs_0_.1, bf16[2,512,1024]{2,1,0:T(8,128)(2,1)} %collective-permute-done.15.refs_1_, ...), custom_call_target="tpu_custom_call" | custom-call | tf_op jit(solution)/shard_map/pallas_call | solution.py:330
  362.9 6.3 fusion.55
  398.7 12.3 %fusion.12 = bf16[1024,2048]{1,0:T(8,128)(2,1)S(1)} fusion(bf16[1024,2048]{1,0:T(8,128)(2,1)} %get-tuple-element.89, bf16[2048,512]{1,0:T(8,128)(2,1)} %bitcast.44, bf16[2048,512]{1,0:T(8,128)(2,1)} %bitcast.43, bf16[2048,512]{1,0:T(8,128)(2,1)} %bitcast.42, bf16[2048,512]{1,0:T(8,128)(2,1)S(1)} %bitcast.285), kind=kOutput, calls=%fused_computation.25 | convolution fusion | flops 8625586176 | bytes 16777216 | tf_op jit(solution)/shard_map/dot_general | solution.py:65
  423.0 6.5 all-to-all-start.1
  437.7 33.5 %collective-permute-done.24 = bf16[2,2,128,2048]{3,2,0,1:T(8,128)(2,1)} collective-permute-done((bf16[2,2,128,2048]{3,2,0,1:T(8,128)(2,1)}, bf16[2,2,128,2048]{3,2,0,1:T(8,128)(2,1)}, u32[]{:S(2)}, u32[]{:S(2)}) %collective-permute-start.24) | collective-permute-done | bytes 2097184 | tf_op jit(solution)/shard_map/ppermute | solution.py:78
  492.5 15.8 %collective-permute-done.25 = bf16[2,128,2048]{2,1,0:T(8,128)(2,1)S(1)} collective-permute-done((bf16[2,128,2048]{2,1,0:T(8,128)(2,1)S(1)}, bf16[2,128,2048]{2,1,0:T(8,128)(2,1)S(1)}, u32[]{:S(2)}, u32[]{:S(2)}) %collective-permute-start.25) | collective-permute-done | bytes 1048608 | tf_op jit(solution)/shard_map/ppermute | solution.py:78
  514.2 18.4 %collective-permute-done.26 = bf16[128,2048]{1,0:T(8,128)(2,1)S(1)} collective-permute-done((bf16[128,2048]{1,0:T(8,128)(2,1)S(1)}, bf16[128,2048]{1,0:T(8,128)(2,1)S(1)}, u32[]{:S(2)}, u32[]{:S(2)}) %collective-permute-start.26) | collective-permute-done | bytes 524320 | tf_op jit(solution)/shard_map/ppermute | solution.py:78
  543.4 6.3 collective-permute-done.28
  557.3 7.1 shard_map.265
  608.1 50.9 %collective-permute-done.35 = bf16[128,2048]{1,0:T(8,128)(2,1)S(1)} collective-permute-done((bf16[128,2048]{1,0:T(8,128)(2,1)S(1)}, bf16[128,2048]{1,0:T(8,128)(2,1)S(1)}, u32[]{:S(2)}, u32[]{:S(2)}) %collective-permute-start.35) | collective-permute-done | bytes 524320 | tf_op jit(solution)/shard_map/ppermute | solution.py:78
  677.7 11.7 %all-to-all-done.2 = f32[8,20,256]{2,1,0:T(8,128)S(1)} async-done(((f32[8,20,256]{2,1,0:T(8,128)}), f32[8,20,256]{2,1,0:T(8,128)S(1)}, u32[]{:S(2)}, u32[]{:S(2)}) %all-to-all-start.2) | async-done | bytes 163872 | tf_op jit(solution)/shard_map/all_to_all | solution.py:608
  696.1 9.1 %all-to-all-done.3 = f32[4,1,1280]{2,1,0:T(1,128)S(1)} async-done(((f32[4,1,1280]{2,1,0:T(1,128)}), f32[4,1,1280]{2,1,0:T(1,128)S(1)}, u32[]{:S(2)}, u32[]{:S(2)}) %all-to-all-start.3) | async-done | bytes 20512 | tf_op jit(solution)/shard_map/all_to_all | solution.py:611
  715.3 10.4 %collective-permute-done.37 = bf16[2,256,512]{2,1,0:T(8,128)(2,1)S(1)} collective-permute-done((bf16[2,256,512]{2,1,0:T(8,128)(2,1)}, bf16[2,256,512]{2,1,0:T(8,128)(2,1)S(1)}, u32[]{:S(2)}, u32[]{:S(2)}) %collective-permute-start.37) | collective-permute-done | bytes 524320 | tf_op jit(solution)/shard_map/ppermute | solution.py:78
  732.2 14.0 %collective-permute-done.41 = bf16[256,512]{1,0:T(8,128)(2,1)S(1)} collective-permute-done((bf16[256,512]{1,0:T(8,128)(2,1)S(1)}, bf16[256,512]{1,0:T(8,128)(2,1)S(1)}, u32[]{:S(2)}, u32[]{:S(2)}) %collective-permute-start.41) | collective-permute-done | bytes 262176 | tf_op jit(solution)/shard_map/ppermute | solution.py:78
  752.9 7.9 %all-to-all-start.4 = ((bf16[4,64,1536]{2,1,0:T(8,128)(2,1)}), bf16[4,64,1536]{2,1,0:T(8,128)(2,1)S(1)}, u32[]{:S(2)}, u32[]{:S(2)}) async-start(bf16[4,64,1536]{2,1,0:T(8,128)(2,1)} %bitcast.284), calls=%async_computation.5 | async-start | bytes 1572864 | tf_op jit(solution)/shard_map/all_to_all | solution.py:593
  (539 shorter events, 316.5 us)
Async XLA Ops:
  7.2 290.5 %all-gather.7.cloned.1.call-start = ((), (), s32[]{:S(2)}) async-start(), calls=%async_computation.7 | async-start | bytes 4718592 | tf_op jit(solution)/shard_map/all_gather | solution.py:408
  21.0 276.7 %all-gather.5.cloned.1.call-start = ((), (), s32[]{:S(2)}) async-start(), calls=%async_computation.6 | async-start | bytes 4718592 | tf_op jit(solution)/shard_map/all_gather | solution.py:478
  47.8 57.9 %collective-permute-start.7 = (bf16[256,1536]{1,0:T(8,128)(2,1)}, bf16[256,1536]{1,0:T(8,128)(2,1)S(1)}, u32[]{:S(2)}, u32[]{:S(2)}) collective-permute-start(bf16[256,1536]{1,0:T(8,128)(2,1)} %collective-permute-done.5), channel_id=1, source_target_pairs={{0,4},{4,0},{8,12},{12,8},{16,20},{20,16},{24,28},{28,24},{1,5},{5... | collective-permute-start | bytes 2359304 | tf_op jit(solution)/shard_map/ppermute | solution.py:78
  140.0 90.4 %collective-permute-start.22 = (bf16[2,1024,512]{2,1,0:T(8,128)(2,1)}, bf16[2,1024,512]{2,1,0:T(8,128)(2,1)}, u32[]{:S(2)}, u32[]{:S(2)}) collective-permute-start(bf16[2,1024,512]{2,1,0:T(8,128)(2,1)} %refs_8_), channel_id=1, source_target_pairs={{0,2},{1,3},{2,0},{3,1},{4,6},{5,7},{6,4},{7,5},{8,10},{9,11},{10,... | collective-permute-start | bytes 6291464 | tf_op jit(solution)/shard_map/ppermute | solution.py:78
  141.5 156.1 %collective-permute-start.21 = (bf16[2,1024,512]{2,1,0:T(8,128)(2,1)}, bf16[2,1024,512]{2,1,0:T(8,128)(2,1)}, u32[]{:S(2)}, u32[]{:S(2)}) collective-permute-start(bf16[2,1024,512]{2,1,0:T(8,128)(2,1)} %refs_8_), channel_id=1, source_target_pairs={{0,1},{1,0},{2,3},{3,2},{4,5},{5,4},{6,7},{7,6},{8,9},{9,8},{10,11... | collective-permute-start | bytes 6291464 | tf_op jit(solution)/shard_map/ppermute | solution.py:78
  143.1 154.5 %collective-permute-start.15 = (bf16[2,512,1024]{2,1,0:T(8,128)(2,1)}, bf16[2,512,1024]{2,1,0:T(8,128)(2,1)}, u32[]{:S(2)}, u32[]{:S(2)}) collective-permute-start(bf16[2,512,1024]{2,1,0:T(8,128)(2,1)} %refs_0_.1), channel_id=1, source_target_pairs={{0,1},{1,0},{2,3},{3,2},{4,5},{5,4},{6,7},{7,6},{8,9},{9,8},{10,11... | collective-permute-start | bytes 6291464 | tf_op jit(solution)/shard_map/ppermute | solution.py:78
  143.1 132.3 %collective-permute-start.19 = (bf16[2,512,1024]{2,1,0:T(8,128)(2,1)}, bf16[2,512,1024]{2,1,0:T(8,128)(2,1)}, u32[]{:S(2)}, u32[]{:S(2)}) collective-permute-start(bf16[2,512,1024]{2,1,0:T(8,128)(2,1)} %refs_4_.1), channel_id=1, source_target_pairs={{0,2},{1,3},{2,0},{3,1},{4,6},{5,7},{6,4},{7,5},{8,10},{9,11},{10,... | collective-permute-start | bytes 6291464 | tf_op jit(solution)/shard_map/ppermute | solution.py:78
  185.5 91.7 %collective-permute-start.17 = (bf16[2,512,1024]{2,1,0:T(8,128)(2,1)}, bf16[2,512,1024]{2,1,0:T(8,128)(2,1)}, u32[]{:S(2)}, u32[]{:S(2)}) collective-permute-start(bf16[2,512,1024]{2,1,0:T(8,128)(2,1)} %collective-permute-done.16.refs_2_), channel_id=1, source_target_pairs={{0,1},{1,0},{2,3},{3,2},{4,5},{5,4},{6,7},{7,6},{8,9},{9,8},{10,11... | collective-permute-start | bytes 6291464 | tf_op jit(solution)/shard_map/ppermute | solution.py:78
  190.8 86.5 %all-to-all-start = ((f32[8,2,128]{2,1,0:T(2,128)}), f32[8,2,128]{2,1,0:T(2,128)S(1)}, u32[]{:S(2)}, u32[]{:S(2)}) async-start(f32[8,2,128]{2,1,0:T(2,128)} %bitcast.37), calls=%async_computation | async-start | bytes 16384 | tf_op jit(solution)/shard_map/all_to_all | solution.py:479
  196.5 337.1 %reduce-scatter.2.cloned.1.call-start = ((), (), s32[]{:S(2)}) async-start(), calls=%async_computation.8 | async-start | bytes 4718592 | tf_op jit(solution)/shard_map/reduce_scatter | solution.py:496
  230.5 67.1 %collective-permute-start.18 = (bf16[2,512,1024]{2,1,0:T(8,128)(2,1)}, bf16[2,512,1024]{2,1,0:T(8,128)(2,1)}, u32[]{:S(2)}, u32[]{:S(2)}) collective-permute-start(bf16[2,512,1024]{2,1,0:T(8,128)(2,1)} %refs_4_.1), channel_id=1, source_target_pairs={{0,1},{1,0},{2,3},{3,2},{4,5},{5,4},{6,7},{7,6},{8,9},{9,8},{10,11... | collective-permute-start | bytes 6291464 | tf_op jit(solution)/shard_map/ppermute | solution.py:78
  414.5 56.7 %collective-permute-start.24 = (bf16[2,2,128,2048]{3,2,0,1:T(8,128)(2,1)}, bf16[2,2,128,2048]{3,2,0,1:T(8,128)(2,1)}, u32[]{:S(2)}, u32[]{:S(2)}) collective-permute-start(bf16[2,2,128,2048]{3,2,0,1:T(8,128)(2,1)} %bitcast.274), channel_id=1, source_target_pairs={{0,4},{4,0},{8,12},{12,8},{16,20},{20,16},{24,28},{28,24},{1,5},{5... | collective-permute-start | bytes 6291464 | tf_op jit(solution)/shard_map/ppermute | solution.py:78
  418.6 55.9 %collective-permute-start.50 = (bf16[512,2048]{1,0:T(8,128)(2,1)}, bf16[512,2048]{1,0:T(8,128)(2,1)}, u32[]{:S(2)}, u32[]{:S(2)}) collective-permute-start(bf16[512,2048]{1,0:T(8,128)(2,1)} %fusion.55), channel_id=1, source_target_pairs={{0,1},{1,0},{2,3},{3,2},{4,5},{5,4},{6,7},{7,6},{8,9},{9,8},{10,11... | collective-permute-start | bytes 6291464 | tf_op jit(solution)/shard_map/ppermute | solution.py:78
  420.3 67.9 %collective-permute-start.52 = (bf16[512,2048]{1,0:T(8,128)(2,1)}, bf16[512,2048]{1,0:T(8,128)(2,1)}, u32[]{:S(2)}, u32[]{:S(2)}) collective-permute-start(bf16[512,2048]{1,0:T(8,128)(2,1)} %fusion.61), channel_id=1, source_target_pairs={{0,1},{1,0},{2,3},{3,2},{4,5},{5,4},{6,7},{7,6},{8,9},{9,8},{10,11... | collective-permute-start | bytes 6291464 | tf_op jit(solution)/shard_map/ppermute | solution.py:78
  420.3 90.0 %collective-permute-start.53 = (bf16[512,2048]{1,0:T(8,128)(2,1)}, bf16[512,2048]{1,0:T(8,128)(2,1)}, u32[]{:S(2)}, u32[]{:S(2)}) collective-permute-start(bf16[512,2048]{1,0:T(8,128)(2,1)} %fusion.53), channel_id=1, source_target_pairs={{0,1},{1,0},{2,3},{3,2},{4,5},{5,4},{6,7},{7,6},{8,9},{9,8},{10,11... | collective-permute-start | bytes 6291464 | tf_op jit(solution)/shard_map/ppermute | solution.py:78
  423.0 110.6 %all-to-all-start.1 = ((f32[8,2,128]{2,1,0:T(2,128)}), f32[8,2,128]{2,1,0:T(2,128)S(1)}, u32[]{:S(2)}, u32[]{:S(2)}) async-start(f32[8,2,128]{2,1,0:T(2,128)} %bitcast.53), calls=%async_computation.2 | async-start | bytes 16384 | tf_op jit(solution)/shard_map/all_to_all | solution.py:498
  474.6 63.1 %collective-permute-start.49 = (bf16[512,2048]{1,0:T(8,128)(2,1)}, bf16[512,2048]{1,0:T(8,128)(2,1)}, u32[]{:S(2)}, u32[]{:S(2)}) collective-permute-start(bf16[512,2048]{1,0:T(8,128)(2,1)} %fusion.63), channel_id=1, source_target_pairs={{0,1},{1,0},{2,3},{3,2},{4,5},{5,4},{6,7},{7,6},{8,9},{9,8},{10,11... | collective-permute-start | bytes 6291464 | tf_op jit(solution)/shard_map/ppermute | solution.py:78
  478.4 59.2 %collective-permute-start.51 = (bf16[512,2048]{1,0:T(8,128)(2,1)}, bf16[512,2048]{1,0:T(8,128)(2,1)}, u32[]{:S(2)}, u32[]{:S(2)}) collective-permute-start(bf16[512,2048]{1,0:T(8,128)(2,1)} %add_convert_fusion), channel_id=1, source_target_pairs={{0,2},{1,3},{2,0},{3,1},{4,6},{5,7},{6,4},{7,5},{8,10},{9,11},{10,... | collective-permute-start | bytes 6291464 | tf_op jit(solution)/shard_map/ppermute | solution.py:78
  587.6 79.6 %collective-permute-start.39 = (bf16[2,2,256,512]{3,2,0,1:T(8,128)(2,1)}, bf16[2,2,256,512]{3,2,0,1:T(8,128)(2,1)}, u32[]{:S(2)}, u32[]{:S(2)}) collective-permute-start(bf16[2,2,256,512]{3,2,0,1:T(8,128)(2,1)} %bitcast.276), channel_id=1, source_target_pairs={{0,4},{4,0},{8,12},{12,8},{16,20},{20,16},{24,28},{28,24},{1,5},{5... | collective-permute-start | bytes 3145736 | tf_op jit(solution)/shard_map/ppermute | solution.py:78
  590.7 83.3 %collective-permute-start.36 = (bf16[2,2,256,512]{3,2,0,1:T(8,128)(2,1)}, bf16[2,2,256,512]{3,2,0,1:T(8,128)(2,1)}, u32[]{:S(2)}, u32[]{:S(2)}) collective-permute-start(bf16[2,2,256,512]{3,2,0,1:T(8,128)(2,1)} %bitcast.277), channel_id=1, source_target_pairs={{0,4},{4,0},{8,12},{12,8},{16,20},{20,16},{24,28},{28,24},{1,5},{5... | collective-permute-start | bytes 3145736 | tf_op jit(solution)/shard_map/ppermute | solution.py:78
  601.0 162.8 %collective-permute-start.54 = (bf16[512,2048]{1,0:T(8,128)(2,1)}, bf16[512,2048]{1,0:T(8,128)(2,1)}, u32[]{:S(2)}, u32[]{:S(2)}) collective-permute-start(bf16[512,2048]{1,0:T(8,128)(2,1)} %convert_add_fusion.5), channel_id=1, source_target_pairs={{0,2},{1,3},{2,0},{3,1},{4,6},{5,7},{6,4},{7,5},{8,10},{9,11},{10,... | collective-permute-start | bytes 6291464 | tf_op jit(solution)/shard_map/ppermute | solution.py:78
  603.6 55.4 %collective-permute-start.35 = (bf16[128,2048]{1,0:T(8,128)(2,1)S(1)}, bf16[128,2048]{1,0:T(8,128)(2,1)S(1)}, u32[]{:S(2)}, u32[]{:S(2)}) collective-permute-start(bf16[128,2048]{1,0:T(8,128)(2,1)S(1)} %fusion.44), channel_id=1, source_target_pairs={{0,2},{1,3},{2,0},{3,1},{4,6},{5,7},{6,4},{7,5},{8,10},{9,11},{10,... | collective-permute-start | bytes 1572872 | tf_op jit(solution)/shard_map/ppermute | solution.py:78
  606.7 163.4 %collective-permute-start.57 = (bf16[2048,512]{1,0:T(8,128)(2,1)}, bf16[2048,512]{1,0:T(8,128)(2,1)}, u32[]{:S(2)}, u32[]{:S(2)}) collective-permute-start(bf16[2048,512]{1,0:T(8,128)(2,1)} %convert_add_fusion.2), channel_id=1, source_target_pairs={{0,2},{1,3},{2,0},{3,1},{4,6},{5,7},{6,4},{7,5},{8,10},{9,11},{10,... | collective-permute-start | bytes 6291464 | tf_op jit(solution)/shard_map/ppermute | solution.py:78
  659.0 48.7 %collective-permute-start.46 = (bf16[2,64,2048]{2,1,0:T(8,128)(2,1)}, bf16[2,64,2048]{2,1,0:T(8,128)(2,1)}, u32[]{:S(2)}, u32[]{:S(2)}) collective-permute-start(bf16[2,64,2048]{2,1,0:T(8,128)(2,1)} %dynamic-slice_bitcast_fusion.2), channel_id=1, source_target_pairs={{0,16},{4,20},{8,24},{12,28},{16,0},{20,4},{24,8},{28,12},{1,17},{... | collective-permute-start | bytes 1572872 | tf_op jit(solution)/shard_map/ppermute | solution.py:78
  (149 other events, 2615.2 us)
Sparse Core Ops, SparseCore 0:
  21.1 92.4 all-gather.6
  139.1 70.6 all-gather.4
  363.0 95.5 reduce-scatter.1
